TPU v7x, 32 devices: a whole 2x2x4 slice. The times are simulated.
32 devices in a mesh: pair: 8 (over z, x), occ: 4 (over y, core).
Axes of the slice: x: 2, y: 2, z: 4, core: 2. Of those that a mesh axis runs over, the one named last changes fastest.
Arguments:
- integrals: bfloat16 [8, 64, 64, 1024], P('pair', None, None, 'occ'), may hold values from -6 to 6
- occ_coeffs: bfloat16 [6144, 128], replicated, may hold values from -0.125 to 0.125
- virt_coeffs: bfloat16 [6144, 5120], P(None, 'pair'), may hold values from -0.078125 to 0.078125
- block_ids: int32 [2, 8, 64], P(None, 'pair'), may hold values from 0 to 95, as said below
- live_mask: int32 [8, 64], P('pair'), may hold values from 0 to 1, as said below
Outputs:
- factors: bfloat16 [128, 16, 5120], P('occ', None, 'pair')
Inputs may be any that keep to these rules, and one draw needn't show every extreme that they name: `block_ids`: slot s of pair index p holds a nu block N with N // 12 == s // 8; each (mu block, nu block) pair is held by at most one slot of all pair indices. `live_mask`: among the 8 slots s with the same s // 8 of one pair index, at most 4 are 1, and exactly 4 for some such group of every pair index.
All inputs are finite; a program needn't handle non-finite values.
Results may differ from a plain program's by a relative error of at most 0.017.
Values may be sent and summed in bfloat16 or wider, within the bound.
No kernel may reach another device: no remote copies, remote signals or barrier semaphores. Data moves between devices by JAX's collectives and lax.ppermute only.
A program may use at most 64 MiB of HBM per device.

v0:
```python
import functools

import jax
import jax.numpy as jnp
from jax import lax
from jax.experimental import pallas as pl
from jax.experimental.pallas import tpu as pltpu
from jax.sharding import PartitionSpec as P


LIVE = 4
TAIL = 16
GRANT = 16 * 2**20


def pack_kernel(owned, ids_ref, live_ref, blocks_ref, *refs):
    out_refs = refs[:-2]
    pick_ref, sems = refs[-2:]
    owners, _, lanes = out_refs[0].shape
    width = blocks_ref.shape[1]
    group = live_ref.shape[1] // owners
    row = lax.broadcasted_iota(jnp.int32, (TAIL, 128), 0)
    lane = lax.broadcasted_iota(jnp.int32, (TAIL, 128), 1)

    def copy(owner, k, slot, c):
        return pltpu.make_async_copy(
            blocks_ref.at[slot, :, pl.ds(c * lanes, lanes)],
            out_refs[c].at[owner, pl.ds(k * width, width), :],
            sems.at[owner, k, c],
        )

    @pl.loop(0, owners)
    def _(owner):
        base = owner * group
        count = jnp.int32(0)
        for j in range(group):
            pick_ref[jnp.minimum(count, LIVE)] = base + j
            count = count + live_ref[0, base + j]
        tile = jnp.zeros((TAIL, 128), jnp.int32)
        for k in range(LIVE):
            slot = jnp.where(k < count, pick_ref[k], base)
            for c in range(len(out_refs)):
                copy(owner, k, slot, c).start()
            mu = ids_ref[0, 0, slot]
            nu = jnp.where(k < count, lax.rem(ids_ref[1, 0, slot], owned), owned)
            tile = jnp.where((row == 0) & (lane == k), mu, tile)
            tile = jnp.where((row == 0) & (lane == LIVE + k), nu, tile)
        out_refs[0][owner, LIVE * width :, :] = tile.astype(jnp.float32).astype(jnp.bfloat16)

    @pl.loop(0, owners)
    def _(owner):
        for k in range(LIVE):
            for c in range(len(out_refs)):
                copy(owner, k, 0, c).wait()


def pack(block_ids, live_mask, blocks, owners, owned):
    _, width, minor = blocks.shape
    chunks = minor // 128
    shapes = [
        jax.ShapeDtypeStruct((owners, LIVE * width + (0 if c else TAIL), 128), jnp.bfloat16)
        for c in range(chunks)
    ]
    return pl.pallas_call(
        functools.partial(pack_kernel, owned),
        out_shape=shapes,
        in_specs=[
            pl.BlockSpec(memory_space=pltpu.SMEM),
            pl.BlockSpec(memory_space=pltpu.SMEM),
            pl.BlockSpec(memory_space=pl.ANY),
        ],
        out_specs=[pl.BlockSpec(memory_space=pltpu.VMEM)] * chunks,
        scratch_shapes=[
            pltpu.SMEM((LIVE + 1,), jnp.int32),
            pltpu.SemaphoreType.DMA((owners, LIVE, chunks)),
        ],
        compiler_params=pltpu.CompilerParams(vmem_limit_bytes=GRANT),
        name="pack_live",
    )(block_ids, live_mask, blocks)


def half_kernel(owned, width, me_ref, tail_ref, got_ref, coeff_ref, *refs):
    out_refs = refs[:-4]
    ids_vmem, ids_smem, total, sem = refs[-4:]
    owners = got_ref.shape[0]
    aux = got_ref.shape[2] // width
    for p in range(owners):
        ids_vmem[p : p + 1, :] = tail_ref[p, 0:1, :].astype(jnp.float32).astype(jnp.int32)
    ids = pltpu.make_async_copy(ids_vmem, ids_smem, sem)
    ids.start()
    total[...] = jnp.zeros_like(total)
    ids.wait()

    @pl.loop(0, owners)
    def _(p):
        for k in range(LIVE):
            mu = ids_smem[p, k]
            nu = ids_smem[p, LIVE + k]
            block = got_ref[p, k * width : (k + 1) * width, :]
            stacked = jnp.concatenate(
                [block[:, q * width : (q + 1) * width] for q in range(aux)], axis=0
            )
            coeff = coeff_ref[pl.ds(pl.multiple_of(mu * width, width), width), :]
            total[nu] += lax.dot_general(
                coeff, stacked, (((0,), (1,)), ((), ())), preferred_element_type=jnp.float32
            )

    slab = total.shape[1] // len(out_refs)
    for j, out_ref in enumerate(out_refs):
        start = pl.multiple_of((me_ref[0] ^ j) * slab, slab)
        for b in range(0, owned, 2):
            pair = [total[c, pl.ds(start, slab), :] for c in range(b, min(b + 2, owned))]
            for q in range(aux):
                cut = [t[:, q * width : (q + 1) * width] for t in pair]
                piece = cut[0] if len(cut) == 1 else jnp.concatenate(cut, axis=1)
                out_ref[q * slab : (q + 1) * slab, b * width : b * width + piece.shape[1]] = (
                    piece.astype(jnp.bfloat16)
                )


def half_transform(me, first, got, coeffs, owned, width, occ):
    owners, _, lanes = got.shape
    aux = lanes // width
    occ_count = coeffs.shape[1]
    shape = jax.ShapeDtypeStruct((aux * occ_count // occ, owned * width), jnp.bfloat16)
    vmem = pl.BlockSpec(memory_space=pltpu.VMEM)

    def whole(*dims):
        return pl.BlockSpec(dims, lambda g: (0,) * len(dims))

    return pl.pallas_call(
        functools.partial(half_kernel, owned, width),
        grid=(1,),
        out_shape=[shape] * occ,
        in_specs=[
            pl.BlockSpec(memory_space=pltpu.SMEM),
            pl.BlockSpec((owners, TAIL, lanes), lambda g: (0, LIVE * width // TAIL, 0)),
            pl.BlockSpec((owners, LIVE * width, lanes), lambda g: (0, 0, 0)),
            whole(*coeffs.shape),
        ],
        out_specs=[whole(*shape.shape)] * occ,
        scratch_shapes=[
            pltpu.VMEM((owners, lanes), jnp.int32),
            pltpu.SMEM((owners, lanes), jnp.int32),
            pltpu.VMEM((owned + 1, occ_count, lanes), jnp.float32),
            pltpu.SemaphoreType.DMA,
        ],
        cost_estimate=pl.CostEstimate(
            flops=2 * owners * LIVE * width * lanes * occ_count,
            bytes_accessed=2 * (got.size + coeffs.size + occ * shape.size),
            transcendentals=0,
        ),
        compiler_params=pltpu.CompilerParams(vmem_limit_bytes=GRANT),
        name="half_transform",
    )(me, first, got, coeffs)


def place_kernel(occ, me_ref, *refs):
    in_refs, (out_ref, wide) = refs[:-2], refs[-2:]
    slab, aux, _ = out_ref.shape
    chunks = len(in_refs)
    local = aux // (occ * chunks)
    for c, in_ref in enumerate(in_refs):
        for j in range(occ):
            for q in range(local):
                at = (me_ref[0] ^ j) * (chunks * local) + c * local + q
                row = (j * local + q) * slab
                for t in range(wide.shape[0]):
                    wide[t, pl.ds(at, slab, stride=aux), :] = in_ref[
                        row : row + slab, t * 128 : (t + 1) * 128
                    ]
    for t in range(wide.shape[0]):
        out_ref[:, :, t * 128 : (t + 1) * 128] = (
            wide[t].reshape(slab, aux, 128).astype(out_ref.dtype)
        )


def place(me, parts, occ, slab):
    rows, columns = parts[0].shape
    aux = rows * len(parts) // slab
    vmem = pl.BlockSpec(memory_space=pltpu.VMEM)
    return pl.pallas_call(
        functools.partial(place_kernel, occ),
        out_shape=jax.ShapeDtypeStruct((slab, aux, columns), jnp.bfloat16),
        in_specs=[pl.BlockSpec(memory_space=pltpu.SMEM)] + [vmem] * len(parts),
        out_specs=vmem,
        scratch_shapes=[pltpu.VMEM((columns // 128, slab * aux, 128), jnp.float32)],
        compiler_params=pltpu.CompilerParams(vmem_limit_bytes=GRANT),
        name="place",
    )(me, *parts)


def on_device(integrals, occ_coeffs, virt_coeffs, block_ids, live_mask):
    blocks = integrals[0]
    width = blocks.shape[1]
    occ_count = occ_coeffs.shape[1]
    owners = lax.axis_size("pair")
    occ = lax.axis_size("occ")
    owned = occ_coeffs.shape[0] // width // owners
    slab = occ_count // occ
    outer = owners // 2
    rows = owned * width
    me = lax.axis_index("occ").astype(jnp.int32)
    here = lax.axis_index("pair")

    def across(array, j):
        if j == 0:
            return array
        return lax.ppermute(array, "occ", [(o, o ^ j) for o in range(occ)])

    def along(array):
        return lax.ppermute(
            array, "pair", [(p, (p // 2 + 1) % outer * 2 + p % 2) for p in range(owners)]
        )

    def swap(array):
        return lax.ppermute(array, "pair", [(p, p ^ 1) for p in range(owners)])

    def gather(piece, last):
        own, other = [piece], [swap(piece)]
        for shift in range(1, outer):
            own.append(along(own[-1]))
            if last and shift == outer - 1:
                other.append(along(other[-1]))
            else:
                other.append(swap(own[-1]))
        return own, other

    def second_half(own, other):
        total = None
        for shift in range(outer):
            for flip, array in enumerate((own[shift], other[shift])):
                source = (here // 2 - shift) % outer * 2 + (here % 2 ^ flip)
                part = lax.dynamic_slice_in_dim(virt_coeffs, source * rows, rows, axis=0)
                term = jnp.dot(array, part, preferred_element_type=jnp.float32)
                total = term if total is None else total + term
        return total

    sends = pack(block_ids, live_mask, blocks, owners, owned)
    gots = []
    for send in sends:
        gots.append(lax.all_to_all(send, "pair", split_axis=0, concat_axis=0, tiled=True))
    results = []
    for c, got in enumerate(gots):
        halves = half_transform(me.reshape(1), gots[0], got, occ_coeffs, owned, width, occ)
        parts = [across(halves[j], j) for j in range(occ)]
        piece = jnp.concatenate(parts, axis=0) if occ > 1 else parts[0]
        results.append(second_half(*gather(piece, c == len(gots) - 1)))
    return place(me.reshape(1), results, occ, slab)


def solution(mesh):
    return jax.shard_map(
        on_device,
        mesh=mesh,
        in_specs=(
            P("pair", None, None, "occ"),
            P(),
            P(None, "pair"),
            P(None, "pair", None),
            P("pair", None),
        ),
        out_specs=P("occ", None, "pair"),
        check_vma=False,
    )
```

profile of v0, /device:TPU:0, one launch (start us, length us, event | category | flops | bytes accessed | tf_op | source)
XLA Modules:
  0.0 126.9 jit_solution(2286048707699429368)
XLA Ops:
  0.0 1.6 %copy-done.1 = bf16[1,64,64,256]{3,2,1,0:T(8,128)(2,1)S(1)} copy-done((bf16[1,64,64,256]{3,2,1,0:T(8,128)(2,1)S(1)}, bf16[1,64,64,256]{3,2,1,0:T(8,128)(2,1)}, u32[]{:S(2)}) %copy-start.1) | copy-done | bytes 2097176
  1.6 0.7 copy-done.2
  2.3 0.7 copy-done.3
  2.9 2.8 %pack_live.1 = (bf16[8,272,128]{2,1,0:T(8,128)(2,1)}, bf16[8,256,128]{2,1,0:T(8,128)(2,1)S(1)}) custom-call(s32[2,1,64]{2,1,0:T(1,128)S(1)} %copy-done.2, s32[1,64]{1,0:T(1,128)S(1)} %copy-done.3, bf16[64,64,256]{2,1,0:T(8,128)(2,1)S(1)} %bitcast.18), custom_call_target="tpu_custom_call" | custom-call | tf_op jit(solution)/shard_map/pack_live/pallas_call | solution.py:64
  5.8 21.6 %all_to_all.10.got_ref = bf16[8,256,128]{2,1,0:T(8,128)(2,1)S(1)} all-to-all(bf16[8,256,128]{2,1,0:T(8,128)(2,1)S(1)} %get-tuple-element.20), channel_id=1, replica_groups=mesh['pair'=8,'occ'=4] {'pair'}, dimensions={0} | all-to-all | bytes 1048576 | tf_op jit(solution)/shard_map/all_to_all | solution.py:242
  27.4 3.6 %all-to-all-start = ((bf16[8,272,128]{2,1,0:T(8,128)(2,1)}), bf16[8,272,128]{2,1,0:T(8,128)(2,1)S(1)}, u32[]{:S(2)}, u32[]{:S(2)}) async-start(bf16[8,272,128]{2,1,0:T(8,128)(2,1)} %get-tuple-element.15), calls=%async_computation | async-start | bytes 1114112 | tf_op jit(solution)/shard_map/all_to_all | solution.py:242
  31.0 14.9 %all-to-all-done.tail_ref.got_ref = bf16[8,272,128]{2,1,0:T(8,128)(2,1)S(1)} async-done(((bf16[8,272,128]{2,1,0:T(8,128)(2,1)}), bf16[8,272,128]{2,1,0:T(8,128)(2,1)S(1)}, u32[]{:S(2)}, u32[]{:S(2)}) %all-to-all-start) | async-done | bytes 557088 | tf_op jit(solution)/shard_map/all_to_all | solution.py:242
  45.8 1.4 %copy-done = bf16[6144,128]{1,0:T(8,128)(2,1)S(1)} copy-done((bf16[6144,128]{1,0:T(8,128)(2,1)S(1)}, bf16[6144,128]{1,0:T(8,128)(2,1)}, u32[]{:S(2)}) %copy-start) | copy-done | bytes 1572888
  47.3 3.0 %half_transform.3 = (bf16[64,768]{1,0:T(8,128)(2,1)S(1)}, bf16[64,768]{1,0:T(8,128)(2,1)S(1)}, bf16[64,768]{1,0:T(8,128)(2,1)S(1)}, bf16[64,768]{1,0:T(8,128)(2,1)S(1)}) custom-call(s32[1]{0:T(128)} %bitcast.me_ref, bf16[8,272,128]{2,1,0:T(8,128)(2,1)S(1)} %all-to-all-done.tail_ref.got_ref, bf16[8,256,128]{2,1,0:T(8,128)(2,1)S(1)} %all_to_all.10.got_ref, ...), custom_call_target="tpu_custom_call" | custom-call | flops 67108864 | bytes 2490368 | tf_op jit(solution)/shard_map/half_transform/pallas_call | solution.py:131
  50.4 1.6 %collective-permute-start.11 = (bf16[64,768]{1,0:T(8,128)(2,1)S(1)}, bf16[64,768]{1,0:T(8,128)(2,1)S(1)}, u32[]{:S(2)}, u32[]{:S(2)}) collective-permute-start(bf16[64,768]{1,0:T(8,128)(2,1)S(1)} %get-tuple-element.23), channel_id=1, source_target_pairs={{0,2},{1,3},{2,0},{3,1},{4,6},{5,7},{6,4},{7,5},{8,10},{9,11},{10,... | collective-permute-start | bytes 294920 | tf_op jit(solution)/shard_map/ppermute | solution.py:209
  52.2 3.0 %half_transform.2 = (bf16[64,768]{1,0:T(8,128)(2,1)S(1)}, bf16[64,768]{1,0:T(8,128)(2,1)S(1)}, bf16[64,768]{1,0:T(8,128)(2,1)S(1)}, bf16[64,768]{1,0:T(8,128)(2,1)S(1)}) custom-call(s32[1]{0:T(128)} %bitcast.me_ref, bf16[8,272,128]{2,1,0:T(8,128)(2,1)S(1)} %all-to-all-done.tail_ref.got_ref, bf16[8,272,128]{2,1,0:T(8,128)(2,1)S(1)} %all-to-all-done.tail_ref.got_ref, ...), custom_call_target="tpu_custom_call" | custom-call | flops 67108864 | bytes 2523136 | tf_op jit(solution)/shard_map/half_transform/pallas_call | solution.py:131
  55.7 1.5 %collective-permute-start.1 = (bf16[64,768]{1,0:T(8,128)(2,1)S(1)}, bf16[64,768]{1,0:T(8,128)(2,1)S(1)}, u32[]{:S(2)}, u32[]{:S(2)}) collective-permute-start(bf16[64,768]{1,0:T(8,128)(2,1)S(1)} %get-tuple-element.18), channel_id=1, source_target_pairs={{0,2},{1,3},{2,0},{3,1},{4,6},{5,7},{6,4},{7,5},{8,10},{9,11},{10,... | collective-permute-start | bytes 294920 | tf_op jit(solution)/shard_map/ppermute | solution.py:209
  57.4 0.7 collective-permute-start.14
  58.1 2.7 %collective-permute-done.1 = bf16[64,768]{1,0:T(8,128)(2,1)S(1)} collective-permute-done((bf16[64,768]{1,0:T(8,128)(2,1)S(1)}, bf16[64,768]{1,0:T(8,128)(2,1)S(1)}, u32[]{:S(2)}, u32[]{:S(2)}) %collective-permute-start.1) | collective-permute-done | bytes 98336 | tf_op jit(solution)/shard_map/ppermute | solution.py:209
  60.8 1.6 %collective-permute-done.2 = bf16[64,768]{1,0:T(8,128)(2,1)S(1)} collective-permute-done((bf16[64,768]{1,0:T(8,128)(2,1)S(1)}, bf16[64,768]{1,0:T(8,128)(2,1)S(1)}, u32[]{:S(2)}, u32[]{:S(2)}) %collective-permute-start.2) | collective-permute-done | bytes 98336 | tf_op jit(solution)/shard_map/ppermute | solution.py:209
  62.4 0.7 collective-permute-start.4
  63.1 1.0 collective-permute-start.13
  64.1 1.1 collective-permute-start.3
  65.1 6.1 %collective-permute-done.14 = bf16[256,768]{1,0:T(8,128)(2,1)S(1)} collective-permute-done((bf16[256,768]{1,0:T(8,128)(2,1)S(1)}, bf16[256,768]{1,0:T(8,128)(2,1)S(1)}, u32[]{:S(2)}, u32[]{:S(2)}) %collective-permute-start.14) | collective-permute-done | bytes 393248 | tf_op jit(solution)/shard_map/ppermute | solution.py:212
  71.2 1.4 %collective-permute-start.15 = (bf16[256,768]{1,0:T(8,128)(2,1)S(1)}, bf16[256,768]{1,0:T(8,128)(2,1)S(1)}, u32[]{:S(2)}, u32[]{:S(2)}) collective-permute-start(bf16[256,768]{1,0:T(8,128)(2,1)S(1)} %collective-permute-done.14), channel_id=1, source_target_pairs={{0,4},{4,0},{8,12},{12,8},{16,20},{20,16},{24,28},{28,24},{1,5},{5... | collective-permute-start | bytes 1179656 | tf_op jit(solution)/shard_map/ppermute | solution.py:217
  72.6 7.0 %collective-permute-done.4 = bf16[256,768]{1,0:T(8,128)(2,1)S(1)} collective-permute-done((bf16[256,768]{1,0:T(8,128)(2,1)S(1)}, bf16[256,768]{1,0:T(8,128)(2,1)S(1)}, u32[]{:S(2)}, u32[]{:S(2)}) %collective-permute-start.4) | collective-permute-done | bytes 393248 | tf_op jit(solution)/shard_map/ppermute | solution.py:212
  79.6 1.8 %fusion.20 = f32[256,640]{1,0:T(8,128)S(1)} fusion(bf16[256,768]{1,0:T(8,128)(2,1)S(1)} %collective-permute-done.14, bf16[6144,640]{1,0:T(8,128)(2,1)} %param.7, s32[]{:T(128)S(6)} %select_n.134), kind=kOutput, calls=%fused_computation.28 | convolution fusion | flops 251658240 | bytes 2031620 | tf_op jit(solution)/shard_map/dot_general | solution.py:235
  81.5 1.7 %fusion.22 = f32[256,640]{1,0:T(8,128)S(1)} fusion(bf16[256,768]{1,0:T(8,128)(2,1)S(1)} %collective-permute-done.4, bf16[6144,640]{1,0:T(8,128)(2,1)} %param.7, s32[]{:T(128)S(6)} %select_n.134), kind=kOutput, calls=%fused_computation.30 | convolution fusion | flops 251658240 | bytes 2031620 | tf_op jit(solution)/shard_map/dot_general | solution.py:235
  83.2 1.5 %collective-permute-start.5 = (bf16[256,768]{1,0:T(8,128)(2,1)S(1)}, bf16[256,768]{1,0:T(8,128)(2,1)S(1)}, u32[]{:S(2)}, u32[]{:S(2)}) collective-permute-start(bf16[256,768]{1,0:T(8,128)(2,1)S(1)} %collective-permute-done.4), channel_id=1, source_target_pairs={{0,4},{4,0},{8,12},{12,8},{16,20},{20,16},{24,28},{28,24},{1,5},{5... | collective-permute-start | bytes 1179656 | tf_op jit(solution)/shard_map/ppermute | solution.py:217
  84.7 1.7 %fusion.24 = f32[256,640]{1,0:T(8,128)S(1)} fusion(bf16[256,768]{1,0:T(8,128)(2,1)S(1)} %collective-permute-done.13, bf16[6144,640]{1,0:T(8,128)(2,1)} %param.7, s32[]{:T(128)S(6)} %select_n.132), kind=kOutput, calls=%fused_computation.32 | convolution fusion | flops 251658240 | bytes 2031620 | tf_op jit(solution)/shard_map/dot_general | solution.py:235
  86.4 1.8 %fusion.2 = f32[256,640]{1,0:T(8,128)S(1)} fusion(f32[256,640]{1,0:T(8,128)S(1)} %fusion.20, f32[256,640]{1,0:T(8,128)S(1)} %fusion.24, bf16[256,768]{1,0:T(8,128)(2,1)S(1)} %constant_dynamic-update-slice_fusion.4, bf16[6144,640]{1,0:T(8,128)(2,1)} %param.7, s32[]{:T(128)S(6)} %select_n.131), kind=kOutput, calls=%fused_computation.6 | convolution fusion | flops 251985920 | bytes 3342340 | tf_op jit(solution)/shard_map/dot_general | solution.py:235
  88.2 1.7 %fusion.26 = f32[256,640]{1,0:T(8,128)S(1)} fusion(bf16[256,768]{1,0:T(8,128)(2,1)S(1)} %collective-permute-done.3, bf16[6144,640]{1,0:T(8,128)(2,1)} %param.7, s32[]{:T(128)S(6)} %select_n.132), kind=kOutput, calls=%fused_computation.34 | convolution fusion | flops 251658240 | bytes 2031620 | tf_op jit(solution)/shard_map/dot_general | solution.py:235
  89.9 1.7 %fusion.5 = f32[256,640]{1,0:T(8,128)S(1)} fusion(f32[256,640]{1,0:T(8,128)S(1)} %fusion.22, f32[256,640]{1,0:T(8,128)S(1)} %fusion.26, bf16[256,768]{1,0:T(8,128)(2,1)S(1)} %constant_dynamic-update-slice_fusion, bf16[6144,640]{1,0:T(8,128)(2,1)} %param.7, s32[]{:T(128)S(6)} %select_n.131), kind=kOutput, calls=%fused_computation.13 | convolution fusion | flops 251985920 | bytes 3342340 | tf_op jit(solution)/shard_map/dot_general | solution.py:235
  91.7 0.7 collective-permute-start.17
  92.3 4.2 %collective-permute-done.6 = bf16[256,768]{1,0:T(8,128)(2,1)S(1)} collective-permute-done((bf16[256,768]{1,0:T(8,128)(2,1)S(1)}, bf16[256,768]{1,0:T(8,128)(2,1)S(1)}, u32[]{:S(2)}, u32[]{:S(2)}) %collective-permute-start.6) | collective-permute-done | bytes 393248 | tf_op jit(solution)/shard_map/ppermute | solution.py:212
  96.5 1.7 %fusion.14 = f32[256,640]{1,0:T(8,128)S(1)} fusion(bf16[256,768]{1,0:T(8,128)(2,1)S(1)} %collective-permute-done.16, bf16[6144,640]{1,0:T(8,128)(2,1)} %param.7, s32[]{:T(128)S(6)} %select_n.137), kind=kOutput, calls=%fused_computation.22 | convolution fusion | flops 251658240 | bytes 2031620 | tf_op jit(solution)/shard_map/dot_general | solution.py:235
  98.2 1.5 %collective-permute-start.7 = (bf16[256,768]{1,0:T(8,128)(2,1)S(1)}, bf16[256,768]{1,0:T(8,128)(2,1)S(1)}, u32[]{:S(2)}, u32[]{:S(2)}) collective-permute-start(bf16[256,768]{1,0:T(8,128)(2,1)S(1)} %collective-permute-done.6), channel_id=1, source_target_pairs={{0,4},{4,0},{8,12},{12,8},{16,20},{20,16},{24,28},{28,24},{1,5},{5... | collective-permute-start | bytes 1179656 | tf_op jit(solution)/shard_map/ppermute | solution.py:217
  99.7 0.5 fusion.1
  100.2 0.5 fusion.16
  100.7 0.5 fusion.4
  101.2 7.6 %collective-permute-done.17 = bf16[256,768]{1,0:T(8,128)(2,1)S(1)} collective-permute-done((bf16[256,768]{1,0:T(8,128)(2,1)S(1)}, bf16[256,768]{1,0:T(8,128)(2,1)S(1)}, u32[]{:S(2)}, u32[]{:S(2)}) %collective-permute-start.17) | collective-permute-done | bytes 393248 | tf_op jit(solution)/shard_map/ppermute | solution.py:217
  109.0 4.9 %collective-permute-done.8 = bf16[256,768]{1,0:T(8,128)(2,1)S(1)} collective-permute-done((bf16[256,768]{1,0:T(8,128)(2,1)S(1)}, bf16[256,768]{1,0:T(8,128)(2,1)S(1)}, u32[]{:S(2)}, u32[]{:S(2)}) %collective-permute-start.8) | collective-permute-done | bytes 393248 | tf_op jit(solution)/shard_map/ppermute | solution.py:212
  113.9 0.9 collective-permute-start.9
  114.8 0.5 fusion.8
  115.2 0.5 fusion
  115.7 0.5 fusion.10
  116.2 1.0 collective-permute-done.7
  117.2 0.5 fusion.3
  117.7 3.7 %collective-permute-done.19 = bf16[256,768]{1,0:T(8,128)(2,1)S(1)} collective-permute-done((bf16[256,768]{1,0:T(8,128)(2,1)S(1)}, bf16[256,768]{1,0:T(8,128)(2,1)S(1)}, u32[]{:S(2)}, u32[]{:S(2)}) %collective-permute-start.19) | collective-permute-done | bytes 393248 | tf_op jit(solution)/shard_map/ppermute | solution.py:212
  121.4 0.5 convolution_add_fusion.refs_1_
  121.9 2.9 %collective-permute-done.9 = bf16[256,768]{1,0:T(8,128)(2,1)S(1)} collective-permute-done((bf16[256,768]{1,0:T(8,128)(2,1)S(1)}, bf16[256,768]{1,0:T(8,128)(2,1)S(1)}, u32[]{:S(2)}, u32[]{:S(2)}) %collective-permute-start.9) | collective-permute-done | bytes 393248 | tf_op jit(solution)/shard_map/ppermute | solution.py:217
  124.8 0.5 convolution_add_fusion.4.refs_0_
  125.3 1.6 %place.1 = bf16[32,16,640]{2,1,0:T(8,128)(2,1)} custom-call(s32[1]{0:T(128)} %bitcast.me_ref, f32[256,640]{1,0:T(8,128)S(1)} %convolution_add_fusion.4.refs_0_, f32[256,640]{1,0:T(8,128)S(1)} %convolution_add_fusion.refs_1_), custom_call_target="tpu_custom_call" | custom-call | tf_op jit(solution)/shard_map/place/pallas_call | solution.py:182
  (36 shorter events, 1.2 us)
Async XLA Ops:
  0.0 1.6 %copy-start.1 = (bf16[1,64,64,256]{3,2,1,0:T(8,128)(2,1)S(1)}, bf16[1,64,64,256]{3,2,1,0:T(8,128)(2,1)}, u32[]{:S(2)}) copy-start(bf16[1,64,64,256]{3,2,1,0:T(8,128)(2,1)} %param.5) | copy-start | bytes 6291460
  1.6 0.7 copy-start.2
  2.3 0.7 copy-start.3
  27.4 18.5 %all-to-all-start = ((bf16[8,272,128]{2,1,0:T(8,128)(2,1)}), bf16[8,272,128]{2,1,0:T(8,128)(2,1)S(1)}, u32[]{:S(2)}, u32[]{:S(2)}) async-start(bf16[8,272,128]{2,1,0:T(8,128)(2,1)} %get-tuple-element.15), calls=%async_computation | async-start | bytes 1114112 | tf_op jit(solution)/shard_map/all_to_all | solution.py:242
  45.8 1.4 %copy-start = (bf16[6144,128]{1,0:T(8,128)(2,1)S(1)}, bf16[6144,128]{1,0:T(8,128)(2,1)}, u32[]{:S(2)}) copy-start(bf16[6144,128]{1,0:T(8,128)(2,1)} %coeff_ref.3) | copy-start | bytes 4718596
  50.3 6.9 %collective-permute-start.10 = (bf16[64,768]{1,0:T(8,128)(2,1)S(1)}, bf16[64,768]{1,0:T(8,128)(2,1)S(1)}, u32[]{:S(2)}, u32[]{:S(2)}) collective-permute-start(bf16[64,768]{1,0:T(8,128)(2,1)S(1)} %get-tuple-element.22), channel_id=1, source_target_pairs={{0,1},{1,0},{2,3},{3,2},{4,5},{5,4},{6,7},{7,6},{8,9},{9,8},{10,11... | collective-permute-start | bytes 294920 | tf_op jit(solution)/shard_map/ppermute | solution.py:209
  50.4 6.9 %collective-permute-start.11 = (bf16[64,768]{1,0:T(8,128)(2,1)S(1)}, bf16[64,768]{1,0:T(8,128)(2,1)S(1)}, u32[]{:S(2)}, u32[]{:S(2)}) collective-permute-start(bf16[64,768]{1,0:T(8,128)(2,1)S(1)} %get-tuple-element.23), channel_id=1, source_target_pairs={{0,2},{1,3},{2,0},{3,1},{4,6},{5,7},{6,4},{7,5},{8,10},{9,11},{10,... | collective-permute-start | bytes 294920 | tf_op jit(solution)/shard_map/ppermute | solution.py:209
  51.9 5.4 %collective-permute-start.12 = (bf16[64,768]{1,0:T(8,128)(2,1)S(1)}, bf16[64,768]{1,0:T(8,128)(2,1)S(1)}, u32[]{:S(2)}, u32[]{:S(2)}) collective-permute-start(bf16[64,768]{1,0:T(8,128)(2,1)S(1)} %get-tuple-element.24), channel_id=1, source_target_pairs={{0,3},{1,2},{2,1},{3,0},{4,7},{5,6},{6,5},{7,4},{8,11},{9,10},{10,... | collective-permute-start | bytes 294920 | tf_op jit(solution)/shard_map/ppermute | solution.py:209
  55.3 2.8 %collective-permute-start = (bf16[64,768]{1,0:T(8,128)(2,1)S(1)}, bf16[64,768]{1,0:T(8,128)(2,1)S(1)}, u32[]{:S(2)}, u32[]{:S(2)}) collective-permute-start(bf16[64,768]{1,0:T(8,128)(2,1)S(1)} %get-tuple-element.17), channel_id=1, source_target_pairs={{0,1},{1,0},{2,3},{3,2},{4,5},{5,4},{6,7},{7,6},{8,9},{9,8},{10,11... | collective-permute-start | bytes 294920 | tf_op jit(solution)/shard_map/ppermute | solution.py:209
  55.7 5.1 %collective-permute-start.1 = (bf16[64,768]{1,0:T(8,128)(2,1)S(1)}, bf16[64,768]{1,0:T(8,128)(2,1)S(1)}, u32[]{:S(2)}, u32[]{:S(2)}) collective-permute-start(bf16[64,768]{1,0:T(8,128)(2,1)S(1)} %get-tuple-element.18), channel_id=1, source_target_pairs={{0,2},{1,3},{2,0},{3,1},{4,6},{5,7},{6,4},{7,5},{8,10},{9,11},{10,... | collective-permute-start | bytes 294920 | tf_op jit(solution)/shard_map/ppermute | solution.py:209
  57.2 5.2 %collective-permute-start.2 = (bf16[64,768]{1,0:T(8,128)(2,1)S(1)}, bf16[64,768]{1,0:T(8,128)(2,1)S(1)}, u32[]{:S(2)}, u32[]{:S(2)}) collective-permute-start(bf16[64,768]{1,0:T(8,128)(2,1)S(1)} %get-tuple-element.19), channel_id=1, source_target_pairs={{0,3},{1,2},{2,1},{3,0},{4,7},{5,6},{6,5},{7,4},{8,11},{9,10},{10,... | collective-permute-start | bytes 294920 | tf_op jit(solution)/shard_map/ppermute | solution.py:209
  57.4 13.8 %collective-permute-start.14 = (bf16[256,768]{1,0:T(8,128)(2,1)S(1)}, bf16[256,768]{1,0:T(8,128)(2,1)S(1)}, u32[]{:S(2)}, u32[]{:S(2)}) collective-permute-start(bf16[256,768]{1,0:T(8,128)(2,1)S(1)} %constant_dynamic-update-slice_fusion.4), channel_id=1, source_target_pairs={{0,8},{4,12},{8,16},{12,20},{16,24},{20,28},{24,0},{28,4},{1,9},{5... | collective-permute-start | bytes 1179656 | tf_op jit(solution)/shard_map/ppermute | solution.py:212
  62.4 17.2 %collective-permute-start.4 = (bf16[256,768]{1,0:T(8,128)(2,1)S(1)}, bf16[256,768]{1,0:T(8,128)(2,1)S(1)}, u32[]{:S(2)}, u32[]{:S(2)}) collective-permute-start(bf16[256,768]{1,0:T(8,128)(2,1)S(1)} %constant_dynamic-update-slice_fusion), channel_id=1, source_target_pairs={{0,8},{4,12},{8,16},{12,20},{16,24},{20,28},{24,0},{28,4},{1,9},{5... | collective-permute-start | bytes 1179656 | tf_op jit(solution)/shard_map/ppermute | solution.py:212
  63.1 20.1 %collective-permute-start.13 = (bf16[256,768]{1,0:T(8,128)(2,1)S(1)}, bf16[256,768]{1,0:T(8,128)(2,1)S(1)}, u32[]{:S(2)}, u32[]{:S(2)}) collective-permute-start(bf16[256,768]{1,0:T(8,128)(2,1)S(1)} %constant_dynamic-update-slice_fusion.4), channel_id=1, source_target_pairs={{0,4},{4,0},{8,12},{12,8},{16,20},{20,16},{24,28},{28,24},{1,5},{5... | collective-permute-start | bytes 1179656 | tf_op jit(solution)/shard_map/ppermute | solution.py:217
  64.1 24.1 %collective-permute-start.3 = (bf16[256,768]{1,0:T(8,128)(2,1)S(1)}, bf16[256,768]{1,0:T(8,128)(2,1)S(1)}, u32[]{:S(2)}, u32[]{:S(2)}) collective-permute-start(bf16[256,768]{1,0:T(8,128)(2,1)S(1)} %constant_dynamic-update-slice_fusion), channel_id=1, source_target_pairs={{0,4},{4,0},{8,12},{12,8},{16,20},{20,16},{24,28},{28,24},{1,5},{5... | collective-permute-start | bytes 1179656 | tf_op jit(solution)/shard_map/ppermute | solution.py:217
  71.2 20.4 %collective-permute-start.16 = (bf16[256,768]{1,0:T(8,128)(2,1)S(1)}, bf16[256,768]{1,0:T(8,128)(2,1)S(1)}, u32[]{:S(2)}, u32[]{:S(2)}) collective-permute-start(bf16[256,768]{1,0:T(8,128)(2,1)S(1)} %collective-permute-done.14), channel_id=1, source_target_pairs={{0,8},{4,12},{8,16},{12,20},{16,24},{20,28},{24,0},{28,4},{1,9},{5... | collective-permute-start | bytes 1179656 | tf_op jit(solution)/shard_map/ppermute | solution.py:212
  71.2 27.0 %collective-permute-start.15 = (bf16[256,768]{1,0:T(8,128)(2,1)S(1)}, bf16[256,768]{1,0:T(8,128)(2,1)S(1)}, u32[]{:S(2)}, u32[]{:S(2)}) collective-permute-start(bf16[256,768]{1,0:T(8,128)(2,1)S(1)} %collective-permute-done.14), channel_id=1, source_target_pairs={{0,4},{4,0},{8,12},{12,8},{16,20},{20,16},{24,28},{28,24},{1,5},{5... | collective-permute-start | bytes 1179656 | tf_op jit(solution)/shard_map/ppermute | solution.py:217
  79.6 16.9 %collective-permute-start.6 = (bf16[256,768]{1,0:T(8,128)(2,1)S(1)}, bf16[256,768]{1,0:T(8,128)(2,1)S(1)}, u32[]{:S(2)}, u32[]{:S(2)}) collective-permute-start(bf16[256,768]{1,0:T(8,128)(2,1)S(1)} %collective-permute-done.4), channel_id=1, source_target_pairs={{0,8},{4,12},{8,16},{12,20},{16,24},{20,28},{24,0},{28,4},{1,9},{5... | collective-permute-start | bytes 1179656 | tf_op jit(solution)/shard_map/ppermute | solution.py:212
  79.6 20.0 %slice-start = ((s8[7864320]{0:T(1024)(128)(4,1)}), s8[4194304]{0:T(1024)(128)(4,1)S(1)}, s32[]{:S(2)}) async-start(s8[7864320]{0:T(1024)(128)(4,1)} %bitcast.19), calls=%async_computation.2 | async-start | bytes 8388608
  83.2 17.5 %collective-permute-start.5 = (bf16[256,768]{1,0:T(8,128)(2,1)S(1)}, bf16[256,768]{1,0:T(8,128)(2,1)S(1)}, u32[]{:S(2)}, u32[]{:S(2)}) collective-permute-start(bf16[256,768]{1,0:T(8,128)(2,1)S(1)} %collective-permute-done.4), channel_id=1, source_target_pairs={{0,4},{4,0},{8,12},{12,8},{16,20},{20,16},{24,28},{28,24},{1,5},{5... | collective-permute-start | bytes 1179656 | tf_op jit(solution)/shard_map/ppermute | solution.py:217
  86.3 13.3 %slice-start.1 = ((s8[7864320]{0:T(1024)(128)(4,1)}), s8[3670016]{0:T(1024)(128)(4,1)S(1)}, s32[]{:S(2)}) async-start(s8[7864320]{0:T(1024)(128)(4,1)} %bitcast.19), calls=%async_computation.3 | async-start | bytes 7340032
  91.6 23.2 %collective-permute-start.18 = (bf16[256,768]{1,0:T(8,128)(2,1)S(1)}, bf16[256,768]{1,0:T(8,128)(2,1)S(1)}, u32[]{:S(2)}, u32[]{:S(2)}) collective-permute-start(bf16[256,768]{1,0:T(8,128)(2,1)S(1)} %collective-permute-done.16), channel_id=1, source_target_pairs={{0,8},{4,12},{8,16},{12,20},{16,24},{20,28},{24,0},{28,4},{1,9},{5... | collective-permute-start | bytes 1179656 | tf_op jit(solution)/shard_map/ppermute | solution.py:212
  91.7 17.1 %collective-permute-start.17 = (bf16[256,768]{1,0:T(8,128)(2,1)S(1)}, bf16[256,768]{1,0:T(8,128)(2,1)S(1)}, u32[]{:S(2)}, u32[]{:S(2)}) collective-permute-start(bf16[256,768]{1,0:T(8,128)(2,1)S(1)} %collective-permute-done.16), channel_id=1, source_target_pairs={{0,4},{4,0},{8,12},{12,8},{16,20},{20,16},{24,28},{28,24},{1,5},{5... | collective-permute-start | bytes 1179656 | tf_op jit(solution)/shard_map/ppermute | solution.py:217
  96.5 17.4 %collective-permute-start.8 = (bf16[256,768]{1,0:T(8,128)(2,1)S(1)}, bf16[256,768]{1,0:T(8,128)(2,1)S(1)}, u32[]{:S(2)}, u32[]{:S(2)}) collective-permute-start(bf16[256,768]{1,0:T(8,128)(2,1)S(1)} %collective-permute-done.6), channel_id=1, source_target_pairs={{0,8},{4,12},{8,16},{12,20},{16,24},{20,28},{24,0},{28,4},{1,9},{5... | collective-permute-start | bytes 1179656 | tf_op jit(solution)/shard_map/ppermute | solution.py:212
  98.2 19.1 %collective-permute-start.7 = (bf16[256,768]{1,0:T(8,128)(2,1)S(1)}, bf16[256,768]{1,0:T(8,128)(2,1)S(1)}, u32[]{:S(2)}, u32[]{:S(2)}) collective-permute-start(bf16[256,768]{1,0:T(8,128)(2,1)S(1)} %collective-permute-done.6), channel_id=1, source_target_pairs={{0,4},{4,0},{8,12},{12,8},{16,20},{20,16},{24,28},{28,24},{1,5},{5... | collective-permute-start | bytes 1179656 | tf_op jit(solution)/shard_map/ppermute | solution.py:217
  108.8 12.6 %collective-permute-start.19 = (bf16[256,768]{1,0:T(8,128)(2,1)S(1)}, bf16[256,768]{1,0:T(8,128)(2,1)S(1)}, u32[]{:S(2)}, u32[]{:S(2)}) collective-permute-start(bf16[256,768]{1,0:T(8,128)(2,1)S(1)} %collective-permute-done.17), channel_id=1, source_target_pairs={{0,8},{4,12},{8,16},{12,20},{16,24},{20,28},{24,0},{28,4},{1,9},{5... | collective-permute-start | bytes 1179656 | tf_op jit(solution)/shard_map/ppermute | solution.py:212
  113.9 10.9 %collective-permute-start.9 = (bf16[256,768]{1,0:T(8,128)(2,1)S(1)}, bf16[256,768]{1,0:T(8,128)(2,1)S(1)}, u32[]{:S(2)}, u32[]{:S(2)}) collective-permute-start(bf16[256,768]{1,0:T(8,128)(2,1)S(1)} %collective-permute-done.8), channel_id=1, source_target_pairs={{0,4},{4,0},{8,12},{12,8},{16,20},{20,16},{24,28},{28,24},{1,5},{5... | collective-permute-start | bytes 1179656 | tf_op jit(solution)/shard_map/ppermute | solution.py:217
where the time goes:
time: 127 us
  waiting for transfers between devices  56.5 us (44%)
  blocking collectives  21.6 us (17%)
  starting transfers between devices  17.2 us (14%)
  matrix products  16.4 us (13%)
  Pallas kernels  10.5 us (8%)
  local copies, waits for them, and re-layouts  4.41 us (3%)
    ppermute x7, waiting for transfers between devices, along(): lax.ppermute(array, 'pair', [(p, (p // 2 + 1) % outer * 2 + p % 2) for p...  25.7 us
    all_to_all x1, blocking collectives, on_device(): lax.all_to_all(send, 'pair', split_axis=0, concat_axis=0, tiled=True)  21.6 us
    dot_general x16, matrix products, second_half(): term = jnp.dot(array, part, preferred_element_type=jnp.float32)  16.4 us
    all_to_all x1, waiting for transfers between devices, on_device(): lax.all_to_all(send, 'pair', split_axis=0, concat_axis=0, tiled=True)  14.9 us
    ppermute x7, waiting for transfers between devices, swap(): return lax.ppermute(array, 'pair', [(p, p ^ 1) for p in range(owners)])  11.6 us
    ppermute x7, starting transfers between devices, swap(): return lax.ppermute(array, 'pair', [(p, p ^ 1) for p in range(owners)])  7.97 us
    pallas_call x2, Pallas kernels, half_transform(): pl.pallas_call(functools.partial(half_kernel, owned, width), grid=(1,), o...  6.04 us
    unnamed x18, local copies, waits for them, and re-layouts  4.39 us
  transfers between devices with their start and end apart: 21, of which 11 were waited for; matrix products, arithmetic and copies ran while one was open for 13% of the time, Pallas kernels for 2%

commit v1 on v0

--- a/solution.py
+++ b/solution.py
@@ -74,9 +74,8 @@
             pltpu.SMEM((LIVE + 1,), jnp.int32),
             pltpu.SemaphoreType.DMA((owners, LIVE, chunks)),
         ],
-        compiler_params=pltpu.CompilerParams(vmem_limit_bytes=GRANT),
         name="pack_live",
-    )(block_ids, live_mask, blocks)
+    )(block_ids, live_mask, pltpu.with_memory_space_constraint(blocks, pltpu.HBM))
 
 
 def half_kernel(owned, width, me_ref, tail_ref, got_ref, coeff_ref, *refs):
@@ -152,7 +151,7 @@
         ),
         compiler_params=pltpu.CompilerParams(vmem_limit_bytes=GRANT),
         name="half_transform",
-    )(me, first, got, coeffs)
+    )(me, first, got, pltpu.with_memory_space_constraint(coeffs, pltpu.HBM))
 
 
 def place_kernel(occ, me_ref, *refs):

time: 127 us -> 127 us (level)
  local copies, waits for them, and re-layouts: 4.41 us -> 0.08 us
  Pallas kernels: 10.5 us -> 14 us
    unnamed x18 -> x10, local copies, waits for them, and re-layouts: 4.39 us -> 0.06 us
    pallas_call x2, Pallas kernels: 6.04 us -> 8.85 us  [half_transform(): pl.pallas_call(functools.partial(half_kernel, owned, width), grid=(1,), o...]
  transfers between devices with their start and end apart: 21 -> 21, of which waited for: 11 -> 11; matrix products, arithmetic and copies ran while one was open for 13% -> 13% of each run, Pallas kernels for 2% -> 4%
where the time goes in v1:
time: 127 us; the launch traced here: 126 us
  waiting for transfers between devices  56.5 us (44%)
  blocking collectives  21.8 us (17%)
  starting transfers between devices  17.2 us (14%)
  matrix products  16.4 us (13%)
  Pallas kernels  14 us (11%)
    ppermute x7, waiting for transfers between devices, along(): lax.ppermute(array, 'pair', [(p, (p // 2 + 1) % outer * 2 + p % 2) for p...  25.7 us
    all_to_all x1, blocking collectives, on_device(): lax.all_to_all(send, 'pair', split_axis=0, concat_axis=0, tiled=True)  21.8 us
    dot_general x16, matrix products, second_half(): term = jnp.dot(array, part, preferred_element_type=jnp.float32)  16.4 us
    all_to_all x1, waiting for transfers between devices, on_device(): lax.all_to_all(send, 'pair', split_axis=0, concat_axis=0, tiled=True)  14.9 us
    ppermute x7, waiting for transfers between devices, swap(): return lax.ppermute(array, 'pair', [(p, p ^ 1) for p in range(owners)])  11.6 us
    pallas_call x2, Pallas kernels, half_transform(): pl.pallas_call(functools.partial(half_kernel, owned, width), grid=(1,), o...  8.85 us
    ppermute x7, starting transfers between devices, swap(): return lax.ppermute(array, 'pair', [(p, p ^ 1) for p in range(owners)])  7.99 us
    ppermute x6, waiting for transfers between devices, across(): return lax.ppermute(array, 'occ', [(o, o ^ j) for o in range(occ)])  4.26 us
  transfers between devices with their start and end apart: 21, of which 11 were waited for; matrix products, arithmetic and copies ran while one was open for 13% of the time, Pallas kernels for 4%

profile of v1, /device:TPU:0, one launch (start us, length us, event | category | flops | bytes accessed | tf_op | source)
XLA Modules:
  0.0 126.3 jit_solution(18146480334098176290)
XLA Ops:
  0.0 3.5 %pack_live.1 = (bf16[8,272,128]{2,1,0:T(8,128)(2,1)}, bf16[8,256,128]{2,1,0:T(8,128)(2,1)}) custom-call(s32[2,1,64]{2,1,0:T(1,128)} %ids_ref.1, s32[1,64]{1,0:T(1,128)} %live_ref.1, bf16[64,64,256]{2,1,0:T(8,128)(2,1)} %bitcast.20), custom_call_target="tpu_custom_call" | custom-call | tf_op jit(solution)/shard_map/pack_live/pallas_call | solution.py:64
  3.6 21.8 %all_to_all.10.got_ref = bf16[8,256,128]{2,1,0:T(8,128)(2,1)S(1)} all-to-all(bf16[8,256,128]{2,1,0:T(8,128)(2,1)} %get-tuple-element.20), channel_id=1, replica_groups=mesh['pair'=8,'occ'=4] {'pair'}, dimensions={0} | all-to-all | bytes 1048576 | tf_op jit(solution)/shard_map/all_to_all | solution.py:241
  25.4 3.6 %all-to-all-start = ((bf16[8,272,128]{2,1,0:T(8,128)(2,1)}), bf16[8,272,128]{2,1,0:T(8,128)(2,1)S(1)}, u32[]{:S(2)}, u32[]{:S(2)}) async-start(bf16[8,272,128]{2,1,0:T(8,128)(2,1)} %get-tuple-element.15), calls=%async_computation | async-start | bytes 1114112 | tf_op jit(solution)/shard_map/all_to_all | solution.py:241
  29.0 14.9 %all-to-all-done.tail_ref.got_ref = bf16[8,272,128]{2,1,0:T(8,128)(2,1)S(1)} async-done(((bf16[8,272,128]{2,1,0:T(8,128)(2,1)}), bf16[8,272,128]{2,1,0:T(8,128)(2,1)S(1)}, u32[]{:S(2)}, u32[]{:S(2)}) %all-to-all-start) | async-done | bytes 557088 | tf_op jit(solution)/shard_map/all_to_all | solution.py:241
  43.8 4.4 %half_transform.3 = (bf16[64,768]{1,0:T(8,128)(2,1)S(1)}, bf16[64,768]{1,0:T(8,128)(2,1)S(1)}, bf16[64,768]{1,0:T(8,128)(2,1)S(1)}, bf16[64,768]{1,0:T(8,128)(2,1)S(1)}) custom-call(s32[1]{0:T(128)} %bitcast.me_ref, bf16[8,272,128]{2,1,0:T(8,128)(2,1)S(1)} %all-to-all-done.tail_ref.got_ref, bf16[8,256,128]{2,1,0:T(8,128)(2,1)S(1)} %all_to_all.10.got_ref, ...), custom_call_target="tpu_custom_call" | custom-call | flops 67108864 | bytes 2490368 | tf_op jit(solution)/shard_map/half_transform/pallas_call | solution.py:130
  48.3 0.1 collective-permute-start.10
  48.4 1.6 %collective-permute-start.11 = (bf16[64,768]{1,0:T(8,128)(2,1)S(1)}, bf16[64,768]{1,0:T(8,128)(2,1)S(1)}, u32[]{:S(2)}, u32[]{:S(2)}) collective-permute-start(bf16[64,768]{1,0:T(8,128)(2,1)S(1)} %get-tuple-element.23), channel_id=1, source_target_pairs={{0,2},{1,3},{2,0},{3,1},{4,6},{5,7},{6,4},{7,5},{8,10},{9,11},{10,... | collective-permute-start | bytes 294920 | tf_op jit(solution)/shard_map/ppermute | solution.py:208
  49.9 0.3 collective-permute-start.12
  50.2 4.4 %half_transform.2 = (bf16[64,768]{1,0:T(8,128)(2,1)S(1)}, bf16[64,768]{1,0:T(8,128)(2,1)S(1)}, bf16[64,768]{1,0:T(8,128)(2,1)S(1)}, bf16[64,768]{1,0:T(8,128)(2,1)S(1)}) custom-call(s32[1]{0:T(128)} %bitcast.me_ref, bf16[8,272,128]{2,1,0:T(8,128)(2,1)S(1)} %all-to-all-done.tail_ref.got_ref, bf16[8,272,128]{2,1,0:T(8,128)(2,1)S(1)} %all-to-all-done.tail_ref.got_ref, ...), custom_call_target="tpu_custom_call" | custom-call | flops 67108864 | bytes 2523136 | tf_op jit(solution)/shard_map/half_transform/pallas_call | solution.py:130
  54.6 0.4 collective-permute-start
  55.1 1.5 %collective-permute-start.1 = (bf16[64,768]{1,0:T(8,128)(2,1)S(1)}, bf16[64,768]{1,0:T(8,128)(2,1)S(1)}, u32[]{:S(2)}, u32[]{:S(2)}) collective-permute-start(bf16[64,768]{1,0:T(8,128)(2,1)S(1)} %get-tuple-element.18), channel_id=1, source_target_pairs={{0,2},{1,3},{2,0},{3,1},{4,6},{5,7},{6,4},{7,5},{8,10},{9,11},{10,... | collective-permute-start | bytes 294920 | tf_op jit(solution)/shard_map/ppermute | solution.py:208
  56.8 0.7 collective-permute-start.14
  57.5 2.7 %collective-permute-done.1 = bf16[64,768]{1,0:T(8,128)(2,1)S(1)} collective-permute-done((bf16[64,768]{1,0:T(8,128)(2,1)S(1)}, bf16[64,768]{1,0:T(8,128)(2,1)S(1)}, u32[]{:S(2)}, u32[]{:S(2)}) %collective-permute-start.1) | collective-permute-done | bytes 98336 | tf_op jit(solution)/shard_map/ppermute | solution.py:208
  60.2 1.6 %collective-permute-done.2 = bf16[64,768]{1,0:T(8,128)(2,1)S(1)} collective-permute-done((bf16[64,768]{1,0:T(8,128)(2,1)S(1)}, bf16[64,768]{1,0:T(8,128)(2,1)S(1)}, u32[]{:S(2)}, u32[]{:S(2)}) %collective-permute-start.2) | collective-permute-done | bytes 98336 | tf_op jit(solution)/shard_map/ppermute | solution.py:208
  61.8 0.7 collective-permute-start.4
  62.5 1.0 collective-permute-start.13
  63.5 1.1 collective-permute-start.3
  64.5 6.1 %collective-permute-done.14 = bf16[256,768]{1,0:T(8,128)(2,1)S(1)} collective-permute-done((bf16[256,768]{1,0:T(8,128)(2,1)S(1)}, bf16[256,768]{1,0:T(8,128)(2,1)S(1)}, u32[]{:S(2)}, u32[]{:S(2)}) %collective-permute-start.14) | collective-permute-done | bytes 393248 | tf_op jit(solution)/shard_map/ppermute | solution.py:211
  70.6 1.4 %collective-permute-start.15 = (bf16[256,768]{1,0:T(8,128)(2,1)S(1)}, bf16[256,768]{1,0:T(8,128)(2,1)S(1)}, u32[]{:S(2)}, u32[]{:S(2)}) collective-permute-start(bf16[256,768]{1,0:T(8,128)(2,1)S(1)} %collective-permute-done.14), channel_id=1, source_target_pairs={{0,4},{4,0},{8,12},{12,8},{16,20},{20,16},{24,28},{28,24},{1,5},{5... | collective-permute-start | bytes 1179656 | tf_op jit(solution)/shard_map/ppermute | solution.py:216
  72.0 7.0 %collective-permute-done.4 = bf16[256,768]{1,0:T(8,128)(2,1)S(1)} collective-permute-done((bf16[256,768]{1,0:T(8,128)(2,1)S(1)}, bf16[256,768]{1,0:T(8,128)(2,1)S(1)}, u32[]{:S(2)}, u32[]{:S(2)}) %collective-permute-start.4) | collective-permute-done | bytes 393248 | tf_op jit(solution)/shard_map/ppermute | solution.py:211
  79.0 1.8 %fusion.20 = f32[256,640]{1,0:T(8,128)S(1)} fusion(bf16[256,768]{1,0:T(8,128)(2,1)S(1)} %collective-permute-done.14, bf16[6144,640]{1,0:T(8,128)(2,1)} %param.7, s32[]{:T(128)S(6)} %select_n.134), kind=kOutput, calls=%fused_computation.28 | convolution fusion | flops 251658240 | bytes 2031620 | tf_op jit(solution)/shard_map/dot_general | solution.py:234
  80.9 1.7 %fusion.22 = f32[256,640]{1,0:T(8,128)S(1)} fusion(bf16[256,768]{1,0:T(8,128)(2,1)S(1)} %collective-permute-done.4, bf16[6144,640]{1,0:T(8,128)(2,1)} %param.7, s32[]{:T(128)S(6)} %select_n.134), kind=kOutput, calls=%fused_computation.30 | convolution fusion | flops 251658240 | bytes 2031620 | tf_op jit(solution)/shard_map/dot_general | solution.py:234
  82.6 1.5 %collective-permute-start.5 = (bf16[256,768]{1,0:T(8,128)(2,1)S(1)}, bf16[256,768]{1,0:T(8,128)(2,1)S(1)}, u32[]{:S(2)}, u32[]{:S(2)}) collective-permute-start(bf16[256,768]{1,0:T(8,128)(2,1)S(1)} %collective-permute-done.4), channel_id=1, source_target_pairs={{0,4},{4,0},{8,12},{12,8},{16,20},{20,16},{24,28},{28,24},{1,5},{5... | collective-permute-start | bytes 1179656 | tf_op jit(solution)/shard_map/ppermute | solution.py:216
  84.0 1.7 %fusion.24 = f32[256,640]{1,0:T(8,128)S(1)} fusion(bf16[256,768]{1,0:T(8,128)(2,1)S(1)} %collective-permute-done.13, bf16[6144,640]{1,0:T(8,128)(2,1)} %param.7, s32[]{:T(128)S(6)} %select_n.132), kind=kOutput, calls=%fused_computation.32 | convolution fusion | flops 251658240 | bytes 2031620 | tf_op jit(solution)/shard_map/dot_general | solution.py:234
  85.7 1.8 %fusion.2 = f32[256,640]{1,0:T(8,128)S(1)} fusion(f32[256,640]{1,0:T(8,128)S(1)} %fusion.20, f32[256,640]{1,0:T(8,128)S(1)} %fusion.24, bf16[256,768]{1,0:T(8,128)(2,1)S(1)} %constant_dynamic-update-slice_fusion.4, bf16[6144,640]{1,0:T(8,128)(2,1)} %param.7, s32[]{:T(128)S(6)} %select_n.131), kind=kOutput, calls=%fused_computation.6 | convolution fusion | flops 251985920 | bytes 3342340 | tf_op jit(solution)/shard_map/dot_general | solution.py:234
  87.6 1.7 %fusion.26 = f32[256,640]{1,0:T(8,128)S(1)} fusion(bf16[256,768]{1,0:T(8,128)(2,1)S(1)} %collective-permute-done.3, bf16[6144,640]{1,0:T(8,128)(2,1)} %param.7, s32[]{:T(128)S(6)} %select_n.132), kind=kOutput, calls=%fused_computation.34 | convolution fusion | flops 251658240 | bytes 2031620 | tf_op jit(solution)/shard_map/dot_general | solution.py:234
  89.3 1.7 %fusion.5 = f32[256,640]{1,0:T(8,128)S(1)} fusion(f32[256,640]{1,0:T(8,128)S(1)} %fusion.22, f32[256,640]{1,0:T(8,128)S(1)} %fusion.26, bf16[256,768]{1,0:T(8,128)(2,1)S(1)} %constant_dynamic-update-slice_fusion, bf16[6144,640]{1,0:T(8,128)(2,1)} %param.7, s32[]{:T(128)S(6)} %select_n.131), kind=kOutput, calls=%fused_computation.13 | convolution fusion | flops 251985920 | bytes 3342340 | tf_op jit(solution)/shard_map/dot_general | solution.py:234
  91.1 0.7 collective-permute-start.17
  91.7 4.2 %collective-permute-done.6 = bf16[256,768]{1,0:T(8,128)(2,1)S(1)} collective-permute-done((bf16[256,768]{1,0:T(8,128)(2,1)S(1)}, bf16[256,768]{1,0:T(8,128)(2,1)S(1)}, u32[]{:S(2)}, u32[]{:S(2)}) %collective-permute-start.6) | collective-permute-done | bytes 393248 | tf_op jit(solution)/shard_map/ppermute | solution.py:211
  95.9 1.7 %fusion.14 = f32[256,640]{1,0:T(8,128)S(1)} fusion(bf16[256,768]{1,0:T(8,128)(2,1)S(1)} %collective-permute-done.16, bf16[6144,640]{1,0:T(8,128)(2,1)} %param.7, s32[]{:T(128)S(6)} %select_n.137), kind=kOutput, calls=%fused_computation.22 | convolution fusion | flops 251658240 | bytes 2031620 | tf_op jit(solution)/shard_map/dot_general | solution.py:234
  97.6 1.5 %collective-permute-start.7 = (bf16[256,768]{1,0:T(8,128)(2,1)S(1)}, bf16[256,768]{1,0:T(8,128)(2,1)S(1)}, u32[]{:S(2)}, u32[]{:S(2)}) collective-permute-start(bf16[256,768]{1,0:T(8,128)(2,1)S(1)} %collective-permute-done.6), channel_id=1, source_target_pairs={{0,4},{4,0},{8,12},{12,8},{16,20},{20,16},{24,28},{28,24},{1,5},{5... | collective-permute-start | bytes 1179656 | tf_op jit(solution)/shard_map/ppermute | solution.py:216
  99.1 0.5 fusion.1
  99.6 0.5 fusion.16
  100.1 0.5 fusion.4
  100.5 7.6 %collective-permute-done.17 = bf16[256,768]{1,0:T(8,128)(2,1)S(1)} collective-permute-done((bf16[256,768]{1,0:T(8,128)(2,1)S(1)}, bf16[256,768]{1,0:T(8,128)(2,1)S(1)}, u32[]{:S(2)}, u32[]{:S(2)}) %collective-permute-start.17) | collective-permute-done | bytes 393248 | tf_op jit(solution)/shard_map/ppermute | solution.py:216
  108.2 0.2 collective-permute-start.19
  108.4 4.8 %collective-permute-done.8 = bf16[256,768]{1,0:T(8,128)(2,1)S(1)} collective-permute-done((bf16[256,768]{1,0:T(8,128)(2,1)S(1)}, bf16[256,768]{1,0:T(8,128)(2,1)S(1)}, u32[]{:S(2)}, u32[]{:S(2)}) %collective-permute-start.8) | collective-permute-done | bytes 393248 | tf_op jit(solution)/shard_map/ppermute | solution.py:211
  113.3 0.9 collective-permute-start.9
  114.2 0.5 fusion.8
  114.6 0.5 fusion
  115.1 0.5 fusion.10
  115.6 1.0 collective-permute-done.7
  116.6 0.5 fusion.3
  117.1 3.7 %collective-permute-done.19 = bf16[256,768]{1,0:T(8,128)(2,1)S(1)} collective-permute-done((bf16[256,768]{1,0:T(8,128)(2,1)S(1)}, bf16[256,768]{1,0:T(8,128)(2,1)S(1)}, u32[]{:S(2)}, u32[]{:S(2)}) %collective-permute-start.19) | collective-permute-done | bytes 393248 | tf_op jit(solution)/shard_map/ppermute | solution.py:211
  120.8 0.5 convolution_add_fusion.refs_1_
  121.3 2.9 %collective-permute-done.9 = bf16[256,768]{1,0:T(8,128)(2,1)S(1)} collective-permute-done((bf16[256,768]{1,0:T(8,128)(2,1)S(1)}, bf16[256,768]{1,0:T(8,128)(2,1)S(1)}, u32[]{:S(2)}, u32[]{:S(2)}) %collective-permute-start.9) | collective-permute-done | bytes 393248 | tf_op jit(solution)/shard_map/ppermute | solution.py:216
  124.2 0.5 convolution_add_fusion.4.refs_0_
  124.7 1.6 %place.1 = bf16[32,16,640]{2,1,0:T(8,128)(2,1)} custom-call(s32[1]{0:T(128)} %bitcast.me_ref, f32[256,640]{1,0:T(8,128)S(1)} %convolution_add_fusion.4.refs_0_, f32[256,640]{1,0:T(8,128)S(1)} %convolution_add_fusion.refs_1_), custom_call_target="tpu_custom_call" | custom-call | tf_op jit(solution)/shard_map/place/pallas_call | solution.py:181
  (28 shorter events, 0.2 us)
Async XLA Ops:
  25.4 18.5 %all-to-all-start = ((bf16[8,272,128]{2,1,0:T(8,128)(2,1)}), bf16[8,272,128]{2,1,0:T(8,128)(2,1)S(1)}, u32[]{:S(2)}, u32[]{:S(2)}) async-start(bf16[8,272,128]{2,1,0:T(8,128)(2,1)} %get-tuple-element.15), calls=%async_computation | async-start | bytes 1114112 | tf_op jit(solution)/shard_map/all_to_all | solution.py:241
  48.3 8.3 %collective-permute-start.10 = (bf16[64,768]{1,0:T(8,128)(2,1)S(1)}, bf16[64,768]{1,0:T(8,128)(2,1)S(1)}, u32[]{:S(2)}, u32[]{:S(2)}) collective-permute-start(bf16[64,768]{1,0:T(8,128)(2,1)S(1)} %get-tuple-element.22), channel_id=1, source_target_pairs={{0,1},{1,0},{2,3},{3,2},{4,5},{5,4},{6,7},{7,6},{8,9},{9,8},{10,11... | collective-permute-start | bytes 294920 | tf_op jit(solution)/shard_map/ppermute | solution.py:208
  48.4 8.4 %collective-permute-start.11 = (bf16[64,768]{1,0:T(8,128)(2,1)S(1)}, bf16[64,768]{1,0:T(8,128)(2,1)S(1)}, u32[]{:S(2)}, u32[]{:S(2)}) collective-permute-start(bf16[64,768]{1,0:T(8,128)(2,1)S(1)} %get-tuple-element.23), channel_id=1, source_target_pairs={{0,2},{1,3},{2,0},{3,1},{4,6},{5,7},{6,4},{7,5},{8,10},{9,11},{10,... | collective-permute-start | bytes 294920 | tf_op jit(solution)/shard_map/ppermute | solution.py:208
  49.9 6.8 %collective-permute-start.12 = (bf16[64,768]{1,0:T(8,128)(2,1)S(1)}, bf16[64,768]{1,0:T(8,128)(2,1)S(1)}, u32[]{:S(2)}, u32[]{:S(2)}) collective-permute-start(bf16[64,768]{1,0:T(8,128)(2,1)S(1)} %get-tuple-element.24), channel_id=1, source_target_pairs={{0,3},{1,2},{2,1},{3,0},{4,7},{5,6},{6,5},{7,4},{8,11},{9,10},{10,... | collective-permute-start | bytes 294920 | tf_op jit(solution)/shard_map/ppermute | solution.py:208
  54.6 2.8 %collective-permute-start = (bf16[64,768]{1,0:T(8,128)(2,1)S(1)}, bf16[64,768]{1,0:T(8,128)(2,1)S(1)}, u32[]{:S(2)}, u32[]{:S(2)}) collective-permute-start(bf16[64,768]{1,0:T(8,128)(2,1)S(1)} %get-tuple-element.17), channel_id=1, source_target_pairs={{0,1},{1,0},{2,3},{3,2},{4,5},{5,4},{6,7},{7,6},{8,9},{9,8},{10,11... | collective-permute-start | bytes 294920 | tf_op jit(solution)/shard_map/ppermute | solution.py:208
  55.1 5.1 %collective-permute-start.1 = (bf16[64,768]{1,0:T(8,128)(2,1)S(1)}, bf16[64,768]{1,0:T(8,128)(2,1)S(1)}, u32[]{:S(2)}, u32[]{:S(2)}) collective-permute-start(bf16[64,768]{1,0:T(8,128)(2,1)S(1)} %get-tuple-element.18), channel_id=1, source_target_pairs={{0,2},{1,3},{2,0},{3,1},{4,6},{5,7},{6,4},{7,5},{8,10},{9,11},{10,... | collective-permute-start | bytes 294920 | tf_op jit(solution)/shard_map/ppermute | solution.py:208
  56.6 5.2 %collective-permute-start.2 = (bf16[64,768]{1,0:T(8,128)(2,1)S(1)}, bf16[64,768]{1,0:T(8,128)(2,1)S(1)}, u32[]{:S(2)}, u32[]{:S(2)}) collective-permute-start(bf16[64,768]{1,0:T(8,128)(2,1)S(1)} %get-tuple-element.19), channel_id=1, source_target_pairs={{0,3},{1,2},{2,1},{3,0},{4,7},{5,6},{6,5},{7,4},{8,11},{9,10},{10,... | collective-permute-start | bytes 294920 | tf_op jit(solution)/shard_map/ppermute | solution.py:208
  56.8 13.8 %collective-permute-start.14 = (bf16[256,768]{1,0:T(8,128)(2,1)S(1)}, bf16[256,768]{1,0:T(8,128)(2,1)S(1)}, u32[]{:S(2)}, u32[]{:S(2)}) collective-permute-start(bf16[256,768]{1,0:T(8,128)(2,1)S(1)} %constant_dynamic-update-slice_fusion.4), channel_id=1, source_target_pairs={{0,8},{4,12},{8,16},{12,20},{16,24},{20,28},{24,0},{28,4},{1,9},{5... | collective-permute-start | bytes 1179656 | tf_op jit(solution)/shard_map/ppermute | solution.py:211
  61.8 17.2 %collective-permute-start.4 = (bf16[256,768]{1,0:T(8,128)(2,1)S(1)}, bf16[256,768]{1,0:T(8,128)(2,1)S(1)}, u32[]{:S(2)}, u32[]{:S(2)}) collective-permute-start(bf16[256,768]{1,0:T(8,128)(2,1)S(1)} %constant_dynamic-update-slice_fusion), channel_id=1, source_target_pairs={{0,8},{4,12},{8,16},{12,20},{16,24},{20,28},{24,0},{28,4},{1,9},{5... | collective-permute-start | bytes 1179656 | tf_op jit(solution)/shard_map/ppermute | solution.py:211
  62.5 20.0 %collective-permute-start.13 = (bf16[256,768]{1,0:T(8,128)(2,1)S(1)}, bf16[256,768]{1,0:T(8,128)(2,1)S(1)}, u32[]{:S(2)}, u32[]{:S(2)}) collective-permute-start(bf16[256,768]{1,0:T(8,128)(2,1)S(1)} %constant_dynamic-update-slice_fusion.4), channel_id=1, source_target_pairs={{0,4},{4,0},{8,12},{12,8},{16,20},{20,16},{24,28},{28,24},{1,5},{5... | collective-permute-start | bytes 1179656 | tf_op jit(solution)/shard_map/ppermute | solution.py:216
  63.5 24.1 %collective-permute-start.3 = (bf16[256,768]{1,0:T(8,128)(2,1)S(1)}, bf16[256,768]{1,0:T(8,128)(2,1)S(1)}, u32[]{:S(2)}, u32[]{:S(2)}) collective-permute-start(bf16[256,768]{1,0:T(8,128)(2,1)S(1)} %constant_dynamic-update-slice_fusion), channel_id=1, source_target_pairs={{0,4},{4,0},{8,12},{12,8},{16,20},{20,16},{24,28},{28,24},{1,5},{5... | collective-permute-start | bytes 1179656 | tf_op jit(solution)/shard_map/ppermute | solution.py:216
  70.6 20.4 %collective-permute-start.16 = (bf16[256,768]{1,0:T(8,128)(2,1)S(1)}, bf16[256,768]{1,0:T(8,128)(2,1)S(1)}, u32[]{:S(2)}, u32[]{:S(2)}) collective-permute-start(bf16[256,768]{1,0:T(8,128)(2,1)S(1)} %collective-permute-done.14), channel_id=1, source_target_pairs={{0,8},{4,12},{8,16},{12,20},{16,24},{20,28},{24,0},{28,4},{1,9},{5... | collective-permute-start | bytes 1179656 | tf_op jit(solution)/shard_map/ppermute | solution.py:211
  70.6 27.0 %collective-permute-start.15 = (bf16[256,768]{1,0:T(8,128)(2,1)S(1)}, bf16[256,768]{1,0:T(8,128)(2,1)S(1)}, u32[]{:S(2)}, u32[]{:S(2)}) collective-permute-start(bf16[256,768]{1,0:T(8,128)(2,1)S(1)} %collective-permute-done.14), channel_id=1, source_target_pairs={{0,4},{4,0},{8,12},{12,8},{16,20},{20,16},{24,28},{28,24},{1,5},{5... | collective-permute-start | bytes 1179656 | tf_op jit(solution)/shard_map/ppermute | solution.py:216
  79.0 16.9 %collective-permute-start.6 = (bf16[256,768]{1,0:T(8,128)(2,1)S(1)}, bf16[256,768]{1,0:T(8,128)(2,1)S(1)}, u32[]{:S(2)}, u32[]{:S(2)}) collective-permute-start(bf16[256,768]{1,0:T(8,128)(2,1)S(1)} %collective-permute-done.4), channel_id=1, source_target_pairs={{0,8},{4,12},{8,16},{12,20},{16,24},{20,28},{24,0},{28,4},{1,9},{5... | collective-permute-start | bytes 1179656 | tf_op jit(solution)/shard_map/ppermute | solution.py:211
  79.0 20.0 %slice-start = ((s8[7864320]{0:T(1024)(128)(4,1)}), s8[4194304]{0:T(1024)(128)(4,1)S(1)}, s32[]{:S(2)}) async-start(s8[7864320]{0:T(1024)(128)(4,1)} %bitcast.18), calls=%async_computation.2 | async-start | bytes 8388608
  82.6 17.5 %collective-permute-start.5 = (bf16[256,768]{1,0:T(8,128)(2,1)S(1)}, bf16[256,768]{1,0:T(8,128)(2,1)S(1)}, u32[]{:S(2)}, u32[]{:S(2)}) collective-permute-start(bf16[256,768]{1,0:T(8,128)(2,1)S(1)} %collective-permute-done.4), channel_id=1, source_target_pairs={{0,4},{4,0},{8,12},{12,8},{16,20},{20,16},{24,28},{28,24},{1,5},{5... | collective-permute-start | bytes 1179656 | tf_op jit(solution)/shard_map/ppermute | solution.py:216
  85.7 13.3 %slice-start.1 = ((s8[7864320]{0:T(1024)(128)(4,1)}), s8[3670016]{0:T(1024)(128)(4,1)S(1)}, s32[]{:S(2)}) async-start(s8[7864320]{0:T(1024)(128)(4,1)} %bitcast.18), calls=%async_computation.3 | async-start | bytes 7340032
  91.0 23.2 %collective-permute-start.18 = (bf16[256,768]{1,0:T(8,128)(2,1)S(1)}, bf16[256,768]{1,0:T(8,128)(2,1)S(1)}, u32[]{:S(2)}, u32[]{:S(2)}) collective-permute-start(bf16[256,768]{1,0:T(8,128)(2,1)S(1)} %collective-permute-done.16), channel_id=1, source_target_pairs={{0,8},{4,12},{8,16},{12,20},{16,24},{20,28},{24,0},{28,4},{1,9},{5... | collective-permute-start | bytes 1179656 | tf_op jit(solution)/shard_map/ppermute | solution.py:211
  91.1 17.1 %collective-permute-start.17 = (bf16[256,768]{1,0:T(8,128)(2,1)S(1)}, bf16[256,768]{1,0:T(8,128)(2,1)S(1)}, u32[]{:S(2)}, u32[]{:S(2)}) collective-permute-start(bf16[256,768]{1,0:T(8,128)(2,1)S(1)} %collective-permute-done.16), channel_id=1, source_target_pairs={{0,4},{4,0},{8,12},{12,8},{16,20},{20,16},{24,28},{28,24},{1,5},{5... | collective-permute-start | bytes 1179656 | tf_op jit(solution)/shard_map/ppermute | solution.py:216
  95.9 17.4 %collective-permute-start.8 = (bf16[256,768]{1,0:T(8,128)(2,1)S(1)}, bf16[256,768]{1,0:T(8,128)(2,1)S(1)}, u32[]{:S(2)}, u32[]{:S(2)}) collective-permute-start(bf16[256,768]{1,0:T(8,128)(2,1)S(1)} %collective-permute-done.6), channel_id=1, source_target_pairs={{0,8},{4,12},{8,16},{12,20},{16,24},{20,28},{24,0},{28,4},{1,9},{5... | collective-permute-start | bytes 1179656 | tf_op jit(solution)/shard_map/ppermute | solution.py:211
  97.6 19.1 %collective-permute-start.7 = (bf16[256,768]{1,0:T(8,128)(2,1)S(1)}, bf16[256,768]{1,0:T(8,128)(2,1)S(1)}, u32[]{:S(2)}, u32[]{:S(2)}) collective-permute-start(bf16[256,768]{1,0:T(8,128)(2,1)S(1)} %collective-permute-done.6), channel_id=1, source_target_pairs={{0,4},{4,0},{8,12},{12,8},{16,20},{20,16},{24,28},{28,24},{1,5},{5... | collective-permute-start | bytes 1179656 | tf_op jit(solution)/shard_map/ppermute | solution.py:216
  108.2 12.6 %collective-permute-start.19 = (bf16[256,768]{1,0:T(8,128)(2,1)S(1)}, bf16[256,768]{1,0:T(8,128)(2,1)S(1)}, u32[]{:S(2)}, u32[]{:S(2)}) collective-permute-start(bf16[256,768]{1,0:T(8,128)(2,1)S(1)} %collective-permute-done.17), channel_id=1, source_target_pairs={{0,8},{4,12},{8,16},{12,20},{16,24},{20,28},{24,0},{28,4},{1,9},{5... | collective-permute-start | bytes 1179656 | tf_op jit(solution)/shard_map/ppermute | solution.py:211
  113.3 10.9 %collective-permute-start.9 = (bf16[256,768]{1,0:T(8,128)(2,1)S(1)}, bf16[256,768]{1,0:T(8,128)(2,1)S(1)}, u32[]{:S(2)}, u32[]{:S(2)}) collective-permute-start(bf16[256,768]{1,0:T(8,128)(2,1)S(1)} %collective-permute-done.8), channel_id=1, source_target_pairs={{0,4},{4,0},{8,12},{12,8},{16,20},{20,16},{24,28},{28,24},{1,5},{5... | collective-permute-start | bytes 1179656 | tf_op jit(solution)/shard_map/ppermute | solution.py:216

commit v2 on v1

--- a/solution.py
+++ b/solution.py
@@ -13,76 +13,83 @@
 GRANT = 16 * 2**20
 
 
-def pack_kernel(owned, ids_ref, live_ref, blocks_ref, *refs):
-    out_refs = refs[:-2]
+def relative(here, k, owners, sign):
+    outer = owners // 2
+    return lax.rem(here // 2 + sign * (k // 2) + outer, outer) * 2 + lax.rem(here + k, 2)
+
+
+def pack_kernel(owned, here_ref, ids_ref, live_ref, blocks_ref, first_ref, *refs):
+    rest_refs = refs[:-2]
     pick_ref, sems = refs[-2:]
-    owners, _, lanes = out_refs[0].shape
+    owners, _, lanes = first_ref.shape
     width = blocks_ref.shape[1]
     group = live_ref.shape[1] // owners
     row = lax.broadcasted_iota(jnp.int32, (TAIL, 128), 0)
     lane = lax.broadcasted_iota(jnp.int32, (TAIL, 128), 1)
 
-    def copy(owner, k, slot, c):
-        return pltpu.make_async_copy(
-            blocks_ref.at[slot, :, pl.ds(c * lanes, lanes)],
-            out_refs[c].at[owner, pl.ds(k * width, width), :],
-            sems.at[owner, k, c],
-        )
-
-    @pl.loop(0, owners)
-    def _(owner):
+    def copies(owner, n, k, slot):
+        block = blocks_ref.at[slot]
+        rows = pl.ds(k * width, width)
+        yield pltpu.make_async_copy(
+            block.at[:, pl.ds(0, lanes)], first_ref.at[owner, rows, :], sems.at[n, k, 0]
+        )
+        for c in range(1, len(rest_refs) // owners + 1):
+            yield pltpu.make_async_copy(
+                block.at[:, pl.ds(c * lanes, lanes)],
+                rest_refs[(c - 1) * owners + n].at[rows, :],
+                sems.at[n, k, c],
+            )
+
+    for n in range(owners):
+        owner = relative(here_ref[0], n, owners, 1)
         base = owner * group
         count = jnp.int32(0)
         for j in range(group):
-            pick_ref[jnp.minimum(count, LIVE)] = base + j
+            pick_ref[n, jnp.minimum(count, LIVE)] = base + j
             count = count + live_ref[0, base + j]
         tile = jnp.zeros((TAIL, 128), jnp.int32)
         for k in range(LIVE):
-            slot = jnp.where(k < count, pick_ref[k], base)
-            for c in range(len(out_refs)):
-                copy(owner, k, slot, c).start()
+            slot = jnp.where(k < count, pick_ref[n, k], base)
+            for copy in copies(owner, n, k, slot):
+                copy.start()
             mu = ids_ref[0, 0, slot]
             nu = jnp.where(k < count, lax.rem(ids_ref[1, 0, slot], owned), owned)
             tile = jnp.where((row == 0) & (lane == k), mu, tile)
             tile = jnp.where((row == 0) & (lane == LIVE + k), nu, tile)
-        out_refs[0][owner, LIVE * width :, :] = tile.astype(jnp.float32).astype(jnp.bfloat16)
-
-    @pl.loop(0, owners)
-    def _(owner):
+        first_ref[owner, LIVE * width :, :] = tile.astype(jnp.float32).astype(jnp.bfloat16)
+    for n in range(owners):
         for k in range(LIVE):
-            for c in range(len(out_refs)):
-                copy(owner, k, 0, c).wait()
-
-
-def pack(block_ids, live_mask, blocks, owners, owned):
+            for copy in copies(relative(here_ref[0], n, owners, 1), n, k, 0):
+                copy.wait()
+
+
+def pack(here, block_ids, live_mask, blocks, owners, owned):
     _, width, minor = blocks.shape
     chunks = minor // 128
-    shapes = [
-        jax.ShapeDtypeStruct((owners, LIVE * width + (0 if c else TAIL), 128), jnp.bfloat16)
-        for c in range(chunks)
-    ]
+    shapes = [jax.ShapeDtypeStruct((owners, LIVE * width + TAIL, 128), jnp.bfloat16)]
+    shapes += [jax.ShapeDtypeStruct((LIVE * width, 128), jnp.bfloat16)] * (
+        owners * (chunks - 1)
+    )
+    smem = pl.BlockSpec(memory_space=pltpu.SMEM)
     return pl.pallas_call(
         functools.partial(pack_kernel, owned),
         out_shape=shapes,
-        in_specs=[
-            pl.BlockSpec(memory_space=pltpu.SMEM),
-            pl.BlockSpec(memory_space=pltpu.SMEM),
-            pl.BlockSpec(memory_space=pl.ANY),
-        ],
-        out_specs=[pl.BlockSpec(memory_space=pltpu.VMEM)] * chunks,
+        in_specs=[smem, smem, smem, pl.BlockSpec(memory_space=pl.ANY)],
+        out_specs=[pl.BlockSpec(memory_space=pltpu.VMEM)] * len(shapes),
         scratch_shapes=[
-            pltpu.SMEM((LIVE + 1,), jnp.int32),
+            pltpu.SMEM((owners, LIVE + 1), jnp.int32),
             pltpu.SemaphoreType.DMA((owners, LIVE, chunks)),
         ],
         name="pack_live",
-    )(block_ids, live_mask, pltpu.with_memory_space_constraint(blocks, pltpu.HBM))
-
-
-def half_kernel(owned, width, me_ref, tail_ref, got_ref, coeff_ref, *refs):
+    )(here, block_ids, live_mask, pltpu.with_memory_space_constraint(blocks, pltpu.HBM))
+
+
+def half_kernel(owned, width, rest, place_ref, tail_ref, coeff_ref, *refs):
+    got_refs, refs = refs[:rest], refs[rest:]
     out_refs = refs[:-4]
     ids_vmem, ids_smem, total, sem = refs[-4:]
-    owners = got_ref.shape[0]
-    aux = got_ref.shape[2] // width
+    owners, _, lanes = tail_ref.shape
+    aux = lanes // width
     for p in range(owners):
         ids_vmem[p : p + 1, :] = tail_ref[p, 0:1, :].astype(jnp.float32).astype(jnp.int32)
     ids = pltpu.make_async_copy(ids_vmem, ids_smem, sem)
@@ -90,23 +97,32 @@
     total[...] = jnp.zeros_like(total)
     ids.wait()
 
-    @pl.loop(0, owners)
-    def _(p):
-        for k in range(LIVE):
-            mu = ids_smem[p, k]
-            nu = ids_smem[p, LIVE + k]
-            block = got_ref[p, k * width : (k + 1) * width, :]
-            stacked = jnp.concatenate(
-                [block[:, q * width : (q + 1) * width] for q in range(aux)], axis=0
-            )
-            coeff = coeff_ref[pl.ds(pl.multiple_of(mu * width, width), width), :]
-            total[nu] += lax.dot_general(
-                coeff, stacked, (((0,), (1,)), ((), ())), preferred_element_type=jnp.float32
-            )
+    def add(p, k, block):
+        mu = ids_smem[p, k]
+        nu = ids_smem[p, LIVE + k]
+        stacked = jnp.concatenate(
+            [block[:, q * width : (q + 1) * width] for q in range(aux)], axis=0
+        )
+        coeff = coeff_ref[pl.ds(pl.multiple_of(mu * width, width), width), :]
+        total[nu] += lax.dot_general(
+            coeff, stacked, (((0,), (1,)), ((), ())), preferred_element_type=jnp.float32
+        )
+
+    if rest > 1:
+        for n, got_ref in enumerate(got_refs):
+            p = relative(place_ref[1], n, owners, -1)
+            for k in range(LIVE):
+                add(p, k, got_ref[k * width : (k + 1) * width, :])
+    else:
+
+        @pl.loop(0, owners)
+        def _(p):
+            for k in range(LIVE):
+                add(p, k, got_refs[0][p, k * width : (k + 1) * width, :])
 
     slab = total.shape[1] // len(out_refs)
     for j, out_ref in enumerate(out_refs):
-        start = pl.multiple_of((me_ref[0] ^ j) * slab, slab)
+        start = pl.multiple_of((place_ref[0] ^ j) * slab, slab)
         for b in range(0, owned, 2):
             pair = [total[c, pl.ds(start, slab), :] for c in range(b, min(b + 2, owned))]
             for q in range(aux):
@@ -117,25 +133,28 @@
                 )
 
 
-def half_transform(me, first, got, coeffs, owned, width, occ):
-    owners, _, lanes = got.shape
+def half_transform(place, first, gots, coeffs, owned, width, occ):
+    owners, _, lanes = first.shape
     aux = lanes // width
     occ_count = coeffs.shape[1]
     shape = jax.ShapeDtypeStruct((aux * occ_count // occ, owned * width), jnp.bfloat16)
-    vmem = pl.BlockSpec(memory_space=pltpu.VMEM)
 
     def whole(*dims):
         return pl.BlockSpec(dims, lambda g: (0,) * len(dims))
 
+    if len(gots) == 1:
+        blocks = [whole(owners, LIVE * width, lanes)]
+    else:
+        blocks = [whole(*got.shape) for got in gots]
     return pl.pallas_call(
-        functools.partial(half_kernel, owned, width),
+        functools.partial(half_kernel, owned, width, len(gots)),
         grid=(1,),
         out_shape=[shape] * occ,
         in_specs=[
             pl.BlockSpec(memory_space=pltpu.SMEM),
             pl.BlockSpec((owners, TAIL, lanes), lambda g: (0, LIVE * width // TAIL, 0)),
-            pl.BlockSpec((owners, LIVE * width, lanes), lambda g: (0, 0, 0)),
             whole(*coeffs.shape),
+            *blocks,
         ],
         out_specs=[whole(*shape.shape)] * occ,
         scratch_shapes=[
@@ -146,12 +165,12 @@
         ],
         cost_estimate=pl.CostEstimate(
             flops=2 * owners * LIVE * width * lanes * occ_count,
-            bytes_accessed=2 * (got.size + coeffs.size + occ * shape.size),
+            bytes_accessed=2 * (first.size + coeffs.size + occ * shape.size),
             transcendentals=0,
         ),
         compiler_params=pltpu.CompilerParams(vmem_limit_bytes=GRANT),
         name="half_transform",
-    )(me, first, got, pltpu.with_memory_space_constraint(coeffs, pltpu.HBM))
+    )(place, first, pltpu.with_memory_space_constraint(coeffs, pltpu.HBM), *gots)
 
 
 def place_kernel(occ, me_ref, *refs):
@@ -235,13 +254,22 @@
                 total = term if total is None else total + term
         return total
 
-    sends = pack(block_ids, live_mask, blocks, owners, owned)
-    gots = []
-    for send in sends:
-        gots.append(lax.all_to_all(send, "pair", split_axis=0, concat_axis=0, tiled=True))
+    spot = jnp.stack([me, here.astype(jnp.int32)])
+    sends = pack(spot[1:], block_ids, live_mask, blocks, owners, owned)
+    first = lax.all_to_all(sends[0], "pair", split_axis=0, concat_axis=0, tiled=True)
+    gots = [[first]]
+    for c in range(1, 1 + len(sends[1:]) // owners):
+        mine = sends[1 + (c - 1) * owners : 1 + c * owners]
+        got = [pltpu.with_memory_space_constraint(mine[0], pltpu.HBM)]
+        for n in range(1, owners):
+            target = [
+                (p, (p // 2 + n // 2) % outer * 2 + (p + n) % 2) for p in range(owners)
+            ]
+            got.append(lax.ppermute(mine[n], "pair", target))
+        gots.append(got)
     results = []
     for c, got in enumerate(gots):
-        halves = half_transform(me.reshape(1), gots[0], got, occ_coeffs, owned, width, occ)
+        halves = half_transform(spot, first, got, occ_coeffs, owned, width, occ)
         parts = [across(halves[j], j) for j in range(occ)]
         piece = jnp.concatenate(parts, axis=0) if occ > 1 else parts[0]
         results.append(second_half(*gather(piece, c == len(gots) - 1)))

time: 127 us -> 120 us (0.945)
  blocking collectives: 21.8 us -> 0 us
  starting transfers between devices: 17.2 us -> 36.3 us
  waiting for transfers between devices: 56.5 us -> 53.5 us
  Pallas kernels: 14 us -> 12.6 us
    all_to_all x1 -> x0, blocking collectives: 21.8 us -> none  [on_device(): lax.all_to_all(send, 'pair', split_axis=0, concat_axis=0, tiled=True)]
    all_to_all x1, waiting for transfers between devices: 14.9 us -> 0.01 us  [on_device(): lax.all_to_all(sends[0], 'pair', split_axis=0, concat_axis=0, tiled=True)]
    ppermute x0 -> x7, waiting for transfers between devices: none -> 13.8 us  [on_device(): got.append(lax.ppermute(mine[n], 'pair', target))]
    ppermute x0 -> x7, starting transfers between devices: none -> 12.1 us  [on_device(): got.append(lax.ppermute(mine[n], 'pair', target))]
    ppermute x7, waiting for transfers between devices: 25.7 us -> 19.4 us  [along(): lax.ppermute(array, 'pair', [(p, (p // 2 + 1) % outer * 2 + p % 2) for p...]
    ppermute x7, starting transfers between devices: 1.74 us -> 7.6 us  [along(): lax.ppermute(array, 'pair', [(p, (p // 2 + 1) % outer * 2 + p % 2) for p...]
    ppermute x7, waiting for transfers between devices: 11.6 us -> 17.3 us  [swap(): return lax.ppermute(array, 'pair', [(p, p ^ 1) for p in range(owners)])]
    all_to_all x1, starting transfers between devices: 3.59 us -> 7.32 us  [on_device(): lax.all_to_all(sends[0], 'pair', split_axis=0, concat_axis=0, tiled=True)]
  transfers between devices with their start and end apart: 21 -> 28, of which waited for: 11 -> 16; matrix products, arithmetic and copies ran while one was open for 13% -> 14% of each run, Pallas kernels for 4% -> 4%
where the time goes in v2:
time: 120 us; the launch traced here: 119 us
  waiting for transfers between devices  53.5 us (45%)
  starting transfers between devices  36.3 us (30%)
  matrix products  16.4 us (14%)
  Pallas kernels  12.6 us (10%)
    ppermute x7, waiting for transfers between devices, along(): lax.ppermute(array, 'pair', [(p, (p // 2 + 1) % outer * 2 + p % 2) for p...  19.4 us
    ppermute x7, waiting for transfers between devices, swap(): return lax.ppermute(array, 'pair', [(p, p ^ 1) for p in range(owners)])  17.3 us
    dot_general x16, matrix products, second_half(): term = jnp.dot(array, part, preferred_element_type=jnp.float32)  16.4 us
    ppermute x7, waiting for transfers between devices, on_device(): got.append(lax.ppermute(mine[n], 'pair', target))  13.8 us
    ppermute x7, starting transfers between devices, on_device(): got.append(lax.ppermute(mine[n], 'pair', target))  12.1 us
    ppermute x7, starting transfers between devices, along(): lax.ppermute(array, 'pair', [(p, (p // 2 + 1) % outer * 2 + p % 2) for p...  7.6 us
    pallas_call x2, Pallas kernels, half_transform(): pl.pallas_call(functools.partial(half_kernel, owned, width, len(gots)), g...  7.46 us
    all_to_all x1, starting transfers between devices, on_device(): lax.all_to_all(sends[0], 'pair', split_axis=0, concat_axis=0, tiled=True)  7.32 us
  transfers between devices with their start and end apart: 28, of which 16 were waited for; matrix products, arithmetic and copies ran while one was open for 14% of the time, Pallas kernels for 4%

profile of v2, /device:TPU:0, one launch (start us, length us, event | category | flops | bytes accessed | tf_op | source)
XLA Modules:
  0.0 119.1 jit_solution(8597448560408966438)
XLA Ops:
  0.0 3.5 %pack_live.1 = (bf16[8,272,128]{2,1,0:T(8,128)(2,1)}, bf16[256,128]{1,0:T(8,128)(2,1)}, bf16[256,128]{1,0:T(8,128)(2,1)}, bf16[256,128]{1,0:T(8,128)(2,1)}, bf16...) custom-call(s32[1]{0:T(128)} %bitcast.1.here_ref, ...), custom_call_target="tpu_custom_call" | custom-call | tf_op jit(solution)/shard_map/pack_live/pallas_call | solution.py:74
  3.5 7.3 %all-to-all-start = ((bf16[8,272,128]{2,1,0:T(8,128)(2,1)}), bf16[8,272,128]{2,1,0:T(8,128)(2,1)S(1)}, u32[]{:S(2)}, u32[]{:S(2)}) async-start(bf16[8,272,128]{2,1,0:T(8,128)(2,1)} %get-tuple-element.22), calls=%async_computation | async-start | bytes 1114112 | tf_op jit(solution)/shard_map/all_to_all | solution.py:259
  10.8 2.0 %collective-permute-start.10 = (bf16[256,128]{1,0:T(8,128)(2,1)}, bf16[256,128]{1,0:T(8,128)(2,1)S(1)}, u32[]{:S(2)}, u32[]{:S(2)}) collective-permute-start(bf16[256,128]{1,0:T(8,128)(2,1)} %get-tuple-element.28), channel_id=1, source_target_pairs={{0,4},{4,0},{8,12},{12,8},{16,20},{20,16},{24,28},{28,24},{1,5},{5... | collective-permute-start | bytes 196616 | tf_op jit(solution)/shard_map/ppermute | solution.py:268
  12.9 1.5 %collective-permute-start.11 = (bf16[256,128]{1,0:T(8,128)(2,1)}, bf16[256,128]{1,0:T(8,128)(2,1)S(1)}, u32[]{:S(2)}, u32[]{:S(2)}) collective-permute-start(bf16[256,128]{1,0:T(8,128)(2,1)} %get-tuple-element.29), channel_id=1, source_target_pairs={{0,8},{4,12},{8,16},{12,20},{16,24},{20,28},{24,0},{28,4},{1,9},{5... | collective-permute-start | bytes 196616 | tf_op jit(solution)/shard_map/ppermute | solution.py:268
  14.3 1.5 %collective-permute-start.12 = (bf16[256,128]{1,0:T(8,128)(2,1)}, bf16[256,128]{1,0:T(8,128)(2,1)S(1)}, u32[]{:S(2)}, u32[]{:S(2)}) collective-permute-start(bf16[256,128]{1,0:T(8,128)(2,1)} %get-tuple-element.30), channel_id=1, source_target_pairs={{0,12},{4,8},{8,20},{12,16},{16,28},{20,24},{24,4},{28,0},{1,13},{... | collective-permute-start | bytes 196616 | tf_op jit(solution)/shard_map/ppermute | solution.py:268
  15.8 0.9 collective-permute-start.13
  16.7 2.9 %collective-permute-start.14 = (bf16[256,128]{1,0:T(8,128)(2,1)}, bf16[256,128]{1,0:T(8,128)(2,1)S(1)}, u32[]{:S(2)}, u32[]{:S(2)}) collective-permute-start(bf16[256,128]{1,0:T(8,128)(2,1)} %get-tuple-element.32), channel_id=1, source_target_pairs={{0,20},{4,16},{8,28},{12,24},{16,4},{20,0},{24,12},{28,8},{1,21},{... | collective-permute-start | bytes 196616 | tf_op jit(solution)/shard_map/ppermute | solution.py:268
  19.6 2.7 %collective-permute-start.15 = (bf16[256,128]{1,0:T(8,128)(2,1)}, bf16[256,128]{1,0:T(8,128)(2,1)S(1)}, u32[]{:S(2)}, u32[]{:S(2)}) collective-permute-start(bf16[256,128]{1,0:T(8,128)(2,1)} %get-tuple-element.33), channel_id=1, source_target_pairs={{0,24},{4,28},{8,0},{12,4},{16,8},{20,12},{24,16},{28,20},{1,25},{... | collective-permute-start | bytes 196616 | tf_op jit(solution)/shard_map/ppermute | solution.py:268
  22.3 4.5 %collective-permute-done.11.refs_2_ = bf16[256,128]{1,0:T(8,128)(2,1)S(1)} collective-permute-done((bf16[256,128]{1,0:T(8,128)(2,1)}, bf16[256,128]{1,0:T(8,128)(2,1)S(1)}, u32[]{:S(2)}, u32[]{:S(2)}) %collective-permute-start.11) | collective-permute-done | bytes 65568 | tf_op jit(solution)/shard_map/ppermute | solution.py:268
  26.8 0.6 collective-permute-start.16
  27.5 1.7 %collective-permute-done.12.refs_3_ = bf16[256,128]{1,0:T(8,128)(2,1)S(1)} collective-permute-done((bf16[256,128]{1,0:T(8,128)(2,1)}, bf16[256,128]{1,0:T(8,128)(2,1)S(1)}, u32[]{:S(2)}, u32[]{:S(2)}) %collective-permute-start.12) | collective-permute-done | bytes 65568 | tf_op jit(solution)/shard_map/ppermute | solution.py:268
  29.2 5.3 %collective-permute-done.13.refs_4_ = bf16[256,128]{1,0:T(8,128)(2,1)S(1)} collective-permute-done((bf16[256,128]{1,0:T(8,128)(2,1)}, bf16[256,128]{1,0:T(8,128)(2,1)S(1)}, u32[]{:S(2)}, u32[]{:S(2)}) %collective-permute-start.13) | collective-permute-done | bytes 65568 | tf_op jit(solution)/shard_map/ppermute | solution.py:268
  34.5 1.9 %collective-permute-done.14.refs_5_ = bf16[256,128]{1,0:T(8,128)(2,1)S(1)} collective-permute-done((bf16[256,128]{1,0:T(8,128)(2,1)}, bf16[256,128]{1,0:T(8,128)(2,1)S(1)}, u32[]{:S(2)}, u32[]{:S(2)}) %collective-permute-start.14) | collective-permute-done | bytes 65568 | tf_op jit(solution)/shard_map/ppermute | solution.py:268
  36.8 3.1 %half_transform.3 = (bf16[64,768]{1,0:T(8,128)(2,1)S(1)}, bf16[64,768]{1,0:T(8,128)(2,1)S(1)}, bf16[64,768]{1,0:T(8,128)(2,1)S(1)}, bf16[64,768]{1,0:T(8,128)(2,1)S(1)}) custom-call(s32[2]{0:T(128)S(1)} %pad_add_fusion.place_ref, bf16[8,272,128]{2,1,0:T(8,128)(2,1)S(1)} %all-to-all-done.tail_ref.refs_0_, bf16[6144,128]{1,0:T(8,128)(2,1)} %coeff_ref.3, ...), custom_call_target="tpu_custom_call" | custom-call | flops 67108864 | bytes 2523136 | tf_op jit(solution)/shard_map/half_transform/pallas_call | solution.py:149
  39.9 1.6 %collective-permute-start.18 = (bf16[64,768]{1,0:T(8,128)(2,1)S(1)}, bf16[64,768]{1,0:T(8,128)(2,1)S(1)}, u32[]{:S(2)}, u32[]{:S(2)}) collective-permute-start(bf16[64,768]{1,0:T(8,128)(2,1)S(1)} %get-tuple-element.37), channel_id=1, source_target_pairs={{0,2},{1,3},{2,0},{3,1},{4,6},{5,7},{6,4},{7,5},{8,10},{9,11},{10,... | collective-permute-start | bytes 294920 | tf_op jit(solution)/shard_map/ppermute | solution.py:227
  41.8 4.4 %half_transform.2 = (bf16[64,768]{1,0:T(8,128)(2,1)S(1)}, bf16[64,768]{1,0:T(8,128)(2,1)S(1)}, bf16[64,768]{1,0:T(8,128)(2,1)S(1)}, bf16[64,768]{1,0:T(8,128)(2,1)S(1)}) custom-call(s32[2]{0:T(128)S(1)} %pad_add_fusion.place_ref, bf16[8,272,128]{2,1,0:T(8,128)(2,1)S(1)} %all-to-all-done.tail_ref.refs_0_, bf16[6144,128]{1,0:T(8,128)(2,1)} %coeff_ref.3, ...), custom_call_target="tpu_custom_call" | custom-call | flops 67108864 | bytes 2523136 | tf_op jit(solution)/shard_map/half_transform/pallas_call | solution.py:149
  46.6 1.5 %collective-permute-start.1 = (bf16[64,768]{1,0:T(8,128)(2,1)S(1)}, bf16[64,768]{1,0:T(8,128)(2,1)S(1)}, u32[]{:S(2)}, u32[]{:S(2)}) collective-permute-start(bf16[64,768]{1,0:T(8,128)(2,1)S(1)} %get-tuple-element.25), channel_id=1, source_target_pairs={{0,2},{1,3},{2,0},{3,1},{4,6},{5,7},{6,4},{7,5},{8,10},{9,11},{10,... | collective-permute-start | bytes 294920 | tf_op jit(solution)/shard_map/ppermute | solution.py:227
  48.3 2.0 %collective-permute-start.21 = (bf16[256,768]{1,0:T(8,128)(2,1)S(1)}, bf16[256,768]{1,0:T(8,128)(2,1)S(1)}, u32[]{:S(2)}, u32[]{:S(2)}) collective-permute-start(bf16[256,768]{1,0:T(8,128)(2,1)S(1)} %constant_dynamic-update-slice_fusion.4), channel_id=1, source_target_pairs={{0,8},{4,12},{8,16},{12,20},{16,24},{20,28},{24,0},{28,4},{1,9},{5... | collective-permute-start | bytes 1179656 | tf_op jit(solution)/shard_map/ppermute | solution.py:230
  50.3 1.4 %collective-permute-done.1 = bf16[64,768]{1,0:T(8,128)(2,1)S(1)} collective-permute-done((bf16[64,768]{1,0:T(8,128)(2,1)S(1)}, bf16[64,768]{1,0:T(8,128)(2,1)S(1)}, u32[]{:S(2)}, u32[]{:S(2)}) %collective-permute-start.1) | collective-permute-done | bytes 98336 | tf_op jit(solution)/shard_map/ppermute | solution.py:227
  51.7 1.6 %collective-permute-done.2 = bf16[64,768]{1,0:T(8,128)(2,1)S(1)} collective-permute-done((bf16[64,768]{1,0:T(8,128)(2,1)S(1)}, bf16[64,768]{1,0:T(8,128)(2,1)S(1)}, u32[]{:S(2)}, u32[]{:S(2)}) %collective-permute-start.2) | collective-permute-done | bytes 98336 | tf_op jit(solution)/shard_map/ppermute | solution.py:227
  53.3 2.0 %collective-permute-start.4 = (bf16[256,768]{1,0:T(8,128)(2,1)S(1)}, bf16[256,768]{1,0:T(8,128)(2,1)S(1)}, u32[]{:S(2)}, u32[]{:S(2)}) collective-permute-start(bf16[256,768]{1,0:T(8,128)(2,1)S(1)} %constant_dynamic-update-slice_fusion), channel_id=1, source_target_pairs={{0,8},{4,12},{8,16},{12,20},{16,24},{20,28},{24,0},{28,4},{1,9},{5... | collective-permute-start | bytes 1179656 | tf_op jit(solution)/shard_map/ppermute | solution.py:230
  55.3 0.6 collective-permute-start.20
  55.9 1.4 %collective-permute-start.3 = (bf16[256,768]{1,0:T(8,128)(2,1)S(1)}, bf16[256,768]{1,0:T(8,128)(2,1)S(1)}, u32[]{:S(2)}, u32[]{:S(2)}) collective-permute-start(bf16[256,768]{1,0:T(8,128)(2,1)S(1)} %constant_dynamic-update-slice_fusion), channel_id=1, source_target_pairs={{0,4},{4,0},{8,12},{12,8},{16,20},{20,16},{24,28},{28,24},{1,5},{5... | collective-permute-start | bytes 1179656 | tf_op jit(solution)/shard_map/ppermute | solution.py:235
  57.4 4.8 %collective-permute-done.21 = bf16[256,768]{1,0:T(8,128)(2,1)S(1)} collective-permute-done((bf16[256,768]{1,0:T(8,128)(2,1)S(1)}, bf16[256,768]{1,0:T(8,128)(2,1)S(1)}, u32[]{:S(2)}, u32[]{:S(2)}) %collective-permute-start.21) | collective-permute-done | bytes 393248 | tf_op jit(solution)/shard_map/ppermute | solution.py:230
  62.3 0.6 collective-permute-start.22
  62.9 7.7 %collective-permute-done.4 = bf16[256,768]{1,0:T(8,128)(2,1)S(1)} collective-permute-done((bf16[256,768]{1,0:T(8,128)(2,1)S(1)}, bf16[256,768]{1,0:T(8,128)(2,1)S(1)}, u32[]{:S(2)}, u32[]{:S(2)}) %collective-permute-start.4) | collective-permute-done | bytes 393248 | tf_op jit(solution)/shard_map/ppermute | solution.py:230
  70.7 1.8 %fusion.20 = f32[256,640]{1,0:T(8,128)S(1)} fusion(bf16[256,768]{1,0:T(8,128)(2,1)S(1)} %collective-permute-done.21, bf16[6144,640]{1,0:T(8,128)(2,1)} %param.7, s32[]{:T(128)S(6)} %select_n.134), kind=kOutput, calls=%fused_computation.28 | convolution fusion | flops 251658240 | bytes 2031620 | tf_op jit(solution)/shard_map/dot_general | solution.py:253
  72.6 1.7 %fusion.22 = f32[256,640]{1,0:T(8,128)S(1)} fusion(bf16[256,768]{1,0:T(8,128)(2,1)S(1)} %collective-permute-done.4, bf16[6144,640]{1,0:T(8,128)(2,1)} %param.7, s32[]{:T(128)S(6)} %select_n.134), kind=kOutput, calls=%fused_computation.30 | convolution fusion | flops 251658240 | bytes 2031620 | tf_op jit(solution)/shard_map/dot_general | solution.py:253
  74.3 0.7 collective-permute-start.5
  74.9 1.7 %fusion.24 = f32[256,640]{1,0:T(8,128)S(1)} fusion(bf16[256,768]{1,0:T(8,128)(2,1)S(1)} %collective-permute-done.20, bf16[6144,640]{1,0:T(8,128)(2,1)} %param.7, s32[]{:T(128)S(6)} %select_n.132), kind=kOutput, calls=%fused_computation.32 | convolution fusion | flops 251658240 | bytes 2031620 | tf_op jit(solution)/shard_map/dot_general | solution.py:253
  76.6 1.8 %fusion.2 = f32[256,640]{1,0:T(8,128)S(1)} fusion(f32[256,640]{1,0:T(8,128)S(1)} %fusion.20, f32[256,640]{1,0:T(8,128)S(1)} %fusion.24, bf16[256,768]{1,0:T(8,128)(2,1)S(1)} %constant_dynamic-update-slice_fusion.4, bf16[6144,640]{1,0:T(8,128)(2,1)} %param.7, s32[]{:T(128)S(6)} %select_n.131), kind=kOutput, calls=%fused_computation.6 | convolution fusion | flops 251985920 | bytes 3342340 | tf_op jit(solution)/shard_map/dot_general | solution.py:253
  78.5 1.7 %fusion.26 = f32[256,640]{1,0:T(8,128)S(1)} fusion(bf16[256,768]{1,0:T(8,128)(2,1)S(1)} %collective-permute-done.3, bf16[6144,640]{1,0:T(8,128)(2,1)} %param.7, s32[]{:T(128)S(6)} %select_n.132), kind=kOutput, calls=%fused_computation.34 | convolution fusion | flops 251658240 | bytes 2031620 | tf_op jit(solution)/shard_map/dot_general | solution.py:253
  80.2 1.7 %fusion.5 = f32[256,640]{1,0:T(8,128)S(1)} fusion(f32[256,640]{1,0:T(8,128)S(1)} %fusion.22, f32[256,640]{1,0:T(8,128)S(1)} %fusion.26, bf16[256,768]{1,0:T(8,128)(2,1)S(1)} %constant_dynamic-update-slice_fusion, bf16[6144,640]{1,0:T(8,128)(2,1)} %param.7, s32[]{:T(128)S(6)} %select_n.131), kind=kOutput, calls=%fused_computation.13 | convolution fusion | flops 251985920 | bytes 3342340 | tf_op jit(solution)/shard_map/dot_general | solution.py:253
  81.9 1.8 %collective-permute-start.25 = (bf16[256,768]{1,0:T(8,128)(2,1)S(1)}, bf16[256,768]{1,0:T(8,128)(2,1)S(1)}, u32[]{:S(2)}, u32[]{:S(2)}) collective-permute-start(bf16[256,768]{1,0:T(8,128)(2,1)S(1)} %collective-permute-done.23), channel_id=1, source_target_pairs={{0,8},{4,12},{8,16},{12,20},{16,24},{20,28},{24,0},{28,4},{1,9},{5... | collective-permute-start | bytes 1179656 | tf_op jit(solution)/shard_map/ppermute | solution.py:230
  83.7 0.9 collective-permute-start.24
  84.6 2.8 %collective-permute-done.6 = bf16[256,768]{1,0:T(8,128)(2,1)S(1)} collective-permute-done((bf16[256,768]{1,0:T(8,128)(2,1)S(1)}, bf16[256,768]{1,0:T(8,128)(2,1)S(1)}, u32[]{:S(2)}, u32[]{:S(2)}) %collective-permute-start.6) | collective-permute-done | bytes 393248 | tf_op jit(solution)/shard_map/ppermute | solution.py:230
  87.6 1.7 %fusion.14 = f32[256,640]{1,0:T(8,128)S(1)} fusion(bf16[256,768]{1,0:T(8,128)(2,1)S(1)} %collective-permute-done.23, bf16[6144,640]{1,0:T(8,128)(2,1)} %param.7, s32[]{:T(128)S(6)} %select_n.137), kind=kOutput, calls=%fused_computation.22 | convolution fusion | flops 251658240 | bytes 2031620 | tf_op jit(solution)/shard_map/dot_general | solution.py:253
  89.3 0.7 collective-permute-start.7
  90.9 1.7 %collective-permute-done.5 = bf16[256,768]{1,0:T(8,128)(2,1)S(1)} collective-permute-done((bf16[256,768]{1,0:T(8,128)(2,1)S(1)}, bf16[256,768]{1,0:T(8,128)(2,1)S(1)}, u32[]{:S(2)}, u32[]{:S(2)}) %collective-permute-start.5) | collective-permute-done | bytes 393248 | tf_op jit(solution)/shard_map/ppermute | solution.py:235
  93.1 7.9 %collective-permute-done.24 = bf16[256,768]{1,0:T(8,128)(2,1)S(1)} collective-permute-done((bf16[256,768]{1,0:T(8,128)(2,1)S(1)}, bf16[256,768]{1,0:T(8,128)(2,1)S(1)}, u32[]{:S(2)}, u32[]{:S(2)}) %collective-permute-start.24) | collective-permute-done | bytes 393248 | tf_op jit(solution)/shard_map/ppermute | solution.py:235
  101.0 1.2 %collective-permute-start.26 = (bf16[256,768]{1,0:T(8,128)(2,1)S(1)}, bf16[256,768]{1,0:T(8,128)(2,1)S(1)}, u32[]{:S(2)}, u32[]{:S(2)}) collective-permute-start(bf16[256,768]{1,0:T(8,128)(2,1)S(1)} %collective-permute-done.24), channel_id=1, source_target_pairs={{0,8},{4,12},{8,16},{12,20},{16,24},{20,28},{24,0},{28,4},{1,9},{5... | collective-permute-start | bytes 1179656 | tf_op jit(solution)/shard_map/ppermute | solution.py:230
  102.2 1.7 %collective-permute-done.8 = bf16[256,768]{1,0:T(8,128)(2,1)S(1)} collective-permute-done((bf16[256,768]{1,0:T(8,128)(2,1)S(1)}, bf16[256,768]{1,0:T(8,128)(2,1)S(1)}, u32[]{:S(2)}, u32[]{:S(2)}) %collective-permute-start.8) | collective-permute-done | bytes 393248 | tf_op jit(solution)/shard_map/ppermute | solution.py:230
  104.0 0.5 collective-permute-start.9
  105.0 0.5 fusion
  106.0 3.5 %collective-permute-done.7 = bf16[256,768]{1,0:T(8,128)(2,1)S(1)} collective-permute-done((bf16[256,768]{1,0:T(8,128)(2,1)S(1)}, bf16[256,768]{1,0:T(8,128)(2,1)S(1)}, u32[]{:S(2)}, u32[]{:S(2)}) %collective-permute-start.7) | collective-permute-done | bytes 393248 | tf_op jit(solution)/shard_map/ppermute | solution.py:235
  110.0 2.4 %collective-permute-done.26 = bf16[256,768]{1,0:T(8,128)(2,1)S(1)} collective-permute-done((bf16[256,768]{1,0:T(8,128)(2,1)S(1)}, bf16[256,768]{1,0:T(8,128)(2,1)S(1)}, u32[]{:S(2)}, u32[]{:S(2)}) %collective-permute-start.26) | collective-permute-done | bytes 393248 | tf_op jit(solution)/shard_map/ppermute | solution.py:230
  112.8 4.2 %collective-permute-done.9 = bf16[256,768]{1,0:T(8,128)(2,1)S(1)} collective-permute-done((bf16[256,768]{1,0:T(8,128)(2,1)S(1)}, bf16[256,768]{1,0:T(8,128)(2,1)S(1)}, u32[]{:S(2)}, u32[]{:S(2)}) %collective-permute-start.9) | collective-permute-done | bytes 393248 | tf_op jit(solution)/shard_map/ppermute | solution.py:235
  117.5 1.6 %place.1 = bf16[32,16,640]{2,1,0:T(8,128)(2,1)} custom-call(s32[1]{0:T(128)} %bitcast.me_ref, f32[256,640]{1,0:T(8,128)S(1)} %convolution_add_fusion.4.refs_0_, f32[256,640]{1,0:T(8,128)S(1)} %convolution_add_fusion.refs_1_), custom_call_target="tpu_custom_call" | custom-call | tf_op jit(solution)/shard_map/place/pallas_call | solution.py:200
  (42 shorter events, 5.8 us)
Async XLA Ops:
  3.5 33.2 %all-to-all-start = ((bf16[8,272,128]{2,1,0:T(8,128)(2,1)}), bf16[8,272,128]{2,1,0:T(8,128)(2,1)S(1)}, u32[]{:S(2)}, u32[]{:S(2)}) async-start(bf16[8,272,128]{2,1,0:T(8,128)(2,1)} %get-tuple-element.22), calls=%async_computation | async-start | bytes 1114112 | tf_op jit(solution)/shard_map/all_to_all | solution.py:259
  10.8 8.8 %collective-permute-start.10 = (bf16[256,128]{1,0:T(8,128)(2,1)}, bf16[256,128]{1,0:T(8,128)(2,1)S(1)}, u32[]{:S(2)}, u32[]{:S(2)}) collective-permute-start(bf16[256,128]{1,0:T(8,128)(2,1)} %get-tuple-element.28), channel_id=1, source_target_pairs={{0,4},{4,0},{8,12},{12,8},{16,20},{20,16},{24,28},{28,24},{1,5},{5... | collective-permute-start | bytes 196616 | tf_op jit(solution)/shard_map/ppermute | solution.py:268
  12.9 13.9 %collective-permute-start.11 = (bf16[256,128]{1,0:T(8,128)(2,1)}, bf16[256,128]{1,0:T(8,128)(2,1)S(1)}, u32[]{:S(2)}, u32[]{:S(2)}) collective-permute-start(bf16[256,128]{1,0:T(8,128)(2,1)} %get-tuple-element.29), channel_id=1, source_target_pairs={{0,8},{4,12},{8,16},{12,20},{16,24},{20,28},{24,0},{28,4},{1,9},{5... | collective-permute-start | bytes 196616 | tf_op jit(solution)/shard_map/ppermute | solution.py:268
  14.3 14.8 %collective-permute-start.12 = (bf16[256,128]{1,0:T(8,128)(2,1)}, bf16[256,128]{1,0:T(8,128)(2,1)S(1)}, u32[]{:S(2)}, u32[]{:S(2)}) collective-permute-start(bf16[256,128]{1,0:T(8,128)(2,1)} %get-tuple-element.30), channel_id=1, source_target_pairs={{0,12},{4,8},{8,20},{12,16},{16,28},{20,24},{24,4},{28,0},{1,13},{... | collective-permute-start | bytes 196616 | tf_op jit(solution)/shard_map/ppermute | solution.py:268
  15.8 18.7 %collective-permute-start.13 = (bf16[256,128]{1,0:T(8,128)(2,1)}, bf16[256,128]{1,0:T(8,128)(2,1)S(1)}, u32[]{:S(2)}, u32[]{:S(2)}) collective-permute-start(bf16[256,128]{1,0:T(8,128)(2,1)} %get-tuple-element.31), channel_id=1, source_target_pairs={{0,16},{4,20},{8,24},{12,28},{16,0},{20,4},{24,8},{28,12},{1,17},{... | collective-permute-start | bytes 196616 | tf_op jit(solution)/shard_map/ppermute | solution.py:268
  16.7 19.6 %collective-permute-start.14 = (bf16[256,128]{1,0:T(8,128)(2,1)}, bf16[256,128]{1,0:T(8,128)(2,1)S(1)}, u32[]{:S(2)}, u32[]{:S(2)}) collective-permute-start(bf16[256,128]{1,0:T(8,128)(2,1)} %get-tuple-element.32), channel_id=1, source_target_pairs={{0,20},{4,16},{8,28},{12,24},{16,4},{20,0},{24,12},{28,8},{1,21},{... | collective-permute-start | bytes 196616 | tf_op jit(solution)/shard_map/ppermute | solution.py:268
  19.6 16.7 %collective-permute-start.15 = (bf16[256,128]{1,0:T(8,128)(2,1)}, bf16[256,128]{1,0:T(8,128)(2,1)S(1)}, u32[]{:S(2)}, u32[]{:S(2)}) collective-permute-start(bf16[256,128]{1,0:T(8,128)(2,1)} %get-tuple-element.33), channel_id=1, source_target_pairs={{0,24},{4,28},{8,0},{12,4},{16,8},{20,12},{24,16},{28,20},{1,25},{... | collective-permute-start | bytes 196616 | tf_op jit(solution)/shard_map/ppermute | solution.py:268
  26.8 10.0 %collective-permute-start.16 = (bf16[256,128]{1,0:T(8,128)(2,1)}, bf16[256,128]{1,0:T(8,128)(2,1)S(1)}, u32[]{:S(2)}, u32[]{:S(2)}) collective-permute-start(bf16[256,128]{1,0:T(8,128)(2,1)} %get-tuple-element.34), channel_id=1, source_target_pairs={{0,28},{4,24},{8,4},{12,0},{16,12},{20,8},{24,20},{28,16},{1,29},{... | collective-permute-start | bytes 196616 | tf_op jit(solution)/shard_map/ppermute | solution.py:268
  39.8 8.3 %collective-permute-start.17 = (bf16[64,768]{1,0:T(8,128)(2,1)S(1)}, bf16[64,768]{1,0:T(8,128)(2,1)S(1)}, u32[]{:S(2)}, u32[]{:S(2)}) collective-permute-start(bf16[64,768]{1,0:T(8,128)(2,1)S(1)} %get-tuple-element.36), channel_id=1, source_target_pairs={{0,1},{1,0},{2,3},{3,2},{4,5},{5,4},{6,7},{7,6},{8,9},{9,8},{10,11... | collective-permute-start | bytes 294920 | tf_op jit(solution)/shard_map/ppermute | solution.py:227
  39.9 8.3 %collective-permute-start.18 = (bf16[64,768]{1,0:T(8,128)(2,1)S(1)}, bf16[64,768]{1,0:T(8,128)(2,1)S(1)}, u32[]{:S(2)}, u32[]{:S(2)}) collective-permute-start(bf16[64,768]{1,0:T(8,128)(2,1)S(1)} %get-tuple-element.37), channel_id=1, source_target_pairs={{0,2},{1,3},{2,0},{3,1},{4,6},{5,7},{6,4},{7,5},{8,10},{9,11},{10,... | collective-permute-start | bytes 294920 | tf_op jit(solution)/shard_map/ppermute | solution.py:227
  41.5 6.8 %collective-permute-start.19 = (bf16[64,768]{1,0:T(8,128)(2,1)S(1)}, bf16[64,768]{1,0:T(8,128)(2,1)S(1)}, u32[]{:S(2)}, u32[]{:S(2)}) collective-permute-start(bf16[64,768]{1,0:T(8,128)(2,1)S(1)} %get-tuple-element.38), channel_id=1, source_target_pairs={{0,3},{1,2},{2,1},{3,0},{4,7},{5,6},{6,5},{7,4},{8,11},{9,10},{10,... | collective-permute-start | bytes 294920 | tf_op jit(solution)/shard_map/ppermute | solution.py:227
  46.2 4.1 %collective-permute-start = (bf16[64,768]{1,0:T(8,128)(2,1)S(1)}, bf16[64,768]{1,0:T(8,128)(2,1)S(1)}, u32[]{:S(2)}, u32[]{:S(2)}) collective-permute-start(bf16[64,768]{1,0:T(8,128)(2,1)S(1)} %get-tuple-element.24), channel_id=1, source_target_pairs={{0,1},{1,0},{2,3},{3,2},{4,5},{5,4},{6,7},{7,6},{8,9},{9,8},{10,11... | collective-permute-start | bytes 294920 | tf_op jit(solution)/shard_map/ppermute | solution.py:227
  46.6 5.1 %collective-permute-start.1 = (bf16[64,768]{1,0:T(8,128)(2,1)S(1)}, bf16[64,768]{1,0:T(8,128)(2,1)S(1)}, u32[]{:S(2)}, u32[]{:S(2)}) collective-permute-start(bf16[64,768]{1,0:T(8,128)(2,1)S(1)} %get-tuple-element.25), channel_id=1, source_target_pairs={{0,2},{1,3},{2,0},{3,1},{4,6},{5,7},{6,4},{7,5},{8,10},{9,11},{10,... | collective-permute-start | bytes 294920 | tf_op jit(solution)/shard_map/ppermute | solution.py:227
  48.2 5.2 %collective-permute-start.2 = (bf16[64,768]{1,0:T(8,128)(2,1)S(1)}, bf16[64,768]{1,0:T(8,128)(2,1)S(1)}, u32[]{:S(2)}, u32[]{:S(2)}) collective-permute-start(bf16[64,768]{1,0:T(8,128)(2,1)S(1)} %get-tuple-element.26), channel_id=1, source_target_pairs={{0,3},{1,2},{2,1},{3,0},{4,7},{5,6},{6,5},{7,4},{8,11},{9,10},{10,... | collective-permute-start | bytes 294920 | tf_op jit(solution)/shard_map/ppermute | solution.py:227
  48.3 13.8 %collective-permute-start.21 = (bf16[256,768]{1,0:T(8,128)(2,1)S(1)}, bf16[256,768]{1,0:T(8,128)(2,1)S(1)}, u32[]{:S(2)}, u32[]{:S(2)}) collective-permute-start(bf16[256,768]{1,0:T(8,128)(2,1)S(1)} %constant_dynamic-update-slice_fusion.4), channel_id=1, source_target_pairs={{0,8},{4,12},{8,16},{12,20},{16,24},{20,28},{24,0},{28,4},{1,9},{5... | collective-permute-start | bytes 1179656 | tf_op jit(solution)/shard_map/ppermute | solution.py:230
  53.3 17.2 %collective-permute-start.4 = (bf16[256,768]{1,0:T(8,128)(2,1)S(1)}, bf16[256,768]{1,0:T(8,128)(2,1)S(1)}, u32[]{:S(2)}, u32[]{:S(2)}) collective-permute-start(bf16[256,768]{1,0:T(8,128)(2,1)S(1)} %constant_dynamic-update-slice_fusion), channel_id=1, source_target_pairs={{0,8},{4,12},{8,16},{12,20},{16,24},{20,28},{24,0},{28,4},{1,9},{5... | collective-permute-start | bytes 1179656 | tf_op jit(solution)/shard_map/ppermute | solution.py:230
  55.3 18.9 %collective-permute-start.20 = (bf16[256,768]{1,0:T(8,128)(2,1)S(1)}, bf16[256,768]{1,0:T(8,128)(2,1)S(1)}, u32[]{:S(2)}, u32[]{:S(2)}) collective-permute-start(bf16[256,768]{1,0:T(8,128)(2,1)S(1)} %constant_dynamic-update-slice_fusion.4), channel_id=1, source_target_pairs={{0,4},{4,0},{8,12},{12,8},{16,20},{20,16},{24,28},{28,24},{1,5},{5... | collective-permute-start | bytes 1179656 | tf_op jit(solution)/shard_map/ppermute | solution.py:235
  55.9 22.5 %collective-permute-start.3 = (bf16[256,768]{1,0:T(8,128)(2,1)S(1)}, bf16[256,768]{1,0:T(8,128)(2,1)S(1)}, u32[]{:S(2)}, u32[]{:S(2)}) collective-permute-start(bf16[256,768]{1,0:T(8,128)(2,1)S(1)} %constant_dynamic-update-slice_fusion), channel_id=1, source_target_pairs={{0,4},{4,0},{8,12},{12,8},{16,20},{20,16},{24,28},{28,24},{1,5},{5... | collective-permute-start | bytes 1179656 | tf_op jit(solution)/shard_map/ppermute | solution.py:235
  62.1 19.7 %collective-permute-start.23 = (bf16[256,768]{1,0:T(8,128)(2,1)S(1)}, bf16[256,768]{1,0:T(8,128)(2,1)S(1)}, u32[]{:S(2)}, u32[]{:S(2)}) collective-permute-start(bf16[256,768]{1,0:T(8,128)(2,1)S(1)} %collective-permute-done.21), channel_id=1, source_target_pairs={{0,8},{4,12},{8,16},{12,20},{16,24},{20,28},{24,0},{28,4},{1,9},{5... | collective-permute-start | bytes 1179656 | tf_op jit(solution)/shard_map/ppermute | solution.py:230
  62.3 27.0 %collective-permute-start.22 = (bf16[256,768]{1,0:T(8,128)(2,1)S(1)}, bf16[256,768]{1,0:T(8,128)(2,1)S(1)}, u32[]{:S(2)}, u32[]{:S(2)}) collective-permute-start(bf16[256,768]{1,0:T(8,128)(2,1)S(1)} %collective-permute-done.21), channel_id=1, source_target_pairs={{0,4},{4,0},{8,12},{12,8},{16,20},{20,16},{24,28},{28,24},{1,5},{5... | collective-permute-start | bytes 1179656 | tf_op jit(solution)/shard_map/ppermute | solution.py:235
  70.6 16.9 %collective-permute-start.6 = (bf16[256,768]{1,0:T(8,128)(2,1)S(1)}, bf16[256,768]{1,0:T(8,128)(2,1)S(1)}, u32[]{:S(2)}, u32[]{:S(2)}) collective-permute-start(bf16[256,768]{1,0:T(8,128)(2,1)S(1)} %collective-permute-done.4), channel_id=1, source_target_pairs={{0,8},{4,12},{8,16},{12,20},{16,24},{20,28},{24,0},{28,4},{1,9},{5... | collective-permute-start | bytes 1179656 | tf_op jit(solution)/shard_map/ppermute | solution.py:230
  70.7 19.2 %slice-start = ((s8[7864320]{0:T(1024)(128)(4,1)}), s8[4194304]{0:T(1024)(128)(4,1)S(1)}, s32[]{:S(2)}) async-start(s8[7864320]{0:T(1024)(128)(4,1)} %bitcast.19), calls=%async_computation.1 | async-start | bytes 8388608
  74.3 18.3 %collective-permute-start.5 = (bf16[256,768]{1,0:T(8,128)(2,1)S(1)}, bf16[256,768]{1,0:T(8,128)(2,1)S(1)}, u32[]{:S(2)}, u32[]{:S(2)}) collective-permute-start(bf16[256,768]{1,0:T(8,128)(2,1)S(1)} %collective-permute-done.4), channel_id=1, source_target_pairs={{0,4},{4,0},{8,12},{12,8},{16,20},{20,16},{24,28},{28,24},{1,5},{5... | collective-permute-start | bytes 1179656 | tf_op jit(solution)/shard_map/ppermute | solution.py:235
  76.6 13.3 %slice-start.1 = ((s8[7864320]{0:T(1024)(128)(4,1)}), s8[3670016]{0:T(1024)(128)(4,1)S(1)}, s32[]{:S(2)}) async-start(s8[7864320]{0:T(1024)(128)(4,1)} %bitcast.19), calls=%async_computation.2 | async-start | bytes 7340032
  81.9 22.6 %collective-permute-start.25 = (bf16[256,768]{1,0:T(8,128)(2,1)S(1)}, bf16[256,768]{1,0:T(8,128)(2,1)S(1)}, u32[]{:S(2)}, u32[]{:S(2)}) collective-permute-start(bf16[256,768]{1,0:T(8,128)(2,1)S(1)} %collective-permute-done.23), channel_id=1, source_target_pairs={{0,8},{4,12},{8,16},{12,20},{16,24},{20,28},{24,0},{28,4},{1,9},{5... | collective-permute-start | bytes 1179656 | tf_op jit(solution)/shard_map/ppermute | solution.py:230
  83.7 17.3 %collective-permute-start.24 = (bf16[256,768]{1,0:T(8,128)(2,1)S(1)}, bf16[256,768]{1,0:T(8,128)(2,1)S(1)}, u32[]{:S(2)}, u32[]{:S(2)}) collective-permute-start(bf16[256,768]{1,0:T(8,128)(2,1)S(1)} %collective-permute-done.23), channel_id=1, source_target_pairs={{0,4},{4,0},{8,12},{12,8},{16,20},{20,16},{24,28},{28,24},{1,5},{5... | collective-permute-start | bytes 1179656 | tf_op jit(solution)/shard_map/ppermute | solution.py:235
  87.4 16.6 %collective-permute-start.8 = (bf16[256,768]{1,0:T(8,128)(2,1)S(1)}, bf16[256,768]{1,0:T(8,128)(2,1)S(1)}, u32[]{:S(2)}, u32[]{:S(2)}) collective-permute-start(bf16[256,768]{1,0:T(8,128)(2,1)S(1)} %collective-permute-done.6), channel_id=1, source_target_pairs={{0,8},{4,12},{8,16},{12,20},{16,24},{20,28},{24,0},{28,4},{1,9},{5... | collective-permute-start | bytes 1179656 | tf_op jit(solution)/shard_map/ppermute | solution.py:230
  89.3 20.2 %collective-permute-start.7 = (bf16[256,768]{1,0:T(8,128)(2,1)S(1)}, bf16[256,768]{1,0:T(8,128)(2,1)S(1)}, u32[]{:S(2)}, u32[]{:S(2)}) collective-permute-start(bf16[256,768]{1,0:T(8,128)(2,1)S(1)} %collective-permute-done.6), channel_id=1, source_target_pairs={{0,4},{4,0},{8,12},{12,8},{16,20},{20,16},{24,28},{28,24},{1,5},{5... | collective-permute-start | bytes 1179656 | tf_op jit(solution)/shard_map/ppermute | solution.py:235
  101.0 11.3 %collective-permute-start.26 = (bf16[256,768]{1,0:T(8,128)(2,1)S(1)}, bf16[256,768]{1,0:T(8,128)(2,1)S(1)}, u32[]{:S(2)}, u32[]{:S(2)}) collective-permute-start(bf16[256,768]{1,0:T(8,128)(2,1)S(1)} %collective-permute-done.24), channel_id=1, source_target_pairs={{0,8},{4,12},{8,16},{12,20},{16,24},{20,28},{24,0},{28,4},{1,9},{5... | collective-permute-start | bytes 1179656 | tf_op jit(solution)/shard_map/ppermute | solution.py:230
  104.0 13.0 %collective-permute-start.9 = (bf16[256,768]{1,0:T(8,128)(2,1)S(1)}, bf16[256,768]{1,0:T(8,128)(2,1)S(1)}, u32[]{:S(2)}, u32[]{:S(2)}) collective-permute-start(bf16[256,768]{1,0:T(8,128)(2,1)S(1)} %collective-permute-done.8), channel_id=1, source_target_pairs={{0,4},{4,0},{8,12},{12,8},{16,20},{20,16},{24,28},{28,24},{1,5},{5... | collective-permute-start | bytes 1179656 | tf_op jit(solution)/shard_map/ppermute | solution.py:235

commit v3 on v1

--- a/solution.py
+++ b/solution.py
@@ -13,95 +13,103 @@
 GRANT = 16 * 2**20
 
 
-def pack_kernel(owned, ids_ref, live_ref, blocks_ref, *refs):
+def relative(here, n, owners):
+    outer = owners // 2
+    return lax.rem(here // 2 + n // 2, outer) * 2 + lax.rem(here + n, 2)
+
+
+def pack_kernel(owned, here_ref, ids_ref, live_ref, blocks_ref, *refs):
     out_refs = refs[:-2]
     pick_ref, sems = refs[-2:]
-    owners, _, lanes = out_refs[0].shape
+    owners = pick_ref.shape[0]
+    lanes = out_refs[0].shape[1]
     width = blocks_ref.shape[1]
     group = live_ref.shape[1] // owners
     row = lax.broadcasted_iota(jnp.int32, (TAIL, 128), 0)
     lane = lax.broadcasted_iota(jnp.int32, (TAIL, 128), 1)
 
-    def copy(owner, k, slot, c):
-        return pltpu.make_async_copy(
-            blocks_ref.at[slot, :, pl.ds(c * lanes, lanes)],
-            out_refs[c].at[owner, pl.ds(k * width, width), :],
-            sems.at[owner, k, c],
-        )
-
-    @pl.loop(0, owners)
-    def _(owner):
-        base = owner * group
+    def copies(n, k, slot):
+        for c in range(len(out_refs) // owners):
+            yield pltpu.make_async_copy(
+                blocks_ref.at[slot, :, pl.ds(c * lanes, lanes)],
+                out_refs[c * owners + n].at[pl.ds(k * width, width), :],
+                sems.at[n, k, c],
+            )
+
+    for n in range(owners):
+        base = relative(here_ref[0], n, owners) * group
         count = jnp.int32(0)
         for j in range(group):
-            pick_ref[jnp.minimum(count, LIVE)] = base + j
+            pick_ref[n, jnp.minimum(count, LIVE)] = base + j
             count = count + live_ref[0, base + j]
         tile = jnp.zeros((TAIL, 128), jnp.int32)
         for k in range(LIVE):
-            slot = jnp.where(k < count, pick_ref[k], base)
-            for c in range(len(out_refs)):
-                copy(owner, k, slot, c).start()
+            slot = jnp.where(k < count, pick_ref[n, k], base)
+            for copy in copies(n, k, slot):
+                copy.start()
             mu = ids_ref[0, 0, slot]
             nu = jnp.where(k < count, lax.rem(ids_ref[1, 0, slot], owned), owned)
             tile = jnp.where((row == 0) & (lane == k), mu, tile)
             tile = jnp.where((row == 0) & (lane == LIVE + k), nu, tile)
-        out_refs[0][owner, LIVE * width :, :] = tile.astype(jnp.float32).astype(jnp.bfloat16)
-
-    @pl.loop(0, owners)
-    def _(owner):
+        out_refs[n][LIVE * width :, :] = tile.astype(jnp.float32).astype(jnp.bfloat16)
+    for n in range(owners):
         for k in range(LIVE):
-            for c in range(len(out_refs)):
-                copy(owner, k, 0, c).wait()
-
-
-def pack(block_ids, live_mask, blocks, owners, owned):
+            for copy in copies(n, k, 0):
+                copy.wait()
+
+
+def pack(here, block_ids, live_mask, blocks, owners, owned):
     _, width, minor = blocks.shape
     chunks = minor // 128
     shapes = [
-        jax.ShapeDtypeStruct((owners, LIVE * width + (0 if c else TAIL), 128), jnp.bfloat16)
+        jax.ShapeDtypeStruct((LIVE * width + (0 if c else TAIL), 128), jnp.bfloat16)
         for c in range(chunks)
+        for _ in range(owners)
     ]
+    smem = pl.BlockSpec(memory_space=pltpu.SMEM)
     return pl.pallas_call(
         functools.partial(pack_kernel, owned),
         out_shape=shapes,
-        in_specs=[
-            pl.BlockSpec(memory_space=pltpu.SMEM),
-            pl.BlockSpec(memory_space=pltpu.SMEM),
-            pl.BlockSpec(memory_space=pl.ANY),
-        ],
-        out_specs=[pl.BlockSpec(memory_space=pltpu.VMEM)] * chunks,
+        in_specs=[smem, smem, smem, pl.BlockSpec(memory_space=pl.ANY)],
+        out_specs=[pl.BlockSpec(memory_space=pltpu.VMEM)] * len(shapes),
         scratch_shapes=[
-            pltpu.SMEM((LIVE + 1,), jnp.int32),
+            pltpu.SMEM((owners, LIVE + 1), jnp.int32),
             pltpu.SemaphoreType.DMA((owners, LIVE, chunks)),
         ],
         name="pack_live",
-    )(block_ids, live_mask, pltpu.with_memory_space_constraint(blocks, pltpu.HBM))
-
-
-def half_kernel(owned, width, me_ref, tail_ref, got_ref, coeff_ref, *refs):
-    out_refs = refs[:-4]
-    ids_vmem, ids_smem, total, sem = refs[-4:]
-    owners = got_ref.shape[0]
-    aux = got_ref.shape[2] // width
-    for p in range(owners):
-        ids_vmem[p : p + 1, :] = tail_ref[p, 0:1, :].astype(jnp.float32).astype(jnp.int32)
-    ids = pltpu.make_async_copy(ids_vmem, ids_smem, sem)
-    ids.start()
-    total[...] = jnp.zeros_like(total)
-    ids.wait()
-
-    @pl.loop(0, owners)
-    def _(p):
+    )(here, block_ids, live_mask, pltpu.with_memory_space_constraint(blocks, pltpu.HBM))
+
+
+def half_kernel(owned, width, owners, me_ref, *refs):
+    refs = list(refs)
+    given = refs.pop(0) if refs[0].dtype == jnp.int32 else None
+    coeff_ref = refs.pop(0)
+    got_refs, refs = refs[:owners], refs[owners:]
+    if given is None:
+        total, ids_smem, sem = refs[-3:]
+        out_refs, ids_vmem = refs[:-4], refs[-4]
+        for n, got_ref in enumerate(got_refs):
+            ids_vmem[n : n + 1, :] = (
+                got_ref[LIVE * width :, :][0:1].astype(jnp.float32).astype(jnp.int32)
+            )
+        ids = pltpu.make_async_copy(ids_vmem, ids_smem, sem)
+        ids.start()
+        total[...] = jnp.zeros_like(total)
+        ids.wait()
+    else:
+        ids_smem, out_refs, total = given, refs[:-1], refs[-1]
+        total[...] = jnp.zeros_like(total)
+    aux = got_refs[0].shape[1] // width
+    for n, got_ref in enumerate(got_refs):
         for k in range(LIVE):
-            mu = ids_smem[p, k]
-            nu = ids_smem[p, LIVE + k]
-            block = got_ref[p, k * width : (k + 1) * width, :]
+            mu = ids_smem[n, k]
+            nu = ids_smem[n, LIVE + k]
+            block = got_ref[k * width : (k + 1) * width, :]
             stacked = jnp.concatenate(
                 [block[:, q * width : (q + 1) * width] for q in range(aux)], axis=0
             )
-            coeff = coeff_ref[pl.ds(pl.multiple_of(mu * width, width), width), :]
             total[nu] += lax.dot_general(
-                coeff, stacked, (((0,), (1,)), ((), ())), preferred_element_type=jnp.float32
+                coeff_ref[mu], stacked, (((1,), (1,)), ((), ())), preferred_element_type=jnp.float32
             )
 
     slab = total.shape[1] // len(out_refs)
@@ -117,41 +125,35 @@
                 )
 
 
-def half_transform(me, first, got, coeffs, owned, width, occ):
-    owners, _, lanes = got.shape
+def half_transform(me, ids, gots, coeffs, owned, width, occ):
+    owners = len(gots)
+    lanes = gots[0].shape[1]
     aux = lanes // width
     occ_count = coeffs.shape[1]
+    assert coeffs.shape[2] == width
     shape = jax.ShapeDtypeStruct((aux * occ_count // occ, owned * width), jnp.bfloat16)
+    smem = pl.BlockSpec(memory_space=pltpu.SMEM)
     vmem = pl.BlockSpec(memory_space=pltpu.VMEM)
-
-    def whole(*dims):
-        return pl.BlockSpec(dims, lambda g: (0,) * len(dims))
-
-    return pl.pallas_call(
-        functools.partial(half_kernel, owned, width),
-        grid=(1,),
-        out_shape=[shape] * occ,
-        in_specs=[
-            pl.BlockSpec(memory_space=pltpu.SMEM),
-            pl.BlockSpec((owners, TAIL, lanes), lambda g: (0, LIVE * width // TAIL, 0)),
-            pl.BlockSpec((owners, LIVE * width, lanes), lambda g: (0, 0, 0)),
-            whole(*coeffs.shape),
-        ],
-        out_specs=[whole(*shape.shape)] * occ,
-        scratch_shapes=[
-            pltpu.VMEM((owners, lanes), jnp.int32),
-            pltpu.SMEM((owners, lanes), jnp.int32),
-            pltpu.VMEM((owned + 1, occ_count, lanes), jnp.float32),
-            pltpu.SemaphoreType.DMA,
-        ],
+    shapes = [shape] * occ
+    scratch = [pltpu.VMEM((owned + 1, occ_count, lanes), jnp.float32)]
+    if ids is None:
+        shapes.append(jax.ShapeDtypeStruct((owners, lanes), jnp.int32))
+        scratch += [pltpu.SMEM((owners, lanes), jnp.int32), pltpu.SemaphoreType.DMA]
+    result = pl.pallas_call(
+        functools.partial(half_kernel, owned, width, owners),
+        out_shape=shapes,
+        in_specs=[smem] + ([] if ids is None else [smem]) + [vmem] * (1 + owners),
+        out_specs=[vmem] * len(shapes),
+        scratch_shapes=scratch,
         cost_estimate=pl.CostEstimate(
             flops=2 * owners * LIVE * width * lanes * occ_count,
-            bytes_accessed=2 * (got.size + coeffs.size + occ * shape.size),
+            bytes_accessed=2 * (owners * gots[0].size + coeffs.size + occ * shape.size),
             transcendentals=0,
         ),
         compiler_params=pltpu.CompilerParams(vmem_limit_bytes=GRANT),
         name="half_transform",
-    )(me, first, got, pltpu.with_memory_space_constraint(coeffs, pltpu.HBM))
+    )(me, *([] if ids is None else [ids]), coeffs, *gots)
+    return result[:occ], result[occ] if ids is None else ids
 
 
 def place_kernel(occ, me_ref, *refs):
@@ -235,13 +237,23 @@
                 total = term if total is None else total + term
         return total
 
-    sends = pack(block_ids, live_mask, blocks, owners, owned)
+    sends = pack(here.astype(jnp.int32).reshape(1), block_ids, live_mask, blocks, owners, owned)
     gots = []
-    for send in sends:
-        gots.append(lax.all_to_all(send, "pair", split_axis=0, concat_axis=0, tiled=True))
-    results = []
+    for c in range(len(sends) // owners):
+        mine = sends[c * owners : (c + 1) * owners]
+        got = [pltpu.with_memory_space_constraint(mine[0], pltpu.HBM)]
+        for n in range(1, owners):
+            target = [
+                (p, (p // 2 + n // 2) % outer * 2 + (p + n) % 2) for p in range(owners)
+            ]
+            got.append(lax.ppermute(mine[n], "pair", target))
+        gots.append(got)
+    coeffs = occ_coeffs.reshape(-1, width, occ_count).transpose(0, 2, 1)
+    results, ids = [], None
     for c, got in enumerate(gots):
-        halves = half_transform(me.reshape(1), gots[0], got, occ_coeffs, owned, width, occ)
+        halves, ids = half_transform(
+            me.reshape(1), ids, got, coeffs, owned, width, occ
+        )
         parts = [across(halves[j], j) for j in range(occ)]
         piece = jnp.concatenate(parts, axis=0) if occ > 1 else parts[0]
         results.append(second_half(*gather(piece, c == len(gots) - 1)))

time: 127 us -> 121 us (0.953)
  starting transfers between devices: 17.2 us -> 42 us
  blocking collectives: 21.8 us -> 0 us
  waiting for transfers between devices: 56.5 us -> 42.5 us
  local copies, waits for them, and re-layouts: 0.08 us -> 9.25 us
  Pallas kernels: 14 us -> 9.82 us
    ppermute x0 -> x14, starting transfers between devices: none -> 24.8 us  [on_device(): got.append(lax.ppermute(mine[n], 'pair', target))]
    all_to_all x1 -> x0, blocking collectives: 21.8 us -> none  [on_device(): lax.all_to_all(send, 'pair', split_axis=0, concat_axis=0, tiled=True)]
    all_to_all x1 -> x0, waiting for transfers between devices: 14.9 us -> none  [on_device(): lax.all_to_all(send, 'pair', split_axis=0, concat_axis=0, tiled=True)]
    unnamed x10 -> x26, local copies, waits for them, and re-layouts: 0.06 us -> 5.98 us
    pallas_call x2, Pallas kernels: 8.85 us -> 4.7 us  [half_transform(): pl.pallas_call(functools.partial(half_kernel, owned, width, owners), out_...]
    all_to_all x1 -> x0, starting transfers between devices: 3.59 us -> none  [on_device(): lax.all_to_all(send, 'pair', split_axis=0, concat_axis=0, tiled=True)]
    reshape x0 -> x1, local copies, waits for them, and re-layouts: none -> 3.26 us  [on_device(): coeffs = occ_coeffs.reshape(-1, width, occ_count).transpose(0, 2, 1)]
    ppermute x7, starting transfers between devices: 1.74 us -> 4.55 us  [along(): lax.ppermute(array, 'pair', [(p, (p // 2 + 1) % outer * 2 + p % 2) for p...]
  transfers between devices with their start and end apart: 21 -> 34, of which waited for: 11 -> 13; matrix products, arithmetic and copies ran while one was open for 13% -> 16% of each run, Pallas kernels for 4% -> 2%
where the time goes in v3:
time: 121 us; the launch traced here: 120 us
  waiting for transfers between devices  42.5 us (35%)
  starting transfers between devices  42 us (35%)
  matrix products  16.4 us (14%)
  Pallas kernels  9.82 us (8%)
  local copies, waits for them, and re-layouts  9.25 us (8%)
    ppermute x14, starting transfers between devices, on_device(): got.append(lax.ppermute(mine[n], 'pair', target))  24.8 us
    ppermute x7, waiting for transfers between devices, along(): lax.ppermute(array, 'pair', [(p, (p // 2 + 1) % outer * 2 + p % 2) for p...  24.8 us
    dot_general x16, matrix products, second_half(): term = jnp.dot(array, part, preferred_element_type=jnp.float32)  16.4 us
    ppermute x7, waiting for transfers between devices, swap(): return lax.ppermute(array, 'pair', [(p, p ^ 1) for p in range(owners)])  10.5 us
    ppermute x7, starting transfers between devices, swap(): return lax.ppermute(array, 'pair', [(p, p ^ 1) for p in range(owners)])  8.73 us
    ppermute x6, waiting for transfers between devices, across(): return lax.ppermute(array, 'occ', [(o, o ^ j) for o in range(occ)])  6.16 us
    unnamed x26, local copies, waits for them, and re-layouts  5.98 us
    pallas_call x2, Pallas kernels, half_transform(): pl.pallas_call(functools.partial(half_kernel, owned, width, owners), out_...  4.7 us
  transfers between devices with their start and end apart: 34, of which 13 were waited for; matrix products, arithmetic and copies ran while one was open for 16% of the time, Pallas kernels for 2%

profile of v3, /device:TPU:0, one launch (start us, length us, event | category | flops | bytes accessed | tf_op | source)
XLA Modules:
  0.0 120.3 jit_solution(9831540777101947493)
XLA Ops:
  0.0 3.5 %pack_live.1 = (bf16[272,128]{1,0:T(8,128)(2,1)}, bf16[272,128]{1,0:T(8,128)(2,1)}, bf16[272,128]{1,0:T(8,128)(2,1)}, bf16[272,128]{1,0:T(8,128)(2,1)}, bf16[272...) custom-call(s32[1]{0:T(128)} %bitcast.3.here_ref, ...), custom_call_target="tpu_custom_call" | custom-call | tf_op jit(solution)/shard_map/pack_live/pallas_call | solution.py:70
  3.5 3.0 %collective-permute-start = (bf16[272,128]{1,0:T(8,128)(2,1)}, bf16[272,128]{1,0:T(8,128)(2,1)S(1)}, u32[]{:S(2)}, u32[]{:S(2)}) collective-permute-start(bf16[272,128]{1,0:T(8,128)(2,1)} %get-tuple-element.31), channel_id=1, source_target_pairs={{0,4},{4,0},{8,12},{12,8},{16,20},{20,16},{24,28},{28,24},{1,5},{5... | collective-permute-start | bytes 208904 | tf_op jit(solution)/shard_map/ppermute | solution.py:249
  6.5 1.6 %collective-permute-start.1 = (bf16[272,128]{1,0:T(8,128)(2,1)}, bf16[272,128]{1,0:T(8,128)(2,1)S(1)}, u32[]{:S(2)}, u32[]{:S(2)}) collective-permute-start(bf16[272,128]{1,0:T(8,128)(2,1)} %get-tuple-element.32), channel_id=1, source_target_pairs={{0,8},{4,12},{8,16},{12,20},{16,24},{20,28},{24,0},{28,4},{1,9},{5... | collective-permute-start | bytes 208904 | tf_op jit(solution)/shard_map/ppermute | solution.py:249
  8.6 1.6 %collective-permute-start.18 = (bf16[256,128]{1,0:T(8,128)(2,1)}, bf16[256,128]{1,0:T(8,128)(2,1)S(1)}, u32[]{:S(2)}, u32[]{:S(2)}) collective-permute-start(bf16[256,128]{1,0:T(8,128)(2,1)} %get-tuple-element.45), channel_id=1, source_target_pairs={{0,8},{4,12},{8,16},{12,20},{16,24},{20,28},{24,0},{28,4},{1,9},{5... | collective-permute-start | bytes 196616 | tf_op jit(solution)/shard_map/ppermute | solution.py:249
  10.2 2.5 %collective-permute-start.2 = (bf16[272,128]{1,0:T(8,128)(2,1)}, bf16[272,128]{1,0:T(8,128)(2,1)S(1)}, u32[]{:S(2)}, u32[]{:S(2)}) collective-permute-start(bf16[272,128]{1,0:T(8,128)(2,1)} %get-tuple-element.33), channel_id=1, source_target_pairs={{0,12},{4,8},{8,20},{12,16},{16,28},{20,24},{24,4},{28,0},{1,13},{... | collective-permute-start | bytes 208904 | tf_op jit(solution)/shard_map/ppermute | solution.py:249
  13.4 3.2 %collective-permute-start.3 = (bf16[272,128]{1,0:T(8,128)(2,1)}, bf16[272,128]{1,0:T(8,128)(2,1)S(1)}, u32[]{:S(2)}, u32[]{:S(2)}) collective-permute-start(bf16[272,128]{1,0:T(8,128)(2,1)} %get-tuple-element.34), channel_id=1, source_target_pairs={{0,16},{4,20},{8,24},{12,28},{16,0},{20,4},{24,8},{28,12},{1,17},{... | collective-permute-start | bytes 208904 | tf_op jit(solution)/shard_map/ppermute | solution.py:249
  17.3 2.0 %collective-permute-start.5 = (bf16[272,128]{1,0:T(8,128)(2,1)}, bf16[272,128]{1,0:T(8,128)(2,1)S(1)}, u32[]{:S(2)}, u32[]{:S(2)}) collective-permute-start(bf16[272,128]{1,0:T(8,128)(2,1)} %get-tuple-element.36), channel_id=1, source_target_pairs={{0,24},{4,28},{8,0},{12,4},{16,8},{20,12},{24,16},{28,20},{1,25},{... | collective-permute-start | bytes 208904 | tf_op jit(solution)/shard_map/ppermute | solution.py:249
  19.3 3.2 %collective-permute-start.6 = (bf16[272,128]{1,0:T(8,128)(2,1)}, bf16[272,128]{1,0:T(8,128)(2,1)S(1)}, u32[]{:S(2)}, u32[]{:S(2)}) collective-permute-start(bf16[272,128]{1,0:T(8,128)(2,1)} %get-tuple-element.37), channel_id=1, source_target_pairs={{0,28},{4,24},{8,4},{12,0},{16,12},{20,8},{24,20},{28,16},{1,29},{... | collective-permute-start | bytes 208904 | tf_op jit(solution)/shard_map/ppermute | solution.py:249
  23.1 1.0 collective-permute-done.4.refs_6_
  24.1 1.8 %collective-permute-start.21 = (bf16[256,128]{1,0:T(8,128)(2,1)}, bf16[256,128]{1,0:T(8,128)(2,1)}, u32[]{:S(2)}, u32[]{:S(2)}) collective-permute-start(bf16[256,128]{1,0:T(8,128)(2,1)} %get-tuple-element.48), channel_id=1, source_target_pairs={{0,20},{4,16},{8,28},{12,24},{16,4},{20,0},{24,12},{28,8},{1,21},{... | collective-permute-start | bytes 196616 | tf_op jit(solution)/shard_map/ppermute | solution.py:249
  26.6 4.7 %collective-permute-start.22 = (bf16[256,128]{1,0:T(8,128)(2,1)}, bf16[256,128]{1,0:T(8,128)(2,1)}, u32[]{:S(2)}, u32[]{:S(2)}) collective-permute-start(bf16[256,128]{1,0:T(8,128)(2,1)} %get-tuple-element.49), channel_id=1, source_target_pairs={{0,24},{4,28},{8,0},{12,4},{16,8},{20,12},{24,16},{28,20},{1,25},{... | collective-permute-start | bytes 196616 | tf_op jit(solution)/shard_map/ppermute | solution.py:249
  31.9 3.3 %copy.6 = bf16[96,64,128]{1,2,0:T(8,128)(2,1)S(1)} copy(bf16[96,64,128]{2,1,0:T(8,128)(2,1)} %bitcast.26) | data formatting | bytes 3145728 | tf_op jit(solution)/shard_map/reshape | solution.py:251
  35.2 0.9 copy-done.1
  36.0 0.9 copy-done.3
  36.9 2.6 %half_transform.2 = (bf16[64,768]{1,0:T(8,128)(2,1)S(1)}, bf16[64,768]{1,0:T(8,128)(2,1)S(1)}, bf16[64,768]{1,0:T(8,128)(2,1)S(1)}, bf16[64,768]{1,0:T(8,128)(2,1)S(1)}, s32[8,128]{1,0:T(8,128)S(1)}) custom-call(s32[1]{0:T(128)} %bitcast.me_ref, bf16[96,128,64]{2,1,0:T(8,128)(2,1)S(1)} %bitcast.21, bf16[272,128]{1,0:T(8,128)(2,1)} %get-tuple-element.30.refs_1_, ...), custom_call_target="tpu_custom_call" | custom-call | flops 67108864 | bytes 2523136 | tf_op jit(solution)/shard_map/half_transform/pallas_call | solution.py:142
  39.6 0.8 copy-done.5
  40.4 0.8 copy-done.7
  41.3 2.1 %half_transform.3 = (bf16[64,768]{1,0:T(8,128)(2,1)S(1)}, bf16[64,768]{1,0:T(8,128)(2,1)S(1)}, bf16[64,768]{1,0:T(8,128)(2,1)S(1)}, bf16[64,768]{1,0:T(8,128)(2,1)S(1)}) custom-call(s32[1]{0:T(128)} %bitcast.me_ref, s32[8,128]{1,0:T(8,128)S(1)} %get-tuple-element.42.refs_0_, bf16[96,128,64]{2,1,0:T(8,128)(2,1)S(1)} %bitcast.22, ...), custom_call_target="tpu_custom_call" | custom-call | flops 67108864 | bytes 2490368 | tf_op jit(solution)/shard_map/half_transform/pallas_call | solution.py:142
  43.5 1.6 %collective-permute-start.25 = (bf16[64,768]{1,0:T(8,128)(2,1)S(1)}, bf16[64,768]{1,0:T(8,128)(2,1)S(1)}, u32[]{:S(2)}, u32[]{:S(2)}) collective-permute-start(bf16[64,768]{1,0:T(8,128)(2,1)S(1)} %get-tuple-element.53), channel_id=1, source_target_pairs={{0,2},{1,3},{2,0},{3,1},{4,6},{5,7},{6,4},{7,5},{8,10},{9,11},{10,... | collective-permute-start | bytes 294920 | tf_op jit(solution)/shard_map/ppermute | solution.py:210
  45.7 1.5 %collective-permute-start.8 = (bf16[64,768]{1,0:T(8,128)(2,1)S(1)}, bf16[64,768]{1,0:T(8,128)(2,1)S(1)}, u32[]{:S(2)}, u32[]{:S(2)}) collective-permute-start(bf16[64,768]{1,0:T(8,128)(2,1)S(1)} %get-tuple-element.40), channel_id=1, source_target_pairs={{0,2},{1,3},{2,0},{3,1},{4,6},{5,7},{6,4},{7,5},{8,10},{9,11},{10,... | collective-permute-start | bytes 294920 | tf_op jit(solution)/shard_map/ppermute | solution.py:210
  47.3 1.9 %collective-permute-done.25 = bf16[64,768]{1,0:T(8,128)(2,1)S(1)} collective-permute-done((bf16[64,768]{1,0:T(8,128)(2,1)S(1)}, bf16[64,768]{1,0:T(8,128)(2,1)S(1)}, u32[]{:S(2)}, u32[]{:S(2)}) %collective-permute-start.25) | collective-permute-done | bytes 98336 | tf_op jit(solution)/shard_map/ppermute | solution.py:210
  49.2 1.1 collective-permute-done.26
  50.4 0.9 collective-permute-start.28
  51.3 2.1 %collective-permute-done.8 = bf16[64,768]{1,0:T(8,128)(2,1)S(1)} collective-permute-done((bf16[64,768]{1,0:T(8,128)(2,1)S(1)}, bf16[64,768]{1,0:T(8,128)(2,1)S(1)}, u32[]{:S(2)}, u32[]{:S(2)}) %collective-permute-start.8) | collective-permute-done | bytes 98336 | tf_op jit(solution)/shard_map/ppermute | solution.py:210
  53.4 1.0 collective-permute-done.9
  54.4 1.0 collective-permute-start.11
  55.4 2.6 %collective-permute-start.27 = (bf16[256,768]{1,0:T(8,128)(2,1)S(1)}, bf16[256,768]{1,0:T(8,128)(2,1)S(1)}, u32[]{:S(2)}, u32[]{:S(2)}) collective-permute-start(bf16[256,768]{1,0:T(8,128)(2,1)S(1)} %constant_dynamic-update-slice_fusion.4), channel_id=1, source_target_pairs={{0,4},{4,0},{8,12},{12,8},{16,20},{20,16},{24,28},{28,24},{1,5},{5... | collective-permute-start | bytes 1179656 | tf_op jit(solution)/shard_map/ppermute | solution.py:218
  58.0 6.6 %collective-permute-done.28 = bf16[256,768]{1,0:T(8,128)(2,1)S(1)} collective-permute-done((bf16[256,768]{1,0:T(8,128)(2,1)S(1)}, bf16[256,768]{1,0:T(8,128)(2,1)S(1)}, u32[]{:S(2)}, u32[]{:S(2)}) %collective-permute-start.28) | collective-permute-done | bytes 393248 | tf_op jit(solution)/shard_map/ppermute | solution.py:213
  64.6 1.3 %collective-permute-start.29 = (bf16[256,768]{1,0:T(8,128)(2,1)S(1)}, bf16[256,768]{1,0:T(8,128)(2,1)S(1)}, u32[]{:S(2)}, u32[]{:S(2)}) collective-permute-start(bf16[256,768]{1,0:T(8,128)(2,1)S(1)} %collective-permute-done.28), channel_id=1, source_target_pairs={{0,4},{4,0},{8,12},{12,8},{16,20},{20,16},{24,28},{28,24},{1,5},{5... | collective-permute-start | bytes 1179656 | tf_op jit(solution)/shard_map/ppermute | solution.py:218
  65.8 7.2 %collective-permute-done.11 = bf16[256,768]{1,0:T(8,128)(2,1)S(1)} collective-permute-done((bf16[256,768]{1,0:T(8,128)(2,1)S(1)}, bf16[256,768]{1,0:T(8,128)(2,1)S(1)}, u32[]{:S(2)}, u32[]{:S(2)}) %collective-permute-start.11) | collective-permute-done | bytes 393248 | tf_op jit(solution)/shard_map/ppermute | solution.py:213
  73.0 1.8 %fusion.20 = f32[256,640]{1,0:T(8,128)S(1)} fusion(bf16[256,768]{1,0:T(8,128)(2,1)S(1)} %collective-permute-done.28, bf16[6144,640]{1,0:T(8,128)(2,1)} %param.7, s32[]{:T(128)S(6)} %select_n.134), kind=kOutput, calls=%fused_computation.28 | convolution fusion | flops 251658240 | bytes 2031620 | tf_op jit(solution)/shard_map/dot_general | solution.py:236
  74.9 1.7 %fusion.22 = f32[256,640]{1,0:T(8,128)S(1)} fusion(bf16[256,768]{1,0:T(8,128)(2,1)S(1)} %collective-permute-done.11, bf16[6144,640]{1,0:T(8,128)(2,1)} %param.7, s32[]{:T(128)S(6)} %select_n.134), kind=kOutput, calls=%fused_computation.30 | convolution fusion | flops 251658240 | bytes 2031620 | tf_op jit(solution)/shard_map/dot_general | solution.py:236
  76.5 1.3 %collective-permute-start.12 = (bf16[256,768]{1,0:T(8,128)(2,1)S(1)}, bf16[256,768]{1,0:T(8,128)(2,1)S(1)}, u32[]{:S(2)}, u32[]{:S(2)}) collective-permute-start(bf16[256,768]{1,0:T(8,128)(2,1)S(1)} %collective-permute-done.11), channel_id=1, source_target_pairs={{0,4},{4,0},{8,12},{12,8},{16,20},{20,16},{24,28},{28,24},{1,5},{5... | collective-permute-start | bytes 1179656 | tf_op jit(solution)/shard_map/ppermute | solution.py:218
  77.9 1.7 %fusion.24 = f32[256,640]{1,0:T(8,128)S(1)} fusion(bf16[256,768]{1,0:T(8,128)(2,1)S(1)} %collective-permute-done.27, bf16[6144,640]{1,0:T(8,128)(2,1)} %param.7, s32[]{:T(128)S(6)} %select_n.132), kind=kOutput, calls=%fused_computation.32 | convolution fusion | flops 251658240 | bytes 2031620 | tf_op jit(solution)/shard_map/dot_general | solution.py:236
  79.6 1.8 %fusion.2 = f32[256,640]{1,0:T(8,128)S(1)} fusion(f32[256,640]{1,0:T(8,128)S(1)} %fusion.20, f32[256,640]{1,0:T(8,128)S(1)} %fusion.24, bf16[256,768]{1,0:T(8,128)(2,1)S(1)} %constant_dynamic-update-slice_fusion.4, bf16[6144,640]{1,0:T(8,128)(2,1)} %param.7, s32[]{:T(128)S(6)} %select_n.131), kind=kOutput, calls=%fused_computation.6 | convolution fusion | flops 251985920 | bytes 3342340 | tf_op jit(solution)/shard_map/dot_general | solution.py:236
  81.4 1.7 %fusion.26 = f32[256,640]{1,0:T(8,128)S(1)} fusion(bf16[256,768]{1,0:T(8,128)(2,1)S(1)} %collective-permute-done.10, bf16[6144,640]{1,0:T(8,128)(2,1)} %param.7, s32[]{:T(128)S(6)} %select_n.132), kind=kOutput, calls=%fused_computation.34 | convolution fusion | flops 251658240 | bytes 2031620 | tf_op jit(solution)/shard_map/dot_general | solution.py:236
  83.1 1.7 %fusion.5 = f32[256,640]{1,0:T(8,128)S(1)} fusion(f32[256,640]{1,0:T(8,128)S(1)} %fusion.22, f32[256,640]{1,0:T(8,128)S(1)} %fusion.26, bf16[256,768]{1,0:T(8,128)(2,1)S(1)} %constant_dynamic-update-slice_fusion, bf16[6144,640]{1,0:T(8,128)(2,1)} %param.7, s32[]{:T(128)S(6)} %select_n.131), kind=kOutput, calls=%fused_computation.13 | convolution fusion | flops 251985920 | bytes 3342340 | tf_op jit(solution)/shard_map/dot_general | solution.py:236
  85.4 1.5 %collective-permute-start.31 = (bf16[256,768]{1,0:T(8,128)(2,1)S(1)}, bf16[256,768]{1,0:T(8,128)(2,1)S(1)}, u32[]{:S(2)}, u32[]{:S(2)}) collective-permute-start(bf16[256,768]{1,0:T(8,128)(2,1)S(1)} %collective-permute-done.30), channel_id=1, source_target_pairs={{0,4},{4,0},{8,12},{12,8},{16,20},{20,16},{24,28},{28,24},{1,5},{5... | collective-permute-start | bytes 1179656 | tf_op jit(solution)/shard_map/ppermute | solution.py:218
  86.9 3.0 %collective-permute-done.13 = bf16[256,768]{1,0:T(8,128)(2,1)S(1)} collective-permute-done((bf16[256,768]{1,0:T(8,128)(2,1)S(1)}, bf16[256,768]{1,0:T(8,128)(2,1)S(1)}, u32[]{:S(2)}, u32[]{:S(2)}) %collective-permute-start.13) | collective-permute-done | bytes 393248 | tf_op jit(solution)/shard_map/ppermute | solution.py:213
  89.9 1.7 %fusion.14 = f32[256,640]{1,0:T(8,128)S(1)} fusion(bf16[256,768]{1,0:T(8,128)(2,1)S(1)} %collective-permute-done.30, bf16[6144,640]{1,0:T(8,128)(2,1)} %param.7, s32[]{:T(128)S(6)} %select_n.137), kind=kOutput, calls=%fused_computation.22 | convolution fusion | flops 251658240 | bytes 2031620 | tf_op jit(solution)/shard_map/dot_general | solution.py:236
  91.6 1.3 %collective-permute-start.14 = (bf16[256,768]{1,0:T(8,128)(2,1)S(1)}, bf16[256,768]{1,0:T(8,128)(2,1)S(1)}, u32[]{:S(2)}, u32[]{:S(2)}) collective-permute-start(bf16[256,768]{1,0:T(8,128)(2,1)S(1)} %collective-permute-done.13), channel_id=1, source_target_pairs={{0,4},{4,0},{8,12},{12,8},{16,20},{20,16},{24,28},{28,24},{1,5},{5... | collective-permute-start | bytes 1179656 | tf_op jit(solution)/shard_map/ppermute | solution.py:218
  94.4 7.3 %collective-permute-done.31 = bf16[256,768]{1,0:T(8,128)(2,1)S(1)} collective-permute-done((bf16[256,768]{1,0:T(8,128)(2,1)S(1)}, bf16[256,768]{1,0:T(8,128)(2,1)S(1)}, u32[]{:S(2)}, u32[]{:S(2)}) %collective-permute-start.31) | collective-permute-done | bytes 393248 | tf_op jit(solution)/shard_map/ppermute | solution.py:218
  101.7 2.0 %collective-permute-start.33 = (bf16[256,768]{1,0:T(8,128)(2,1)S(1)}, bf16[256,768]{1,0:T(8,128)(2,1)S(1)}, u32[]{:S(2)}, u32[]{:S(2)}) collective-permute-start(bf16[256,768]{1,0:T(8,128)(2,1)S(1)} %collective-permute-done.31), channel_id=1, source_target_pairs={{0,8},{4,12},{8,16},{12,20},{16,24},{20,28},{24,0},{28,4},{1,9},{5... | collective-permute-start | bytes 1179656 | tf_op jit(solution)/shard_map/ppermute | solution.py:213
  103.7 3.4 %collective-permute-done.15 = bf16[256,768]{1,0:T(8,128)(2,1)S(1)} collective-permute-done((bf16[256,768]{1,0:T(8,128)(2,1)S(1)}, bf16[256,768]{1,0:T(8,128)(2,1)S(1)}, u32[]{:S(2)}, u32[]{:S(2)}) %collective-permute-start.15) | collective-permute-done | bytes 393248 | tf_op jit(solution)/shard_map/ppermute | solution.py:213
  107.1 0.8 collective-permute-start.16
  110.6 4.7 %collective-permute-done.33 = bf16[256,768]{1,0:T(8,128)(2,1)S(1)} collective-permute-done((bf16[256,768]{1,0:T(8,128)(2,1)S(1)}, bf16[256,768]{1,0:T(8,128)(2,1)S(1)}, u32[]{:S(2)}, u32[]{:S(2)}) %collective-permute-start.33) | collective-permute-done | bytes 393248 | tf_op jit(solution)/shard_map/ppermute | solution.py:213
  115.8 2.4 %collective-permute-done.16 = bf16[256,768]{1,0:T(8,128)(2,1)S(1)} collective-permute-done((bf16[256,768]{1,0:T(8,128)(2,1)S(1)}, bf16[256,768]{1,0:T(8,128)(2,1)S(1)}, u32[]{:S(2)}, u32[]{:S(2)}) %collective-permute-start.16) | collective-permute-done | bytes 393248 | tf_op jit(solution)/shard_map/ppermute | solution.py:218
  118.7 1.6 %place.1 = bf16[32,16,640]{2,1,0:T(8,128)(2,1)} custom-call(s32[1]{0:T(128)} %bitcast.me_ref, f32[256,640]{1,0:T(8,128)S(1)} %convolution_add_fusion.4.refs_0_, f32[256,640]{1,0:T(8,128)S(1)} %convolution_add_fusion.refs_1_), custom_call_target="tpu_custom_call" | custom-call | tf_op jit(solution)/shard_map/place/pallas_call | solution.py:183
  (70 shorter events, 10.4 us)
Async XLA Ops:
  3.5 13.8 %collective-permute-start = (bf16[272,128]{1,0:T(8,128)(2,1)}, bf16[272,128]{1,0:T(8,128)(2,1)S(1)}, u32[]{:S(2)}, u32[]{:S(2)}) collective-permute-start(bf16[272,128]{1,0:T(8,128)(2,1)} %get-tuple-element.31), channel_id=1, source_target_pairs={{0,4},{4,0},{8,12},{12,8},{16,20},{20,16},{24,28},{28,24},{1,5},{5... | collective-permute-start | bytes 208904 | tf_op jit(solution)/shard_map/ppermute | solution.py:249
  6.5 12.8 %collective-permute-start.1 = (bf16[272,128]{1,0:T(8,128)(2,1)}, bf16[272,128]{1,0:T(8,128)(2,1)S(1)}, u32[]{:S(2)}, u32[]{:S(2)}) collective-permute-start(bf16[272,128]{1,0:T(8,128)(2,1)} %get-tuple-element.32), channel_id=1, source_target_pairs={{0,8},{4,12},{8,16},{12,20},{16,24},{20,28},{24,0},{28,4},{1,9},{5... | collective-permute-start | bytes 208904 | tf_op jit(solution)/shard_map/ppermute | solution.py:249
  8.1 4.6 %collective-permute-start.17 = (bf16[256,128]{1,0:T(8,128)(2,1)}, bf16[256,128]{1,0:T(8,128)(2,1)S(1)}, u32[]{:S(2)}, u32[]{:S(2)}) collective-permute-start(bf16[256,128]{1,0:T(8,128)(2,1)} %get-tuple-element.44), channel_id=1, source_target_pairs={{0,4},{4,0},{8,12},{12,8},{16,20},{20,16},{24,28},{28,24},{1,5},{5... | collective-permute-start | bytes 196616 | tf_op jit(solution)/shard_map/ppermute | solution.py:249
  8.6 7.9 %collective-permute-start.18 = (bf16[256,128]{1,0:T(8,128)(2,1)}, bf16[256,128]{1,0:T(8,128)(2,1)S(1)}, u32[]{:S(2)}, u32[]{:S(2)}) collective-permute-start(bf16[256,128]{1,0:T(8,128)(2,1)} %get-tuple-element.45), channel_id=1, source_target_pairs={{0,8},{4,12},{8,16},{12,20},{16,24},{20,28},{24,0},{28,4},{1,9},{5... | collective-permute-start | bytes 196616 | tf_op jit(solution)/shard_map/ppermute | solution.py:249
  10.2 12.2 %collective-permute-start.2 = (bf16[272,128]{1,0:T(8,128)(2,1)}, bf16[272,128]{1,0:T(8,128)(2,1)S(1)}, u32[]{:S(2)}, u32[]{:S(2)}) collective-permute-start(bf16[272,128]{1,0:T(8,128)(2,1)} %get-tuple-element.33), channel_id=1, source_target_pairs={{0,12},{4,8},{8,20},{12,16},{16,28},{20,24},{24,4},{28,0},{1,13},{... | collective-permute-start | bytes 208904 | tf_op jit(solution)/shard_map/ppermute | solution.py:249
  12.7 0.6 copy-start.4
  13.4 9.1 %collective-permute-start.3 = (bf16[272,128]{1,0:T(8,128)(2,1)}, bf16[272,128]{1,0:T(8,128)(2,1)S(1)}, u32[]{:S(2)}, u32[]{:S(2)}) collective-permute-start(bf16[272,128]{1,0:T(8,128)(2,1)} %get-tuple-element.34), channel_id=1, source_target_pairs={{0,16},{4,20},{8,24},{12,28},{16,0},{20,4},{24,8},{28,12},{1,17},{... | collective-permute-start | bytes 208904 | tf_op jit(solution)/shard_map/ppermute | solution.py:249
  16.6 0.6 copy-start.6
  17.2 6.9 %collective-permute-start.4 = (bf16[272,128]{1,0:T(8,128)(2,1)}, bf16[272,128]{1,0:T(8,128)(2,1)S(1)}, u32[]{:S(2)}, u32[]{:S(2)}) collective-permute-start(bf16[272,128]{1,0:T(8,128)(2,1)} %get-tuple-element.35), channel_id=1, source_target_pairs={{0,20},{4,16},{8,28},{12,24},{16,4},{20,0},{24,12},{28,8},{1,21},{... | collective-permute-start | bytes 208904 | tf_op jit(solution)/shard_map/ppermute | solution.py:249
  17.3 8.7 %collective-permute-start.5 = (bf16[272,128]{1,0:T(8,128)(2,1)}, bf16[272,128]{1,0:T(8,128)(2,1)S(1)}, u32[]{:S(2)}, u32[]{:S(2)}) collective-permute-start(bf16[272,128]{1,0:T(8,128)(2,1)} %get-tuple-element.36), channel_id=1, source_target_pairs={{0,24},{4,28},{8,0},{12,4},{16,8},{20,12},{24,16},{28,20},{1,25},{... | collective-permute-start | bytes 208904 | tf_op jit(solution)/shard_map/ppermute | solution.py:249
  19.3 12.0 %collective-permute-start.6 = (bf16[272,128]{1,0:T(8,128)(2,1)}, bf16[272,128]{1,0:T(8,128)(2,1)S(1)}, u32[]{:S(2)}, u32[]{:S(2)}) collective-permute-start(bf16[272,128]{1,0:T(8,128)(2,1)} %get-tuple-element.37), channel_id=1, source_target_pairs={{0,28},{4,24},{8,4},{12,0},{16,12},{20,8},{24,20},{28,16},{1,29},{... | collective-permute-start | bytes 208904 | tf_op jit(solution)/shard_map/ppermute | solution.py:249
  22.5 17.1 %collective-permute-start.19 = (bf16[256,128]{1,0:T(8,128)(2,1)}, bf16[256,128]{1,0:T(8,128)(2,1)}, u32[]{:S(2)}, u32[]{:S(2)}) collective-permute-start(bf16[256,128]{1,0:T(8,128)(2,1)} %get-tuple-element.46), channel_id=1, source_target_pairs={{0,12},{4,8},{8,20},{12,16},{16,28},{20,24},{24,4},{28,0},{1,13},{... | collective-permute-start | bytes 196616 | tf_op jit(solution)/shard_map/ppermute | solution.py:249
  22.5 17.1 %collective-permute-start.20 = (bf16[256,128]{1,0:T(8,128)(2,1)}, bf16[256,128]{1,0:T(8,128)(2,1)}, u32[]{:S(2)}, u32[]{:S(2)}) collective-permute-start(bf16[256,128]{1,0:T(8,128)(2,1)} %get-tuple-element.47), channel_id=1, source_target_pairs={{0,16},{4,20},{8,24},{12,28},{16,0},{20,4},{24,8},{28,12},{1,17},{... | collective-permute-start | bytes 196616 | tf_op jit(solution)/shard_map/ppermute | solution.py:249
  24.1 15.5 %collective-permute-start.21 = (bf16[256,128]{1,0:T(8,128)(2,1)}, bf16[256,128]{1,0:T(8,128)(2,1)}, u32[]{:S(2)}, u32[]{:S(2)}) collective-permute-start(bf16[256,128]{1,0:T(8,128)(2,1)} %get-tuple-element.48), channel_id=1, source_target_pairs={{0,20},{4,16},{8,28},{12,24},{16,4},{20,0},{24,12},{28,8},{1,21},{... | collective-permute-start | bytes 196616 | tf_op jit(solution)/shard_map/ppermute | solution.py:249
  25.9 0.6 copy-start
  26.6 13.0 %collective-permute-start.22 = (bf16[256,128]{1,0:T(8,128)(2,1)}, bf16[256,128]{1,0:T(8,128)(2,1)}, u32[]{:S(2)}, u32[]{:S(2)}) collective-permute-start(bf16[256,128]{1,0:T(8,128)(2,1)} %get-tuple-element.49), channel_id=1, source_target_pairs={{0,24},{4,28},{8,0},{12,4},{16,8},{20,12},{24,16},{28,20},{1,25},{... | collective-permute-start | bytes 196616 | tf_op jit(solution)/shard_map/ppermute | solution.py:249
  31.2 0.6 copy-start.2
  31.9 7.7 %collective-permute-start.23 = (bf16[256,128]{1,0:T(8,128)(2,1)}, bf16[256,128]{1,0:T(8,128)(2,1)}, u32[]{:S(2)}, u32[]{:S(2)}) collective-permute-start(bf16[256,128]{1,0:T(8,128)(2,1)} %get-tuple-element.50), channel_id=1, source_target_pairs={{0,28},{4,24},{8,4},{12,0},{16,12},{20,8},{24,20},{28,16},{1,29},{... | collective-permute-start | bytes 196616 | tf_op jit(solution)/shard_map/ppermute | solution.py:249
  35.1 0.9 copy-start.1
  36.0 0.9 copy-start.3
  39.6 0.8 copy-start.5
  40.4 0.8 copy-start.7
  43.4 3.8 %collective-permute-start.24 = (bf16[64,768]{1,0:T(8,128)(2,1)S(1)}, bf16[64,768]{1,0:T(8,128)(2,1)S(1)}, u32[]{:S(2)}, u32[]{:S(2)}) collective-permute-start(bf16[64,768]{1,0:T(8,128)(2,1)S(1)} %get-tuple-element.52), channel_id=1, source_target_pairs={{0,1},{1,0},{2,3},{3,2},{4,5},{5,4},{6,7},{7,6},{8,9},{9,8},{10,11... | collective-permute-start | bytes 294920 | tf_op jit(solution)/shard_map/ppermute | solution.py:210
  43.5 5.7 %collective-permute-start.25 = (bf16[64,768]{1,0:T(8,128)(2,1)S(1)}, bf16[64,768]{1,0:T(8,128)(2,1)S(1)}, u32[]{:S(2)}, u32[]{:S(2)}) collective-permute-start(bf16[64,768]{1,0:T(8,128)(2,1)S(1)} %get-tuple-element.53), channel_id=1, source_target_pairs={{0,2},{1,3},{2,0},{3,1},{4,6},{5,7},{6,4},{7,5},{8,10},{9,11},{10,... | collective-permute-start | bytes 294920 | tf_op jit(solution)/shard_map/ppermute | solution.py:210
  45.0 5.3 %collective-permute-start.26 = (bf16[64,768]{1,0:T(8,128)(2,1)S(1)}, bf16[64,768]{1,0:T(8,128)(2,1)S(1)}, u32[]{:S(2)}, u32[]{:S(2)}) collective-permute-start(bf16[64,768]{1,0:T(8,128)(2,1)S(1)} %get-tuple-element.54), channel_id=1, source_target_pairs={{0,3},{1,2},{2,1},{3,0},{4,7},{5,6},{6,5},{7,4},{8,11},{9,10},{10,... | collective-permute-start | bytes 294920 | tf_op jit(solution)/shard_map/ppermute | solution.py:210
  45.3 6.0 %collective-permute-start.7 = (bf16[64,768]{1,0:T(8,128)(2,1)S(1)}, bf16[64,768]{1,0:T(8,128)(2,1)S(1)}, u32[]{:S(2)}, u32[]{:S(2)}) collective-permute-start(bf16[64,768]{1,0:T(8,128)(2,1)S(1)} %get-tuple-element.39), channel_id=1, source_target_pairs={{0,1},{1,0},{2,3},{3,2},{4,5},{5,4},{6,7},{7,6},{8,9},{9,8},{10,11... | collective-permute-start | bytes 294920 | tf_op jit(solution)/shard_map/ppermute | solution.py:210
  45.7 7.7 %collective-permute-start.8 = (bf16[64,768]{1,0:T(8,128)(2,1)S(1)}, bf16[64,768]{1,0:T(8,128)(2,1)S(1)}, u32[]{:S(2)}, u32[]{:S(2)}) collective-permute-start(bf16[64,768]{1,0:T(8,128)(2,1)S(1)} %get-tuple-element.40), channel_id=1, source_target_pairs={{0,2},{1,3},{2,0},{3,1},{4,6},{5,7},{6,4},{7,5},{8,10},{9,11},{10,... | collective-permute-start | bytes 294920 | tf_op jit(solution)/shard_map/ppermute | solution.py:210
  47.2 7.2 %collective-permute-start.9 = (bf16[64,768]{1,0:T(8,128)(2,1)S(1)}, bf16[64,768]{1,0:T(8,128)(2,1)S(1)}, u32[]{:S(2)}, u32[]{:S(2)}) collective-permute-start(bf16[64,768]{1,0:T(8,128)(2,1)S(1)} %get-tuple-element.41), channel_id=1, source_target_pairs={{0,3},{1,2},{2,1},{3,0},{4,7},{5,6},{6,5},{7,4},{8,11},{9,10},{10,... | collective-permute-start | bytes 294920 | tf_op jit(solution)/shard_map/ppermute | solution.py:210
  50.4 14.2 %collective-permute-start.28 = (bf16[256,768]{1,0:T(8,128)(2,1)S(1)}, bf16[256,768]{1,0:T(8,128)(2,1)S(1)}, u32[]{:S(2)}, u32[]{:S(2)}) collective-permute-start(bf16[256,768]{1,0:T(8,128)(2,1)S(1)} %constant_dynamic-update-slice_fusion.4), channel_id=1, source_target_pairs={{0,8},{4,12},{8,16},{12,20},{16,24},{20,28},{24,0},{28,4},{1,9},{5... | collective-permute-start | bytes 1179656 | tf_op jit(solution)/shard_map/ppermute | solution.py:213
  54.4 18.6 %collective-permute-start.11 = (bf16[256,768]{1,0:T(8,128)(2,1)S(1)}, bf16[256,768]{1,0:T(8,128)(2,1)S(1)}, u32[]{:S(2)}, u32[]{:S(2)}) collective-permute-start(bf16[256,768]{1,0:T(8,128)(2,1)S(1)} %constant_dynamic-update-slice_fusion), channel_id=1, source_target_pairs={{0,8},{4,12},{8,16},{12,20},{16,24},{20,28},{24,0},{28,4},{1,9},{5... | collective-permute-start | bytes 1179656 | tf_op jit(solution)/shard_map/ppermute | solution.py:213
  55.4 21.1 %collective-permute-start.27 = (bf16[256,768]{1,0:T(8,128)(2,1)S(1)}, bf16[256,768]{1,0:T(8,128)(2,1)S(1)}, u32[]{:S(2)}, u32[]{:S(2)}) collective-permute-start(bf16[256,768]{1,0:T(8,128)(2,1)S(1)} %constant_dynamic-update-slice_fusion.4), channel_id=1, source_target_pairs={{0,4},{4,0},{8,12},{12,8},{16,20},{20,16},{24,28},{28,24},{1,5},{5... | collective-permute-start | bytes 1179656 | tf_op jit(solution)/shard_map/ppermute | solution.py:218
  58.0 23.4 %collective-permute-start.10 = (bf16[256,768]{1,0:T(8,128)(2,1)S(1)}, bf16[256,768]{1,0:T(8,128)(2,1)S(1)}, u32[]{:S(2)}, u32[]{:S(2)}) collective-permute-start(bf16[256,768]{1,0:T(8,128)(2,1)S(1)} %constant_dynamic-update-slice_fusion), channel_id=1, source_target_pairs={{0,4},{4,0},{8,12},{12,8},{16,20},{20,16},{24,28},{28,24},{1,5},{5... | collective-permute-start | bytes 1179656 | tf_op jit(solution)/shard_map/ppermute | solution.py:218
  64.6 20.2 %collective-permute-start.30 = (bf16[256,768]{1,0:T(8,128)(2,1)S(1)}, bf16[256,768]{1,0:T(8,128)(2,1)S(1)}, u32[]{:S(2)}, u32[]{:S(2)}) collective-permute-start(bf16[256,768]{1,0:T(8,128)(2,1)S(1)} %collective-permute-done.28), channel_id=1, source_target_pairs={{0,8},{4,12},{8,16},{12,20},{16,24},{20,28},{24,0},{28,4},{1,9},{5... | collective-permute-start | bytes 1179656 | tf_op jit(solution)/shard_map/ppermute | solution.py:213
  64.6 27.0 %collective-permute-start.29 = (bf16[256,768]{1,0:T(8,128)(2,1)S(1)}, bf16[256,768]{1,0:T(8,128)(2,1)S(1)}, u32[]{:S(2)}, u32[]{:S(2)}) collective-permute-start(bf16[256,768]{1,0:T(8,128)(2,1)S(1)} %collective-permute-done.28), channel_id=1, source_target_pairs={{0,4},{4,0},{8,12},{12,8},{16,20},{20,16},{24,28},{28,24},{1,5},{5... | collective-permute-start | bytes 1179656 | tf_op jit(solution)/shard_map/ppermute | solution.py:218
  73.0 16.9 %collective-permute-start.13 = (bf16[256,768]{1,0:T(8,128)(2,1)S(1)}, bf16[256,768]{1,0:T(8,128)(2,1)S(1)}, u32[]{:S(2)}, u32[]{:S(2)}) collective-permute-start(bf16[256,768]{1,0:T(8,128)(2,1)S(1)} %collective-permute-done.11), channel_id=1, source_target_pairs={{0,8},{4,12},{8,16},{12,20},{16,24},{20,28},{24,0},{28,4},{1,9},{5... | collective-permute-start | bytes 1179656 | tf_op jit(solution)/shard_map/ppermute | solution.py:213
  73.0 19.9 %slice-start = ((s8[7864320]{0:T(1024)(128)(4,1)}), s8[4194304]{0:T(1024)(128)(4,1)S(1)}, s32[]{:S(2)}) async-start(s8[7864320]{0:T(1024)(128)(4,1)} %bitcast.23), calls=%async_computation | async-start | bytes 8388608
  76.5 17.3 %collective-permute-start.12 = (bf16[256,768]{1,0:T(8,128)(2,1)S(1)}, bf16[256,768]{1,0:T(8,128)(2,1)S(1)}, u32[]{:S(2)}, u32[]{:S(2)}) collective-permute-start(bf16[256,768]{1,0:T(8,128)(2,1)S(1)} %collective-permute-done.11), channel_id=1, source_target_pairs={{0,4},{4,0},{8,12},{12,8},{16,20},{20,16},{24,28},{28,24},{1,5},{5... | collective-permute-start | bytes 1179656 | tf_op jit(solution)/shard_map/ppermute | solution.py:218
  79.6 13.3 %slice-start.1 = ((s8[7864320]{0:T(1024)(128)(4,1)}), s8[3670016]{0:T(1024)(128)(4,1)S(1)}, s32[]{:S(2)}) async-start(s8[7864320]{0:T(1024)(128)(4,1)} %bitcast.23), calls=%async_computation.1 | async-start | bytes 7340032
  84.8 23.0 %collective-permute-start.32 = (bf16[256,768]{1,0:T(8,128)(2,1)S(1)}, bf16[256,768]{1,0:T(8,128)(2,1)S(1)}, u32[]{:S(2)}, u32[]{:S(2)}) collective-permute-start(bf16[256,768]{1,0:T(8,128)(2,1)S(1)} %collective-permute-done.30), channel_id=1, source_target_pairs={{0,8},{4,12},{8,16},{12,20},{16,24},{20,28},{24,0},{28,4},{1,9},{5... | collective-permute-start | bytes 1179656 | tf_op jit(solution)/shard_map/ppermute | solution.py:213
  85.4 16.2 %collective-permute-start.31 = (bf16[256,768]{1,0:T(8,128)(2,1)S(1)}, bf16[256,768]{1,0:T(8,128)(2,1)S(1)}, u32[]{:S(2)}, u32[]{:S(2)}) collective-permute-start(bf16[256,768]{1,0:T(8,128)(2,1)S(1)} %collective-permute-done.30), channel_id=1, source_target_pairs={{0,4},{4,0},{8,12},{12,8},{16,20},{20,16},{24,28},{28,24},{1,5},{5... | collective-permute-start | bytes 1179656 | tf_op jit(solution)/shard_map/ppermute | solution.py:218
  89.9 17.2 %collective-permute-start.15 = (bf16[256,768]{1,0:T(8,128)(2,1)S(1)}, bf16[256,768]{1,0:T(8,128)(2,1)S(1)}, u32[]{:S(2)}, u32[]{:S(2)}) collective-permute-start(bf16[256,768]{1,0:T(8,128)(2,1)S(1)} %collective-permute-done.13), channel_id=1, source_target_pairs={{0,8},{4,12},{8,16},{12,20},{16,24},{20,28},{24,0},{28,4},{1,9},{5... | collective-permute-start | bytes 1179656 | tf_op jit(solution)/shard_map/ppermute | solution.py:213
  91.6 18.5 %collective-permute-start.14 = (bf16[256,768]{1,0:T(8,128)(2,1)S(1)}, bf16[256,768]{1,0:T(8,128)(2,1)S(1)}, u32[]{:S(2)}, u32[]{:S(2)}) collective-permute-start(bf16[256,768]{1,0:T(8,128)(2,1)S(1)} %collective-permute-done.13), channel_id=1, source_target_pairs={{0,4},{4,0},{8,12},{12,8},{16,20},{20,16},{24,28},{28,24},{1,5},{5... | collective-permute-start | bytes 1179656 | tf_op jit(solution)/shard_map/ppermute | solution.py:218
  101.7 13.6 %collective-permute-start.33 = (bf16[256,768]{1,0:T(8,128)(2,1)S(1)}, bf16[256,768]{1,0:T(8,128)(2,1)S(1)}, u32[]{:S(2)}, u32[]{:S(2)}) collective-permute-start(bf16[256,768]{1,0:T(8,128)(2,1)S(1)} %collective-permute-done.31), channel_id=1, source_target_pairs={{0,8},{4,12},{8,16},{12,20},{16,24},{20,28},{24,0},{28,4},{1,9},{5... | collective-permute-start | bytes 1179656 | tf_op jit(solution)/shard_map/ppermute | solution.py:213
  107.1 11.1 %collective-permute-start.16 = (bf16[256,768]{1,0:T(8,128)(2,1)S(1)}, bf16[256,768]{1,0:T(8,128)(2,1)S(1)}, u32[]{:S(2)}, u32[]{:S(2)}) collective-permute-start(bf16[256,768]{1,0:T(8,128)(2,1)S(1)} %collective-permute-done.15), channel_id=1, source_target_pairs={{0,4},{4,0},{8,12},{12,8},{16,20},{20,16},{24,28},{28,24},{1,5},{5... | collective-permute-start | bytes 1179656 | tf_op jit(solution)/shard_map/ppermute | solution.py:218

commit v4 on v3

--- a/solution.py
+++ b/solution.py
@@ -13,9 +13,9 @@
 GRANT = 16 * 2**20
 
 
-def relative(here, n, owners):
+def relative(here, n, owners, sign=1):
     outer = owners // 2
-    return lax.rem(here // 2 + n // 2, outer) * 2 + lax.rem(here + n, 2)
+    return lax.rem(here // 2 + sign * (n // 2) + outer, outer) * 2 + lax.rem(here + n, 2)
 
 
 def pack_kernel(owned, here_ref, ids_ref, live_ref, blocks_ref, *refs):
@@ -29,10 +29,12 @@
     lane = lax.broadcasted_iota(jnp.int32, (TAIL, 128), 1)
 
     def copies(n, k, slot):
-        for c in range(len(out_refs) // owners):
+        owner = relative(here_ref[0], n, owners)
+        for c in range(1 + len(out_refs) - owners):
+            out = out_refs[owners + c - 1].at[owner] if c else out_refs[n]
             yield pltpu.make_async_copy(
                 blocks_ref.at[slot, :, pl.ds(c * lanes, lanes)],
-                out_refs[c * owners + n].at[pl.ds(k * width, width), :],
+                out.at[pl.ds(k * width, width), :],
                 sems.at[n, k, c],
             )
 
@@ -61,11 +63,8 @@
 def pack(here, block_ids, live_mask, blocks, owners, owned):
     _, width, minor = blocks.shape
     chunks = minor // 128
-    shapes = [
-        jax.ShapeDtypeStruct((LIVE * width + (0 if c else TAIL), 128), jnp.bfloat16)
-        for c in range(chunks)
-        for _ in range(owners)
-    ]
+    shapes = [jax.ShapeDtypeStruct((LIVE * width + TAIL, 128), jnp.bfloat16)] * owners
+    shapes += [jax.ShapeDtypeStruct((owners, LIVE * width, 128), jnp.bfloat16)] * (chunks - 1)
     smem = pl.BlockSpec(memory_space=pltpu.SMEM)
     return pl.pallas_call(
         functools.partial(pack_kernel, owned),
@@ -76,16 +75,17 @@
             pltpu.SMEM((owners, LIVE + 1), jnp.int32),
             pltpu.SemaphoreType.DMA((owners, LIVE, chunks)),
         ],
+        compiler_params=pltpu.CompilerParams(vmem_limit_bytes=GRANT),
         name="pack_live",
-    )(here, block_ids, live_mask, pltpu.with_memory_space_constraint(blocks, pltpu.HBM))
-
-
-def half_kernel(owned, width, owners, me_ref, *refs):
+    )(here, *(pltpu.with_memory_space_constraint(x, pltpu.HBM) for x in (block_ids, live_mask, blocks)))
+
+
+def half_kernel(owned, width, owners, place_ref, *refs):
     refs = list(refs)
     given = refs.pop(0) if refs[0].dtype == jnp.int32 else None
     coeff_ref = refs.pop(0)
-    got_refs, refs = refs[:owners], refs[owners:]
     if given is None:
+        got_refs, refs = refs[:owners], refs[owners:]
         total, ids_smem, sem = refs[-3:]
         out_refs, ids_vmem = refs[:-4], refs[-4]
         for n, got_ref in enumerate(got_refs):
@@ -97,7 +97,8 @@
         total[...] = jnp.zeros_like(total)
         ids.wait()
     else:
-        ids_smem, out_refs, total = given, refs[:-1], refs[-1]
+        got_ref, ids_smem, out_refs, total = refs[0], given, refs[1:-1], refs[-1]
+        got_refs = [got_ref.at[relative(place_ref[1], n, owners, -1)] for n in range(owners)]
         total[...] = jnp.zeros_like(total)
     aux = got_refs[0].shape[1] // width
     for n, got_ref in enumerate(got_refs):
@@ -114,7 +115,7 @@
 
     slab = total.shape[1] // len(out_refs)
     for j, out_ref in enumerate(out_refs):
-        start = pl.multiple_of((me_ref[0] ^ j) * slab, slab)
+        start = pl.multiple_of((place_ref[0] ^ j) * slab, slab)
         for b in range(0, owned, 2):
             pair = [total[c, pl.ds(start, slab), :] for c in range(b, min(b + 2, owned))]
             for q in range(aux):
@@ -125,9 +126,8 @@
                 )
 
 
-def half_transform(me, ids, gots, coeffs, owned, width, occ):
-    owners = len(gots)
-    lanes = gots[0].shape[1]
+def half_transform(place, ids, gots, coeffs, owners, owned, width, occ):
+    lanes = gots[0].shape[-1]
     aux = lanes // width
     occ_count = coeffs.shape[1]
     assert coeffs.shape[2] == width
@@ -142,17 +142,17 @@
     result = pl.pallas_call(
         functools.partial(half_kernel, owned, width, owners),
         out_shape=shapes,
-        in_specs=[smem] + ([] if ids is None else [smem]) + [vmem] * (1 + owners),
+        in_specs=[smem] + ([] if ids is None else [smem]) + [vmem] * (1 + len(gots)),
         out_specs=[vmem] * len(shapes),
         scratch_shapes=scratch,
         cost_estimate=pl.CostEstimate(
             flops=2 * owners * LIVE * width * lanes * occ_count,
-            bytes_accessed=2 * (owners * gots[0].size + coeffs.size + occ * shape.size),
+            bytes_accessed=2 * (len(gots) * gots[0].size + coeffs.size + occ * shape.size),
             transcendentals=0,
         ),
         compiler_params=pltpu.CompilerParams(vmem_limit_bytes=GRANT),
         name="half_transform",
-    )(me, *([] if ids is None else [ids]), coeffs, *gots)
+    )(place, *([] if ids is None else [ids]), coeffs, *gots)
     return result[:occ], result[occ] if ids is None else ids
 
 
@@ -238,21 +238,19 @@
         return total
 
     sends = pack(here.astype(jnp.int32).reshape(1), block_ids, live_mask, blocks, owners, owned)
-    gots = []
-    for c in range(len(sends) // owners):
-        mine = sends[c * owners : (c + 1) * owners]
-        got = [pltpu.with_memory_space_constraint(mine[0], pltpu.HBM)]
-        for n in range(1, owners):
-            target = [
-                (p, (p // 2 + n // 2) % outer * 2 + (p + n) % 2) for p in range(owners)
-            ]
-            got.append(lax.ppermute(mine[n], "pair", target))
-        gots.append(got)
+    got = [sends[0]]
+    for n in range(1, owners):
+        target = [(p, (p // 2 + n // 2) % outer * 2 + (p + n) % 2) for p in range(owners)]
+        got.append(lax.ppermute(sends[n], "pair", target))
+    gots = [got]
+    for c, send in enumerate(sends[owners:], 1):
+        gots.append([lax.all_to_all(send, "pair", split_axis=0, concat_axis=0, tiled=True)])
+    spot = jnp.stack([me, here.astype(jnp.int32)])
     coeffs = occ_coeffs.reshape(-1, width, occ_count).transpose(0, 2, 1)
     results, ids = [], None
     for c, got in enumerate(gots):
         halves, ids = half_transform(
-            me.reshape(1), ids, got, coeffs, owned, width, occ
+            spot, ids, got, coeffs, owners, owned, width, occ
         )
         parts = [across(halves[j], j) for j in range(occ)]
         piece = jnp.concatenate(parts, axis=0) if occ > 1 else parts[0]

time: 121 us -> 135 us (1.12)
  waiting for transfers between devices: 42.5 us -> 73.7 us
  starting transfers between devices: 42 us -> 27.3 us
  local copies, waits for them, and re-layouts: 9.25 us -> 5.17 us
  matrix products: 16.4 us -> 18.1 us
    ppermute x14 -> x7, starting transfers between devices: 24.8 us -> 12.5 us  [on_device(): got.append(lax.ppermute(sends[n], 'pair', target))]
    all_to_all x0 -> x1, waiting for transfers between devices: none -> 12.2 us  [on_device(): lax.all_to_all(send, 'pair', split_axis=0, concat_axis=0, tiled=True)]
    ppermute x7, waiting for transfers between devices: 24.8 us -> 33 us  [along(): lax.ppermute(array, 'pair', [(p, (p // 2 + 1) % outer * 2 + p % 2) for p...]
    ppermute x7, waiting for transfers between devices: 10.5 us -> 18.5 us  [swap(): return lax.ppermute(array, 'pair', [(p, p ^ 1) for p in range(owners)])]
    all_to_all x0 -> x1, starting transfers between devices: none -> 5.65 us  [on_device(): lax.all_to_all(send, 'pair', split_axis=0, concat_axis=0, tiled=True)]
    ppermute x7, starting transfers between devices: 4.55 us -> 0.21 us  [along(): lax.ppermute(array, 'pair', [(p, (p // 2 + 1) % outer * 2 + p % 2) for p...]
    ppermute x14 -> x7, waiting for transfers between devices: 1.05 us -> 5.12 us  [on_device(): got.append(lax.ppermute(sends[n], 'pair', target))]
    unnamed x26 -> x16, local copies, waits for them, and re-layouts: 5.98 us -> 2.1 us
  transfers between devices with their start and end apart: 34 -> 28, of which waited for: 13 -> 15; matrix products, arithmetic and copies ran while one was open for 16% -> 15% of each run, Pallas kernels for 2% -> 2%
where the time goes in v4:
time: 135 us
  waiting for transfers between devices  73.7 us (55%)
  starting transfers between devices  27.3 us (20%)
  matrix products  18.1 us (13%)
  Pallas kernels  9.84 us (7%)
  local copies, waits for them, and re-layouts  5.17 us (4%)
    ppermute x7, waiting for transfers between devices, along(): lax.ppermute(array, 'pair', [(p, (p // 2 + 1) % outer * 2 + p % 2) for p...  33 us
    ppermute x7, waiting for transfers between devices, swap(): return lax.ppermute(array, 'pair', [(p, p ^ 1) for p in range(owners)])  18.5 us
    dot_general x16, matrix products, second_half(): term = jnp.dot(array, part, preferred_element_type=jnp.float32)  18.1 us
    ppermute x7, starting transfers between devices, on_device(): got.append(lax.ppermute(sends[n], 'pair', target))  12.5 us
    all_to_all x1, waiting for transfers between devices, on_device(): lax.all_to_all(send, 'pair', split_axis=0, concat_axis=0, tiled=True)  12.2 us
    all_to_all x1, starting transfers between devices, on_device(): lax.all_to_all(send, 'pair', split_axis=0, concat_axis=0, tiled=True)  5.65 us
    ppermute x7, starting transfers between devices, swap(): return lax.ppermute(array, 'pair', [(p, p ^ 1) for p in range(owners)])  5.16 us
    ppermute x7, waiting for transfers between devices, on_device(): got.append(lax.ppermute(sends[n], 'pair', target))  5.12 us
  transfers between devices with their start and end apart: 28, of which 15 were waited for; matrix products, arithmetic and copies ran while one was open for 15% of the time, Pallas kernels for 2%

profile of v4, /device:TPU:0, one launch (start us, length us, event | category | flops | bytes accessed | tf_op | source)
XLA Modules:
  0.0 134.5 jit_solution(2390646732600212000)
XLA Ops:
  0.0 3.3 %pack_live.1 = (bf16[272,128]{1,0:T(8,128)(2,1)S(1)}, bf16[272,128]{1,0:T(8,128)(2,1)}, bf16[272,128]{1,0:T(8,128)(2,1)}, bf16[272,128]{1,0:T(8,128)(2,1)}, bf16...) custom-call(s32[1]{0:T(128)} %bitcast.1.here_ref, ...), custom_call_target="tpu_custom_call" | custom-call | tf_op jit(solution)/shard_map/pack_live/pallas_call | solution.py:69
  3.3 0.8 copy-done
  4.1 0.6 copy-done.1
  4.7 0.6 copy-done.2
  5.3 3.0 %collective-permute-start = (bf16[272,128]{1,0:T(8,128)(2,1)}, bf16[272,128]{1,0:T(8,128)(2,1)S(1)}, u32[]{:S(2)}, u32[]{:S(2)}) collective-permute-start(bf16[272,128]{1,0:T(8,128)(2,1)} %get-tuple-element.24), channel_id=1, source_target_pairs={{0,4},{4,0},{8,12},{12,8},{16,20},{20,16},{24,28},{28,24},{1,5},{5... | collective-permute-start | bytes 208904 | tf_op jit(solution)/shard_map/ppermute | solution.py:244
  8.3 1.6 %collective-permute-start.1 = (bf16[272,128]{1,0:T(8,128)(2,1)}, bf16[272,128]{1,0:T(8,128)(2,1)S(1)}, u32[]{:S(2)}, u32[]{:S(2)}) collective-permute-start(bf16[272,128]{1,0:T(8,128)(2,1)} %get-tuple-element.25), channel_id=1, source_target_pairs={{0,8},{4,12},{8,16},{12,20},{16,24},{20,28},{24,0},{28,4},{1,9},{5... | collective-permute-start | bytes 208904 | tf_op jit(solution)/shard_map/ppermute | solution.py:244
  9.9 1.5 %collective-permute-start.2 = (bf16[272,128]{1,0:T(8,128)(2,1)}, bf16[272,128]{1,0:T(8,128)(2,1)S(1)}, u32[]{:S(2)}, u32[]{:S(2)}) collective-permute-start(bf16[272,128]{1,0:T(8,128)(2,1)} %get-tuple-element.26), channel_id=1, source_target_pairs={{0,12},{4,8},{8,20},{12,16},{16,28},{20,24},{24,4},{28,0},{1,13},{... | collective-permute-start | bytes 208904 | tf_op jit(solution)/shard_map/ppermute | solution.py:244
  11.4 1.0 collective-permute-start.3
  12.5 2.8 %collective-permute-start.4 = (bf16[272,128]{1,0:T(8,128)(2,1)}, bf16[272,128]{1,0:T(8,128)(2,1)}, u32[]{:S(2)}, u32[]{:S(2)}) collective-permute-start(bf16[272,128]{1,0:T(8,128)(2,1)} %get-tuple-element.28), channel_id=1, source_target_pairs={{0,20},{4,16},{8,28},{12,24},{16,4},{20,0},{24,12},{28,8},{1,21},{... | collective-permute-start | bytes 208904 | tf_op jit(solution)/shard_map/ppermute | solution.py:244
  15.3 3.1 %copy.6 = bf16[96,64,128]{1,2,0:T(8,128)(2,1)S(1)} copy(bf16[96,64,128]{2,1,0:T(8,128)(2,1)} %bitcast.26) | data formatting | bytes 3145728 | tf_op jit(solution)/shard_map/reshape | solution.py:249
  18.4 2.3 %collective-permute-start.5 = (bf16[272,128]{1,0:T(8,128)(2,1)}, bf16[272,128]{1,0:T(8,128)(2,1)S(1)}, u32[]{:S(2)}, u32[]{:S(2)}) collective-permute-start(bf16[272,128]{1,0:T(8,128)(2,1)} %copy-done.2), channel_id=1, source_target_pairs={{0,24},{4,28},{8,0},{12,4},{16,8},{20,12},{24,16},{28,20},{1,25},{... | collective-permute-start | bytes 208904 | tf_op jit(solution)/shard_map/ppermute | solution.py:244
  21.0 2.1 %collective-permute-done.4.refs_6_ = bf16[272,128]{1,0:T(8,128)(2,1)} collective-permute-done((bf16[272,128]{1,0:T(8,128)(2,1)}, bf16[272,128]{1,0:T(8,128)(2,1)}, u32[]{:S(2)}, u32[]{:S(2)}) %collective-permute-start.4) | collective-permute-done | bytes 69664 | tf_op jit(solution)/shard_map/ppermute | solution.py:244
  23.0 0.6 collective-permute-done.5.refs_7_
  23.7 2.4 %collective-permute-done.6.refs_8_ = bf16[272,128]{1,0:T(8,128)(2,1)S(1)} collective-permute-done((bf16[272,128]{1,0:T(8,128)(2,1)}, bf16[272,128]{1,0:T(8,128)(2,1)S(1)}, u32[]{:S(2)}, u32[]{:S(2)}) %collective-permute-start.6) | collective-permute-done | bytes 69664 | tf_op jit(solution)/shard_map/ppermute | solution.py:244
  26.1 2.6 %half_transform.2 = (bf16[64,768]{1,0:T(8,128)(2,1)S(1)}, bf16[64,768]{1,0:T(8,128)(2,1)S(1)}, bf16[64,768]{1,0:T(8,128)(2,1)S(1)}, bf16[64,768]{1,0:T(8,128)(2,1)S(1)}, s32[8,128]{1,0:T(8,128)S(1)}) custom-call(s32[2]{0:T(128)S(1)} %pad_add_fusion.place_ref, bf16[96,128,64]{2,1,0:T(8,128)(2,1)S(1)} %bitcast.21, ...), custom_call_target="tpu_custom_call" | custom-call | flops 67108864 | bytes 2523136 | tf_op jit(solution)/shard_map/half_transform/pallas_call | solution.py:142
  28.8 1.6 %collective-permute-start.8 = (bf16[64,768]{1,0:T(8,128)(2,1)S(1)}, bf16[64,768]{1,0:T(8,128)(2,1)S(1)}, u32[]{:S(2)}, u32[]{:S(2)}) collective-permute-start(bf16[64,768]{1,0:T(8,128)(2,1)S(1)} %get-tuple-element.33), channel_id=1, source_target_pairs={{0,2},{1,3},{2,0},{3,1},{4,6},{5,7},{6,4},{7,5},{8,10},{9,11},{10,... | collective-permute-start | bytes 294920 | tf_op jit(solution)/shard_map/ppermute | solution.py:210
  30.7 3.9 %collective-permute-done.8 = bf16[64,768]{1,0:T(8,128)(2,1)S(1)} collective-permute-done((bf16[64,768]{1,0:T(8,128)(2,1)S(1)}, bf16[64,768]{1,0:T(8,128)(2,1)S(1)}, u32[]{:S(2)}, u32[]{:S(2)}) %collective-permute-start.8) | collective-permute-done | bytes 98336 | tf_op jit(solution)/shard_map/ppermute | solution.py:210
  34.6 1.0 collective-permute-done.9
  35.7 0.9 collective-permute-start.10
  36.5 5.7 %all-to-all-start = ((bf16[8,256,128]{2,1,0:T(8,128)(2,1)}), bf16[8,256,128]{2,1,0:T(8,128)(2,1)}, u32[]{:S(2)}, u32[]{:S(2)}) async-start(bf16[8,256,128]{2,1,0:T(8,128)(2,1)} %copy-done), calls=%async_computation | async-start | bytes 1048576 | tf_op jit(solution)/shard_map/all_to_all | solution.py:247
  42.2 7.4 %collective-permute-done.11 = bf16[256,768]{1,0:T(8,128)(2,1)} collective-permute-done((bf16[256,768]{1,0:T(8,128)(2,1)S(1)}, bf16[256,768]{1,0:T(8,128)(2,1)}, u32[]{:S(2)}, u32[]{:S(2)}) %collective-permute-start.11) | collective-permute-done | bytes 393248 | tf_op jit(solution)/shard_map/ppermute | solution.py:213
  49.6 0.6 collective-permute-start.12
  50.2 1.8 %fusion.22 = f32[256,640]{1,0:T(8,128)S(1)} fusion(bf16[256,768]{1,0:T(8,128)(2,1)} %collective-permute-done.11, bf16[6144,640]{1,0:T(8,128)(2,1)} %param.7, s32[]{:T(128)S(6)} %select_n.134), kind=kOutput, calls=%fused_computation.30 | convolution fusion | flops 251658240 | bytes 2031620 | tf_op jit(solution)/shard_map/dot_general | solution.py:236
  52.0 1.8 %fusion.26 = f32[256,640]{1,0:T(8,128)S(1)} fusion(bf16[256,768]{1,0:T(8,128)(2,1)} %collective-permute-done.10, bf16[6144,640]{1,0:T(8,128)(2,1)} %param.7, s32[]{:T(128)S(6)} %select_n.132), kind=kOutput, calls=%fused_computation.34 | convolution fusion | flops 251658240 | bytes 2031620 | tf_op jit(solution)/shard_map/dot_general | solution.py:236
  53.8 2.5 %fusion.5 = f32[256,640]{1,0:T(8,128)} fusion(f32[256,640]{1,0:T(8,128)S(1)} %fusion.22, f32[256,640]{1,0:T(8,128)S(1)} %fusion.26, bf16[256,768]{1,0:T(8,128)(2,1)S(1)} %constant_dynamic-update-slice_fusion, bf16[6144,640]{1,0:T(8,128)(2,1)} %param.7, s32[]{:T(128)S(6)} %select_n.131), kind=kOutput, calls=%fused_computation.13 | convolution fusion | flops 251985920 | bytes 3342340 | tf_op jit(solution)/shard_map/dot_general | solution.py:236
  56.4 12.2 %all-to-all-done.refs_2_ = bf16[8,256,128]{2,1,0:T(8,128)(2,1)} async-done(((bf16[8,256,128]{2,1,0:T(8,128)(2,1)}), bf16[8,256,128]{2,1,0:T(8,128)(2,1)}, u32[]{:S(2)}, u32[]{:S(2)}) %all-to-all-start) | async-done | bytes 524320 | tf_op jit(solution)/shard_map/all_to_all | solution.py:247
  68.6 2.3 %half_transform.3 = (bf16[64,768]{1,0:T(8,128)(2,1)S(1)}, bf16[64,768]{1,0:T(8,128)(2,1)S(1)}, bf16[64,768]{1,0:T(8,128)(2,1)S(1)}, bf16[64,768]{1,0:T(8,128)(2,1)S(1)}) custom-call(s32[2]{0:T(128)S(1)} %pad_add_fusion.place_ref, s32[8,128]{1,0:T(8,128)S(1)} %get-tuple-element.35.refs_0_, bf16[96,128,64]{2,1,0:T(8,128)(2,1)S(1)} %bitcast.22, ...), custom_call_target="tpu_custom_call" | custom-call | flops 67108864 | bytes 2490368 | tf_op jit(solution)/shard_map/half_transform/pallas_call | solution.py:142
  71.0 1.6 %collective-permute-start.18 = (bf16[64,768]{1,0:T(8,128)(2,1)S(1)}, bf16[64,768]{1,0:T(8,128)(2,1)S(1)}, u32[]{:S(2)}, u32[]{:S(2)}) collective-permute-start(bf16[64,768]{1,0:T(8,128)(2,1)S(1)} %get-tuple-element.39), channel_id=1, source_target_pairs={{0,2},{1,3},{2,0},{3,1},{4,6},{5,7},{6,4},{7,5},{8,10},{9,11},{10,... | collective-permute-start | bytes 294920 | tf_op jit(solution)/shard_map/ppermute | solution.py:210
  72.9 1.8 %fusion.16 = f32[256,640]{1,0:T(8,128)S(1)} fusion(bf16[256,768]{1,0:T(8,128)(2,1)} %collective-permute-done.13, bf16[6144,640]{1,0:T(8,128)(2,1)} %param.7, s32[]{:T(128)S(6)} %select_n.137), kind=kOutput, calls=%fused_computation.24 | convolution fusion | flops 251658240 | bytes 2031620 | tf_op jit(solution)/shard_map/dot_general | solution.py:236
  74.7 0.6 collective-permute-start.14
  75.4 2.3 %fusion.4 = f32[256,640]{1,0:T(8,128)S(1)} fusion(f32[256,640]{1,0:T(8,128)S(1)} %fusion.16, f32[256,640]{1,0:T(8,128)} %fusion.5, bf16[256,768]{1,0:T(8,128)(2,1)} %collective-permute-done.12, bf16[6144,640]{1,0:T(8,128)(2,1)} %param.7, s32[]{:T(128)S(6)} %select_n.135), kind=kOutput, calls=%fused_computation.11 | convolution fusion | flops 251985920 | bytes 3342340 | tf_op jit(solution)/shard_map/dot_general | solution.py:236
  77.8 1.2 collective-permute-start.20
  79.1 7.8 %collective-permute-done.15 = bf16[256,768]{1,0:T(8,128)(2,1)S(1)} collective-permute-done((bf16[256,768]{1,0:T(8,128)(2,1)}, bf16[256,768]{1,0:T(8,128)(2,1)S(1)}, u32[]{:S(2)}, u32[]{:S(2)}) %collective-permute-start.15) | collective-permute-done | bytes 393248 | tf_op jit(solution)/shard_map/ppermute | solution.py:213
  86.9 0.6 collective-permute-start.16
  87.5 1.7 %fusion.10 = f32[256,640]{1,0:T(8,128)S(1)} fusion(bf16[256,768]{1,0:T(8,128)(2,1)S(1)} %collective-permute-done.15, bf16[6144,640]{1,0:T(8,128)(2,1)} %param.7, s32[]{:T(128)S(6)} %select_n.140), kind=kOutput, calls=%fused_computation.18 | convolution fusion | flops 251658240 | bytes 2031620 | tf_op jit(solution)/shard_map/dot_general | solution.py:236
  89.2 1.7 %fusion.3 = f32[256,640]{1,0:T(8,128)S(1)} fusion(f32[256,640]{1,0:T(8,128)S(1)} %fusion.10, f32[256,640]{1,0:T(8,128)S(1)} %fusion.4, bf16[256,768]{1,0:T(8,128)(2,1)S(1)} %collective-permute-done.14, bf16[6144,640]{1,0:T(8,128)(2,1)} %param.7, s32[]{:T(128)S(6)} %select_n.138), kind=kOutput, calls=%fused_computation.9 | convolution fusion | flops 251985920 | bytes 3342340 | tf_op jit(solution)/shard_map/dot_general | solution.py:236
  90.9 3.8 %collective-permute-done.21 = bf16[256,768]{1,0:T(8,128)(2,1)S(1)} collective-permute-done((bf16[256,768]{1,0:T(8,128)(2,1)S(1)}, bf16[256,768]{1,0:T(8,128)(2,1)S(1)}, u32[]{:S(2)}, u32[]{:S(2)}) %collective-permute-start.21) | collective-permute-done | bytes 393248 | tf_op jit(solution)/shard_map/ppermute | solution.py:213
  95.9 0.5 fusion.2
  96.4 0.6 collective-permute-start.22
  97.1 6.8 %collective-permute-done.16 = bf16[256,768]{1,0:T(8,128)(2,1)S(1)} collective-permute-done((bf16[256,768]{1,0:T(8,128)(2,1)S(1)}, bf16[256,768]{1,0:T(8,128)(2,1)S(1)}, u32[]{:S(2)}, u32[]{:S(2)}) %collective-permute-start.16) | collective-permute-done | bytes 393248 | tf_op jit(solution)/shard_map/ppermute | solution.py:218
  104.3 2.7 %collective-permute-done.23 = bf16[256,768]{1,0:T(8,128)(2,1)S(1)} collective-permute-done((bf16[256,768]{1,0:T(8,128)(2,1)S(1)}, bf16[256,768]{1,0:T(8,128)(2,1)S(1)}, u32[]{:S(2)}, u32[]{:S(2)}) %collective-permute-start.23) | collective-permute-done | bytes 393248 | tf_op jit(solution)/shard_map/ppermute | solution.py:213
  107.0 0.6 collective-permute-start.24
  108.1 4.2 %collective-permute-done.22 = bf16[256,768]{1,0:T(8,128)(2,1)S(1)} collective-permute-done((bf16[256,768]{1,0:T(8,128)(2,1)S(1)}, bf16[256,768]{1,0:T(8,128)(2,1)S(1)}, u32[]{:S(2)}, u32[]{:S(2)}) %collective-permute-start.22) | collective-permute-done | bytes 393248 | tf_op jit(solution)/shard_map/ppermute | solution.py:218
  112.3 0.5 fusion.1
  112.8 7.3 %collective-permute-done.24 = bf16[256,768]{1,0:T(8,128)(2,1)S(1)} collective-permute-done((bf16[256,768]{1,0:T(8,128)(2,1)S(1)}, bf16[256,768]{1,0:T(8,128)(2,1)S(1)}, u32[]{:S(2)}, u32[]{:S(2)}) %collective-permute-start.24) | collective-permute-done | bytes 393248 | tf_op jit(solution)/shard_map/ppermute | solution.py:218
  120.6 0.5 fusion
  121.1 11.3 %collective-permute-done.26 = bf16[256,768]{1,0:T(8,128)(2,1)S(1)} collective-permute-done((bf16[256,768]{1,0:T(8,128)(2,1)S(1)}, bf16[256,768]{1,0:T(8,128)(2,1)S(1)}, u32[]{:S(2)}, u32[]{:S(2)}) %collective-permute-start.26) | collective-permute-done | bytes 393248 | tf_op jit(solution)/shard_map/ppermute | solution.py:213
  132.9 1.6 %place.1 = bf16[32,16,640]{2,1,0:T(8,128)(2,1)} custom-call(s32[1]{0:T(128)} %bitcast.me_ref, f32[256,640]{1,0:T(8,128)S(1)} %convolution_add_fusion.4.refs_0_, f32[256,640]{1,0:T(8,128)S(1)} %convolution_add_fusion.refs_1_), custom_call_target="tpu_custom_call" | custom-call | tf_op jit(solution)/shard_map/place/pallas_call | solution.py:183
  (49 shorter events, 4.4 us)
Async XLA Ops:
  3.3 0.8 copy-start
  4.1 0.6 copy-start.1
  4.7 0.6 copy-start.2
  5.3 13.0 %collective-permute-start = (bf16[272,128]{1,0:T(8,128)(2,1)}, bf16[272,128]{1,0:T(8,128)(2,1)S(1)}, u32[]{:S(2)}, u32[]{:S(2)}) collective-permute-start(bf16[272,128]{1,0:T(8,128)(2,1)} %get-tuple-element.24), channel_id=1, source_target_pairs={{0,4},{4,0},{8,12},{12,8},{16,20},{20,16},{24,28},{28,24},{1,5},{5... | collective-permute-start | bytes 208904 | tf_op jit(solution)/shard_map/ppermute | solution.py:244
  8.3 12.4 %collective-permute-start.1 = (bf16[272,128]{1,0:T(8,128)(2,1)}, bf16[272,128]{1,0:T(8,128)(2,1)S(1)}, u32[]{:S(2)}, u32[]{:S(2)}) collective-permute-start(bf16[272,128]{1,0:T(8,128)(2,1)} %get-tuple-element.25), channel_id=1, source_target_pairs={{0,8},{4,12},{8,16},{12,20},{16,24},{20,28},{24,0},{28,4},{1,9},{5... | collective-permute-start | bytes 208904 | tf_op jit(solution)/shard_map/ppermute | solution.py:244
  9.9 11.1 %collective-permute-start.2 = (bf16[272,128]{1,0:T(8,128)(2,1)}, bf16[272,128]{1,0:T(8,128)(2,1)S(1)}, u32[]{:S(2)}, u32[]{:S(2)}) collective-permute-start(bf16[272,128]{1,0:T(8,128)(2,1)} %get-tuple-element.26), channel_id=1, source_target_pairs={{0,12},{4,8},{8,20},{12,16},{16,28},{20,24},{24,4},{28,0},{1,13},{... | collective-permute-start | bytes 208904 | tf_op jit(solution)/shard_map/ppermute | solution.py:244
  11.4 9.5 %collective-permute-start.3 = (bf16[272,128]{1,0:T(8,128)(2,1)}, bf16[272,128]{1,0:T(8,128)(2,1)S(1)}, u32[]{:S(2)}, u32[]{:S(2)}) collective-permute-start(bf16[272,128]{1,0:T(8,128)(2,1)} %get-tuple-element.27), channel_id=1, source_target_pairs={{0,16},{4,20},{8,24},{12,28},{16,0},{20,4},{24,8},{28,12},{1,17},{... | collective-permute-start | bytes 208904 | tf_op jit(solution)/shard_map/ppermute | solution.py:244
  12.5 10.6 %collective-permute-start.4 = (bf16[272,128]{1,0:T(8,128)(2,1)}, bf16[272,128]{1,0:T(8,128)(2,1)}, u32[]{:S(2)}, u32[]{:S(2)}) collective-permute-start(bf16[272,128]{1,0:T(8,128)(2,1)} %get-tuple-element.28), channel_id=1, source_target_pairs={{0,20},{4,16},{8,28},{12,24},{16,4},{20,0},{24,12},{28,8},{1,21},{... | collective-permute-start | bytes 208904 | tf_op jit(solution)/shard_map/ppermute | solution.py:244
  18.4 5.3 %collective-permute-start.5 = (bf16[272,128]{1,0:T(8,128)(2,1)}, bf16[272,128]{1,0:T(8,128)(2,1)S(1)}, u32[]{:S(2)}, u32[]{:S(2)}) collective-permute-start(bf16[272,128]{1,0:T(8,128)(2,1)} %copy-done.2), channel_id=1, source_target_pairs={{0,24},{4,28},{8,0},{12,4},{16,8},{20,12},{24,16},{28,20},{1,25},{... | collective-permute-start | bytes 208904 | tf_op jit(solution)/shard_map/ppermute | solution.py:244
  20.7 5.4 %collective-permute-start.6 = (bf16[272,128]{1,0:T(8,128)(2,1)}, bf16[272,128]{1,0:T(8,128)(2,1)S(1)}, u32[]{:S(2)}, u32[]{:S(2)}) collective-permute-start(bf16[272,128]{1,0:T(8,128)(2,1)} %copy-done.1), channel_id=1, source_target_pairs={{0,28},{4,24},{8,4},{12,0},{16,12},{20,8},{24,20},{28,16},{1,29},{... | collective-permute-start | bytes 208904 | tf_op jit(solution)/shard_map/ppermute | solution.py:244
  28.7 1.9 %collective-permute-start.7 = (bf16[64,768]{1,0:T(8,128)(2,1)S(1)}, bf16[64,768]{1,0:T(8,128)(2,1)S(1)}, u32[]{:S(2)}, u32[]{:S(2)}) collective-permute-start(bf16[64,768]{1,0:T(8,128)(2,1)S(1)} %get-tuple-element.32), channel_id=1, source_target_pairs={{0,1},{1,0},{2,3},{3,2},{4,5},{5,4},{6,7},{7,6},{8,9},{9,8},{10,11... | collective-permute-start | bytes 294920 | tf_op jit(solution)/shard_map/ppermute | solution.py:210
  28.8 5.7 %collective-permute-start.8 = (bf16[64,768]{1,0:T(8,128)(2,1)S(1)}, bf16[64,768]{1,0:T(8,128)(2,1)S(1)}, u32[]{:S(2)}, u32[]{:S(2)}) collective-permute-start(bf16[64,768]{1,0:T(8,128)(2,1)S(1)} %get-tuple-element.33), channel_id=1, source_target_pairs={{0,2},{1,3},{2,0},{3,1},{4,6},{5,7},{6,4},{7,5},{8,10},{9,11},{10,... | collective-permute-start | bytes 294920 | tf_op jit(solution)/shard_map/ppermute | solution.py:210
  30.4 5.2 %collective-permute-start.9 = (bf16[64,768]{1,0:T(8,128)(2,1)S(1)}, bf16[64,768]{1,0:T(8,128)(2,1)S(1)}, u32[]{:S(2)}, u32[]{:S(2)}) collective-permute-start(bf16[64,768]{1,0:T(8,128)(2,1)S(1)} %get-tuple-element.34), channel_id=1, source_target_pairs={{0,3},{1,2},{2,1},{3,0},{4,7},{5,6},{6,5},{7,4},{8,11},{9,10},{10,... | collective-permute-start | bytes 294920 | tf_op jit(solution)/shard_map/ppermute | solution.py:210
  35.6 14.0 %collective-permute-start.11 = (bf16[256,768]{1,0:T(8,128)(2,1)S(1)}, bf16[256,768]{1,0:T(8,128)(2,1)}, u32[]{:S(2)}, u32[]{:S(2)}) collective-permute-start(bf16[256,768]{1,0:T(8,128)(2,1)S(1)} %constant_dynamic-update-slice_fusion), channel_id=1, source_target_pairs={{0,8},{4,12},{8,16},{12,20},{16,24},{20,28},{24,0},{28,4},{1,9},{5... | collective-permute-start | bytes 1179656 | tf_op jit(solution)/shard_map/ppermute | solution.py:213
  35.7 16.4 %collective-permute-start.10 = (bf16[256,768]{1,0:T(8,128)(2,1)S(1)}, bf16[256,768]{1,0:T(8,128)(2,1)}, u32[]{:S(2)}, u32[]{:S(2)}) collective-permute-start(bf16[256,768]{1,0:T(8,128)(2,1)S(1)} %constant_dynamic-update-slice_fusion), channel_id=1, source_target_pairs={{0,4},{4,0},{8,12},{12,8},{16,20},{20,16},{24,28},{28,24},{1,5},{5... | collective-permute-start | bytes 1179656 | tf_op jit(solution)/shard_map/ppermute | solution.py:218
  36.5 32.0 %all-to-all-start = ((bf16[8,256,128]{2,1,0:T(8,128)(2,1)}), bf16[8,256,128]{2,1,0:T(8,128)(2,1)}, u32[]{:S(2)}, u32[]{:S(2)}) async-start(bf16[8,256,128]{2,1,0:T(8,128)(2,1)} %copy-done), calls=%async_computation | async-start | bytes 1048576 | tf_op jit(solution)/shard_map/all_to_all | solution.py:247
  49.6 23.3 %collective-permute-start.13 = (bf16[256,768]{1,0:T(8,128)(2,1)}, bf16[256,768]{1,0:T(8,128)(2,1)}, u32[]{:S(2)}, u32[]{:S(2)}) collective-permute-start(bf16[256,768]{1,0:T(8,128)(2,1)} %collective-permute-done.11), channel_id=1, source_target_pairs={{0,8},{4,12},{8,16},{12,20},{16,24},{20,28},{24,0},{28,4},{1,9},{5... | collective-permute-start | bytes 1179656 | tf_op jit(solution)/shard_map/ppermute | solution.py:213
  49.6 25.2 %collective-permute-start.12 = (bf16[256,768]{1,0:T(8,128)(2,1)}, bf16[256,768]{1,0:T(8,128)(2,1)}, u32[]{:S(2)}, u32[]{:S(2)}) collective-permute-start(bf16[256,768]{1,0:T(8,128)(2,1)} %collective-permute-done.11), channel_id=1, source_target_pairs={{0,4},{4,0},{8,12},{12,8},{16,20},{20,16},{24,28},{28,24},{1,5},{5... | collective-permute-start | bytes 1179656 | tf_op jit(solution)/shard_map/ppermute | solution.py:218
  68.6 26.1 %slice-start = ((s8[7864320]{0:T(1024)(128)(4,1)}), s8[3670016]{0:T(1024)(128)(4,1)S(1)}, s32[]{:S(2)}) async-start(s8[7864320]{0:T(1024)(128)(4,1)} %bitcast.23), calls=%async_computation.1 | async-start | bytes 7340032
  70.9 6.8 %collective-permute-start.17 = (bf16[64,768]{1,0:T(8,128)(2,1)S(1)}, bf16[64,768]{1,0:T(8,128)(2,1)S(1)}, u32[]{:S(2)}, u32[]{:S(2)}) collective-permute-start(bf16[64,768]{1,0:T(8,128)(2,1)S(1)} %get-tuple-element.38), channel_id=1, source_target_pairs={{0,1},{1,0},{2,3},{3,2},{4,5},{5,4},{6,7},{7,6},{8,9},{9,8},{10,11... | collective-permute-start | bytes 294920 | tf_op jit(solution)/shard_map/ppermute | solution.py:210
  71.0 6.8 %collective-permute-start.18 = (bf16[64,768]{1,0:T(8,128)(2,1)S(1)}, bf16[64,768]{1,0:T(8,128)(2,1)S(1)}, u32[]{:S(2)}, u32[]{:S(2)}) collective-permute-start(bf16[64,768]{1,0:T(8,128)(2,1)S(1)} %get-tuple-element.39), channel_id=1, source_target_pairs={{0,2},{1,3},{2,0},{3,1},{4,6},{5,7},{6,4},{7,5},{8,10},{9,11},{10,... | collective-permute-start | bytes 294920 | tf_op jit(solution)/shard_map/ppermute | solution.py:210
  72.6 5.2 %collective-permute-start.19 = (bf16[64,768]{1,0:T(8,128)(2,1)S(1)}, bf16[64,768]{1,0:T(8,128)(2,1)S(1)}, u32[]{:S(2)}, u32[]{:S(2)}) collective-permute-start(bf16[64,768]{1,0:T(8,128)(2,1)S(1)} %get-tuple-element.40), channel_id=1, source_target_pairs={{0,3},{1,2},{2,1},{3,0},{4,7},{5,6},{6,5},{7,4},{8,11},{9,10},{10,... | collective-permute-start | bytes 294920 | tf_op jit(solution)/shard_map/ppermute | solution.py:210
  72.8 14.0 %collective-permute-start.15 = (bf16[256,768]{1,0:T(8,128)(2,1)}, bf16[256,768]{1,0:T(8,128)(2,1)S(1)}, u32[]{:S(2)}, u32[]{:S(2)}) collective-permute-start(bf16[256,768]{1,0:T(8,128)(2,1)} %collective-permute-done.13), channel_id=1, source_target_pairs={{0,8},{4,12},{8,16},{12,20},{16,24},{20,28},{24,0},{28,4},{1,9},{5... | collective-permute-start | bytes 1179656 | tf_op jit(solution)/shard_map/ppermute | solution.py:213
  74.7 20.0 %slice-start.1 = ((s8[7864320]{0:T(1024)(128)(4,1)}), s8[4194304]{0:T(1024)(128)(4,1)S(1)}, s32[]{:S(2)}) async-start(s8[7864320]{0:T(1024)(128)(4,1)} %bitcast.23), calls=%async_computation.2 | async-start | bytes 8388608
  74.7 14.4 %collective-permute-start.14 = (bf16[256,768]{1,0:T(8,128)(2,1)}, bf16[256,768]{1,0:T(8,128)(2,1)S(1)}, u32[]{:S(2)}, u32[]{:S(2)}) collective-permute-start(bf16[256,768]{1,0:T(8,128)(2,1)} %collective-permute-done.13), channel_id=1, source_target_pairs={{0,4},{4,0},{8,12},{12,8},{16,20},{20,16},{24,28},{28,24},{1,5},{5... | collective-permute-start | bytes 1179656 | tf_op jit(solution)/shard_map/ppermute | solution.py:218
  77.8 17.6 %collective-permute-start.20 = (bf16[256,768]{1,0:T(8,128)(2,1)S(1)}, bf16[256,768]{1,0:T(8,128)(2,1)S(1)}, u32[]{:S(2)}, u32[]{:S(2)}) collective-permute-start(bf16[256,768]{1,0:T(8,128)(2,1)S(1)} %constant_dynamic-update-slice_fusion.4), channel_id=1, source_target_pairs={{0,4},{4,0},{8,12},{12,8},{16,20},{20,16},{24,28},{28,24},{1,5},{5... | collective-permute-start | bytes 1179656 | tf_op jit(solution)/shard_map/ppermute | solution.py:218
  79.0 15.7 %collective-permute-start.21 = (bf16[256,768]{1,0:T(8,128)(2,1)S(1)}, bf16[256,768]{1,0:T(8,128)(2,1)S(1)}, u32[]{:S(2)}, u32[]{:S(2)}) collective-permute-start(bf16[256,768]{1,0:T(8,128)(2,1)S(1)} %constant_dynamic-update-slice_fusion.4), channel_id=1, source_target_pairs={{0,8},{4,12},{8,16},{12,20},{16,24},{20,28},{24,0},{28,4},{1,9},{5... | collective-permute-start | bytes 1179656 | tf_op jit(solution)/shard_map/ppermute | solution.py:213
  86.9 17.0 %collective-permute-start.16 = (bf16[256,768]{1,0:T(8,128)(2,1)S(1)}, bf16[256,768]{1,0:T(8,128)(2,1)S(1)}, u32[]{:S(2)}, u32[]{:S(2)}) collective-permute-start(bf16[256,768]{1,0:T(8,128)(2,1)S(1)} %collective-permute-done.15), channel_id=1, source_target_pairs={{0,4},{4,0},{8,12},{12,8},{16,20},{20,16},{24,28},{28,24},{1,5},{5... | collective-permute-start | bytes 1179656 | tf_op jit(solution)/shard_map/ppermute | solution.py:218
  94.7 12.3 %collective-permute-start.23 = (bf16[256,768]{1,0:T(8,128)(2,1)S(1)}, bf16[256,768]{1,0:T(8,128)(2,1)S(1)}, u32[]{:S(2)}, u32[]{:S(2)}) collective-permute-start(bf16[256,768]{1,0:T(8,128)(2,1)S(1)} %collective-permute-done.21), channel_id=1, source_target_pairs={{0,8},{4,12},{8,16},{12,20},{16,24},{20,28},{24,0},{28,4},{1,9},{5... | collective-permute-start | bytes 1179656 | tf_op jit(solution)/shard_map/ppermute | solution.py:213
  96.4 15.9 %collective-permute-start.22 = (bf16[256,768]{1,0:T(8,128)(2,1)S(1)}, bf16[256,768]{1,0:T(8,128)(2,1)S(1)}, u32[]{:S(2)}, u32[]{:S(2)}) collective-permute-start(bf16[256,768]{1,0:T(8,128)(2,1)S(1)} %collective-permute-done.21), channel_id=1, source_target_pairs={{0,4},{4,0},{8,12},{12,8},{16,20},{20,16},{24,28},{28,24},{1,5},{5... | collective-permute-start | bytes 1179656 | tf_op jit(solution)/shard_map/ppermute | solution.py:218
  107.0 13.1 %collective-permute-start.25 = (bf16[256,768]{1,0:T(8,128)(2,1)S(1)}, bf16[256,768]{1,0:T(8,128)(2,1)S(1)}, u32[]{:S(2)}, u32[]{:S(2)}) collective-permute-start(bf16[256,768]{1,0:T(8,128)(2,1)S(1)} %collective-permute-done.23), channel_id=1, source_target_pairs={{0,8},{4,12},{8,16},{12,20},{16,24},{20,28},{24,0},{28,4},{1,9},{5... | collective-permute-start | bytes 1179656 | tf_op jit(solution)/shard_map/ppermute | solution.py:213
  107.0 13.1 %collective-permute-start.24 = (bf16[256,768]{1,0:T(8,128)(2,1)S(1)}, bf16[256,768]{1,0:T(8,128)(2,1)S(1)}, u32[]{:S(2)}, u32[]{:S(2)}) collective-permute-start(bf16[256,768]{1,0:T(8,128)(2,1)S(1)} %collective-permute-done.23), channel_id=1, source_target_pairs={{0,4},{4,0},{8,12},{12,8},{16,20},{20,16},{24,28},{28,24},{1,5},{5... | collective-permute-start | bytes 1179656 | tf_op jit(solution)/shard_map/ppermute | solution.py:218
  120.1 12.3 %collective-permute-start.26 = (bf16[256,768]{1,0:T(8,128)(2,1)S(1)}, bf16[256,768]{1,0:T(8,128)(2,1)S(1)}, u32[]{:S(2)}, u32[]{:S(2)}) collective-permute-start(bf16[256,768]{1,0:T(8,128)(2,1)S(1)} %collective-permute-done.24), channel_id=1, source_target_pairs={{0,8},{4,12},{8,16},{12,20},{16,24},{20,28},{24,0},{28,4},{1,9},{5... | collective-permute-start | bytes 1179656 | tf_op jit(solution)/shard_map/ppermute | solution.py:213

commit v5 on v4

--- a/solution.py
+++ b/solution.py
@@ -75,9 +75,8 @@
             pltpu.SMEM((owners, LIVE + 1), jnp.int32),
             pltpu.SemaphoreType.DMA((owners, LIVE, chunks)),
         ],
-        compiler_params=pltpu.CompilerParams(vmem_limit_bytes=GRANT),
         name="pack_live",
-    )(here, *(pltpu.with_memory_space_constraint(x, pltpu.HBM) for x in (block_ids, live_mask, blocks)))
+    )(here, block_ids, live_mask, pltpu.with_memory_space_constraint(blocks, pltpu.HBM))
 
 
 def half_kernel(owned, width, owners, place_ref, *refs):
@@ -101,16 +100,21 @@
         got_refs = [got_ref.at[relative(place_ref[1], n, owners, -1)] for n in range(owners)]
         total[...] = jnp.zeros_like(total)
     aux = got_refs[0].shape[1] // width
+    low = lax.broadcasted_iota(jnp.int32, (width, 2 * width), 1) < width
+    high = lax.broadcasted_iota(jnp.int32, (total.shape[1], 2 * width), 1) // width
     for n, got_ref in enumerate(got_refs):
         for k in range(LIVE):
             mu = ids_smem[n, k]
             nu = ids_smem[n, LIVE + k]
             block = got_ref[k * width : (k + 1) * width, :]
+            turned = pltpu.roll(block.astype(jnp.float32), width, 1).astype(block.dtype)
             stacked = jnp.concatenate(
-                [block[:, q * width : (q + 1) * width] for q in range(aux)], axis=0
-            )
+                [jnp.where(low, block, turned), jnp.where(low, turned, block)], axis=0
+            )
+            coeff = coeff_ref[mu // 2]
+            coeff = jnp.where((high ^ lax.rem(mu, 2)) == 0, coeff, jnp.zeros_like(coeff))
             total[nu] += lax.dot_general(
-                coeff_ref[mu], stacked, (((1,), (1,)), ((), ())), preferred_element_type=jnp.float32
+                coeff, stacked, (((1,), (1,)), ((), ())), preferred_element_type=jnp.float32
             )
 
     slab = total.shape[1] // len(out_refs)
@@ -130,7 +134,7 @@
     lanes = gots[0].shape[-1]
     aux = lanes // width
     occ_count = coeffs.shape[1]
-    assert coeffs.shape[2] == width
+    assert coeffs.shape[2] == lanes == 2 * width
     shape = jax.ShapeDtypeStruct((aux * occ_count // occ, owned * width), jnp.bfloat16)
     smem = pl.BlockSpec(memory_space=pltpu.SMEM)
     vmem = pl.BlockSpec(memory_space=pltpu.VMEM)
@@ -156,39 +160,51 @@
     return result[:occ], result[occ] if ids is None else ids
 
 
-def place_kernel(occ, me_ref, *refs):
+def place_kernel(layout, aux, me_ref, *refs):
     in_refs, (out_ref, wide) = refs[:-2], refs[-2:]
-    slab, aux, _ = out_ref.shape
-    chunks = len(in_refs)
-    local = aux // (occ * chunks)
-    for c, in_ref in enumerate(in_refs):
-        for j in range(occ):
-            for q in range(local):
-                at = (me_ref[0] ^ j) * (chunks * local) + c * local + q
-                row = (j * local + q) * slab
+    slab, all_aux, _ = out_ref.shape
+    chunks = 1 + max(c for parts in layout for c, _ in parts)
+    for in_ref, parts in zip(in_refs, layout):
+        for i, (c, j) in enumerate(parts):
+            for q in range(aux):
+                at = (me_ref[0] ^ j) * (chunks * aux) + c * aux + q
+                row = (i * aux + q) * slab
                 for t in range(wide.shape[0]):
-                    wide[t, pl.ds(at, slab, stride=aux), :] = in_ref[
+                    wide[t, pl.ds(at, slab, stride=all_aux), :] = in_ref[
                         row : row + slab, t * 128 : (t + 1) * 128
                     ]
     for t in range(wide.shape[0]):
         out_ref[:, :, t * 128 : (t + 1) * 128] = (
-            wide[t].reshape(slab, aux, 128).astype(out_ref.dtype)
+            wide[t].reshape(slab, all_aux, 128).astype(out_ref.dtype)
         )
 
 
-def place(me, parts, occ, slab):
-    rows, columns = parts[0].shape
-    aux = rows * len(parts) // slab
+def place(me, sums, layout, slab):
+    columns = sums[0].shape[1]
+    rows = sum(total.shape[0] for total in sums)
+    aux = sums[0].shape[0] // len(layout[0]) // slab
     vmem = pl.BlockSpec(memory_space=pltpu.VMEM)
     return pl.pallas_call(
-        functools.partial(place_kernel, occ),
-        out_shape=jax.ShapeDtypeStruct((slab, aux, columns), jnp.bfloat16),
-        in_specs=[pl.BlockSpec(memory_space=pltpu.SMEM)] + [vmem] * len(parts),
+        functools.partial(place_kernel, layout, aux),
+        out_shape=jax.ShapeDtypeStruct((slab, rows // slab, columns), jnp.bfloat16),
+        in_specs=[pl.BlockSpec(memory_space=pltpu.SMEM)] + [vmem] * len(sums),
         out_specs=vmem,
-        scratch_shapes=[pltpu.VMEM((columns // 128, slab * aux, 128), jnp.float32)],
+        scratch_shapes=[pltpu.VMEM((columns // 128, rows, 128), jnp.float32)],
         compiler_params=pltpu.CompilerParams(vmem_limit_bytes=GRANT),
         name="place",
-    )(me, *parts)
+    )(me, *sums)
+
+
+def piece_layout(chunks, occ):
+    near = min(2, occ)
+    layout = [[(0, j) for j in range(near)]]
+    for c in range(chunks):
+        parts = [(c, j) for j in range(near, occ)]
+        if c + 1 < chunks:
+            parts += [(c + 1, j) for j in range(near)]
+        if parts:
+            layout.append(parts)
+    return layout
 
 
 def on_device(integrals, occ_coeffs, virt_coeffs, block_ids, live_mask):
@@ -238,7 +254,7 @@
         return total
 
     sends = pack(here.astype(jnp.int32).reshape(1), block_ids, live_mask, blocks, owners, owned)
-    got = [sends[0]]
+    got = [pltpu.with_memory_space_constraint(sends[0], pltpu.HBM)]
     for n in range(1, owners):
         target = [(p, (p // 2 + n // 2) % outer * 2 + (p + n) % 2) for p in range(owners)]
         got.append(lax.ppermute(sends[n], "pair", target))
@@ -246,16 +262,20 @@
     for c, send in enumerate(sends[owners:], 1):
         gots.append([lax.all_to_all(send, "pair", split_axis=0, concat_axis=0, tiled=True)])
     spot = jnp.stack([me, here.astype(jnp.int32)])
-    coeffs = occ_coeffs.reshape(-1, width, occ_count).transpose(0, 2, 1)
-    results, ids = [], None
+    coeffs = occ_coeffs.reshape(-1, 2 * width, occ_count).transpose(0, 2, 1)
+    parts, ids = {}, None
     for c, got in enumerate(gots):
         halves, ids = half_transform(
             spot, ids, got, coeffs, owners, owned, width, occ
         )
-        parts = [across(halves[j], j) for j in range(occ)]
-        piece = jnp.concatenate(parts, axis=0) if occ > 1 else parts[0]
-        results.append(second_half(*gather(piece, c == len(gots) - 1)))
-    return place(me.reshape(1), results, occ, slab)
+        for j in range(occ):
+            parts[c, j] = across(halves[j], j)
+    layout = piece_layout(len(gots), occ)
+    results = []
+    for i, names in enumerate(layout):
+        piece = jnp.concatenate([parts[name] for name in names], axis=0)
+        results.append(second_half(*gather(piece, i == 1)))
+    return place(me.reshape(1), results, layout, slab)
 
 
 def solution(mesh):

time: 135 us -> 136 us (level)
  starting transfers between devices: 27.3 us -> 47 us
  waiting for transfers between devices: 73.7 us -> 55.2 us
  matrix products: 18.1 us -> 21.4 us
  local copies, waits for them, and re-layouts: 5.17 us -> 2 us
    ppermute x7 -> x10, starting transfers between devices: 0.21 us -> 14.4 us  [along(): lax.ppermute(array, 'pair', [(p, (p // 2 + 1) % outer * 2 + p % 2) for p...]
    all_to_all x1, waiting for transfers between devices: 12.2 us -> 0.01 us  [on_device(): lax.all_to_all(send, 'pair', split_axis=0, concat_axis=0, tiled=True)]
    ppermute x7 -> x11, waiting for transfers between devices: 18.5 us -> 12.5 us  [swap(): return lax.ppermute(array, 'pair', [(p, p ^ 1) for p in range(owners)])]
    ppermute x7 -> x11, starting transfers between devices: 5.16 us -> 9.34 us  [swap(): return lax.ppermute(array, 'pair', [(p, p ^ 1) for p in range(owners)])]
    dot_general x16 -> x24, matrix products: 18.1 us -> 21.4 us  [second_half(): term = jnp.dot(array, part, preferred_element_type=jnp.float32)]
    ppermute x7, starting transfers between devices: 12.5 us -> 15.2 us  [on_device(): got.append(lax.ppermute(sends[n], 'pair', target))]
    ppermute x7 -> x10, waiting for transfers between devices: 33 us -> 30.7 us  [along(): lax.ppermute(array, 'pair', [(p, (p // 2 + 1) % outer * 2 + p % 2) for p...]
    all_to_all x1, starting transfers between devices: 5.65 us -> 3.52 us  [on_device(): lax.all_to_all(send, 'pair', split_axis=0, concat_axis=0, tiled=True)]
  transfers between devices with their start and end apart: 28 -> 35, of which waited for: 15 -> 14; matrix products, arithmetic and copies ran while one was open for 15% -> 17% of each run, Pallas kernels for 2% -> 3%
where the time goes in v5:
time: 136 us
  waiting for transfers between devices  55.2 us (41%)
  starting transfers between devices  47 us (35%)
  matrix products  21.4 us (16%)
  Pallas kernels  9.58 us (7%)
  local copies, waits for them, and re-layouts  2 us (1%)
    ppermute x10, waiting for transfers between devices, along(): lax.ppermute(array, 'pair', [(p, (p // 2 + 1) % outer * 2 + p % 2) for p...  30.7 us
    dot_general x24, matrix products, second_half(): term = jnp.dot(array, part, preferred_element_type=jnp.float32)  21.4 us
    ppermute x7, starting transfers between devices, on_device(): got.append(lax.ppermute(sends[n], 'pair', target))  15.2 us
    ppermute x10, starting transfers between devices, along(): lax.ppermute(array, 'pair', [(p, (p // 2 + 1) % outer * 2 + p % 2) for p...  14.4 us
    ppermute x11, waiting for transfers between devices, swap(): return lax.ppermute(array, 'pair', [(p, p ^ 1) for p in range(owners)])  12.5 us
    ppermute x11, starting transfers between devices, swap(): return lax.ppermute(array, 'pair', [(p, p ^ 1) for p in range(owners)])  9.34 us
    ppermute x7, waiting for transfers between devices, on_device(): got.append(lax.ppermute(sends[n], 'pair', target))  6.62 us
    ppermute x6, waiting for transfers between devices, across(): return lax.ppermute(array, 'occ', [(o, o ^ j) for o in range(occ)])  5.39 us
  transfers between devices with their start and end apart: 35, of which 14 were waited for; matrix products, arithmetic and copies ran while one was open for 17% of the time, Pallas kernels for 3%

profile of v5, /device:TPU:0, one launch (start us, length us, event | category | flops | bytes accessed | tf_op | source)
XLA Modules:
  0.0 135.8 jit_solution(12869192995934963762)
XLA Ops:
  0.0 3.5 %pack_live.1 = (bf16[272,128]{1,0:T(8,128)(2,1)}, bf16[272,128]{1,0:T(8,128)(2,1)}, bf16[272,128]{1,0:T(8,128)(2,1)}, bf16[272,128]{1,0:T(8,128)(2,1)}, bf16[272...) custom-call(s32[1]{0:T(128)} %bitcast.1.here_ref, ...), custom_call_target="tpu_custom_call" | custom-call | tf_op jit(solution)/shard_map/pack_live/pallas_call | solution.py:69
  3.5 3.0 %collective-permute-start = (bf16[272,128]{1,0:T(8,128)(2,1)}, bf16[272,128]{1,0:T(8,128)(2,1)S(1)}, u32[]{:S(2)}, u32[]{:S(2)}) collective-permute-start(bf16[272,128]{1,0:T(8,128)(2,1)} %get-tuple-element.24), channel_id=1, source_target_pairs={{0,4},{4,0},{8,12},{12,8},{16,20},{20,16},{24,28},{28,24},{1,5},{5... | collective-permute-start | bytes 208904 | tf_op jit(solution)/shard_map/ppermute | solution.py:260
  6.6 1.6 %collective-permute-start.1 = (bf16[272,128]{1,0:T(8,128)(2,1)}, bf16[272,128]{1,0:T(8,128)(2,1)S(1)}, u32[]{:S(2)}, u32[]{:S(2)}) collective-permute-start(bf16[272,128]{1,0:T(8,128)(2,1)} %get-tuple-element.25), channel_id=1, source_target_pairs={{0,8},{4,12},{8,16},{12,20},{16,24},{20,28},{24,0},{28,4},{1,9},{5... | collective-permute-start | bytes 208904 | tf_op jit(solution)/shard_map/ppermute | solution.py:260
  8.2 1.5 %collective-permute-start.2 = (bf16[272,128]{1,0:T(8,128)(2,1)}, bf16[272,128]{1,0:T(8,128)(2,1)S(1)}, u32[]{:S(2)}, u32[]{:S(2)}) collective-permute-start(bf16[272,128]{1,0:T(8,128)(2,1)} %get-tuple-element.26), channel_id=1, source_target_pairs={{0,12},{4,8},{8,20},{12,16},{16,28},{20,24},{24,4},{28,0},{1,13},{... | collective-permute-start | bytes 208904 | tf_op jit(solution)/shard_map/ppermute | solution.py:260
  9.7 1.0 collective-permute-start.3
  10.8 2.8 %collective-permute-start.4 = (bf16[272,128]{1,0:T(8,128)(2,1)}, bf16[272,128]{1,0:T(8,128)(2,1)S(1)}, u32[]{:S(2)}, u32[]{:S(2)}) collective-permute-start(bf16[272,128]{1,0:T(8,128)(2,1)} %get-tuple-element.28), channel_id=1, source_target_pairs={{0,20},{4,16},{8,28},{12,24},{16,4},{20,0},{24,12},{28,8},{1,21},{... | collective-permute-start | bytes 208904 | tf_op jit(solution)/shard_map/ppermute | solution.py:260
  13.6 3.5 %all-to-all-start = ((bf16[8,256,128]{2,1,0:T(8,128)(2,1)}), bf16[8,256,128]{2,1,0:T(8,128)(2,1)S(1)}, u32[]{:S(2)}, u32[]{:S(2)}) async-start(bf16[8,256,128]{2,1,0:T(8,128)(2,1)} %get-tuple-element.36), calls=%async_computation | async-start | bytes 1048576 | tf_op jit(solution)/shard_map/all_to_all | solution.py:263
  17.2 1.9 %copy.6 = bf16[48,128,128]{1,2,0:T(8,128)(2,1)S(1)} copy(bf16[48,128,128]{2,1,0:T(8,128)(2,1)} %bitcast.34) | data formatting | bytes 3145728 | tf_op jit(solution)/shard_map/reshape | solution.py:265
  19.2 3.8 %collective-permute-start.5 = (bf16[272,128]{1,0:T(8,128)(2,1)}, bf16[272,128]{1,0:T(8,128)(2,1)S(1)}, u32[]{:S(2)}, u32[]{:S(2)}) collective-permute-start(bf16[272,128]{1,0:T(8,128)(2,1)} %get-tuple-element.29), channel_id=1, source_target_pairs={{0,24},{4,28},{8,0},{12,4},{16,8},{20,12},{24,16},{28,20},{1,25},{... | collective-permute-start | bytes 208904 | tf_op jit(solution)/shard_map/ppermute | solution.py:260
  22.9 1.5 %collective-permute-start.6 = (bf16[272,128]{1,0:T(8,128)(2,1)}, bf16[272,128]{1,0:T(8,128)(2,1)S(1)}, u32[]{:S(2)}, u32[]{:S(2)}) collective-permute-start(bf16[272,128]{1,0:T(8,128)(2,1)} %get-tuple-element.30), channel_id=1, source_target_pairs={{0,28},{4,24},{8,4},{12,0},{16,12},{20,8},{24,20},{28,16},{1,29},{... | collective-permute-start | bytes 208904 | tf_op jit(solution)/shard_map/ppermute | solution.py:260
  24.5 4.7 %collective-permute-done.5.refs_7_ = bf16[272,128]{1,0:T(8,128)(2,1)S(1)} collective-permute-done((bf16[272,128]{1,0:T(8,128)(2,1)}, bf16[272,128]{1,0:T(8,128)(2,1)S(1)}, u32[]{:S(2)}, u32[]{:S(2)}) %collective-permute-start.5) | collective-permute-done | bytes 69664 | tf_op jit(solution)/shard_map/ppermute | solution.py:260
  29.2 1.9 %collective-permute-done.6.refs_8_ = bf16[272,128]{1,0:T(8,128)(2,1)S(1)} collective-permute-done((bf16[272,128]{1,0:T(8,128)(2,1)}, bf16[272,128]{1,0:T(8,128)(2,1)S(1)}, u32[]{:S(2)}, u32[]{:S(2)}) %collective-permute-start.6) | collective-permute-done | bytes 69664 | tf_op jit(solution)/shard_map/ppermute | solution.py:260
  31.1 2.7 %half_transform.2 = (bf16[64,768]{1,0:T(8,128)(2,1)S(1)}, bf16[64,768]{1,0:T(8,128)(2,1)S(1)}, bf16[64,768]{1,0:T(8,128)(2,1)S(1)}, bf16[64,768]{1,0:T(8,128)(2,1)S(1)}, s32[8,128]{1,0:T(8,128)S(1)}) custom-call(s32[2]{0:T(128)S(1)} %pad_add_fusion.place_ref, bf16[48,128,128]{2,1,0:T(8,128)(2,1)S(1)} %bitcast.29, ...), custom_call_target="tpu_custom_call" | custom-call | flops 67108864 | bytes 2523136 | tf_op jit(solution)/shard_map/half_transform/pallas_call | solution.py:146
  33.8 1.6 %collective-permute-start.15 = (bf16[64,768]{1,0:T(8,128)(2,1)S(1)}, bf16[64,768]{1,0:T(8,128)(2,1)S(1)}, u32[]{:S(2)}, u32[]{:S(2)}) collective-permute-start(bf16[64,768]{1,0:T(8,128)(2,1)S(1)} %get-tuple-element.33), channel_id=1, source_target_pairs={{0,2},{1,3},{2,0},{3,1},{4,6},{5,7},{6,4},{7,5},{8,10},{9,11},{10,... | collective-permute-start | bytes 294920 | tf_op jit(solution)/shard_map/ppermute | solution.py:226
  36.0 0.9 collective-permute-done.7
  37.3 5.1 %collective-permute-start.9 = (bf16[128,768]{1,0:T(8,128)(2,1)S(1)}, bf16[128,768]{1,0:T(8,128)(2,1)S(1)}, u32[]{:S(2)}, u32[]{:S(2)}) collective-permute-start(bf16[128,768]{1,0:T(8,128)(2,1)S(1)} %constant_dynamic-update-slice_fusion), channel_id=1, source_target_pairs={{0,8},{4,12},{8,16},{12,20},{16,24},{20,28},{24,0},{28,4},{1,9},{5... | collective-permute-start | bytes 589832 | tf_op jit(solution)/shard_map/ppermute | solution.py:229
  42.4 4.4 %collective-permute-done.9 = bf16[128,768]{1,0:T(8,128)(2,1)S(1)} collective-permute-done((bf16[128,768]{1,0:T(8,128)(2,1)S(1)}, bf16[128,768]{1,0:T(8,128)(2,1)S(1)}, u32[]{:S(2)}, u32[]{:S(2)}) %collective-permute-start.9) | collective-permute-done | bytes 196640 | tf_op jit(solution)/shard_map/ppermute | solution.py:229
  46.8 2.5 %collective-permute-start.11 = (bf16[128,768]{1,0:T(8,128)(2,1)S(1)}, bf16[128,768]{1,0:T(8,128)(2,1)S(1)}, u32[]{:S(2)}, u32[]{:S(2)}) collective-permute-start(bf16[128,768]{1,0:T(8,128)(2,1)S(1)} %collective-permute-done.9), channel_id=1, source_target_pairs={{0,8},{4,12},{8,16},{12,20},{16,24},{20,28},{24,0},{28,4},{1,9},{5... | collective-permute-start | bytes 589832 | tf_op jit(solution)/shard_map/ppermute | solution.py:229
  50.0 1.5 %fusion.34 = f32[128,640]{1,0:T(8,128)S(1)} fusion(bf16[128,768]{1,0:T(8,128)(2,1)S(1)} %collective-permute-done.9, bf16[6144,640]{1,0:T(8,128)(2,1)} %param.7, s32[]{:T(128)S(6)} %select_n.182), kind=kOutput, calls=%fused_computation.46 | convolution fusion | flops 125829120 | bytes 1507332 | tf_op jit(solution)/shard_map/dot_general | solution.py:252
  51.6 1.5 %fusion.40 = f32[128,640]{1,0:T(8,128)S(1)} fusion(bf16[128,768]{1,0:T(8,128)(2,1)S(1)} %collective-permute-done.8, bf16[6144,640]{1,0:T(8,128)(2,1)} %param.7, s32[]{:T(128)S(6)} %select_n.180), kind=kOutput, calls=%fused_computation.52 | convolution fusion | flops 125829120 | bytes 1507332 | tf_op jit(solution)/shard_map/dot_general | solution.py:252
  53.1 1.6 %fusion.8 = f32[128,640]{1,0:T(8,128)S(1)} fusion(f32[128,640]{1,0:T(8,128)S(1)} %fusion.34, f32[128,640]{1,0:T(8,128)S(1)} %fusion.40, bf16[128,768]{1,0:T(8,128)(2,1)S(1)} %constant_dynamic-update-slice_fusion, bf16[6144,640]{1,0:T(8,128)(2,1)} %param.7, s32[]{:T(128)S(6)} %select_n.179), kind=kOutput, calls=%fused_computation.20 | convolution fusion | flops 125992960 | bytes 2162692 | tf_op jit(solution)/shard_map/dot_general | solution.py:252
  55.4 0.9 collective-permute-start.12
  57.0 5.2 %collective-permute-done.13 = bf16[128,768]{1,0:T(8,128)(2,1)S(1)} collective-permute-done((bf16[128,768]{1,0:T(8,128)(2,1)S(1)}, bf16[128,768]{1,0:T(8,128)(2,1)S(1)}, u32[]{:S(2)}, u32[]{:S(2)}) %collective-permute-start.13) | collective-permute-done | bytes 196640 | tf_op jit(solution)/shard_map/ppermute | solution.py:229
  62.2 1.3 collective-permute-start.14
  64.2 1.8 %half_transform.3 = (bf16[64,768]{1,0:T(8,128)(2,1)S(1)}, bf16[64,768]{1,0:T(8,128)(2,1)S(1)}, bf16[64,768]{1,0:T(8,128)(2,1)S(1)}, bf16[64,768]{1,0:T(8,128)(2,1)S(1)}) custom-call(s32[2]{0:T(128)S(1)} %pad_add_fusion.place_ref, s32[8,128]{1,0:T(8,128)S(1)} %get-tuple-element.35.refs_0_, bf16[48,128,128]{2,1,0:T(8,128)(2,1)S(1)} %bitcast.30, ...), custom_call_target="tpu_custom_call" | custom-call | flops 67108864 | bytes 2490368 | tf_op jit(solution)/shard_map/half_transform/pallas_call | solution.py:146
  66.0 1.6 %collective-permute-start.25 = (bf16[64,768]{1,0:T(8,128)(2,1)S(1)}, bf16[64,768]{1,0:T(8,128)(2,1)S(1)}, u32[]{:S(2)}, u32[]{:S(2)}) collective-permute-start(bf16[64,768]{1,0:T(8,128)(2,1)S(1)} %get-tuple-element.39), channel_id=1, source_target_pairs={{0,2},{1,3},{2,0},{3,1},{4,6},{5,7},{6,4},{7,5},{8,10},{9,11},{10,... | collective-permute-start | bytes 294920 | tf_op jit(solution)/shard_map/ppermute | solution.py:226
  68.2 2.6 %collective-permute-done.25 = bf16[64,768]{1,0:T(8,128)(2,1)S(1)} collective-permute-done((bf16[64,768]{1,0:T(8,128)(2,1)S(1)}, bf16[64,768]{1,0:T(8,128)(2,1)S(1)}, u32[]{:S(2)}, u32[]{:S(2)}) %collective-permute-start.25) | collective-permute-done | bytes 98336 | tf_op jit(solution)/shard_map/ppermute | solution.py:226
  70.8 1.9 %collective-permute-done.26 = bf16[64,768]{1,0:T(8,128)(2,1)S(1)} collective-permute-done((bf16[64,768]{1,0:T(8,128)(2,1)S(1)}, bf16[64,768]{1,0:T(8,128)(2,1)S(1)}, u32[]{:S(2)}, u32[]{:S(2)}) %collective-permute-start.26) | collective-permute-done | bytes 98336 | tf_op jit(solution)/shard_map/ppermute | solution.py:226
  72.7 1.5 %convolution_add_fusion.8.refs_0_ = f32[128,640]{1,0:T(8,128)S(1)} fusion(f32[128,640]{1,0:T(8,128)S(1)} %fusion.6, bf16[128,768]{1,0:T(8,128)(2,1)S(1)} %collective-permute-done.14, bf16[6144,640]{1,0:T(8,128)(2,1)} %param.7, s32[]{:T(128)S(6)} %select_n.189), kind=kOutput, calls=%fused_computation.14 | convolution fusion | flops 125911040 | bytes 1835012 | tf_op jit(solution)/shard_map/dot_general | solution.py:252
  74.3 0.8 collective-permute-start.27
  75.1 1.4 %collective-permute-start.18 = (bf16[256,768]{1,0:T(8,128)(2,1)S(1)}, bf16[256,768]{1,0:T(8,128)(2,1)S(1)}, u32[]{:S(2)}, u32[]{:S(2)}) collective-permute-start(bf16[256,768]{1,0:T(8,128)(2,1)S(1)} %constant_dynamic-update-slice_fusion.2), channel_id=1, source_target_pairs={{0,4},{4,0},{8,12},{12,8},{16,20},{20,16},{24,28},{28,24},{1,5},{5... | collective-permute-start | bytes 1179656 | tf_op jit(solution)/shard_map/ppermute | solution.py:234
  76.9 5.3 %collective-permute-done.28 = bf16[128,768]{1,0:T(8,128)(2,1)S(1)} collective-permute-done((bf16[128,768]{1,0:T(8,128)(2,1)S(1)}, bf16[128,768]{1,0:T(8,128)(2,1)S(1)}, u32[]{:S(2)}, u32[]{:S(2)}) %collective-permute-start.28) | collective-permute-done | bytes 196640 | tf_op jit(solution)/shard_map/ppermute | solution.py:229
  83.0 1.5 %fusion.30 = f32[128,640]{1,0:T(8,128)S(1)} fusion(bf16[128,768]{1,0:T(8,128)(2,1)S(1)} %collective-permute-done.28, bf16[6144,640]{1,0:T(8,128)(2,1)} %param.7, s32[]{:T(128)S(6)} %select_n.182), kind=kOutput, calls=%fused_computation.42 | convolution fusion | flops 125829120 | bytes 1507332 | tf_op jit(solution)/shard_map/dot_general | solution.py:252
  84.6 1.5 %fusion.36 = f32[128,640]{1,0:T(8,128)S(1)} fusion(bf16[128,768]{1,0:T(8,128)(2,1)S(1)} %collective-permute-done.27, bf16[6144,640]{1,0:T(8,128)(2,1)} %param.7, s32[]{:T(128)S(6)} %select_n.180), kind=kOutput, calls=%fused_computation.48 | convolution fusion | flops 125829120 | bytes 1507332 | tf_op jit(solution)/shard_map/dot_general | solution.py:252
  86.1 1.7 %fusion.5 = f32[128,640]{1,0:T(8,128)S(1)} fusion(f32[128,640]{1,0:T(8,128)S(1)} %fusion.30, f32[128,640]{1,0:T(8,128)S(1)} %fusion.36, bf16[128,768]{1,0:T(8,128)(2,1)S(1)} %constant_dynamic-update-slice_fusion.6, bf16[6144,640]{1,0:T(8,128)(2,1)} %param.7, s32[]{:T(128)S(6)} %select_n.179), kind=kOutput, calls=%fused_computation.13 | convolution fusion | flops 125992960 | bytes 2162692 | tf_op jit(solution)/shard_map/dot_general | solution.py:252
  87.8 2.7 %collective-permute-done.18 = bf16[256,768]{1,0:T(8,128)(2,1)S(1)} collective-permute-done((bf16[256,768]{1,0:T(8,128)(2,1)S(1)}, bf16[256,768]{1,0:T(8,128)(2,1)S(1)}, u32[]{:S(2)}, u32[]{:S(2)}) %collective-permute-start.18) | collective-permute-done | bytes 393248 | tf_op jit(solution)/shard_map/ppermute | solution.py:234
  90.6 1.7 %fusion.38 = f32[256,640]{1,0:T(8,128)S(1)} fusion(bf16[256,768]{1,0:T(8,128)(2,1)S(1)} %collective-permute-done.18, bf16[6144,640]{1,0:T(8,128)(2,1)} %param.7, s32[]{:T(128)S(6)} %select_n.180), kind=kOutput, calls=%fused_computation.50 | convolution fusion | flops 251658240 | bytes 2031620 | tf_op jit(solution)/shard_map/dot_general | solution.py:252
  92.3 1.7 %fusion.32 = f32[256,640]{1,0:T(8,128)S(1)} fusion(bf16[256,768]{1,0:T(8,128)(2,1)S(1)} %collective-permute-done.19, bf16[6144,640]{1,0:T(8,128)(2,1)} %param.7, s32[]{:T(128)S(6)} %select_n.182), kind=kOutput, calls=%fused_computation.44 | convolution fusion | flops 251658240 | bytes 2031620 | tf_op jit(solution)/shard_map/dot_general | solution.py:252
  94.0 1.7 %fusion.2 = f32[256,640]{1,0:T(8,128)S(1)} fusion(f32[256,640]{1,0:T(8,128)S(1)} %fusion.32, f32[256,640]{1,0:T(8,128)S(1)} %fusion.38, bf16[256,768]{1,0:T(8,128)(2,1)S(1)} %constant_dynamic-update-slice_fusion.2, bf16[6144,640]{1,0:T(8,128)(2,1)} %param.7, s32[]{:T(128)S(6)} %select_n.179), kind=kOutput, calls=%fused_computation.6 | convolution fusion | flops 251985920 | bytes 3342340 | tf_op jit(solution)/shard_map/dot_general | solution.py:252
  96.2 0.9 collective-permute-start.31
  97.1 3.4 %collective-permute-start.21 = (bf16[256,768]{1,0:T(8,128)(2,1)S(1)}, bf16[256,768]{1,0:T(8,128)(2,1)S(1)}, u32[]{:S(2)}, u32[]{:S(2)}) collective-permute-start(bf16[256,768]{1,0:T(8,128)(2,1)S(1)} %collective-permute-done.19), channel_id=1, source_target_pairs={{0,8},{4,12},{8,16},{12,20},{16,24},{20,28},{24,0},{28,4},{1,9},{5... | collective-permute-start | bytes 1179656 | tf_op jit(solution)/shard_map/ppermute | solution.py:229
  102.0 3.3 %collective-permute-done.32 = bf16[128,768]{1,0:T(8,128)(2,1)S(1)} collective-permute-done((bf16[128,768]{1,0:T(8,128)(2,1)S(1)}, bf16[128,768]{1,0:T(8,128)(2,1)S(1)}, u32[]{:S(2)}, u32[]{:S(2)}) %collective-permute-start.32) | collective-permute-done | bytes 196640 | tf_op jit(solution)/shard_map/ppermute | solution.py:229
  106.7 4.4 %collective-permute-done.21 = bf16[256,768]{1,0:T(8,128)(2,1)S(1)} collective-permute-done((bf16[256,768]{1,0:T(8,128)(2,1)S(1)}, bf16[256,768]{1,0:T(8,128)(2,1)S(1)}, u32[]{:S(2)}, u32[]{:S(2)}) %collective-permute-start.21) | collective-permute-done | bytes 393248 | tf_op jit(solution)/shard_map/ppermute | solution.py:229
  112.4 4.4 %collective-permute-done.33 = bf16[128,768]{1,0:T(8,128)(2,1)S(1)} collective-permute-done((bf16[128,768]{1,0:T(8,128)(2,1)S(1)}, bf16[128,768]{1,0:T(8,128)(2,1)S(1)}, u32[]{:S(2)}, u32[]{:S(2)}) %collective-permute-start.33) | collective-permute-done | bytes 196640 | tf_op jit(solution)/shard_map/ppermute | solution.py:234
  117.6 5.4 %collective-permute-done.22 = bf16[256,768]{1,0:T(8,128)(2,1)S(1)} collective-permute-done((bf16[256,768]{1,0:T(8,128)(2,1)S(1)}, bf16[256,768]{1,0:T(8,128)(2,1)S(1)}, u32[]{:S(2)}, u32[]{:S(2)}) %collective-permute-start.22) | collective-permute-done | bytes 393248 | tf_op jit(solution)/shard_map/ppermute | solution.py:234
  122.9 1.7 %collective-permute-start.24 = (bf16[256,768]{1,0:T(8,128)(2,1)S(1)}, bf16[256,768]{1,0:T(8,128)(2,1)S(1)}, u32[]{:S(2)}, u32[]{:S(2)}) collective-permute-start(bf16[256,768]{1,0:T(8,128)(2,1)S(1)} %collective-permute-done.22), channel_id=1, source_target_pairs={{0,8},{4,12},{8,16},{12,20},{16,24},{20,28},{24,0},{28,4},{1,9},{5... | collective-permute-start | bytes 1179656 | tf_op jit(solution)/shard_map/ppermute | solution.py:229
  125.6 8.0 %collective-permute-done.24 = bf16[256,768]{1,0:T(8,128)(2,1)S(1)} collective-permute-done((bf16[256,768]{1,0:T(8,128)(2,1)S(1)}, bf16[256,768]{1,0:T(8,128)(2,1)S(1)}, u32[]{:S(2)}, u32[]{:S(2)}) %collective-permute-start.24) | collective-permute-done | bytes 393248 | tf_op jit(solution)/shard_map/ppermute | solution.py:229
  134.1 1.6 %place.1 = bf16[32,16,640]{2,1,0:T(8,128)(2,1)} custom-call(s32[1]{0:T(128)} %bitcast.me_ref, f32[128,640]{1,0:T(8,128)S(1)} %convolution_add_fusion.8.refs_0_, f32[256,640]{1,0:T(8,128)S(1)} %convolution_add_fusion.refs_1_, f32[128,640]{1,0:T(8,128)S(1)} %convolution_add_fusion.4.refs_2_), custom_call_target="tpu_custom_call" | custom-call | tf_op jit(solution)/shard_map/place/pallas_call | solution.py:187
  (67 shorter events, 12.7 us)
Async XLA Ops:
  3.5 15.6 %collective-permute-start = (bf16[272,128]{1,0:T(8,128)(2,1)}, bf16[272,128]{1,0:T(8,128)(2,1)S(1)}, u32[]{:S(2)}, u32[]{:S(2)}) collective-permute-start(bf16[272,128]{1,0:T(8,128)(2,1)} %get-tuple-element.24), channel_id=1, source_target_pairs={{0,4},{4,0},{8,12},{12,8},{16,20},{20,16},{24,28},{28,24},{1,5},{5... | collective-permute-start | bytes 208904 | tf_op jit(solution)/shard_map/ppermute | solution.py:260
  6.6 16.4 %collective-permute-start.1 = (bf16[272,128]{1,0:T(8,128)(2,1)}, bf16[272,128]{1,0:T(8,128)(2,1)S(1)}, u32[]{:S(2)}, u32[]{:S(2)}) collective-permute-start(bf16[272,128]{1,0:T(8,128)(2,1)} %get-tuple-element.25), channel_id=1, source_target_pairs={{0,8},{4,12},{8,16},{12,20},{16,24},{20,28},{24,0},{28,4},{1,9},{5... | collective-permute-start | bytes 208904 | tf_op jit(solution)/shard_map/ppermute | solution.py:260
  8.2 16.3 %collective-permute-start.2 = (bf16[272,128]{1,0:T(8,128)(2,1)}, bf16[272,128]{1,0:T(8,128)(2,1)S(1)}, u32[]{:S(2)}, u32[]{:S(2)}) collective-permute-start(bf16[272,128]{1,0:T(8,128)(2,1)} %get-tuple-element.26), channel_id=1, source_target_pairs={{0,12},{4,8},{8,20},{12,16},{16,28},{20,24},{24,4},{28,0},{1,13},{... | collective-permute-start | bytes 208904 | tf_op jit(solution)/shard_map/ppermute | solution.py:260
  9.7 14.8 %collective-permute-start.3 = (bf16[272,128]{1,0:T(8,128)(2,1)}, bf16[272,128]{1,0:T(8,128)(2,1)S(1)}, u32[]{:S(2)}, u32[]{:S(2)}) collective-permute-start(bf16[272,128]{1,0:T(8,128)(2,1)} %get-tuple-element.27), channel_id=1, source_target_pairs={{0,16},{4,20},{8,24},{12,28},{16,0},{20,4},{24,8},{28,12},{1,17},{... | collective-permute-start | bytes 208904 | tf_op jit(solution)/shard_map/ppermute | solution.py:260
  10.8 13.7 %collective-permute-start.4 = (bf16[272,128]{1,0:T(8,128)(2,1)}, bf16[272,128]{1,0:T(8,128)(2,1)S(1)}, u32[]{:S(2)}, u32[]{:S(2)}) collective-permute-start(bf16[272,128]{1,0:T(8,128)(2,1)} %get-tuple-element.28), channel_id=1, source_target_pairs={{0,20},{4,16},{8,28},{12,24},{16,4},{20,0},{24,12},{28,8},{1,21},{... | collective-permute-start | bytes 208904 | tf_op jit(solution)/shard_map/ppermute | solution.py:260
  13.6 50.6 %all-to-all-start = ((bf16[8,256,128]{2,1,0:T(8,128)(2,1)}), bf16[8,256,128]{2,1,0:T(8,128)(2,1)S(1)}, u32[]{:S(2)}, u32[]{:S(2)}) async-start(bf16[8,256,128]{2,1,0:T(8,128)(2,1)} %get-tuple-element.36), calls=%async_computation | async-start | bytes 1048576 | tf_op jit(solution)/shard_map/all_to_all | solution.py:263
  19.2 37.1 %copy-start = (bf16[6144,640]{1,0:T(8,128)(2,1)S(1)}, bf16[6144,640]{1,0:T(8,128)(2,1)}, u32[]{:S(2)}) copy-start(bf16[6144,640]{1,0:T(8,128)(2,1)} %param.7) | copy-start | bytes 23592964
  19.2 10.0 %collective-permute-start.5 = (bf16[272,128]{1,0:T(8,128)(2,1)}, bf16[272,128]{1,0:T(8,128)(2,1)S(1)}, u32[]{:S(2)}, u32[]{:S(2)}) collective-permute-start(bf16[272,128]{1,0:T(8,128)(2,1)} %get-tuple-element.29), channel_id=1, source_target_pairs={{0,24},{4,28},{8,0},{12,4},{16,8},{20,12},{24,16},{28,20},{1,25},{... | collective-permute-start | bytes 208904 | tf_op jit(solution)/shard_map/ppermute | solution.py:260
  22.9 8.2 %collective-permute-start.6 = (bf16[272,128]{1,0:T(8,128)(2,1)}, bf16[272,128]{1,0:T(8,128)(2,1)S(1)}, u32[]{:S(2)}, u32[]{:S(2)}) collective-permute-start(bf16[272,128]{1,0:T(8,128)(2,1)} %get-tuple-element.30), channel_id=1, source_target_pairs={{0,28},{4,24},{8,4},{12,0},{16,12},{20,8},{24,20},{28,16},{1,29},{... | collective-permute-start | bytes 208904 | tf_op jit(solution)/shard_map/ppermute | solution.py:260
  33.8 8.6 %collective-permute-start.15 = (bf16[64,768]{1,0:T(8,128)(2,1)S(1)}, bf16[64,768]{1,0:T(8,128)(2,1)S(1)}, u32[]{:S(2)}, u32[]{:S(2)}) collective-permute-start(bf16[64,768]{1,0:T(8,128)(2,1)S(1)} %get-tuple-element.33), channel_id=1, source_target_pairs={{0,2},{1,3},{2,0},{3,1},{4,6},{5,7},{6,4},{7,5},{8,10},{9,11},{10,... | collective-permute-start | bytes 294920 | tf_op jit(solution)/shard_map/ppermute | solution.py:226
  35.4 7.0 %collective-permute-start.16 = (bf16[64,768]{1,0:T(8,128)(2,1)S(1)}, bf16[64,768]{1,0:T(8,128)(2,1)S(1)}, u32[]{:S(2)}, u32[]{:S(2)}) collective-permute-start(bf16[64,768]{1,0:T(8,128)(2,1)S(1)} %get-tuple-element.34), channel_id=1, source_target_pairs={{0,3},{1,2},{2,1},{3,0},{4,7},{5,6},{6,5},{7,4},{8,11},{9,10},{10,... | collective-permute-start | bytes 294920 | tf_op jit(solution)/shard_map/ppermute | solution.py:226
  35.4 1.6 %collective-permute-start.7 = (bf16[64,768]{1,0:T(8,128)(2,1)S(1)}, bf16[64,768]{1,0:T(8,128)(2,1)S(1)}, u32[]{:S(2)}, u32[]{:S(2)}) collective-permute-start(bf16[64,768]{1,0:T(8,128)(2,1)S(1)} %get-tuple-element.32), channel_id=1, source_target_pairs={{0,1},{1,0},{2,3},{3,2},{4,5},{5,4},{6,7},{7,6},{8,9},{9,8},{10,11... | collective-permute-start | bytes 294920 | tf_op jit(solution)/shard_map/ppermute | solution.py:226
  36.9 14.6 %collective-permute-start.8 = (bf16[128,768]{1,0:T(8,128)(2,1)S(1)}, bf16[128,768]{1,0:T(8,128)(2,1)S(1)}, u32[]{:S(2)}, u32[]{:S(2)}) collective-permute-start(bf16[128,768]{1,0:T(8,128)(2,1)S(1)} %constant_dynamic-update-slice_fusion), channel_id=1, source_target_pairs={{0,4},{4,0},{8,12},{12,8},{16,20},{20,16},{24,28},{28,24},{1,5},{5... | collective-permute-start | bytes 589832 | tf_op jit(solution)/shard_map/ppermute | solution.py:234
  37.3 9.5 %collective-permute-start.9 = (bf16[128,768]{1,0:T(8,128)(2,1)S(1)}, bf16[128,768]{1,0:T(8,128)(2,1)S(1)}, u32[]{:S(2)}, u32[]{:S(2)}) collective-permute-start(bf16[128,768]{1,0:T(8,128)(2,1)S(1)} %constant_dynamic-update-slice_fusion), channel_id=1, source_target_pairs={{0,8},{4,12},{8,16},{12,20},{16,24},{20,28},{24,0},{28,4},{1,9},{5... | collective-permute-start | bytes 589832 | tf_op jit(solution)/shard_map/ppermute | solution.py:229
  46.8 7.9 %collective-permute-start.11 = (bf16[128,768]{1,0:T(8,128)(2,1)S(1)}, bf16[128,768]{1,0:T(8,128)(2,1)S(1)}, u32[]{:S(2)}, u32[]{:S(2)}) collective-permute-start(bf16[128,768]{1,0:T(8,128)(2,1)S(1)} %collective-permute-done.9), channel_id=1, source_target_pairs={{0,8},{4,12},{8,16},{12,20},{16,24},{20,28},{24,0},{28,4},{1,9},{5... | collective-permute-start | bytes 589832 | tf_op jit(solution)/shard_map/ppermute | solution.py:229
  49.3 7.4 %collective-permute-start.10 = (bf16[128,768]{1,0:T(8,128)(2,1)S(1)}, bf16[128,768]{1,0:T(8,128)(2,1)S(1)}, u32[]{:S(2)}, u32[]{:S(2)}) collective-permute-start(bf16[128,768]{1,0:T(8,128)(2,1)S(1)} %collective-permute-done.9), channel_id=1, source_target_pairs={{0,4},{4,0},{8,12},{12,8},{16,20},{20,16},{24,28},{28,24},{1,5},{5... | collective-permute-start | bytes 589832 | tf_op jit(solution)/shard_map/ppermute | solution.py:234
  54.7 7.5 %collective-permute-start.13 = (bf16[128,768]{1,0:T(8,128)(2,1)S(1)}, bf16[128,768]{1,0:T(8,128)(2,1)S(1)}, u32[]{:S(2)}, u32[]{:S(2)}) collective-permute-start(bf16[128,768]{1,0:T(8,128)(2,1)S(1)} %collective-permute-done.11), channel_id=1, source_target_pairs={{0,8},{4,12},{8,16},{12,20},{16,24},{20,28},{24,0},{28,4},{1,9},{5... | collective-permute-start | bytes 589832 | tf_op jit(solution)/shard_map/ppermute | solution.py:229
  55.4 8.5 %collective-permute-start.12 = (bf16[128,768]{1,0:T(8,128)(2,1)S(1)}, bf16[128,768]{1,0:T(8,128)(2,1)S(1)}, u32[]{:S(2)}, u32[]{:S(2)}) collective-permute-start(bf16[128,768]{1,0:T(8,128)(2,1)S(1)} %collective-permute-done.11), channel_id=1, source_target_pairs={{0,4},{4,0},{8,12},{12,8},{16,20},{20,16},{24,28},{28,24},{1,5},{5... | collective-permute-start | bytes 589832 | tf_op jit(solution)/shard_map/ppermute | solution.py:234
  62.2 10.5 %collective-permute-start.14 = (bf16[128,768]{1,0:T(8,128)(2,1)S(1)}, bf16[128,768]{1,0:T(8,128)(2,1)S(1)}, u32[]{:S(2)}, u32[]{:S(2)}) collective-permute-start(bf16[128,768]{1,0:T(8,128)(2,1)S(1)} %collective-permute-done.13), channel_id=1, source_target_pairs={{0,4},{4,0},{8,12},{12,8},{16,20},{20,16},{24,28},{28,24},{1,5},{5... | collective-permute-start | bytes 589832 | tf_op jit(solution)/shard_map/ppermute | solution.py:234
  66.0 35.3 %slice-start = ((s8[7864320]{0:T(1024)(128)(4,1)}), s8[4194304]{0:T(1024)(128)(4,1)S(1)}, s32[]{:S(2)}) async-start(s8[7864320]{0:T(1024)(128)(4,1)} %bitcast.31), calls=%async_computation.1 | async-start | bytes 8388608
  66.0 4.8 %collective-permute-start.25 = (bf16[64,768]{1,0:T(8,128)(2,1)S(1)}, bf16[64,768]{1,0:T(8,128)(2,1)S(1)}, u32[]{:S(2)}, u32[]{:S(2)}) collective-permute-start(bf16[64,768]{1,0:T(8,128)(2,1)S(1)} %get-tuple-element.39), channel_id=1, source_target_pairs={{0,2},{1,3},{2,0},{3,1},{4,6},{5,7},{6,4},{7,5},{8,10},{9,11},{10,... | collective-permute-start | bytes 294920 | tf_op jit(solution)/shard_map/ppermute | solution.py:226
  67.6 5.1 %collective-permute-start.26 = (bf16[64,768]{1,0:T(8,128)(2,1)S(1)}, bf16[64,768]{1,0:T(8,128)(2,1)S(1)}, u32[]{:S(2)}, u32[]{:S(2)}) collective-permute-start(bf16[64,768]{1,0:T(8,128)(2,1)S(1)} %get-tuple-element.40), channel_id=1, source_target_pairs={{0,3},{1,2},{2,1},{3,0},{4,7},{5,6},{6,5},{7,4},{8,11},{9,10},{10,... | collective-permute-start | bytes 294920 | tf_op jit(solution)/shard_map/ppermute | solution.py:226
  67.6 7.5 %collective-permute-start.17 = (bf16[64,768]{1,0:T(8,128)(2,1)S(1)}, bf16[64,768]{1,0:T(8,128)(2,1)S(1)}, u32[]{:S(2)}, u32[]{:S(2)}) collective-permute-start(bf16[64,768]{1,0:T(8,128)(2,1)S(1)} %get-tuple-element.38), channel_id=1, source_target_pairs={{0,1},{1,0},{2,3},{3,2},{4,5},{5,4},{6,7},{7,6},{8,9},{9,8},{10,11... | collective-permute-start | bytes 294920 | tf_op jit(solution)/shard_map/ppermute | solution.py:226
  72.7 9.6 %collective-permute-start.28 = (bf16[128,768]{1,0:T(8,128)(2,1)S(1)}, bf16[128,768]{1,0:T(8,128)(2,1)S(1)}, u32[]{:S(2)}, u32[]{:S(2)}) collective-permute-start(bf16[128,768]{1,0:T(8,128)(2,1)S(1)} %constant_dynamic-update-slice_fusion.6), channel_id=1, source_target_pairs={{0,8},{4,12},{8,16},{12,20},{16,24},{20,28},{24,0},{28,4},{1,9},{5... | collective-permute-start | bytes 589832 | tf_op jit(solution)/shard_map/ppermute | solution.py:229
  74.3 10.3 %collective-permute-start.27 = (bf16[128,768]{1,0:T(8,128)(2,1)S(1)}, bf16[128,768]{1,0:T(8,128)(2,1)S(1)}, u32[]{:S(2)}, u32[]{:S(2)}) collective-permute-start(bf16[128,768]{1,0:T(8,128)(2,1)S(1)} %constant_dynamic-update-slice_fusion.6), channel_id=1, source_target_pairs={{0,4},{4,0},{8,12},{12,8},{16,20},{20,16},{24,28},{28,24},{1,5},{5... | collective-permute-start | bytes 589832 | tf_op jit(solution)/shard_map/ppermute | solution.py:234
  75.1 15.5 %collective-permute-start.18 = (bf16[256,768]{1,0:T(8,128)(2,1)S(1)}, bf16[256,768]{1,0:T(8,128)(2,1)S(1)}, u32[]{:S(2)}, u32[]{:S(2)}) collective-permute-start(bf16[256,768]{1,0:T(8,128)(2,1)S(1)} %constant_dynamic-update-slice_fusion.2), channel_id=1, source_target_pairs={{0,4},{4,0},{8,12},{12,8},{16,20},{20,16},{24,28},{28,24},{1,5},{5... | collective-permute-start | bytes 1179656 | tf_op jit(solution)/shard_map/ppermute | solution.py:234
  76.5 15.8 %collective-permute-start.19 = (bf16[256,768]{1,0:T(8,128)(2,1)S(1)}, bf16[256,768]{1,0:T(8,128)(2,1)S(1)}, u32[]{:S(2)}, u32[]{:S(2)}) collective-permute-start(bf16[256,768]{1,0:T(8,128)(2,1)S(1)} %constant_dynamic-update-slice_fusion.2), channel_id=1, source_target_pairs={{0,8},{4,12},{8,16},{12,20},{16,24},{20,28},{24,0},{28,4},{1,9},{5... | collective-permute-start | bytes 1179656 | tf_op jit(solution)/shard_map/ppermute | solution.py:229
  82.3 13.4 %collective-permute-start.30 = (bf16[128,768]{1,0:T(8,128)(2,1)S(1)}, bf16[128,768]{1,0:T(8,128)(2,1)S(1)}, u32[]{:S(2)}, u32[]{:S(2)}) collective-permute-start(bf16[128,768]{1,0:T(8,128)(2,1)S(1)} %collective-permute-done.28), channel_id=1, source_target_pairs={{0,8},{4,12},{8,16},{12,20},{16,24},{20,28},{24,0},{28,4},{1,9},{5... | collective-permute-start | bytes 589832 | tf_op jit(solution)/shard_map/ppermute | solution.py:229
  82.3 19.3 %collective-permute-start.29 = (bf16[128,768]{1,0:T(8,128)(2,1)S(1)}, bf16[128,768]{1,0:T(8,128)(2,1)S(1)}, u32[]{:S(2)}, u32[]{:S(2)}) collective-permute-start(bf16[128,768]{1,0:T(8,128)(2,1)S(1)} %collective-permute-done.28), channel_id=1, source_target_pairs={{0,4},{4,0},{8,12},{12,8},{16,20},{20,16},{24,28},{28,24},{1,5},{5... | collective-permute-start | bytes 589832 | tf_op jit(solution)/shard_map/ppermute | solution.py:234
  86.1 15.1 %slice-start.1 = ((s8[7864320]{0:T(1024)(128)(4,1)}), s8[3670016]{0:T(1024)(128)(4,1)S(1)}, s32[]{:S(2)}) async-start(s8[7864320]{0:T(1024)(128)(4,1)} %bitcast.31), calls=%async_computation.2 | async-start | bytes 7340032
  95.7 9.6 %collective-permute-start.32 = (bf16[128,768]{1,0:T(8,128)(2,1)S(1)}, bf16[128,768]{1,0:T(8,128)(2,1)S(1)}, u32[]{:S(2)}, u32[]{:S(2)}) collective-permute-start(bf16[128,768]{1,0:T(8,128)(2,1)S(1)} %collective-permute-done.30), channel_id=1, source_target_pairs={{0,8},{4,12},{8,16},{12,20},{16,24},{20,28},{24,0},{28,4},{1,9},{5... | collective-permute-start | bytes 589832 | tf_op jit(solution)/shard_map/ppermute | solution.py:229
  96.2 10.2 %collective-permute-start.31 = (bf16[128,768]{1,0:T(8,128)(2,1)S(1)}, bf16[128,768]{1,0:T(8,128)(2,1)S(1)}, u32[]{:S(2)}, u32[]{:S(2)}) collective-permute-start(bf16[128,768]{1,0:T(8,128)(2,1)S(1)} %collective-permute-done.30), channel_id=1, source_target_pairs={{0,4},{4,0},{8,12},{12,8},{16,20},{20,16},{24,28},{28,24},{1,5},{5... | collective-permute-start | bytes 589832 | tf_op jit(solution)/shard_map/ppermute | solution.py:234
  97.1 14.0 %collective-permute-start.21 = (bf16[256,768]{1,0:T(8,128)(2,1)S(1)}, bf16[256,768]{1,0:T(8,128)(2,1)S(1)}, u32[]{:S(2)}, u32[]{:S(2)}) collective-permute-start(bf16[256,768]{1,0:T(8,128)(2,1)S(1)} %collective-permute-done.19), channel_id=1, source_target_pairs={{0,8},{4,12},{8,16},{12,20},{16,24},{20,28},{24,0},{28,4},{1,9},{5... | collective-permute-start | bytes 1179656 | tf_op jit(solution)/shard_map/ppermute | solution.py:229
  100.5 16.5 %collective-permute-start.20 = (bf16[256,768]{1,0:T(8,128)(2,1)S(1)}, bf16[256,768]{1,0:T(8,128)(2,1)S(1)}, u32[]{:S(2)}, u32[]{:S(2)}) collective-permute-start(bf16[256,768]{1,0:T(8,128)(2,1)S(1)} %collective-permute-done.19), channel_id=1, source_target_pairs={{0,4},{4,0},{8,12},{12,8},{16,20},{20,16},{24,28},{28,24},{1,5},{5... | collective-permute-start | bytes 1179656 | tf_op jit(solution)/shard_map/ppermute | solution.py:234
  105.3 11.4 %collective-permute-start.33 = (bf16[128,768]{1,0:T(8,128)(2,1)S(1)}, bf16[128,768]{1,0:T(8,128)(2,1)S(1)}, u32[]{:S(2)}, u32[]{:S(2)}) collective-permute-start(bf16[128,768]{1,0:T(8,128)(2,1)S(1)} %collective-permute-done.32), channel_id=1, source_target_pairs={{0,4},{4,0},{8,12},{12,8},{16,20},{20,16},{24,28},{28,24},{1,5},{5... | collective-permute-start | bytes 589832 | tf_op jit(solution)/shard_map/ppermute | solution.py:234
  111.1 13.5 %collective-permute-start.23 = (bf16[256,768]{1,0:T(8,128)(2,1)S(1)}, bf16[256,768]{1,0:T(8,128)(2,1)S(1)}, u32[]{:S(2)}, u32[]{:S(2)}) collective-permute-start(bf16[256,768]{1,0:T(8,128)(2,1)S(1)} %collective-permute-done.21), channel_id=1, source_target_pairs={{0,8},{4,12},{8,16},{12,20},{16,24},{20,28},{24,0},{28,4},{1,9},{5... | collective-permute-start | bytes 1179656 | tf_op jit(solution)/shard_map/ppermute | solution.py:229
  111.1 11.8 %collective-permute-start.22 = (bf16[256,768]{1,0:T(8,128)(2,1)S(1)}, bf16[256,768]{1,0:T(8,128)(2,1)S(1)}, u32[]{:S(2)}, u32[]{:S(2)}) collective-permute-start(bf16[256,768]{1,0:T(8,128)(2,1)S(1)} %collective-permute-done.21), channel_id=1, source_target_pairs={{0,4},{4,0},{8,12},{12,8},{16,20},{20,16},{24,28},{28,24},{1,5},{5... | collective-permute-start | bytes 1179656 | tf_op jit(solution)/shard_map/ppermute | solution.py:234
  122.9 10.7 %collective-permute-start.24 = (bf16[256,768]{1,0:T(8,128)(2,1)S(1)}, bf16[256,768]{1,0:T(8,128)(2,1)S(1)}, u32[]{:S(2)}, u32[]{:S(2)}) collective-permute-start(bf16[256,768]{1,0:T(8,128)(2,1)S(1)} %collective-permute-done.22), channel_id=1, source_target_pairs={{0,8},{4,12},{8,16},{12,20},{16,24},{20,28},{24,0},{28,4},{1,9},{5... | collective-permute-start | bytes 1179656 | tf_op jit(solution)/shard_map/ppermute | solution.py:229

commit v6 on v5

--- a/solution.py
+++ b/solution.py
@@ -2,6 +2,7 @@
 
 import jax
 import jax.numpy as jnp
+import numpy as np
 from jax import lax
 from jax.experimental import pallas as pl
 from jax.experimental.pallas import tpu as pltpu
@@ -160,39 +161,68 @@
     return result[:occ], result[occ] if ids is None else ids
 
 
-def place_kernel(layout, aux, me_ref, *refs):
-    in_refs, (out_ref, wide) = refs[:-2], refs[-2:]
-    slab, all_aux, _ = out_ref.shape
-    chunks = 1 + max(c for parts in layout for c, _ in parts)
-    for in_ref, parts in zip(in_refs, layout):
-        for i, (c, j) in enumerate(parts):
-            for q in range(aux):
-                at = (me_ref[0] ^ j) * (chunks * aux) + c * aux + q
-                row = (i * aux + q) * slab
-                for t in range(wide.shape[0]):
-                    wide[t, pl.ds(at, slab, stride=all_aux), :] = in_ref[
-                        row : row + slab, t * 128 : (t + 1) * 128
-                    ]
-    for t in range(wide.shape[0]):
-        out_ref[:, :, t * 128 : (t + 1) * 128] = (
-            wide[t].reshape(slab, all_aux, 128).astype(out_ref.dtype)
-        )
-
-
-def place(me, sums, layout, slab):
+def place_kernel(order_ref, *refs):
+    in_refs, (out_ref, rounded) = refs[:-2], refs[-2:]
+    row = 0
+    for in_ref in in_refs:
+        rounded[row : row + in_ref.shape[0], :] = in_ref[...].astype(rounded.dtype)
+        row += in_ref.shape[0]
+    placed = jnp.dot(order_ref[...], rounded[...], preferred_element_type=jnp.float32)
+    out_ref[...] = placed.astype(out_ref.dtype).reshape(out_ref.shape)
+
+
+def place(order, sums, slab):
     columns = sums[0].shape[1]
-    rows = sum(total.shape[0] for total in sums)
-    aux = sums[0].shape[0] // len(layout[0]) // slab
+    rows = order.shape[0]
     vmem = pl.BlockSpec(memory_space=pltpu.VMEM)
     return pl.pallas_call(
-        functools.partial(place_kernel, layout, aux),
+        place_kernel,
         out_shape=jax.ShapeDtypeStruct((slab, rows // slab, columns), jnp.bfloat16),
-        in_specs=[pl.BlockSpec(memory_space=pltpu.SMEM)] + [vmem] * len(sums),
+        in_specs=[vmem] * (1 + len(sums)),
         out_specs=vmem,
-        scratch_shapes=[pltpu.VMEM((columns // 128, rows, 128), jnp.float32)],
+        scratch_shapes=[pltpu.VMEM((rows, columns), jnp.bfloat16)],
         compiler_params=pltpu.CompilerParams(vmem_limit_bytes=GRANT),
         name="place",
-    )(me, *sums)
+    )(order, *sums)
+
+
+def target_rows(me, layout, occ, chunks, aux, slab):
+    names = [(c, j, q, i) for parts in layout for c, j in parts for q in range(aux) for i in range(slab)]
+    c, j, q, i = (np.array(column, np.int32) for column in zip(*names))
+    return (i * (occ * chunks * aux) + (j ^ me) * (chunks * aux) + c * aux + q).reshape(1, -1)
+
+
+def stage_kernel(in_ref, target_ref, out_ref, order_ref, sems):
+    rows = out_ref.shape[0] // sems.shape[0]
+    copies = [
+        pltpu.make_async_copy(
+            in_ref.at[pl.ds(i * rows, rows), :], out_ref.at[pl.ds(i * rows, rows), :], sems.at[i]
+        )
+        for i in range(sems.shape[0])
+    ]
+    for copy in copies:
+        copy.start()
+    row = lax.broadcasted_iota(jnp.int32, order_ref.shape, 0)
+    order_ref[...] = (row == target_ref[...]).astype(jnp.float32).astype(order_ref.dtype)
+    for copy in copies:
+        copy.wait()
+
+
+def stage(array, target, pieces):
+    vmem = pl.BlockSpec(memory_space=pltpu.VMEM)
+    size = target.shape[1]
+    return pl.pallas_call(
+        stage_kernel,
+        out_shape=[
+            jax.ShapeDtypeStruct(array.shape, array.dtype),
+            jax.ShapeDtypeStruct((size, size), jnp.bfloat16),
+        ],
+        in_specs=[pl.BlockSpec(memory_space=pl.ANY), vmem],
+        out_specs=[vmem] * 2,
+        scratch_shapes=[pltpu.SemaphoreType.DMA((pieces,))],
+        compiler_params=pltpu.CompilerParams(vmem_limit_bytes=GRANT),
+        name="stage",
+    )(pltpu.with_memory_space_constraint(array, pltpu.HBM), target)
 
 
 def piece_layout(chunks, occ):
@@ -201,7 +231,7 @@
     for c in range(chunks):
         parts = [(c, j) for j in range(near, occ)]
         if c + 1 < chunks:
-            parts += [(c + 1, j) for j in range(near)]
+            parts = [(c + 1, j) for j in range(near)] + parts
         if parts:
             layout.append(parts)
     return layout
@@ -248,7 +278,7 @@
         for shift in range(outer):
             for flip, array in enumerate((own[shift], other[shift])):
                 source = (here // 2 - shift) % outer * 2 + (here % 2 ^ flip)
-                part = lax.dynamic_slice_in_dim(virt_coeffs, source * rows, rows, axis=0)
+                part = lax.dynamic_slice_in_dim(virt, source * rows, rows, axis=0)
                 term = jnp.dot(array, part, preferred_element_type=jnp.float32)
                 total = term if total is None else total + term
         return total
@@ -271,11 +301,13 @@
         for j in range(occ):
             parts[c, j] = across(halves[j], j)
     layout = piece_layout(len(gots), occ)
+    target = target_rows(me, layout, occ, len(gots), 2, slab)
+    virt, row_order = stage(virt_coeffs, target, 8)
     results = []
     for i, names in enumerate(layout):
         piece = jnp.concatenate([parts[name] for name in names], axis=0)
         results.append(second_half(*gather(piece, i == 1)))
-    return place(me.reshape(1), results, layout, slab)
+    return place(row_order, results, slab)
 
 
 def solution(mesh):

time: 136 us -> 141 us (1.037)
  starting transfers between devices: 47 us -> 40.5 us
  matrix products: 21.4 us -> 26.3 us
  local copies, waits for them, and re-layouts: 2 us -> 5.94 us
  Pallas kernels: 9.58 us -> 12.8 us
  waiting for transfers between devices: 55.2 us -> 53.7 us
    ppermute x10, starting transfers between devices: 14.4 us -> 5.11 us  [along(): lax.ppermute(array, 'pair', [(p, (p // 2 + 1) % outer * 2 + p % 2) for p...]
    dot_general x24, matrix products: 21.4 us -> 26.3 us  [second_half(): term = jnp.dot(array, part, preferred_element_type=jnp.float32)]
    unnamed x11 -> x15, local copies, waits for them, and re-layouts: 0.06 us -> 4.01 us
    ppermute x11, starting transfers between devices: 9.34 us -> 12.8 us  [swap(): return lax.ppermute(array, 'pair', [(p, p ^ 1) for p in range(owners)])]
    pallas_call x1 -> x2, Pallas kernels: 1.62 us -> 4.75 us  [the longest x1 3.32 us: stage(): pl.pallas_call(stage_kernel, out_shape=[jax.ShapeDtypeStruct(array.shape,...]
  transfers between devices with their start and end apart: 35 -> 35, of which waited for: 14 -> 14; matrix products, arithmetic and copies ran while one was open for 17% -> 21% of each run, Pallas kernels for 3% -> 6%
where the time goes in v6:
time: 141 us; the launch traced here: 140 us
  waiting for transfers between devices  53.7 us (38%)
  starting transfers between devices  40.5 us (29%)
  matrix products  26.3 us (19%)
  Pallas kernels  12.8 us (9%)
  local copies, waits for them, and re-layouts  5.94 us (4%)
    ppermute x10, waiting for transfers between devices, along(): lax.ppermute(array, 'pair', [(p, (p // 2 + 1) % outer * 2 + p % 2) for p...  30.5 us
    dot_general x24, matrix products, second_half(): term = jnp.dot(array, part, preferred_element_type=jnp.float32)  26.3 us
    ppermute x7, starting transfers between devices, on_device(): got.append(lax.ppermute(sends[n], 'pair', target))  15.2 us
    ppermute x11, starting transfers between devices, swap(): return lax.ppermute(array, 'pair', [(p, p ^ 1) for p in range(owners)])  12.8 us
    ppermute x11, waiting for transfers between devices, swap(): return lax.ppermute(array, 'pair', [(p, p ^ 1) for p in range(owners)])  12.4 us
    ppermute x7, waiting for transfers between devices, on_device(): got.append(lax.ppermute(sends[n], 'pair', target))  6.67 us
    ppermute x10, starting transfers between devices, along(): lax.ppermute(array, 'pair', [(p, (p // 2 + 1) % outer * 2 + p % 2) for p...  5.11 us
    pallas_call x2, Pallas kernels, half_transform(): pl.pallas_call(functools.partial(half_kernel, owned, width, owners), out_...  4.41 us
  transfers between devices with their start and end apart: 35, of which 14 were waited for; matrix products, arithmetic and copies ran while one was open for 21% of the time, Pallas kernels for 6%

profile of v6, /device:TPU:0, one launch (start us, length us, event | category | flops | bytes accessed | tf_op | source)
XLA Modules:
  0.0 139.9 jit_solution(13626371970426048493)
XLA Ops:
  0.0 3.7 %pack_live.1 = (bf16[272,128]{1,0:T(8,128)(2,1)}, bf16[272,128]{1,0:T(8,128)(2,1)}, bf16[272,128]{1,0:T(8,128)(2,1)}, bf16[272,128]{1,0:T(8,128)(2,1)}, bf16[272...) custom-call(s32[1]{0:T(128)} %bitcast.2.here_ref, ...), custom_call_target="tpu_custom_call" | custom-call | tf_op jit(solution)/shard_map/pack_live/pallas_call | solution.py:70
  3.7 3.1 %collective-permute-start = (bf16[272,128]{1,0:T(8,128)(2,1)}, bf16[272,128]{1,0:T(8,128)(2,1)S(1)}, u32[]{:S(2)}, u32[]{:S(2)}) collective-permute-start(bf16[272,128]{1,0:T(8,128)(2,1)} %get-tuple-element.27), channel_id=1, source_target_pairs={{0,4},{4,0},{8,12},{12,8},{16,20},{20,16},{24,28},{28,24},{1,5},{5... | collective-permute-start | bytes 208904 | tf_op jit(solution)/shard_map/ppermute | solution.py:290
  6.8 1.5 %collective-permute-start.1 = (bf16[272,128]{1,0:T(8,128)(2,1)}, bf16[272,128]{1,0:T(8,128)(2,1)S(1)}, u32[]{:S(2)}, u32[]{:S(2)}) collective-permute-start(bf16[272,128]{1,0:T(8,128)(2,1)} %get-tuple-element.28), channel_id=1, source_target_pairs={{0,8},{4,12},{8,16},{12,20},{16,24},{20,28},{24,0},{28,4},{1,9},{5... | collective-permute-start | bytes 208904 | tf_op jit(solution)/shard_map/ppermute | solution.py:290
  8.3 1.5 %collective-permute-start.2 = (bf16[272,128]{1,0:T(8,128)(2,1)}, bf16[272,128]{1,0:T(8,128)(2,1)S(1)}, u32[]{:S(2)}, u32[]{:S(2)}) collective-permute-start(bf16[272,128]{1,0:T(8,128)(2,1)} %get-tuple-element.29), channel_id=1, source_target_pairs={{0,12},{4,8},{8,20},{12,16},{16,28},{20,24},{24,4},{28,0},{1,13},{... | collective-permute-start | bytes 208904 | tf_op jit(solution)/shard_map/ppermute | solution.py:290
  11.0 2.7 %collective-permute-start.4 = (bf16[272,128]{1,0:T(8,128)(2,1)}, bf16[272,128]{1,0:T(8,128)(2,1)S(1)}, u32[]{:S(2)}, u32[]{:S(2)}) collective-permute-start(bf16[272,128]{1,0:T(8,128)(2,1)} %get-tuple-element.31), channel_id=1, source_target_pairs={{0,20},{4,16},{8,28},{12,24},{16,4},{20,0},{24,12},{28,8},{1,21},{... | collective-permute-start | bytes 208904 | tf_op jit(solution)/shard_map/ppermute | solution.py:290
  13.7 3.5 %all-to-all-start = ((bf16[8,256,128]{2,1,0:T(8,128)(2,1)}), bf16[8,256,128]{2,1,0:T(8,128)(2,1)S(1)}, u32[]{:S(2)}, u32[]{:S(2)}) async-start(bf16[8,256,128]{2,1,0:T(8,128)(2,1)} %get-tuple-element.38), calls=%async_computation | async-start | bytes 1048576 | tf_op jit(solution)/shard_map/all_to_all | solution.py:293
  17.3 1.9 %copy.10 = bf16[48,128,128]{1,2,0:T(8,128)(2,1)S(1)} copy(bf16[48,128,128]{2,1,0:T(8,128)(2,1)} %bitcast.36) | data formatting | bytes 3145728 | tf_op jit(solution)/shard_map/reshape | solution.py:295
  19.3 3.8 %collective-permute-start.5 = (bf16[272,128]{1,0:T(8,128)(2,1)}, bf16[272,128]{1,0:T(8,128)(2,1)S(1)}, u32[]{:S(2)}, u32[]{:S(2)}) collective-permute-start(bf16[272,128]{1,0:T(8,128)(2,1)} %get-tuple-element.32), channel_id=1, source_target_pairs={{0,24},{4,28},{8,0},{12,4},{16,8},{20,12},{24,16},{28,20},{1,25},{... | collective-permute-start | bytes 208904 | tf_op jit(solution)/shard_map/ppermute | solution.py:290
  23.0 1.5 %collective-permute-start.6 = (bf16[272,128]{1,0:T(8,128)(2,1)}, bf16[272,128]{1,0:T(8,128)(2,1)S(1)}, u32[]{:S(2)}, u32[]{:S(2)}) collective-permute-start(bf16[272,128]{1,0:T(8,128)(2,1)} %get-tuple-element.33), channel_id=1, source_target_pairs={{0,28},{4,24},{8,4},{12,0},{16,12},{20,8},{24,20},{28,16},{1,29},{... | collective-permute-start | bytes 208904 | tf_op jit(solution)/shard_map/ppermute | solution.py:290
  24.6 4.8 %collective-permute-done.5.refs_7_ = bf16[272,128]{1,0:T(8,128)(2,1)S(1)} collective-permute-done((bf16[272,128]{1,0:T(8,128)(2,1)}, bf16[272,128]{1,0:T(8,128)(2,1)S(1)}, u32[]{:S(2)}, u32[]{:S(2)}) %collective-permute-start.5) | collective-permute-done | bytes 69664 | tf_op jit(solution)/shard_map/ppermute | solution.py:290
  29.4 1.9 %collective-permute-done.6.refs_8_ = bf16[272,128]{1,0:T(8,128)(2,1)S(1)} collective-permute-done((bf16[272,128]{1,0:T(8,128)(2,1)}, bf16[272,128]{1,0:T(8,128)(2,1)S(1)}, u32[]{:S(2)}, u32[]{:S(2)}) %collective-permute-start.6) | collective-permute-done | bytes 69664 | tf_op jit(solution)/shard_map/ppermute | solution.py:290
  31.2 2.7 %half_transform.2 = (bf16[64,768]{1,0:T(8,128)(2,1)S(1)}, bf16[64,768]{1,0:T(8,128)(2,1)S(1)}, bf16[64,768]{1,0:T(8,128)(2,1)S(1)}, bf16[64,768]{1,0:T(8,128)(2,1)S(1)}, s32[8,128]{1,0:T(8,128)S(1)}) custom-call(s32[2]{0:T(128)S(1)} %pad_add_fusion.place_ref, bf16[48,128,128]{2,1,0:T(8,128)(2,1)S(1)} %bitcast.32, ...), custom_call_target="tpu_custom_call" | custom-call | flops 67108864 | bytes 2523136 | tf_op jit(solution)/shard_map/half_transform/pallas_call | solution.py:147
  35.3 4.2 %collective-permute-start.9 = (bf16[128,768]{1,0:T(8,128)(2,1)S(1)}, bf16[128,768]{1,0:T(8,128)(2,1)S(1)}, u32[]{:S(2)}, u32[]{:S(2)}) collective-permute-start(bf16[128,768]{1,0:T(8,128)(2,1)S(1)} %constant_dynamic-update-slice_fusion), channel_id=1, source_target_pairs={{0,8},{4,12},{8,16},{12,20},{16,24},{20,28},{24,0},{28,4},{1,9},{5... | collective-permute-start | bytes 589832 | tf_op jit(solution)/shard_map/ppermute | solution.py:259
  39.5 3.3 %stage.1 = (bf16[6144,640]{1,0:T(8,128)(2,1)S(1)}, bf16[512,512]{1,0:T(8,128)(2,1)S(1)}) custom-call(bf16[6144,640]{1,0:T(8,128)(2,1)} %in_ref.1, s32[1,512]{1,0:T(1,128)S(1)} %bitcast.34), custom_call_target="tpu_custom_call" | custom-call | tf_op jit(solution)/shard_map/stage/pallas_call | solution.py:214
  42.8 3.1 %copy-done = bf16[6144,640]{1,0:T(8,128)(2,1)} copy-done((bf16[6144,640]{1,0:T(8,128)(2,1)}, bf16[6144,640]{1,0:T(8,128)(2,1)S(1)}, u32[]{:S(2)}) %copy-start) | copy-done | bytes 7864344
  45.9 1.5 %collective-permute-start.16 = (bf16[64,768]{1,0:T(8,128)(2,1)S(1)}, bf16[64,768]{1,0:T(8,128)(2,1)}, u32[]{:S(2)}, u32[]{:S(2)}) collective-permute-start(bf16[64,768]{1,0:T(8,128)(2,1)S(1)} %get-tuple-element.41), channel_id=1, source_target_pairs={{0,2},{1,3},{2,0},{3,1},{4,6},{5,7},{6,4},{7,5},{8,10},{9,11},{10,... | collective-permute-start | bytes 294920 | tf_op jit(solution)/shard_map/ppermute | solution.py:256
  49.4 1.5 %fusion.34 = f32[128,640]{1,0:T(8,128)S(1)} fusion(bf16[128,768]{1,0:T(8,128)(2,1)S(1)} %collective-permute-done.9, bf16[6144,640]{1,0:T(8,128)(2,1)} %copy-done, s32[]{:T(128)S(6)} %select_n.182), kind=kOutput, calls=%fused_computation.46 | convolution fusion | flops 125829120 | bytes 1507332 | tf_op jit(solution)/shard_map/dot_general | solution.py:282
  51.0 4.2 %collective-permute-done.8 = bf16[128,768]{1,0:T(8,128)(2,1)S(1)} collective-permute-done((bf16[128,768]{1,0:T(8,128)(2,1)S(1)}, bf16[128,768]{1,0:T(8,128)(2,1)S(1)}, u32[]{:S(2)}, u32[]{:S(2)}) %collective-permute-start.8) | collective-permute-done | bytes 196640 | tf_op jit(solution)/shard_map/ppermute | solution.py:264
  55.1 1.5 %fusion.40 = f32[128,640]{1,0:T(8,128)S(1)} fusion(bf16[128,768]{1,0:T(8,128)(2,1)S(1)} %collective-permute-done.8, bf16[6144,640]{1,0:T(8,128)(2,1)} %copy-done, s32[]{:T(128)S(6)} %select_n.180), kind=kOutput, calls=%fused_computation.52 | convolution fusion | flops 125829120 | bytes 1507332 | tf_op jit(solution)/shard_map/dot_general | solution.py:282
  56.7 1.5 %fusion.8 = f32[128,640]{1,0:T(8,128)S(1)} fusion(f32[128,640]{1,0:T(8,128)S(1)} %fusion.34, f32[128,640]{1,0:T(8,128)S(1)} %fusion.40, bf16[128,768]{1,0:T(8,128)(2,1)S(1)} %constant_dynamic-update-slice_fusion, bf16[6144,640]{1,0:T(8,128)(2,1)} %copy-done, s32[]{:T(128)S(6)} %select_n.179), kind=kOutput, calls=%fused_computation.20 | convolution fusion | flops 125992960 | bytes 2162692 | tf_op jit(solution)/shard_map/dot_general | solution.py:282
  58.3 1.3 collective-permute-start.12
  59.7 1.5 %fusion.25 = f32[128,640]{1,0:T(8,128)S(1)} fusion(bf16[128,768]{1,0:T(8,128)(2,1)S(1)} %collective-permute-done.11, bf16[6144,640]{1,0:T(8,128)(2,1)} %copy-done, s32[]{:T(128)S(6)} %select_n.185), kind=kOutput, calls=%fused_computation.37 | convolution fusion | flops 125829120 | bytes 1507332 | tf_op jit(solution)/shard_map/dot_general | solution.py:282
  61.2 1.5 %fusion.7 = f32[128,640]{1,0:T(8,128)S(1)} fusion(f32[128,640]{1,0:T(8,128)S(1)} %fusion.25, f32[128,640]{1,0:T(8,128)S(1)} %fusion.8, bf16[128,768]{1,0:T(8,128)(2,1)S(1)} %collective-permute-done.10, bf16[6144,640]{1,0:T(8,128)(2,1)} %copy-done, s32[]{:T(128)S(6)} %select_n.183), kind=kOutput, calls=%fused_computation.18 | convolution fusion | flops 125992960 | bytes 2162692 | tf_op jit(solution)/shard_map/dot_general | solution.py:282
  62.8 3.6 %collective-permute-done.13 = bf16[128,768]{1,0:T(8,128)(2,1)S(1)} collective-permute-done((bf16[128,768]{1,0:T(8,128)(2,1)S(1)}, bf16[128,768]{1,0:T(8,128)(2,1)S(1)}, u32[]{:S(2)}, u32[]{:S(2)}) %collective-permute-start.13) | collective-permute-done | bytes 196640 | tf_op jit(solution)/shard_map/ppermute | solution.py:259
  66.3 1.3 collective-permute-start.14
  67.6 1.5 %fusion.16 = f32[128,640]{1,0:T(8,128)S(1)} fusion(bf16[128,768]{1,0:T(8,128)(2,1)S(1)} %collective-permute-done.13, bf16[6144,640]{1,0:T(8,128)(2,1)} %copy-done, s32[]{:T(128)S(6)} %select_n.188), kind=kOutput, calls=%fused_computation.28 | convolution fusion | flops 125829120 | bytes 1507332 | tf_op jit(solution)/shard_map/dot_general | solution.py:282
  69.2 1.5 %fusion.6 = f32[128,640]{1,0:T(8,128)S(1)} fusion(f32[128,640]{1,0:T(8,128)S(1)} %fusion.16, f32[128,640]{1,0:T(8,128)S(1)} %fusion.7, bf16[128,768]{1,0:T(8,128)(2,1)S(1)} %collective-permute-done.12, bf16[6144,640]{1,0:T(8,128)(2,1)} %copy-done, s32[]{:T(128)S(6)} %select_n.186), kind=kOutput, calls=%fused_computation.16 | convolution fusion | flops 125992960 | bytes 2162692 | tf_op jit(solution)/shard_map/dot_general | solution.py:282
  70.7 1.7 %half_transform.3 = (bf16[64,768]{1,0:T(8,128)(2,1)S(1)}, bf16[64,768]{1,0:T(8,128)(2,1)S(1)}, bf16[64,768]{1,0:T(8,128)(2,1)S(1)}, bf16[64,768]{1,0:T(8,128)(2,1)S(1)}) custom-call(s32[2]{0:T(128)S(1)} %pad_add_fusion.place_ref, s32[8,128]{1,0:T(8,128)S(1)} %get-tuple-element.37.refs_0_, bf16[48,128,128]{2,1,0:T(8,128)(2,1)S(1)} %bitcast.33, ...), custom_call_target="tpu_custom_call" | custom-call | flops 67108864 | bytes 2490368 | tf_op jit(solution)/shard_map/half_transform/pallas_call | solution.py:147
  72.5 1.9 %collective-permute-start.25 = (bf16[64,768]{1,0:T(8,128)(2,1)S(1)}, bf16[64,768]{1,0:T(8,128)(2,1)S(1)}, u32[]{:S(2)}, u32[]{:S(2)}) collective-permute-start(bf16[64,768]{1,0:T(8,128)(2,1)S(1)} %get-tuple-element.43), channel_id=1, source_target_pairs={{0,2},{1,3},{2,0},{3,1},{4,6},{5,7},{6,4},{7,5},{8,10},{9,11},{10,... | collective-permute-start | bytes 294920 | tf_op jit(solution)/shard_map/ppermute | solution.py:256
  74.8 1.6 %convolution_add_fusion.8.refs_0_ = f32[128,640]{1,0:T(8,128)S(1)} fusion(f32[128,640]{1,0:T(8,128)S(1)} %fusion.6, bf16[128,768]{1,0:T(8,128)(2,1)} %collective-permute-done.14, bf16[6144,640]{1,0:T(8,128)(2,1)} %copy-done, s32[]{:T(128)S(6)} %select_n.189), kind=kOutput, calls=%fused_computation.14 | convolution fusion | flops 125911040 | bytes 1835012 | tf_op jit(solution)/shard_map/dot_general | solution.py:282
  77.2 2.1 %collective-permute-done.26 = bf16[64,768]{1,0:T(8,128)(2,1)S(1)} collective-permute-done((bf16[64,768]{1,0:T(8,128)(2,1)S(1)}, bf16[64,768]{1,0:T(8,128)(2,1)S(1)}, u32[]{:S(2)}, u32[]{:S(2)}) %collective-permute-start.26) | collective-permute-done | bytes 98336 | tf_op jit(solution)/shard_map/ppermute | solution.py:256
  81.0 1.4 collective-permute-start.18
  82.4 7.3 %collective-permute-done.28 = bf16[128,768]{1,0:T(8,128)(2,1)S(1)} collective-permute-done((bf16[128,768]{1,0:T(8,128)(2,1)S(1)}, bf16[128,768]{1,0:T(8,128)(2,1)S(1)}, u32[]{:S(2)}, u32[]{:S(2)}) %collective-permute-start.28) | collective-permute-done | bytes 196640 | tf_op jit(solution)/shard_map/ppermute | solution.py:259
  89.7 1.3 collective-permute-start.29
  91.0 1.5 %fusion.30 = f32[128,640]{1,0:T(8,128)S(1)} fusion(bf16[128,768]{1,0:T(8,128)(2,1)S(1)} %collective-permute-done.28, bf16[6144,640]{1,0:T(8,128)(2,1)} %copy-done, s32[]{:T(128)S(6)} %select_n.182), kind=kOutput, calls=%fused_computation.42 | convolution fusion | flops 125829120 | bytes 1507332 | tf_op jit(solution)/shard_map/dot_general | solution.py:282
  92.5 1.5 %fusion.36 = f32[128,640]{1,0:T(8,128)S(1)} fusion(bf16[128,768]{1,0:T(8,128)(2,1)S(1)} %collective-permute-done.27, bf16[6144,640]{1,0:T(8,128)(2,1)} %copy-done, s32[]{:T(128)S(6)} %select_n.180), kind=kOutput, calls=%fused_computation.48 | convolution fusion | flops 125829120 | bytes 1507332 | tf_op jit(solution)/shard_map/dot_general | solution.py:282
  94.0 1.7 %fusion.5 = f32[128,640]{1,0:T(8,128)S(1)} fusion(f32[128,640]{1,0:T(8,128)S(1)} %fusion.30, f32[128,640]{1,0:T(8,128)S(1)} %fusion.36, bf16[128,768]{1,0:T(8,128)(2,1)S(1)} %constant_dynamic-update-slice_fusion.6, bf16[6144,640]{1,0:T(8,128)(2,1)} %copy-done, s32[]{:T(128)S(6)} %select_n.179), kind=kOutput, calls=%fused_computation.13 | convolution fusion | flops 125992960 | bytes 2162692 | tf_op jit(solution)/shard_map/dot_general | solution.py:282
  95.7 1.7 %fusion.38 = f32[256,640]{1,0:T(8,128)S(1)} fusion(bf16[256,768]{1,0:T(8,128)(2,1)S(1)} %collective-permute-done.18, bf16[6144,640]{1,0:T(8,128)(2,1)} %copy-done, s32[]{:T(128)S(6)} %select_n.180), kind=kOutput, calls=%fused_computation.50 | convolution fusion | flops 251658240 | bytes 2031620 | tf_op jit(solution)/shard_map/dot_general | solution.py:282
  98.1 1.7 %fusion.32 = f32[256,640]{1,0:T(8,128)S(1)} fusion(bf16[256,768]{1,0:T(8,128)(2,1)S(1)} %collective-permute-done.19, bf16[6144,640]{1,0:T(8,128)(2,1)} %copy-done, s32[]{:T(128)S(6)} %select_n.182), kind=kOutput, calls=%fused_computation.44 | convolution fusion | flops 251658240 | bytes 2031620 | tf_op jit(solution)/shard_map/dot_general | solution.py:282
  99.8 1.7 %fusion.2 = f32[256,640]{1,0:T(8,128)S(1)} fusion(f32[256,640]{1,0:T(8,128)S(1)} %fusion.32, f32[256,640]{1,0:T(8,128)S(1)} %fusion.38, bf16[256,768]{1,0:T(8,128)(2,1)S(1)} %constant_dynamic-update-slice_fusion.2, bf16[6144,640]{1,0:T(8,128)(2,1)} %copy-done, s32[]{:T(128)S(6)} %select_n.179), kind=kOutput, calls=%fused_computation.6 | convolution fusion | flops 251985920 | bytes 3342340 | tf_op jit(solution)/shard_map/dot_general | solution.py:282
  101.5 1.4 collective-permute-start.31
  104.3 6.8 %collective-permute-done.32 = bf16[128,768]{1,0:T(8,128)(2,1)S(1)} collective-permute-done((bf16[128,768]{1,0:T(8,128)(2,1)S(1)}, bf16[128,768]{1,0:T(8,128)(2,1)S(1)}, u32[]{:S(2)}, u32[]{:S(2)}) %collective-permute-start.32) | collective-permute-done | bytes 196640 | tf_op jit(solution)/shard_map/ppermute | solution.py:259
  113.1 3.6 %collective-permute-done.21 = bf16[256,768]{1,0:T(8,128)(2,1)S(1)} collective-permute-done((bf16[256,768]{1,0:T(8,128)(2,1)S(1)}, bf16[256,768]{1,0:T(8,128)(2,1)S(1)}, u32[]{:S(2)}, u32[]{:S(2)}) %collective-permute-start.21) | collective-permute-done | bytes 393248 | tf_op jit(solution)/shard_map/ppermute | solution.py:259
  116.7 1.3 collective-permute-start.22
  118.5 3.1 %collective-permute-done.33 = bf16[128,768]{1,0:T(8,128)(2,1)S(1)} collective-permute-done((bf16[128,768]{1,0:T(8,128)(2,1)S(1)}, bf16[128,768]{1,0:T(8,128)(2,1)S(1)}, u32[]{:S(2)}, u32[]{:S(2)}) %collective-permute-start.33) | collective-permute-done | bytes 196640 | tf_op jit(solution)/shard_map/ppermute | solution.py:264
  122.5 5.1 %collective-permute-done.22 = bf16[256,768]{1,0:T(8,128)(2,1)S(1)} collective-permute-done((bf16[256,768]{1,0:T(8,128)(2,1)S(1)}, bf16[256,768]{1,0:T(8,128)(2,1)S(1)}, u32[]{:S(2)}, u32[]{:S(2)}) %collective-permute-start.22) | collective-permute-done | bytes 393248 | tf_op jit(solution)/shard_map/ppermute | solution.py:264
  129.3 8.7 %collective-permute-done.24 = bf16[256,768]{1,0:T(8,128)(2,1)S(1)} collective-permute-done((bf16[256,768]{1,0:T(8,128)(2,1)S(1)}, bf16[256,768]{1,0:T(8,128)(2,1)S(1)}, u32[]{:S(2)}, u32[]{:S(2)}) %collective-permute-start.24) | collective-permute-done | bytes 393248 | tf_op jit(solution)/shard_map/ppermute | solution.py:259
  138.5 1.4 %place.1 = bf16[32,16,640]{2,1,0:T(8,128)(2,1)} custom-call(bf16[512,512]{1,0:T(8,128)(2,1)S(1)} %get-tuple-element.25.order_ref, f32[128,640]{1,0:T(8,128)S(1)} %convolution_add_fusion.8.refs_0_, f32[256,640]{1,0:T(8,128)S(1)} %convolution_add_fusion.refs_1_, f32[128,640]{1,0:T(8,128)S(1)} %convolution_add_fusion.4.refs_2_), custom_call_target="tpu_custom_call" | custom-call | tf_op jit(solution)/shard_map/place/pallas_call | solution.py:178
  (73 shorter events, 15.2 us)
Async XLA Ops:
  0.0 39.4 %copy-start.1 = (s32[512]{0:T(512)S(1)}, s32[512]{0:T(512)}, u32[]{:S(2)}) copy-start(s32[512]{0:T(512)} %constant.208.clone) | copy-start | bytes 6148
  0.0 39.4 %copy-start.2 = (s32[512]{0:T(512)S(1)}, s32[512]{0:T(512)}, u32[]{:S(2)}) copy-start(s32[512]{0:T(512)} %constant.216) | copy-start | bytes 6148
  3.7 15.6 %collective-permute-start = (bf16[272,128]{1,0:T(8,128)(2,1)}, bf16[272,128]{1,0:T(8,128)(2,1)S(1)}, u32[]{:S(2)}, u32[]{:S(2)}) collective-permute-start(bf16[272,128]{1,0:T(8,128)(2,1)} %get-tuple-element.27), channel_id=1, source_target_pairs={{0,4},{4,0},{8,12},{12,8},{16,20},{20,16},{24,28},{28,24},{1,5},{5... | collective-permute-start | bytes 208904 | tf_op jit(solution)/shard_map/ppermute | solution.py:290
  6.8 16.3 %collective-permute-start.1 = (bf16[272,128]{1,0:T(8,128)(2,1)}, bf16[272,128]{1,0:T(8,128)(2,1)S(1)}, u32[]{:S(2)}, u32[]{:S(2)}) collective-permute-start(bf16[272,128]{1,0:T(8,128)(2,1)} %get-tuple-element.28), channel_id=1, source_target_pairs={{0,8},{4,12},{8,16},{12,20},{16,24},{20,28},{24,0},{28,4},{1,9},{5... | collective-permute-start | bytes 208904 | tf_op jit(solution)/shard_map/ppermute | solution.py:290
  8.3 16.3 %collective-permute-start.2 = (bf16[272,128]{1,0:T(8,128)(2,1)}, bf16[272,128]{1,0:T(8,128)(2,1)S(1)}, u32[]{:S(2)}, u32[]{:S(2)}) collective-permute-start(bf16[272,128]{1,0:T(8,128)(2,1)} %get-tuple-element.29), channel_id=1, source_target_pairs={{0,12},{4,8},{8,20},{12,16},{16,28},{20,24},{24,4},{28,0},{1,13},{... | collective-permute-start | bytes 208904 | tf_op jit(solution)/shard_map/ppermute | solution.py:290
  9.8 14.7 %collective-permute-start.3 = (bf16[272,128]{1,0:T(8,128)(2,1)}, bf16[272,128]{1,0:T(8,128)(2,1)S(1)}, u32[]{:S(2)}, u32[]{:S(2)}) collective-permute-start(bf16[272,128]{1,0:T(8,128)(2,1)} %get-tuple-element.30), channel_id=1, source_target_pairs={{0,16},{4,20},{8,24},{12,28},{16,0},{20,4},{24,8},{28,12},{1,17},{... | collective-permute-start | bytes 208904 | tf_op jit(solution)/shard_map/ppermute | solution.py:290
  11.0 13.6 %collective-permute-start.4 = (bf16[272,128]{1,0:T(8,128)(2,1)}, bf16[272,128]{1,0:T(8,128)(2,1)S(1)}, u32[]{:S(2)}, u32[]{:S(2)}) collective-permute-start(bf16[272,128]{1,0:T(8,128)(2,1)} %get-tuple-element.31), channel_id=1, source_target_pairs={{0,20},{4,16},{8,28},{12,24},{16,4},{20,0},{24,12},{28,8},{1,21},{... | collective-permute-start | bytes 208904 | tf_op jit(solution)/shard_map/ppermute | solution.py:290
  13.7 57.0 %all-to-all-start = ((bf16[8,256,128]{2,1,0:T(8,128)(2,1)}), bf16[8,256,128]{2,1,0:T(8,128)(2,1)S(1)}, u32[]{:S(2)}, u32[]{:S(2)}) async-start(bf16[8,256,128]{2,1,0:T(8,128)(2,1)} %get-tuple-element.38), calls=%async_computation | async-start | bytes 1048576 | tf_op jit(solution)/shard_map/all_to_all | solution.py:293
  19.3 10.1 %collective-permute-start.5 = (bf16[272,128]{1,0:T(8,128)(2,1)}, bf16[272,128]{1,0:T(8,128)(2,1)S(1)}, u32[]{:S(2)}, u32[]{:S(2)}) collective-permute-start(bf16[272,128]{1,0:T(8,128)(2,1)} %get-tuple-element.32), channel_id=1, source_target_pairs={{0,24},{4,28},{8,0},{12,4},{16,8},{20,12},{24,16},{28,20},{1,25},{... | collective-permute-start | bytes 208904 | tf_op jit(solution)/shard_map/ppermute | solution.py:290
  23.0 8.2 %collective-permute-start.6 = (bf16[272,128]{1,0:T(8,128)(2,1)}, bf16[272,128]{1,0:T(8,128)(2,1)S(1)}, u32[]{:S(2)}, u32[]{:S(2)}) collective-permute-start(bf16[272,128]{1,0:T(8,128)(2,1)} %get-tuple-element.33), channel_id=1, source_target_pairs={{0,28},{4,24},{8,4},{12,0},{16,12},{20,8},{24,20},{28,16},{1,29},{... | collective-permute-start | bytes 208904 | tf_op jit(solution)/shard_map/ppermute | solution.py:290
  33.9 1.4 collective-permute-start.7
  35.3 13.4 %collective-permute-start.9 = (bf16[128,768]{1,0:T(8,128)(2,1)S(1)}, bf16[128,768]{1,0:T(8,128)(2,1)S(1)}, u32[]{:S(2)}, u32[]{:S(2)}) collective-permute-start(bf16[128,768]{1,0:T(8,128)(2,1)S(1)} %constant_dynamic-update-slice_fusion), channel_id=1, source_target_pairs={{0,8},{4,12},{8,16},{12,20},{16,24},{20,28},{24,0},{28,4},{1,9},{5... | collective-permute-start | bytes 589832 | tf_op jit(solution)/shard_map/ppermute | solution.py:259
  42.8 3.1 %copy-start = (bf16[6144,640]{1,0:T(8,128)(2,1)}, bf16[6144,640]{1,0:T(8,128)(2,1)S(1)}, u32[]{:S(2)}) copy-start(bf16[6144,640]{1,0:T(8,128)(2,1)S(1)} %get-tuple-element.36) | copy-start | bytes 23592964
  45.9 34.2 %collective-permute-start.16 = (bf16[64,768]{1,0:T(8,128)(2,1)S(1)}, bf16[64,768]{1,0:T(8,128)(2,1)}, u32[]{:S(2)}, u32[]{:S(2)}) collective-permute-start(bf16[64,768]{1,0:T(8,128)(2,1)S(1)} %get-tuple-element.41), channel_id=1, source_target_pairs={{0,2},{1,3},{2,0},{3,1},{4,6},{5,7},{6,4},{7,5},{8,10},{9,11},{10,... | collective-permute-start | bytes 294920 | tf_op jit(solution)/shard_map/ppermute | solution.py:256
  47.4 33.6 %collective-permute-start.17 = (bf16[64,768]{1,0:T(8,128)(2,1)S(1)}, bf16[64,768]{1,0:T(8,128)(2,1)S(1)}, u32[]{:S(2)}, u32[]{:S(2)}) collective-permute-start(bf16[64,768]{1,0:T(8,128)(2,1)S(1)} %get-tuple-element.42), channel_id=1, source_target_pairs={{0,3},{1,2},{2,1},{3,0},{4,7},{5,6},{6,5},{7,4},{8,11},{9,10},{10,... | collective-permute-start | bytes 294920 | tf_op jit(solution)/shard_map/ppermute | solution.py:256
  47.4 7.8 %collective-permute-start.8 = (bf16[128,768]{1,0:T(8,128)(2,1)S(1)}, bf16[128,768]{1,0:T(8,128)(2,1)S(1)}, u32[]{:S(2)}, u32[]{:S(2)}) collective-permute-start(bf16[128,768]{1,0:T(8,128)(2,1)S(1)} %constant_dynamic-update-slice_fusion), channel_id=1, source_target_pairs={{0,4},{4,0},{8,12},{12,8},{16,20},{20,16},{24,28},{28,24},{1,5},{5... | collective-permute-start | bytes 589832 | tf_op jit(solution)/shard_map/ppermute | solution.py:264
  48.7 9.5 %collective-permute-start.11 = (bf16[128,768]{1,0:T(8,128)(2,1)S(1)}, bf16[128,768]{1,0:T(8,128)(2,1)S(1)}, u32[]{:S(2)}, u32[]{:S(2)}) collective-permute-start(bf16[128,768]{1,0:T(8,128)(2,1)S(1)} %collective-permute-done.9), channel_id=1, source_target_pairs={{0,8},{4,12},{8,16},{12,20},{16,24},{20,28},{24,0},{28,4},{1,9},{5... | collective-permute-start | bytes 589832 | tf_op jit(solution)/shard_map/ppermute | solution.py:259
  48.7 12.5 %collective-permute-start.10 = (bf16[128,768]{1,0:T(8,128)(2,1)S(1)}, bf16[128,768]{1,0:T(8,128)(2,1)S(1)}, u32[]{:S(2)}, u32[]{:S(2)}) collective-permute-start(bf16[128,768]{1,0:T(8,128)(2,1)S(1)} %collective-permute-done.9), channel_id=1, source_target_pairs={{0,4},{4,0},{8,12},{12,8},{16,20},{20,16},{24,28},{28,24},{1,5},{5... | collective-permute-start | bytes 589832 | tf_op jit(solution)/shard_map/ppermute | solution.py:264
  58.2 8.1 %collective-permute-start.13 = (bf16[128,768]{1,0:T(8,128)(2,1)S(1)}, bf16[128,768]{1,0:T(8,128)(2,1)S(1)}, u32[]{:S(2)}, u32[]{:S(2)}) collective-permute-start(bf16[128,768]{1,0:T(8,128)(2,1)S(1)} %collective-permute-done.11), channel_id=1, source_target_pairs={{0,8},{4,12},{8,16},{12,20},{16,24},{20,28},{24,0},{28,4},{1,9},{5... | collective-permute-start | bytes 589832 | tf_op jit(solution)/shard_map/ppermute | solution.py:259
  58.3 10.8 %collective-permute-start.12 = (bf16[128,768]{1,0:T(8,128)(2,1)S(1)}, bf16[128,768]{1,0:T(8,128)(2,1)S(1)}, u32[]{:S(2)}, u32[]{:S(2)}) collective-permute-start(bf16[128,768]{1,0:T(8,128)(2,1)S(1)} %collective-permute-done.11), channel_id=1, source_target_pairs={{0,4},{4,0},{8,12},{12,8},{16,20},{20,16},{24,28},{28,24},{1,5},{5... | collective-permute-start | bytes 589832 | tf_op jit(solution)/shard_map/ppermute | solution.py:264
  66.3 8.1 %collective-permute-start.14 = (bf16[128,768]{1,0:T(8,128)(2,1)S(1)}, bf16[128,768]{1,0:T(8,128)(2,1)}, u32[]{:S(2)}, u32[]{:S(2)}) collective-permute-start(bf16[128,768]{1,0:T(8,128)(2,1)S(1)} %collective-permute-done.13), channel_id=1, source_target_pairs={{0,4},{4,0},{8,12},{12,8},{16,20},{20,16},{24,28},{28,24},{1,5},{5... | collective-permute-start | bytes 589832 | tf_op jit(solution)/shard_map/ppermute | solution.py:264
  72.5 31.2 %slice-start = ((s8[7864320]{0:T(1024)(128)(4,1)}), s8[4194304]{0:T(1024)(128)(4,1)S(1)}, s32[]{:S(2)}) async-start(s8[7864320]{0:T(1024)(128)(4,1)} %bitcast.30), calls=%async_computation.1 | async-start | bytes 8388608
  72.5 4.7 %collective-permute-start.25 = (bf16[64,768]{1,0:T(8,128)(2,1)S(1)}, bf16[64,768]{1,0:T(8,128)(2,1)S(1)}, u32[]{:S(2)}, u32[]{:S(2)}) collective-permute-start(bf16[64,768]{1,0:T(8,128)(2,1)S(1)} %get-tuple-element.43), channel_id=1, source_target_pairs={{0,2},{1,3},{2,0},{3,1},{4,6},{5,7},{6,4},{7,5},{8,10},{9,11},{10,... | collective-permute-start | bytes 294920 | tf_op jit(solution)/shard_map/ppermute | solution.py:256
  74.4 4.9 %collective-permute-start.26 = (bf16[64,768]{1,0:T(8,128)(2,1)S(1)}, bf16[64,768]{1,0:T(8,128)(2,1)S(1)}, u32[]{:S(2)}, u32[]{:S(2)}) collective-permute-start(bf16[64,768]{1,0:T(8,128)(2,1)S(1)} %get-tuple-element.44), channel_id=1, source_target_pairs={{0,3},{1,2},{2,1},{3,0},{4,7},{5,6},{6,5},{7,4},{8,11},{9,10},{10,... | collective-permute-start | bytes 294920 | tf_op jit(solution)/shard_map/ppermute | solution.py:256
  74.4 5.7 %collective-permute-start.15 = (bf16[64,768]{1,0:T(8,128)(2,1)S(1)}, bf16[64,768]{1,0:T(8,128)(2,1)S(1)}, u32[]{:S(2)}, u32[]{:S(2)}) collective-permute-start(bf16[64,768]{1,0:T(8,128)(2,1)S(1)} %get-tuple-element.40), channel_id=1, source_target_pairs={{0,1},{1,0},{2,3},{3,2},{4,5},{5,4},{6,7},{7,6},{8,9},{9,8},{10,11... | collective-permute-start | bytes 294920 | tf_op jit(solution)/shard_map/ppermute | solution.py:256
  79.3 13.2 %collective-permute-start.27 = (bf16[128,768]{1,0:T(8,128)(2,1)S(1)}, bf16[128,768]{1,0:T(8,128)(2,1)S(1)}, u32[]{:S(2)}, u32[]{:S(2)}) collective-permute-start(bf16[128,768]{1,0:T(8,128)(2,1)S(1)} %constant_dynamic-update-slice_fusion.6), channel_id=1, source_target_pairs={{0,4},{4,0},{8,12},{12,8},{16,20},{20,16},{24,28},{28,24},{1,5},{5... | collective-permute-start | bytes 589832 | tf_op jit(solution)/shard_map/ppermute | solution.py:264
  80.1 9.6 %collective-permute-start.28 = (bf16[128,768]{1,0:T(8,128)(2,1)S(1)}, bf16[128,768]{1,0:T(8,128)(2,1)S(1)}, u32[]{:S(2)}, u32[]{:S(2)}) collective-permute-start(bf16[128,768]{1,0:T(8,128)(2,1)S(1)} %constant_dynamic-update-slice_fusion.6), channel_id=1, source_target_pairs={{0,8},{4,12},{8,16},{12,20},{16,24},{20,28},{24,0},{28,4},{1,9},{5... | collective-permute-start | bytes 589832 | tf_op jit(solution)/shard_map/ppermute | solution.py:259
  81.0 14.7 %collective-permute-start.18 = (bf16[256,768]{1,0:T(8,128)(2,1)S(1)}, bf16[256,768]{1,0:T(8,128)(2,1)S(1)}, u32[]{:S(2)}, u32[]{:S(2)}) collective-permute-start(bf16[256,768]{1,0:T(8,128)(2,1)S(1)} %constant_dynamic-update-slice_fusion.2), channel_id=1, source_target_pairs={{0,4},{4,0},{8,12},{12,8},{16,20},{20,16},{24,28},{28,24},{1,5},{5... | collective-permute-start | bytes 1179656 | tf_op jit(solution)/shard_map/ppermute | solution.py:264
  82.4 15.7 %collective-permute-start.19 = (bf16[256,768]{1,0:T(8,128)(2,1)S(1)}, bf16[256,768]{1,0:T(8,128)(2,1)S(1)}, u32[]{:S(2)}, u32[]{:S(2)}) collective-permute-start(bf16[256,768]{1,0:T(8,128)(2,1)S(1)} %constant_dynamic-update-slice_fusion.2), channel_id=1, source_target_pairs={{0,8},{4,12},{8,16},{12,20},{16,24},{20,28},{24,0},{28,4},{1,9},{5... | collective-permute-start | bytes 1179656 | tf_op jit(solution)/shard_map/ppermute | solution.py:259
  89.7 11.8 %collective-permute-start.30 = (bf16[128,768]{1,0:T(8,128)(2,1)S(1)}, bf16[128,768]{1,0:T(8,128)(2,1)S(1)}, u32[]{:S(2)}, u32[]{:S(2)}) collective-permute-start(bf16[128,768]{1,0:T(8,128)(2,1)S(1)} %collective-permute-done.28), channel_id=1, source_target_pairs={{0,8},{4,12},{8,16},{12,20},{16,24},{20,28},{24,0},{28,4},{1,9},{5... | collective-permute-start | bytes 589832 | tf_op jit(solution)/shard_map/ppermute | solution.py:259
  89.7 14.3 %collective-permute-start.29 = (bf16[128,768]{1,0:T(8,128)(2,1)S(1)}, bf16[128,768]{1,0:T(8,128)(2,1)S(1)}, u32[]{:S(2)}, u32[]{:S(2)}) collective-permute-start(bf16[128,768]{1,0:T(8,128)(2,1)S(1)} %collective-permute-done.28), channel_id=1, source_target_pairs={{0,4},{4,0},{8,12},{12,8},{16,20},{20,16},{24,28},{28,24},{1,5},{5... | collective-permute-start | bytes 589832 | tf_op jit(solution)/shard_map/ppermute | solution.py:264
  94.0 9.6 %slice-start.1 = ((s8[7864320]{0:T(1024)(128)(4,1)}), s8[3670016]{0:T(1024)(128)(4,1)S(1)}, s32[]{:S(2)}) async-start(s8[7864320]{0:T(1024)(128)(4,1)} %bitcast.30), calls=%async_computation.2 | async-start | bytes 7340032
  101.5 9.6 %collective-permute-start.32 = (bf16[128,768]{1,0:T(8,128)(2,1)S(1)}, bf16[128,768]{1,0:T(8,128)(2,1)S(1)}, u32[]{:S(2)}, u32[]{:S(2)}) collective-permute-start(bf16[128,768]{1,0:T(8,128)(2,1)S(1)} %collective-permute-done.30), channel_id=1, source_target_pairs={{0,8},{4,12},{8,16},{12,20},{16,24},{20,28},{24,0},{28,4},{1,9},{5... | collective-permute-start | bytes 589832 | tf_op jit(solution)/shard_map/ppermute | solution.py:259
  101.5 11.2 %collective-permute-start.31 = (bf16[128,768]{1,0:T(8,128)(2,1)S(1)}, bf16[128,768]{1,0:T(8,128)(2,1)S(1)}, u32[]{:S(2)}, u32[]{:S(2)}) collective-permute-start(bf16[128,768]{1,0:T(8,128)(2,1)S(1)} %collective-permute-done.30), channel_id=1, source_target_pairs={{0,4},{4,0},{8,12},{12,8},{16,20},{20,16},{24,28},{28,24},{1,5},{5... | collective-permute-start | bytes 589832 | tf_op jit(solution)/shard_map/ppermute | solution.py:264
  102.9 13.8 %collective-permute-start.21 = (bf16[256,768]{1,0:T(8,128)(2,1)S(1)}, bf16[256,768]{1,0:T(8,128)(2,1)S(1)}, u32[]{:S(2)}, u32[]{:S(2)}) collective-permute-start(bf16[256,768]{1,0:T(8,128)(2,1)S(1)} %collective-permute-done.19), channel_id=1, source_target_pairs={{0,8},{4,12},{8,16},{12,20},{16,24},{20,28},{24,0},{28,4},{1,9},{5... | collective-permute-start | bytes 1179656 | tf_op jit(solution)/shard_map/ppermute | solution.py:259
  102.9 19.1 %collective-permute-start.20 = (bf16[256,768]{1,0:T(8,128)(2,1)S(1)}, bf16[256,768]{1,0:T(8,128)(2,1)S(1)}, u32[]{:S(2)}, u32[]{:S(2)}) collective-permute-start(bf16[256,768]{1,0:T(8,128)(2,1)S(1)} %collective-permute-done.19), channel_id=1, source_target_pairs={{0,4},{4,0},{8,12},{12,8},{16,20},{20,16},{24,28},{28,24},{1,5},{5... | collective-permute-start | bytes 1179656 | tf_op jit(solution)/shard_map/ppermute | solution.py:264
  111.1 10.6 %collective-permute-start.33 = (bf16[128,768]{1,0:T(8,128)(2,1)S(1)}, bf16[128,768]{1,0:T(8,128)(2,1)S(1)}, u32[]{:S(2)}, u32[]{:S(2)}) collective-permute-start(bf16[128,768]{1,0:T(8,128)(2,1)S(1)} %collective-permute-done.32), channel_id=1, source_target_pairs={{0,4},{4,0},{8,12},{12,8},{16,20},{20,16},{24,28},{28,24},{1,5},{5... | collective-permute-start | bytes 589832 | tf_op jit(solution)/shard_map/ppermute | solution.py:264
  116.7 11.6 %collective-permute-start.23 = (bf16[256,768]{1,0:T(8,128)(2,1)S(1)}, bf16[256,768]{1,0:T(8,128)(2,1)S(1)}, u32[]{:S(2)}, u32[]{:S(2)}) collective-permute-start(bf16[256,768]{1,0:T(8,128)(2,1)S(1)} %collective-permute-done.21), channel_id=1, source_target_pairs={{0,8},{4,12},{8,16},{12,20},{16,24},{20,28},{24,0},{28,4},{1,9},{5... | collective-permute-start | bytes 1179656 | tf_op jit(solution)/shard_map/ppermute | solution.py:259
  116.7 10.8 %collective-permute-start.22 = (bf16[256,768]{1,0:T(8,128)(2,1)S(1)}, bf16[256,768]{1,0:T(8,128)(2,1)S(1)}, u32[]{:S(2)}, u32[]{:S(2)}) collective-permute-start(bf16[256,768]{1,0:T(8,128)(2,1)S(1)} %collective-permute-done.21), channel_id=1, source_target_pairs={{0,4},{4,0},{8,12},{12,8},{16,20},{20,16},{24,28},{28,24},{1,5},{5... | collective-permute-start | bytes 1179656 | tf_op jit(solution)/shard_map/ppermute | solution.py:264
  127.6 10.4 %collective-permute-start.24 = (bf16[256,768]{1,0:T(8,128)(2,1)S(1)}, bf16[256,768]{1,0:T(8,128)(2,1)S(1)}, u32[]{:S(2)}, u32[]{:S(2)}) collective-permute-start(bf16[256,768]{1,0:T(8,128)(2,1)S(1)} %collective-permute-done.22), channel_id=1, source_target_pairs={{0,8},{4,12},{8,16},{12,20},{16,24},{20,28},{24,0},{28,4},{1,9},{5... | collective-permute-start | bytes 1179656 | tf_op jit(solution)/shard_map/ppermute | solution.py:259

commit v7 on v5

--- a/solution.py
+++ b/solution.py
@@ -9,7 +9,7 @@
 
 
 LIVE = 4
-TAIL = 16
+TAIL = 8
 GRANT = 16 * 2**20
 
 
@@ -195,13 +195,39 @@
     )(me, *sums)
 
 
+def stage_kernel(in_ref, out_ref, sems):
+    rows = out_ref.shape[0] // sems.shape[0]
+    copies = [
+        pltpu.make_async_copy(
+            in_ref.at[pl.ds(i * rows, rows), :], out_ref.at[pl.ds(i * rows, rows), :], sems.at[i]
+        )
+        for i in range(sems.shape[0])
+    ]
+    for copy in copies:
+        copy.start()
+    for copy in copies:
+        copy.wait()
+
+
+def stage(array, pieces):
+    return pl.pallas_call(
+        stage_kernel,
+        out_shape=jax.ShapeDtypeStruct(array.shape, array.dtype),
+        in_specs=[pl.BlockSpec(memory_space=pl.ANY)],
+        out_specs=pl.BlockSpec(memory_space=pltpu.VMEM),
+        scratch_shapes=[pltpu.SemaphoreType.DMA((pieces,))],
+        compiler_params=pltpu.CompilerParams(vmem_limit_bytes=GRANT),
+        name="stage",
+    )(pltpu.with_memory_space_constraint(array, pltpu.HBM))
+
+
 def piece_layout(chunks, occ):
     near = min(2, occ)
     layout = [[(0, j) for j in range(near)]]
     for c in range(chunks):
         parts = [(c, j) for j in range(near, occ)]
         if c + 1 < chunks:
-            parts += [(c + 1, j) for j in range(near)]
+            parts = [(c + 1, j) for j in range(near)] + parts
         if parts:
             layout.append(parts)
     return layout
@@ -248,7 +274,7 @@
         for shift in range(outer):
             for flip, array in enumerate((own[shift], other[shift])):
                 source = (here // 2 - shift) % outer * 2 + (here % 2 ^ flip)
-                part = lax.dynamic_slice_in_dim(virt_coeffs, source * rows, rows, axis=0)
+                part = lax.dynamic_slice_in_dim(virt, source * rows, rows, axis=0)
                 term = jnp.dot(array, part, preferred_element_type=jnp.float32)
                 total = term if total is None else total + term
         return total
@@ -271,6 +297,7 @@
         for j in range(occ):
             parts[c, j] = across(halves[j], j)
     layout = piece_layout(len(gots), occ)
+    virt = stage(virt_coeffs, 8)
     results = []
     for i, names in enumerate(layout):
         piece = jnp.concatenate([parts[name] for name in names], axis=0)

time: 136 us -> 136 us (level)
  starting transfers between devices: 47 us -> 39.3 us
  matrix products: 21.4 us -> 26.3 us
  waiting for transfers between devices: 55.2 us -> 51.5 us
  Pallas kernels: 9.58 us -> 12.9 us
  local copies, waits for them, and re-layouts: 2 us -> 5.04 us
    ppermute x10, starting transfers between devices: 14.4 us -> 6.46 us  [along(): lax.ppermute(array, 'pair', [(p, (p // 2 + 1) % outer * 2 + p % 2) for p...]
    dot_general x24, matrix products: 21.4 us -> 26.3 us  [second_half(): term = jnp.dot(array, part, preferred_element_type=jnp.float32)]
    pallas_call x0 -> x1, Pallas kernels: none -> 3.32 us  [stage(): pl.pallas_call(stage_kernel, out_shape=jax.ShapeDtypeStruct(array.shape,...]
    unnamed x11, local copies, waits for them, and re-layouts: 0.06 us -> 3.1 us
    ppermute x7, starting transfers between devices: 15.2 us -> 12.6 us  [on_device(): got.append(lax.ppermute(sends[n], 'pair', target))]
    ppermute x11, starting transfers between devices: 9.34 us -> 11.7 us  [swap(): return lax.ppermute(array, 'pair', [(p, p ^ 1) for p in range(owners)])]
    ppermute x7, waiting for transfers between devices: 6.62 us -> 5.02 us  [on_device(): got.append(lax.ppermute(sends[n], 'pair', target))]
    ppermute x10, waiting for transfers between devices: 30.7 us -> 29.2 us  [along(): lax.ppermute(array, 'pair', [(p, (p // 2 + 1) % outer * 2 + p % 2) for p...]
  transfers between devices with their start and end apart: 35 -> 35, of which waited for: 14 -> 15; matrix products, arithmetic and copies ran while one was open for 17% -> 21% of each run, Pallas kernels for 3% -> 4%
where the time goes in v7:
time: 136 us; the launch traced here: 135 us
  waiting for transfers between devices  51.5 us (38%)
  starting transfers between devices  39.3 us (29%)
  matrix products  26.3 us (19%)
  Pallas kernels  12.9 us (9%)
  local copies, waits for them, and re-layouts  5.04 us (4%)
    ppermute x10, waiting for transfers between devices, along(): lax.ppermute(array, 'pair', [(p, (p // 2 + 1) % outer * 2 + p % 2) for p...  29.2 us
    dot_general x24, matrix products, second_half(): term = jnp.dot(array, part, preferred_element_type=jnp.float32)  26.3 us
    ppermute x11, waiting for transfers between devices, swap(): return lax.ppermute(array, 'pair', [(p, p ^ 1) for p in range(owners)])  13.3 us
    ppermute x7, starting transfers between devices, on_device(): got.append(lax.ppermute(sends[n], 'pair', target))  12.6 us
    ppermute x11, starting transfers between devices, swap(): return lax.ppermute(array, 'pair', [(p, p ^ 1) for p in range(owners)])  11.7 us
    ppermute x10, starting transfers between devices, along(): lax.ppermute(array, 'pair', [(p, (p // 2 + 1) % outer * 2 + p % 2) for p...  6.46 us
    ppermute x7, waiting for transfers between devices, on_device(): got.append(lax.ppermute(sends[n], 'pair', target))  5.02 us
    all_to_all x1, starting transfers between devices, on_device(): lax.all_to_all(send, 'pair', split_axis=0, concat_axis=0, tiled=True)  4.65 us
  transfers between devices with their start and end apart: 35, of which 15 were waited for; matrix products, arithmetic and copies ran while one was open for 21% of the time, Pallas kernels for 4%

profile of v7, /device:TPU:0, one launch (start us, length us, event | category | flops | bytes accessed | tf_op | source)
XLA Modules:
  0.0 135.5 jit_solution(9685326856918054508)
XLA Ops:
  0.0 3.5 %pack_live.1 = (bf16[264,128]{1,0:T(8,128)(2,1)}, bf16[264,128]{1,0:T(8,128)(2,1)}, bf16[264,128]{1,0:T(8,128)(2,1)}, bf16[264,128]{1,0:T(8,128)(2,1)}, bf16[264...) custom-call(s32[1]{0:T(128)} %bitcast.1.here_ref, ...), custom_call_target="tpu_custom_call" | custom-call | tf_op jit(solution)/shard_map/pack_live/pallas_call | solution.py:69
  3.5 3.1 %collective-permute-start = (bf16[264,128]{1,0:T(8,128)(2,1)}, bf16[264,128]{1,0:T(8,128)(2,1)S(1)}, u32[]{:S(2)}, u32[]{:S(2)}) collective-permute-start(bf16[264,128]{1,0:T(8,128)(2,1)} %get-tuple-element.24), channel_id=1, source_target_pairs={{0,4},{4,0},{8,12},{12,8},{16,20},{20,16},{24,28},{28,24},{1,5},{5... | collective-permute-start | bytes 202760 | tf_op jit(solution)/shard_map/ppermute | solution.py:286
  6.6 1.5 %collective-permute-start.1 = (bf16[264,128]{1,0:T(8,128)(2,1)}, bf16[264,128]{1,0:T(8,128)(2,1)S(1)}, u32[]{:S(2)}, u32[]{:S(2)}) collective-permute-start(bf16[264,128]{1,0:T(8,128)(2,1)} %get-tuple-element.25), channel_id=1, source_target_pairs={{0,8},{4,12},{8,16},{12,20},{16,24},{20,28},{24,0},{28,4},{1,9},{5... | collective-permute-start | bytes 202760 | tf_op jit(solution)/shard_map/ppermute | solution.py:286
  8.2 1.5 %collective-permute-start.2 = (bf16[264,128]{1,0:T(8,128)(2,1)}, bf16[264,128]{1,0:T(8,128)(2,1)S(1)}, u32[]{:S(2)}, u32[]{:S(2)}) collective-permute-start(bf16[264,128]{1,0:T(8,128)(2,1)} %get-tuple-element.26), channel_id=1, source_target_pairs={{0,12},{4,8},{8,20},{12,16},{16,28},{20,24},{24,4},{28,0},{1,13},{... | collective-permute-start | bytes 202760 | tf_op jit(solution)/shard_map/ppermute | solution.py:286
  10.8 2.7 %collective-permute-start.4 = (bf16[264,128]{1,0:T(8,128)(2,1)}, bf16[264,128]{1,0:T(8,128)(2,1)S(1)}, u32[]{:S(2)}, u32[]{:S(2)}) collective-permute-start(bf16[264,128]{1,0:T(8,128)(2,1)} %get-tuple-element.28), channel_id=1, source_target_pairs={{0,20},{4,16},{8,28},{12,24},{16,4},{20,0},{24,12},{28,8},{1,21},{... | collective-permute-start | bytes 202760 | tf_op jit(solution)/shard_map/ppermute | solution.py:286
  13.6 1.9 %copy.6 = bf16[48,128,128]{1,2,0:T(8,128)(2,1)S(1)} copy(bf16[48,128,128]{2,1,0:T(8,128)(2,1)} %bitcast.34) | data formatting | bytes 3145728 | tf_op jit(solution)/shard_map/reshape | solution.py:291
  15.5 2.3 %collective-permute-start.5 = (bf16[264,128]{1,0:T(8,128)(2,1)}, bf16[264,128]{1,0:T(8,128)(2,1)S(1)}, u32[]{:S(2)}, u32[]{:S(2)}) collective-permute-start(bf16[264,128]{1,0:T(8,128)(2,1)} %get-tuple-element.29), channel_id=1, source_target_pairs={{0,24},{4,28},{8,0},{12,4},{16,8},{20,12},{24,16},{28,20},{1,25},{... | collective-permute-start | bytes 202760 | tf_op jit(solution)/shard_map/ppermute | solution.py:286
  18.2 2.7 %collective-permute-done.4.refs_6_ = bf16[264,128]{1,0:T(8,128)(2,1)S(1)} collective-permute-done((bf16[264,128]{1,0:T(8,128)(2,1)}, bf16[264,128]{1,0:T(8,128)(2,1)S(1)}, u32[]{:S(2)}, u32[]{:S(2)}) %collective-permute-start.4) | collective-permute-done | bytes 67616 | tf_op jit(solution)/shard_map/ppermute | solution.py:286
  21.4 1.8 %collective-permute-done.6.refs_8_ = bf16[264,128]{1,0:T(8,128)(2,1)S(1)} collective-permute-done((bf16[264,128]{1,0:T(8,128)(2,1)}, bf16[264,128]{1,0:T(8,128)(2,1)S(1)}, u32[]{:S(2)}, u32[]{:S(2)}) %collective-permute-start.6) | collective-permute-done | bytes 67616 | tf_op jit(solution)/shard_map/ppermute | solution.py:286
  23.2 2.7 %half_transform.2 = (bf16[64,768]{1,0:T(8,128)(2,1)S(1)}, bf16[64,768]{1,0:T(8,128)(2,1)S(1)}, bf16[64,768]{1,0:T(8,128)(2,1)S(1)}, bf16[64,768]{1,0:T(8,128)(2,1)S(1)}, s32[8,128]{1,0:T(8,128)S(1)}) custom-call(s32[2]{0:T(128)S(1)} %pad_add_fusion.place_ref, bf16[48,128,128]{2,1,0:T(8,128)(2,1)S(1)} %bitcast.31, ...), custom_call_target="tpu_custom_call" | custom-call | flops 67108864 | bytes 2506752 | tf_op jit(solution)/shard_map/half_transform/pallas_call | solution.py:146
  27.7 4.7 %all-to-all-start = ((bf16[8,256,128]{2,1,0:T(8,128)(2,1)}), bf16[8,256,128]{2,1,0:T(8,128)(2,1)S(1)}, u32[]{:S(2)}, u32[]{:S(2)}) async-start(bf16[8,256,128]{2,1,0:T(8,128)(2,1)} %get-tuple-element.34), calls=%async_computation | async-start | bytes 1048576 | tf_op jit(solution)/shard_map/all_to_all | solution.py:289
  32.4 3.3 %stage.1 = bf16[6144,640]{1,0:T(8,128)(2,1)S(1)} custom-call(bf16[6144,640]{1,0:T(8,128)(2,1)} %in_ref.1), custom_call_target="tpu_custom_call" | custom-call | tf_op jit(solution)/shard_map/stage/pallas_call | solution.py:213
  35.7 3.1 %copy-done = bf16[6144,640]{1,0:T(8,128)(2,1)} copy-done((bf16[6144,640]{1,0:T(8,128)(2,1)}, bf16[6144,640]{1,0:T(8,128)(2,1)S(1)}, u32[]{:S(2)}) %copy-start) | copy-done | bytes 7864344
  38.8 1.5 %collective-permute-start.16 = (bf16[64,768]{1,0:T(8,128)(2,1)S(1)}, bf16[64,768]{1,0:T(8,128)(2,1)S(1)}, u32[]{:S(2)}, u32[]{:S(2)}) collective-permute-start(bf16[64,768]{1,0:T(8,128)(2,1)S(1)} %get-tuple-element.37), channel_id=1, source_target_pairs={{0,2},{1,3},{2,0},{3,1},{4,6},{5,7},{6,4},{7,5},{8,10},{9,11},{10,... | collective-permute-start | bytes 294920 | tf_op jit(solution)/shard_map/ppermute | solution.py:252
  40.3 2.0 %collective-permute-start.8 = (bf16[128,768]{1,0:T(8,128)(2,1)S(1)}, bf16[128,768]{1,0:T(8,128)(2,1)S(1)}, u32[]{:S(2)}, u32[]{:S(2)}) collective-permute-start(bf16[128,768]{1,0:T(8,128)(2,1)S(1)} %constant_dynamic-update-slice_fusion), channel_id=1, source_target_pairs={{0,4},{4,0},{8,12},{12,8},{16,20},{20,16},{24,28},{28,24},{1,5},{5... | collective-permute-start | bytes 589832 | tf_op jit(solution)/shard_map/ppermute | solution.py:260
  42.3 1.5 %collective-permute-start.11 = (bf16[128,768]{1,0:T(8,128)(2,1)S(1)}, bf16[128,768]{1,0:T(8,128)(2,1)S(1)}, u32[]{:S(2)}, u32[]{:S(2)}) collective-permute-start(bf16[128,768]{1,0:T(8,128)(2,1)S(1)} %collective-permute-done.9), channel_id=1, source_target_pairs={{0,8},{4,12},{8,16},{12,20},{16,24},{20,28},{24,0},{28,4},{1,9},{5... | collective-permute-start | bytes 589832 | tf_op jit(solution)/shard_map/ppermute | solution.py:255
  44.4 1.5 %fusion.34 = f32[128,640]{1,0:T(8,128)S(1)} fusion(bf16[128,768]{1,0:T(8,128)(2,1)S(1)} %collective-permute-done.9, bf16[6144,640]{1,0:T(8,128)(2,1)} %copy-done, s32[]{:T(128)S(6)} %select_n.182), kind=kOutput, calls=%fused_computation.46 | convolution fusion | flops 125829120 | bytes 1507332 | tf_op jit(solution)/shard_map/dot_general | solution.py:278
  45.9 2.9 %collective-permute-done.8 = bf16[128,768]{1,0:T(8,128)(2,1)S(1)} collective-permute-done((bf16[128,768]{1,0:T(8,128)(2,1)S(1)}, bf16[128,768]{1,0:T(8,128)(2,1)S(1)}, u32[]{:S(2)}, u32[]{:S(2)}) %collective-permute-start.8) | collective-permute-done | bytes 196640 | tf_op jit(solution)/shard_map/ppermute | solution.py:260
  48.8 1.5 %fusion.40 = f32[128,640]{1,0:T(8,128)S(1)} fusion(bf16[128,768]{1,0:T(8,128)(2,1)S(1)} %collective-permute-done.8, bf16[6144,640]{1,0:T(8,128)(2,1)} %copy-done, s32[]{:T(128)S(6)} %select_n.180), kind=kOutput, calls=%fused_computation.52 | convolution fusion | flops 125829120 | bytes 1507332 | tf_op jit(solution)/shard_map/dot_general | solution.py:278
  50.3 1.5 %fusion.8 = f32[128,640]{1,0:T(8,128)S(1)} fusion(f32[128,640]{1,0:T(8,128)S(1)} %fusion.34, f32[128,640]{1,0:T(8,128)S(1)} %fusion.40, bf16[128,768]{1,0:T(8,128)(2,1)S(1)} %constant_dynamic-update-slice_fusion, bf16[6144,640]{1,0:T(8,128)(2,1)} %copy-done, s32[]{:T(128)S(6)} %select_n.179), kind=kOutput, calls=%fused_computation.20 | convolution fusion | flops 125992960 | bytes 2162692 | tf_op jit(solution)/shard_map/dot_general | solution.py:278
  51.9 1.9 %collective-permute-start.13 = (bf16[128,768]{1,0:T(8,128)(2,1)S(1)}, bf16[128,768]{1,0:T(8,128)(2,1)S(1)}, u32[]{:S(2)}, u32[]{:S(2)}) collective-permute-start(bf16[128,768]{1,0:T(8,128)(2,1)S(1)} %collective-permute-done.11), channel_id=1, source_target_pairs={{0,8},{4,12},{8,16},{12,20},{16,24},{20,28},{24,0},{28,4},{1,9},{5... | collective-permute-start | bytes 589832 | tf_op jit(solution)/shard_map/ppermute | solution.py:255
  54.7 1.5 %fusion.25 = f32[128,640]{1,0:T(8,128)S(1)} fusion(bf16[128,768]{1,0:T(8,128)(2,1)S(1)} %collective-permute-done.11, bf16[6144,640]{1,0:T(8,128)(2,1)} %copy-done, s32[]{:T(128)S(6)} %select_n.185), kind=kOutput, calls=%fused_computation.37 | convolution fusion | flops 125829120 | bytes 1507332 | tf_op jit(solution)/shard_map/dot_general | solution.py:278
  56.3 1.5 %fusion.7 = f32[128,640]{1,0:T(8,128)S(1)} fusion(f32[128,640]{1,0:T(8,128)S(1)} %fusion.25, f32[128,640]{1,0:T(8,128)S(1)} %fusion.8, bf16[128,768]{1,0:T(8,128)(2,1)S(1)} %collective-permute-done.10, bf16[6144,640]{1,0:T(8,128)(2,1)} %copy-done, s32[]{:T(128)S(6)} %select_n.183), kind=kOutput, calls=%fused_computation.18 | convolution fusion | flops 125992960 | bytes 2162692 | tf_op jit(solution)/shard_map/dot_general | solution.py:278
  57.8 2.7 %collective-permute-done.13 = bf16[128,768]{1,0:T(8,128)(2,1)S(1)} collective-permute-done((bf16[128,768]{1,0:T(8,128)(2,1)S(1)}, bf16[128,768]{1,0:T(8,128)(2,1)S(1)}, u32[]{:S(2)}, u32[]{:S(2)}) %collective-permute-start.13) | collective-permute-done | bytes 196640 | tf_op jit(solution)/shard_map/ppermute | solution.py:255
  60.5 1.5 %collective-permute-start.14 = (bf16[128,768]{1,0:T(8,128)(2,1)S(1)}, bf16[128,768]{1,0:T(8,128)(2,1)S(1)}, u32[]{:S(2)}, u32[]{:S(2)}) collective-permute-start(bf16[128,768]{1,0:T(8,128)(2,1)S(1)} %collective-permute-done.13), channel_id=1, source_target_pairs={{0,4},{4,0},{8,12},{12,8},{16,20},{20,16},{24,28},{28,24},{1,5},{5... | collective-permute-start | bytes 589832 | tf_op jit(solution)/shard_map/ppermute | solution.py:260
  62.0 1.5 %fusion.16 = f32[128,640]{1,0:T(8,128)S(1)} fusion(bf16[128,768]{1,0:T(8,128)(2,1)S(1)} %collective-permute-done.13, bf16[6144,640]{1,0:T(8,128)(2,1)} %copy-done, s32[]{:T(128)S(6)} %select_n.188), kind=kOutput, calls=%fused_computation.28 | convolution fusion | flops 125829120 | bytes 1507332 | tf_op jit(solution)/shard_map/dot_general | solution.py:278
  63.5 1.5 %fusion.6 = f32[128,640]{1,0:T(8,128)S(1)} fusion(f32[128,640]{1,0:T(8,128)S(1)} %fusion.16, f32[128,640]{1,0:T(8,128)S(1)} %fusion.7, bf16[128,768]{1,0:T(8,128)(2,1)S(1)} %collective-permute-done.12, bf16[6144,640]{1,0:T(8,128)(2,1)} %copy-done, s32[]{:T(128)S(6)} %select_n.186), kind=kOutput, calls=%fused_computation.16 | convolution fusion | flops 125992960 | bytes 2162692 | tf_op jit(solution)/shard_map/dot_general | solution.py:278
  65.1 1.8 %half_transform.3 = (bf16[64,768]{1,0:T(8,128)(2,1)S(1)}, bf16[64,768]{1,0:T(8,128)(2,1)S(1)}, bf16[64,768]{1,0:T(8,128)(2,1)S(1)}, bf16[64,768]{1,0:T(8,128)(2,1)S(1)}) custom-call(s32[2]{0:T(128)S(1)} %pad_add_fusion.place_ref, s32[8,128]{1,0:T(8,128)S(1)} %get-tuple-element.33.refs_0_, bf16[48,128,128]{2,1,0:T(8,128)(2,1)S(1)} %bitcast.32, ...), custom_call_target="tpu_custom_call" | custom-call | flops 67108864 | bytes 2490368 | tf_op jit(solution)/shard_map/half_transform/pallas_call | solution.py:146
  66.9 1.4 %collective-permute-start.25 = (bf16[64,768]{1,0:T(8,128)(2,1)S(1)}, bf16[64,768]{1,0:T(8,128)(2,1)S(1)}, u32[]{:S(2)}, u32[]{:S(2)}) collective-permute-start(bf16[64,768]{1,0:T(8,128)(2,1)S(1)} %get-tuple-element.39), channel_id=1, source_target_pairs={{0,2},{1,3},{2,0},{3,1},{4,6},{5,7},{6,4},{7,5},{8,10},{9,11},{10,... | collective-permute-start | bytes 294920 | tf_op jit(solution)/shard_map/ppermute | solution.py:252
  69.2 1.5 %convolution_add_fusion.8.refs_0_ = f32[128,640]{1,0:T(8,128)S(1)} fusion(f32[128,640]{1,0:T(8,128)S(1)} %fusion.6, bf16[128,768]{1,0:T(8,128)(2,1)S(1)} %collective-permute-done.14, bf16[6144,640]{1,0:T(8,128)(2,1)} %copy-done, s32[]{:T(128)S(6)} %select_n.189), kind=kOutput, calls=%fused_computation.14 | convolution fusion | flops 125911040 | bytes 1835012 | tf_op jit(solution)/shard_map/dot_general | solution.py:278
  71.8 1.6 %collective-permute-done.26 = bf16[64,768]{1,0:T(8,128)(2,1)S(1)} collective-permute-done((bf16[64,768]{1,0:T(8,128)(2,1)S(1)}, bf16[64,768]{1,0:T(8,128)(2,1)S(1)}, u32[]{:S(2)}, u32[]{:S(2)}) %collective-permute-start.26) | collective-permute-done | bytes 98336 | tf_op jit(solution)/shard_map/ppermute | solution.py:252
  74.0 1.7 %collective-permute-start.18 = (bf16[256,768]{1,0:T(8,128)(2,1)S(1)}, bf16[256,768]{1,0:T(8,128)(2,1)S(1)}, u32[]{:S(2)}, u32[]{:S(2)}) collective-permute-start(bf16[256,768]{1,0:T(8,128)(2,1)S(1)} %constant_dynamic-update-slice_fusion.2), channel_id=1, source_target_pairs={{0,4},{4,0},{8,12},{12,8},{16,20},{20,16},{24,28},{28,24},{1,5},{5... | collective-permute-start | bytes 1179656 | tf_op jit(solution)/shard_map/ppermute | solution.py:260
  76.0 7.0 %collective-permute-done.28 = bf16[128,768]{1,0:T(8,128)(2,1)S(1)} collective-permute-done((bf16[128,768]{1,0:T(8,128)(2,1)S(1)}, bf16[128,768]{1,0:T(8,128)(2,1)S(1)}, u32[]{:S(2)}, u32[]{:S(2)}) %collective-permute-start.28) | collective-permute-done | bytes 196640 | tf_op jit(solution)/shard_map/ppermute | solution.py:255
  83.5 1.5 %fusion.30 = f32[128,640]{1,0:T(8,128)S(1)} fusion(bf16[128,768]{1,0:T(8,128)(2,1)S(1)} %collective-permute-done.28, bf16[6144,640]{1,0:T(8,128)(2,1)} %copy-done, s32[]{:T(128)S(6)} %select_n.182), kind=kOutput, calls=%fused_computation.42 | convolution fusion | flops 125829120 | bytes 1507332 | tf_op jit(solution)/shard_map/dot_general | solution.py:278
  85.0 1.5 %fusion.36 = f32[128,640]{1,0:T(8,128)S(1)} fusion(bf16[128,768]{1,0:T(8,128)(2,1)S(1)} %collective-permute-done.27, bf16[6144,640]{1,0:T(8,128)(2,1)} %copy-done, s32[]{:T(128)S(6)} %select_n.180), kind=kOutput, calls=%fused_computation.48 | convolution fusion | flops 125829120 | bytes 1507332 | tf_op jit(solution)/shard_map/dot_general | solution.py:278
  86.6 1.7 %fusion.5 = f32[128,640]{1,0:T(8,128)S(1)} fusion(f32[128,640]{1,0:T(8,128)S(1)} %fusion.30, f32[128,640]{1,0:T(8,128)S(1)} %fusion.36, bf16[128,768]{1,0:T(8,128)(2,1)S(1)} %constant_dynamic-update-slice_fusion.6, bf16[6144,640]{1,0:T(8,128)(2,1)} %copy-done, s32[]{:T(128)S(6)} %select_n.179), kind=kOutput, calls=%fused_computation.13 | convolution fusion | flops 125992960 | bytes 2162692 | tf_op jit(solution)/shard_map/dot_general | solution.py:278
  88.3 1.5 %collective-permute-done.18 = bf16[256,768]{1,0:T(8,128)(2,1)S(1)} collective-permute-done((bf16[256,768]{1,0:T(8,128)(2,1)S(1)}, bf16[256,768]{1,0:T(8,128)(2,1)S(1)}, u32[]{:S(2)}, u32[]{:S(2)}) %collective-permute-start.18) | collective-permute-done | bytes 393248 | tf_op jit(solution)/shard_map/ppermute | solution.py:260
  89.8 1.7 %fusion.38 = f32[256,640]{1,0:T(8,128)S(1)} fusion(bf16[256,768]{1,0:T(8,128)(2,1)S(1)} %collective-permute-done.18, bf16[6144,640]{1,0:T(8,128)(2,1)} %copy-done, s32[]{:T(128)S(6)} %select_n.180), kind=kOutput, calls=%fused_computation.50 | convolution fusion | flops 251658240 | bytes 2031620 | tf_op jit(solution)/shard_map/dot_general | solution.py:278
  91.5 1.7 %fusion.32 = f32[256,640]{1,0:T(8,128)S(1)} fusion(bf16[256,768]{1,0:T(8,128)(2,1)S(1)} %collective-permute-done.19, bf16[6144,640]{1,0:T(8,128)(2,1)} %copy-done, s32[]{:T(128)S(6)} %select_n.182), kind=kOutput, calls=%fused_computation.44 | convolution fusion | flops 251658240 | bytes 2031620 | tf_op jit(solution)/shard_map/dot_general | solution.py:278
  93.2 1.7 %fusion.2 = f32[256,640]{1,0:T(8,128)S(1)} fusion(f32[256,640]{1,0:T(8,128)S(1)} %fusion.32, f32[256,640]{1,0:T(8,128)S(1)} %fusion.38, bf16[256,768]{1,0:T(8,128)(2,1)S(1)} %constant_dynamic-update-slice_fusion.2, bf16[6144,640]{1,0:T(8,128)(2,1)} %copy-done, s32[]{:T(128)S(6)} %select_n.179), kind=kOutput, calls=%fused_computation.6 | convolution fusion | flops 251985920 | bytes 3342340 | tf_op jit(solution)/shard_map/dot_general | solution.py:278
  95.3 1.6 %collective-permute-start.31 = (bf16[128,768]{1,0:T(8,128)(2,1)S(1)}, bf16[128,768]{1,0:T(8,128)(2,1)S(1)}, u32[]{:S(2)}, u32[]{:S(2)}) collective-permute-start(bf16[128,768]{1,0:T(8,128)(2,1)S(1)} %collective-permute-done.30), channel_id=1, source_target_pairs={{0,4},{4,0},{8,12},{12,8},{16,20},{20,16},{24,28},{28,24},{1,5},{5... | collective-permute-start | bytes 589832 | tf_op jit(solution)/shard_map/ppermute | solution.py:260
  97.5 1.6 %collective-permute-start.20 = (bf16[256,768]{1,0:T(8,128)(2,1)S(1)}, bf16[256,768]{1,0:T(8,128)(2,1)S(1)}, u32[]{:S(2)}, u32[]{:S(2)}) collective-permute-start(bf16[256,768]{1,0:T(8,128)(2,1)S(1)} %collective-permute-done.19), channel_id=1, source_target_pairs={{0,4},{4,0},{8,12},{12,8},{16,20},{20,16},{24,28},{28,24},{1,5},{5... | collective-permute-start | bytes 1179656 | tf_op jit(solution)/shard_map/ppermute | solution.py:260
  99.7 4.8 %collective-permute-done.32 = bf16[128,768]{1,0:T(8,128)(2,1)S(1)} collective-permute-done((bf16[128,768]{1,0:T(8,128)(2,1)S(1)}, bf16[128,768]{1,0:T(8,128)(2,1)S(1)}, u32[]{:S(2)}, u32[]{:S(2)}) %collective-permute-start.32) | collective-permute-done | bytes 196640 | tf_op jit(solution)/shard_map/ppermute | solution.py:255
  105.6 5.5 %collective-permute-done.21 = bf16[256,768]{1,0:T(8,128)(2,1)S(1)} collective-permute-done((bf16[256,768]{1,0:T(8,128)(2,1)S(1)}, bf16[256,768]{1,0:T(8,128)(2,1)S(1)}, u32[]{:S(2)}, u32[]{:S(2)}) %collective-permute-start.21) | collective-permute-done | bytes 393248 | tf_op jit(solution)/shard_map/ppermute | solution.py:255
  112.2 2.8 %collective-permute-done.33 = bf16[128,768]{1,0:T(8,128)(2,1)S(1)} collective-permute-done((bf16[128,768]{1,0:T(8,128)(2,1)S(1)}, bf16[128,768]{1,0:T(8,128)(2,1)S(1)}, u32[]{:S(2)}, u32[]{:S(2)}) %collective-permute-start.33) | collective-permute-done | bytes 196640 | tf_op jit(solution)/shard_map/ppermute | solution.py:260
  115.9 6.1 %collective-permute-done.22 = bf16[256,768]{1,0:T(8,128)(2,1)S(1)} collective-permute-done((bf16[256,768]{1,0:T(8,128)(2,1)S(1)}, bf16[256,768]{1,0:T(8,128)(2,1)S(1)}, u32[]{:S(2)}, u32[]{:S(2)}) %collective-permute-start.22) | collective-permute-done | bytes 393248 | tf_op jit(solution)/shard_map/ppermute | solution.py:260
  124.2 9.2 %collective-permute-done.24 = bf16[256,768]{1,0:T(8,128)(2,1)S(1)} collective-permute-done((bf16[256,768]{1,0:T(8,128)(2,1)S(1)}, bf16[256,768]{1,0:T(8,128)(2,1)S(1)}, u32[]{:S(2)}, u32[]{:S(2)}) %collective-permute-start.24) | collective-permute-done | bytes 393248 | tf_op jit(solution)/shard_map/ppermute | solution.py:255
  133.9 1.6 %place.1 = bf16[32,16,640]{2,1,0:T(8,128)(2,1)} custom-call(s32[1]{0:T(128)} %bitcast.me_ref, f32[128,640]{1,0:T(8,128)S(1)} %convolution_add_fusion.8.refs_0_, f32[256,640]{1,0:T(8,128)S(1)} %convolution_add_fusion.refs_1_, f32[128,640]{1,0:T(8,128)S(1)} %convolution_add_fusion.4.refs_2_), custom_call_target="tpu_custom_call" | custom-call | tf_op jit(solution)/shard_map/place/pallas_call | solution.py:187
  (68 shorter events, 16.0 us)
Async XLA Ops:
  3.5 11.9 %collective-permute-start = (bf16[264,128]{1,0:T(8,128)(2,1)}, bf16[264,128]{1,0:T(8,128)(2,1)S(1)}, u32[]{:S(2)}, u32[]{:S(2)}) collective-permute-start(bf16[264,128]{1,0:T(8,128)(2,1)} %get-tuple-element.24), channel_id=1, source_target_pairs={{0,4},{4,0},{8,12},{12,8},{16,20},{20,16},{24,28},{28,24},{1,5},{5... | collective-permute-start | bytes 202760 | tf_op jit(solution)/shard_map/ppermute | solution.py:286
  6.6 11.2 %collective-permute-start.1 = (bf16[264,128]{1,0:T(8,128)(2,1)}, bf16[264,128]{1,0:T(8,128)(2,1)S(1)}, u32[]{:S(2)}, u32[]{:S(2)}) collective-permute-start(bf16[264,128]{1,0:T(8,128)(2,1)} %get-tuple-element.25), channel_id=1, source_target_pairs={{0,8},{4,12},{8,16},{12,20},{16,24},{20,28},{24,0},{28,4},{1,9},{5... | collective-permute-start | bytes 202760 | tf_op jit(solution)/shard_map/ppermute | solution.py:286
  8.2 10.0 %collective-permute-start.2 = (bf16[264,128]{1,0:T(8,128)(2,1)}, bf16[264,128]{1,0:T(8,128)(2,1)S(1)}, u32[]{:S(2)}, u32[]{:S(2)}) collective-permute-start(bf16[264,128]{1,0:T(8,128)(2,1)} %get-tuple-element.26), channel_id=1, source_target_pairs={{0,12},{4,8},{8,20},{12,16},{16,28},{20,24},{24,4},{28,0},{1,13},{... | collective-permute-start | bytes 202760 | tf_op jit(solution)/shard_map/ppermute | solution.py:286
  9.7 8.5 %collective-permute-start.3 = (bf16[264,128]{1,0:T(8,128)(2,1)}, bf16[264,128]{1,0:T(8,128)(2,1)S(1)}, u32[]{:S(2)}, u32[]{:S(2)}) collective-permute-start(bf16[264,128]{1,0:T(8,128)(2,1)} %get-tuple-element.27), channel_id=1, source_target_pairs={{0,16},{4,20},{8,24},{12,28},{16,0},{20,4},{24,8},{28,12},{1,17},{... | collective-permute-start | bytes 202760 | tf_op jit(solution)/shard_map/ppermute | solution.py:286
  10.8 10.1 %collective-permute-start.4 = (bf16[264,128]{1,0:T(8,128)(2,1)}, bf16[264,128]{1,0:T(8,128)(2,1)S(1)}, u32[]{:S(2)}, u32[]{:S(2)}) collective-permute-start(bf16[264,128]{1,0:T(8,128)(2,1)} %get-tuple-element.28), channel_id=1, source_target_pairs={{0,20},{4,16},{8,28},{12,24},{16,4},{20,0},{24,12},{28,8},{1,21},{... | collective-permute-start | bytes 202760 | tf_op jit(solution)/shard_map/ppermute | solution.py:286
  15.5 5.9 %collective-permute-start.5 = (bf16[264,128]{1,0:T(8,128)(2,1)}, bf16[264,128]{1,0:T(8,128)(2,1)S(1)}, u32[]{:S(2)}, u32[]{:S(2)}) collective-permute-start(bf16[264,128]{1,0:T(8,128)(2,1)} %get-tuple-element.29), channel_id=1, source_target_pairs={{0,24},{4,28},{8,0},{12,4},{16,8},{20,12},{24,16},{28,20},{1,25},{... | collective-permute-start | bytes 202760 | tf_op jit(solution)/shard_map/ppermute | solution.py:286
  17.8 5.4 %collective-permute-start.6 = (bf16[264,128]{1,0:T(8,128)(2,1)}, bf16[264,128]{1,0:T(8,128)(2,1)S(1)}, u32[]{:S(2)}, u32[]{:S(2)}) collective-permute-start(bf16[264,128]{1,0:T(8,128)(2,1)} %get-tuple-element.30), channel_id=1, source_target_pairs={{0,28},{4,24},{8,4},{12,0},{16,12},{20,8},{24,20},{28,16},{1,29},{... | collective-permute-start | bytes 202760 | tf_op jit(solution)/shard_map/ppermute | solution.py:286
  25.9 1.4 %collective-permute-start.7 = (bf16[64,768]{1,0:T(8,128)(2,1)S(1)}, bf16[64,768]{1,0:T(8,128)(2,1)S(1)}, u32[]{:S(2)}, u32[]{:S(2)}) collective-permute-start(bf16[64,768]{1,0:T(8,128)(2,1)S(1)} %get-tuple-element.32), channel_id=1, source_target_pairs={{0,1},{1,0},{2,3},{3,2},{4,5},{5,4},{6,7},{7,6},{8,9},{9,8},{10,11... | collective-permute-start | bytes 294920 | tf_op jit(solution)/shard_map/ppermute | solution.py:252
  27.2 15.1 %collective-permute-start.9 = (bf16[128,768]{1,0:T(8,128)(2,1)S(1)}, bf16[128,768]{1,0:T(8,128)(2,1)S(1)}, u32[]{:S(2)}, u32[]{:S(2)}) collective-permute-start(bf16[128,768]{1,0:T(8,128)(2,1)S(1)} %constant_dynamic-update-slice_fusion), channel_id=1, source_target_pairs={{0,8},{4,12},{8,16},{12,20},{16,24},{20,28},{24,0},{28,4},{1,9},{5... | collective-permute-start | bytes 589832 | tf_op jit(solution)/shard_map/ppermute | solution.py:255
  27.7 37.4 %all-to-all-start = ((bf16[8,256,128]{2,1,0:T(8,128)(2,1)}), bf16[8,256,128]{2,1,0:T(8,128)(2,1)S(1)}, u32[]{:S(2)}, u32[]{:S(2)}) async-start(bf16[8,256,128]{2,1,0:T(8,128)(2,1)} %get-tuple-element.34), calls=%async_computation | async-start | bytes 1048576 | tf_op jit(solution)/shard_map/all_to_all | solution.py:289
  35.7 3.1 %copy-start = (bf16[6144,640]{1,0:T(8,128)(2,1)}, bf16[6144,640]{1,0:T(8,128)(2,1)S(1)}, u32[]{:S(2)}) copy-start(bf16[6144,640]{1,0:T(8,128)(2,1)S(1)} %stage.1) | copy-start | bytes 23592964
  38.8 35.2 %collective-permute-start.16 = (bf16[64,768]{1,0:T(8,128)(2,1)S(1)}, bf16[64,768]{1,0:T(8,128)(2,1)S(1)}, u32[]{:S(2)}, u32[]{:S(2)}) collective-permute-start(bf16[64,768]{1,0:T(8,128)(2,1)S(1)} %get-tuple-element.37), channel_id=1, source_target_pairs={{0,2},{1,3},{2,0},{3,1},{4,6},{5,7},{6,4},{7,5},{8,10},{9,11},{10,... | collective-permute-start | bytes 294920 | tf_op jit(solution)/shard_map/ppermute | solution.py:252
  40.3 33.7 %collective-permute-start.17 = (bf16[64,768]{1,0:T(8,128)(2,1)S(1)}, bf16[64,768]{1,0:T(8,128)(2,1)S(1)}, u32[]{:S(2)}, u32[]{:S(2)}) collective-permute-start(bf16[64,768]{1,0:T(8,128)(2,1)S(1)} %get-tuple-element.38), channel_id=1, source_target_pairs={{0,3},{1,2},{2,1},{3,0},{4,7},{5,6},{6,5},{7,4},{8,11},{9,10},{10,... | collective-permute-start | bytes 294920 | tf_op jit(solution)/shard_map/ppermute | solution.py:252
  40.3 8.5 %collective-permute-start.8 = (bf16[128,768]{1,0:T(8,128)(2,1)S(1)}, bf16[128,768]{1,0:T(8,128)(2,1)S(1)}, u32[]{:S(2)}, u32[]{:S(2)}) collective-permute-start(bf16[128,768]{1,0:T(8,128)(2,1)S(1)} %constant_dynamic-update-slice_fusion), channel_id=1, source_target_pairs={{0,4},{4,0},{8,12},{12,8},{16,20},{20,16},{24,28},{28,24},{1,5},{5... | collective-permute-start | bytes 589832 | tf_op jit(solution)/shard_map/ppermute | solution.py:260
  42.3 9.5 %collective-permute-start.11 = (bf16[128,768]{1,0:T(8,128)(2,1)S(1)}, bf16[128,768]{1,0:T(8,128)(2,1)S(1)}, u32[]{:S(2)}, u32[]{:S(2)}) collective-permute-start(bf16[128,768]{1,0:T(8,128)(2,1)S(1)} %collective-permute-done.9), channel_id=1, source_target_pairs={{0,8},{4,12},{8,16},{12,20},{16,24},{20,28},{24,0},{28,4},{1,9},{5... | collective-permute-start | bytes 589832 | tf_op jit(solution)/shard_map/ppermute | solution.py:255
  43.8 12.5 %collective-permute-start.10 = (bf16[128,768]{1,0:T(8,128)(2,1)S(1)}, bf16[128,768]{1,0:T(8,128)(2,1)S(1)}, u32[]{:S(2)}, u32[]{:S(2)}) collective-permute-start(bf16[128,768]{1,0:T(8,128)(2,1)S(1)} %collective-permute-done.9), channel_id=1, source_target_pairs={{0,4},{4,0},{8,12},{12,8},{16,20},{20,16},{24,28},{28,24},{1,5},{5... | collective-permute-start | bytes 589832 | tf_op jit(solution)/shard_map/ppermute | solution.py:260
  51.9 8.6 %collective-permute-start.13 = (bf16[128,768]{1,0:T(8,128)(2,1)S(1)}, bf16[128,768]{1,0:T(8,128)(2,1)S(1)}, u32[]{:S(2)}, u32[]{:S(2)}) collective-permute-start(bf16[128,768]{1,0:T(8,128)(2,1)S(1)} %collective-permute-done.11), channel_id=1, source_target_pairs={{0,8},{4,12},{8,16},{12,20},{16,24},{20,28},{24,0},{28,4},{1,9},{5... | collective-permute-start | bytes 589832 | tf_op jit(solution)/shard_map/ppermute | solution.py:255
  53.8 9.8 %collective-permute-start.12 = (bf16[128,768]{1,0:T(8,128)(2,1)S(1)}, bf16[128,768]{1,0:T(8,128)(2,1)S(1)}, u32[]{:S(2)}, u32[]{:S(2)}) collective-permute-start(bf16[128,768]{1,0:T(8,128)(2,1)S(1)} %collective-permute-done.11), channel_id=1, source_target_pairs={{0,4},{4,0},{8,12},{12,8},{16,20},{20,16},{24,28},{28,24},{1,5},{5... | collective-permute-start | bytes 589832 | tf_op jit(solution)/shard_map/ppermute | solution.py:260
  60.5 7.8 %collective-permute-start.14 = (bf16[128,768]{1,0:T(8,128)(2,1)S(1)}, bf16[128,768]{1,0:T(8,128)(2,1)S(1)}, u32[]{:S(2)}, u32[]{:S(2)}) collective-permute-start(bf16[128,768]{1,0:T(8,128)(2,1)S(1)} %collective-permute-done.13), channel_id=1, source_target_pairs={{0,4},{4,0},{8,12},{12,8},{16,20},{20,16},{24,28},{28,24},{1,5},{5... | collective-permute-start | bytes 589832 | tf_op jit(solution)/shard_map/ppermute | solution.py:260
  66.9 32.2 %slice-start = ((s8[7864320]{0:T(1024)(128)(4,1)}), s8[4194304]{0:T(1024)(128)(4,1)S(1)}, s32[]{:S(2)}) async-start(s8[7864320]{0:T(1024)(128)(4,1)} %bitcast.29), calls=%async_computation.1 | async-start | bytes 8388608
  66.9 4.9 %collective-permute-start.25 = (bf16[64,768]{1,0:T(8,128)(2,1)S(1)}, bf16[64,768]{1,0:T(8,128)(2,1)S(1)}, u32[]{:S(2)}, u32[]{:S(2)}) collective-permute-start(bf16[64,768]{1,0:T(8,128)(2,1)S(1)} %get-tuple-element.39), channel_id=1, source_target_pairs={{0,2},{1,3},{2,0},{3,1},{4,6},{5,7},{6,4},{7,5},{8,10},{9,11},{10,... | collective-permute-start | bytes 294920 | tf_op jit(solution)/shard_map/ppermute | solution.py:252
  68.3 5.1 %collective-permute-start.26 = (bf16[64,768]{1,0:T(8,128)(2,1)S(1)}, bf16[64,768]{1,0:T(8,128)(2,1)S(1)}, u32[]{:S(2)}, u32[]{:S(2)}) collective-permute-start(bf16[64,768]{1,0:T(8,128)(2,1)S(1)} %get-tuple-element.40), channel_id=1, source_target_pairs={{0,3},{1,2},{2,1},{3,0},{4,7},{5,6},{6,5},{7,4},{8,11},{9,10},{10,... | collective-permute-start | bytes 294920 | tf_op jit(solution)/shard_map/ppermute | solution.py:252
  68.3 5.6 %collective-permute-start.15 = (bf16[64,768]{1,0:T(8,128)(2,1)S(1)}, bf16[64,768]{1,0:T(8,128)(2,1)S(1)}, u32[]{:S(2)}, u32[]{:S(2)}) collective-permute-start(bf16[64,768]{1,0:T(8,128)(2,1)S(1)} %get-tuple-element.36), channel_id=1, source_target_pairs={{0,1},{1,0},{2,3},{3,2},{4,5},{5,4},{6,7},{7,6},{8,9},{9,8},{10,11... | collective-permute-start | bytes 294920 | tf_op jit(solution)/shard_map/ppermute | solution.py:252
  73.4 9.6 %collective-permute-start.28 = (bf16[128,768]{1,0:T(8,128)(2,1)S(1)}, bf16[128,768]{1,0:T(8,128)(2,1)S(1)}, u32[]{:S(2)}, u32[]{:S(2)}) collective-permute-start(bf16[128,768]{1,0:T(8,128)(2,1)S(1)} %constant_dynamic-update-slice_fusion.6), channel_id=1, source_target_pairs={{0,8},{4,12},{8,16},{12,20},{16,24},{20,28},{24,0},{28,4},{1,9},{5... | collective-permute-start | bytes 589832 | tf_op jit(solution)/shard_map/ppermute | solution.py:255
  73.5 11.5 %collective-permute-start.27 = (bf16[128,768]{1,0:T(8,128)(2,1)S(1)}, bf16[128,768]{1,0:T(8,128)(2,1)S(1)}, u32[]{:S(2)}, u32[]{:S(2)}) collective-permute-start(bf16[128,768]{1,0:T(8,128)(2,1)S(1)} %constant_dynamic-update-slice_fusion.6), channel_id=1, source_target_pairs={{0,4},{4,0},{8,12},{12,8},{16,20},{20,16},{24,28},{28,24},{1,5},{5... | collective-permute-start | bytes 589832 | tf_op jit(solution)/shard_map/ppermute | solution.py:260
  74.0 15.7 %collective-permute-start.18 = (bf16[256,768]{1,0:T(8,128)(2,1)S(1)}, bf16[256,768]{1,0:T(8,128)(2,1)S(1)}, u32[]{:S(2)}, u32[]{:S(2)}) collective-permute-start(bf16[256,768]{1,0:T(8,128)(2,1)S(1)} %constant_dynamic-update-slice_fusion.2), channel_id=1, source_target_pairs={{0,4},{4,0},{8,12},{12,8},{16,20},{20,16},{24,28},{28,24},{1,5},{5... | collective-permute-start | bytes 1179656 | tf_op jit(solution)/shard_map/ppermute | solution.py:260
  75.7 15.8 %collective-permute-start.19 = (bf16[256,768]{1,0:T(8,128)(2,1)S(1)}, bf16[256,768]{1,0:T(8,128)(2,1)S(1)}, u32[]{:S(2)}, u32[]{:S(2)}) collective-permute-start(bf16[256,768]{1,0:T(8,128)(2,1)S(1)} %constant_dynamic-update-slice_fusion.2), channel_id=1, source_target_pairs={{0,8},{4,12},{8,16},{12,20},{16,24},{20,28},{24,0},{28,4},{1,9},{5... | collective-permute-start | bytes 1179656 | tf_op jit(solution)/shard_map/ppermute | solution.py:255
  83.0 11.8 %collective-permute-start.30 = (bf16[128,768]{1,0:T(8,128)(2,1)S(1)}, bf16[128,768]{1,0:T(8,128)(2,1)S(1)}, u32[]{:S(2)}, u32[]{:S(2)}) collective-permute-start(bf16[128,768]{1,0:T(8,128)(2,1)S(1)} %collective-permute-done.28), channel_id=1, source_target_pairs={{0,8},{4,12},{8,16},{12,20},{16,24},{20,28},{24,0},{28,4},{1,9},{5... | collective-permute-start | bytes 589832 | tf_op jit(solution)/shard_map/ppermute | solution.py:255
  83.0 16.3 %collective-permute-start.29 = (bf16[128,768]{1,0:T(8,128)(2,1)S(1)}, bf16[128,768]{1,0:T(8,128)(2,1)S(1)}, u32[]{:S(2)}, u32[]{:S(2)}) collective-permute-start(bf16[128,768]{1,0:T(8,128)(2,1)S(1)} %collective-permute-done.28), channel_id=1, source_target_pairs={{0,4},{4,0},{8,12},{12,8},{16,20},{20,16},{24,28},{28,24},{1,5},{5... | collective-permute-start | bytes 589832 | tf_op jit(solution)/shard_map/ppermute | solution.py:260
  86.6 12.5 %slice-start.1 = ((s8[7864320]{0:T(1024)(128)(4,1)}), s8[3670016]{0:T(1024)(128)(4,1)S(1)}, s32[]{:S(2)}) async-start(s8[7864320]{0:T(1024)(128)(4,1)} %bitcast.29), calls=%async_computation.2 | async-start | bytes 7340032
  94.9 9.6 %collective-permute-start.32 = (bf16[128,768]{1,0:T(8,128)(2,1)S(1)}, bf16[128,768]{1,0:T(8,128)(2,1)S(1)}, u32[]{:S(2)}, u32[]{:S(2)}) collective-permute-start(bf16[128,768]{1,0:T(8,128)(2,1)S(1)} %collective-permute-done.30), channel_id=1, source_target_pairs={{0,8},{4,12},{8,16},{12,20},{16,24},{20,28},{24,0},{28,4},{1,9},{5... | collective-permute-start | bytes 589832 | tf_op jit(solution)/shard_map/ppermute | solution.py:255
  95.3 10.0 %collective-permute-start.31 = (bf16[128,768]{1,0:T(8,128)(2,1)S(1)}, bf16[128,768]{1,0:T(8,128)(2,1)S(1)}, u32[]{:S(2)}, u32[]{:S(2)}) collective-permute-start(bf16[128,768]{1,0:T(8,128)(2,1)S(1)} %collective-permute-done.30), channel_id=1, source_target_pairs={{0,4},{4,0},{8,12},{12,8},{16,20},{20,16},{24,28},{28,24},{1,5},{5... | collective-permute-start | bytes 589832 | tf_op jit(solution)/shard_map/ppermute | solution.py:260
  96.9 14.3 %collective-permute-start.21 = (bf16[256,768]{1,0:T(8,128)(2,1)S(1)}, bf16[256,768]{1,0:T(8,128)(2,1)S(1)}, u32[]{:S(2)}, u32[]{:S(2)}) collective-permute-start(bf16[256,768]{1,0:T(8,128)(2,1)S(1)} %collective-permute-done.19), channel_id=1, source_target_pairs={{0,8},{4,12},{8,16},{12,20},{16,24},{20,28},{24,0},{28,4},{1,9},{5... | collective-permute-start | bytes 1179656 | tf_op jit(solution)/shard_map/ppermute | solution.py:255
  97.5 17.9 %collective-permute-start.20 = (bf16[256,768]{1,0:T(8,128)(2,1)S(1)}, bf16[256,768]{1,0:T(8,128)(2,1)S(1)}, u32[]{:S(2)}, u32[]{:S(2)}) collective-permute-start(bf16[256,768]{1,0:T(8,128)(2,1)S(1)} %collective-permute-done.19), channel_id=1, source_target_pairs={{0,4},{4,0},{8,12},{12,8},{16,20},{20,16},{24,28},{28,24},{1,5},{5... | collective-permute-start | bytes 1179656 | tf_op jit(solution)/shard_map/ppermute | solution.py:260
  104.5 10.6 %collective-permute-start.33 = (bf16[128,768]{1,0:T(8,128)(2,1)S(1)}, bf16[128,768]{1,0:T(8,128)(2,1)S(1)}, u32[]{:S(2)}, u32[]{:S(2)}) collective-permute-start(bf16[128,768]{1,0:T(8,128)(2,1)S(1)} %collective-permute-done.32), channel_id=1, source_target_pairs={{0,4},{4,0},{8,12},{12,8},{16,20},{20,16},{24,28},{28,24},{1,5},{5... | collective-permute-start | bytes 589832 | tf_op jit(solution)/shard_map/ppermute | solution.py:260
  111.1 12.1 %collective-permute-start.23 = (bf16[256,768]{1,0:T(8,128)(2,1)S(1)}, bf16[256,768]{1,0:T(8,128)(2,1)S(1)}, u32[]{:S(2)}, u32[]{:S(2)}) collective-permute-start(bf16[256,768]{1,0:T(8,128)(2,1)S(1)} %collective-permute-done.21), channel_id=1, source_target_pairs={{0,8},{4,12},{8,16},{12,20},{16,24},{20,28},{24,0},{28,4},{1,9},{5... | collective-permute-start | bytes 1179656 | tf_op jit(solution)/shard_map/ppermute | solution.py:255
  111.1 10.8 %collective-permute-start.22 = (bf16[256,768]{1,0:T(8,128)(2,1)S(1)}, bf16[256,768]{1,0:T(8,128)(2,1)S(1)}, u32[]{:S(2)}, u32[]{:S(2)}) collective-permute-start(bf16[256,768]{1,0:T(8,128)(2,1)S(1)} %collective-permute-done.21), channel_id=1, source_target_pairs={{0,4},{4,0},{8,12},{12,8},{16,20},{20,16},{24,28},{28,24},{1,5},{5... | collective-permute-start | bytes 1179656 | tf_op jit(solution)/shard_map/ppermute | solution.py:260
  122.0 11.4 %collective-permute-start.24 = (bf16[256,768]{1,0:T(8,128)(2,1)S(1)}, bf16[256,768]{1,0:T(8,128)(2,1)S(1)}, u32[]{:S(2)}, u32[]{:S(2)}) collective-permute-start(bf16[256,768]{1,0:T(8,128)(2,1)S(1)} %collective-permute-done.22), channel_id=1, source_target_pairs={{0,8},{4,12},{8,16},{12,20},{16,24},{20,28},{24,0},{28,4},{1,9},{5... | collective-permute-start | bytes 1179656 | tf_op jit(solution)/shard_map/ppermute | solution.py:255

commit v8 on v7

--- a/solution.py
+++ b/solution.py
@@ -9,7 +9,7 @@
 
 
 LIVE = 4
-TAIL = 8
+TAIL = 16
 GRANT = 16 * 2**20
 
 
@@ -175,7 +175,7 @@
                     ]
     for t in range(wide.shape[0]):
         out_ref[:, :, t * 128 : (t + 1) * 128] = (
-            wide[t].reshape(slab, all_aux, 128).astype(out_ref.dtype)
+            wide[t, : slab * all_aux, :].reshape(slab, all_aux, 128).astype(out_ref.dtype)
         )
 
 
@@ -189,7 +189,7 @@
         out_shape=jax.ShapeDtypeStruct((slab, rows // slab, columns), jnp.bfloat16),
         in_specs=[pl.BlockSpec(memory_space=pltpu.SMEM)] + [vmem] * len(sums),
         out_specs=vmem,
-        scratch_shapes=[pltpu.VMEM((columns // 128, rows, 128), jnp.float32)],
+        scratch_shapes=[pltpu.VMEM((columns // 128, rows + rows // slab, 128), jnp.float32)],
         compiler_params=pltpu.CompilerParams(vmem_limit_bytes=GRANT),
         name="place",
     )(me, *sums)

time: 136 us -> 137 us (level)
  transfers between devices with their start and end apart: 35 -> 35, of which waited for: 15 -> 16; matrix products, arithmetic and copies ran while one was open for 21% -> 21% of each run, Pallas kernels for 4% -> 4%
where the time goes in v8:
time: 137 us; the launch traced here: 136 us
  waiting for transfers between devices  51.4 us (38%)
  starting transfers between devices  39.6 us (29%)
  matrix products  26.3 us (19%)
  Pallas kernels  12.9 us (9%)
  local copies, waits for them, and re-layouts  5.04 us (4%)
    ppermute x10, waiting for transfers between devices, along(): lax.ppermute(array, 'pair', [(p, (p // 2 + 1) % outer * 2 + p % 2) for p...  29.1 us
    dot_general x24, matrix products, second_half(): term = jnp.dot(array, part, preferred_element_type=jnp.float32)  26.3 us
    ppermute x11, waiting for transfers between devices, swap(): return lax.ppermute(array, 'pair', [(p, p ^ 1) for p in range(owners)])  13.3 us
    ppermute x7, starting transfers between devices, on_device(): got.append(lax.ppermute(sends[n], 'pair', target))  12.6 us
    ppermute x11, starting transfers between devices, swap(): return lax.ppermute(array, 'pair', [(p, p ^ 1) for p in range(owners)])  11.8 us
    ppermute x10, starting transfers between devices, along(): lax.ppermute(array, 'pair', [(p, (p // 2 + 1) % outer * 2 + p % 2) for p...  6.78 us
    ppermute x7, waiting for transfers between devices, on_device(): got.append(lax.ppermute(sends[n], 'pair', target))  5.04 us
    all_to_all x1, starting transfers between devices, on_device(): lax.all_to_all(send, 'pair', split_axis=0, concat_axis=0, tiled=True)  4.49 us
  transfers between devices with their start and end apart: 35, of which 16 were waited for; matrix products, arithmetic and copies ran while one was open for 21% of the time, Pallas kernels for 4%

profile of v8, /device:TPU:0, one launch (start us, length us, event | category | flops | bytes accessed | tf_op | source)
XLA Modules:
  0.0 135.6 jit_solution(13165743132763298456)
XLA Ops:
  0.0 3.5 %pack_live.1 = (bf16[272,128]{1,0:T(8,128)(2,1)}, bf16[272,128]{1,0:T(8,128)(2,1)}, bf16[272,128]{1,0:T(8,128)(2,1)}, bf16[272,128]{1,0:T(8,128)(2,1)}, bf16[272...) custom-call(s32[1]{0:T(128)} %bitcast.1.here_ref, ...), custom_call_target="tpu_custom_call" | custom-call | tf_op jit(solution)/shard_map/pack_live/pallas_call | solution.py:69
  3.5 3.1 %collective-permute-start = (bf16[272,128]{1,0:T(8,128)(2,1)}, bf16[272,128]{1,0:T(8,128)(2,1)S(1)}, u32[]{:S(2)}, u32[]{:S(2)}) collective-permute-start(bf16[272,128]{1,0:T(8,128)(2,1)} %get-tuple-element.24), channel_id=1, source_target_pairs={{0,4},{4,0},{8,12},{12,8},{16,20},{20,16},{24,28},{28,24},{1,5},{5... | collective-permute-start | bytes 208904 | tf_op jit(solution)/shard_map/ppermute | solution.py:286
  6.6 1.5 %collective-permute-start.1 = (bf16[272,128]{1,0:T(8,128)(2,1)}, bf16[272,128]{1,0:T(8,128)(2,1)S(1)}, u32[]{:S(2)}, u32[]{:S(2)}) collective-permute-start(bf16[272,128]{1,0:T(8,128)(2,1)} %get-tuple-element.25), channel_id=1, source_target_pairs={{0,8},{4,12},{8,16},{12,20},{16,24},{20,28},{24,0},{28,4},{1,9},{5... | collective-permute-start | bytes 208904 | tf_op jit(solution)/shard_map/ppermute | solution.py:286
  8.2 1.5 %collective-permute-start.2 = (bf16[272,128]{1,0:T(8,128)(2,1)}, bf16[272,128]{1,0:T(8,128)(2,1)S(1)}, u32[]{:S(2)}, u32[]{:S(2)}) collective-permute-start(bf16[272,128]{1,0:T(8,128)(2,1)} %get-tuple-element.26), channel_id=1, source_target_pairs={{0,12},{4,8},{8,20},{12,16},{16,28},{20,24},{24,4},{28,0},{1,13},{... | collective-permute-start | bytes 208904 | tf_op jit(solution)/shard_map/ppermute | solution.py:286
  10.8 2.7 %collective-permute-start.4 = (bf16[272,128]{1,0:T(8,128)(2,1)}, bf16[272,128]{1,0:T(8,128)(2,1)S(1)}, u32[]{:S(2)}, u32[]{:S(2)}) collective-permute-start(bf16[272,128]{1,0:T(8,128)(2,1)} %get-tuple-element.28), channel_id=1, source_target_pairs={{0,20},{4,16},{8,28},{12,24},{16,4},{20,0},{24,12},{28,8},{1,21},{... | collective-permute-start | bytes 208904 | tf_op jit(solution)/shard_map/ppermute | solution.py:286
  13.6 1.9 %copy.6 = bf16[48,128,128]{1,2,0:T(8,128)(2,1)S(1)} copy(bf16[48,128,128]{2,1,0:T(8,128)(2,1)} %bitcast.34) | data formatting | bytes 3145728 | tf_op jit(solution)/shard_map/reshape | solution.py:291
  15.5 2.3 %collective-permute-start.5 = (bf16[272,128]{1,0:T(8,128)(2,1)}, bf16[272,128]{1,0:T(8,128)(2,1)S(1)}, u32[]{:S(2)}, u32[]{:S(2)}) collective-permute-start(bf16[272,128]{1,0:T(8,128)(2,1)} %get-tuple-element.29), channel_id=1, source_target_pairs={{0,24},{4,28},{8,0},{12,4},{16,8},{20,12},{24,16},{28,20},{1,25},{... | collective-permute-start | bytes 208904 | tf_op jit(solution)/shard_map/ppermute | solution.py:286
  18.6 2.6 %collective-permute-done.4.refs_6_ = bf16[272,128]{1,0:T(8,128)(2,1)S(1)} collective-permute-done((bf16[272,128]{1,0:T(8,128)(2,1)}, bf16[272,128]{1,0:T(8,128)(2,1)S(1)}, u32[]{:S(2)}, u32[]{:S(2)}) %collective-permute-start.4) | collective-permute-done | bytes 69664 | tf_op jit(solution)/shard_map/ppermute | solution.py:286
  21.7 1.5 %collective-permute-done.6.refs_8_ = bf16[272,128]{1,0:T(8,128)(2,1)S(1)} collective-permute-done((bf16[272,128]{1,0:T(8,128)(2,1)}, bf16[272,128]{1,0:T(8,128)(2,1)S(1)}, u32[]{:S(2)}, u32[]{:S(2)}) %collective-permute-start.6) | collective-permute-done | bytes 69664 | tf_op jit(solution)/shard_map/ppermute | solution.py:286
  23.2 2.7 %half_transform.2 = (bf16[64,768]{1,0:T(8,128)(2,1)S(1)}, bf16[64,768]{1,0:T(8,128)(2,1)S(1)}, bf16[64,768]{1,0:T(8,128)(2,1)S(1)}, bf16[64,768]{1,0:T(8,128)(2,1)S(1)}, s32[8,128]{1,0:T(8,128)S(1)}) custom-call(s32[2]{0:T(128)S(1)} %pad_add_fusion.place_ref, bf16[48,128,128]{2,1,0:T(8,128)(2,1)S(1)} %bitcast.31, ...), custom_call_target="tpu_custom_call" | custom-call | flops 67108864 | bytes 2523136 | tf_op jit(solution)/shard_map/half_transform/pallas_call | solution.py:146
  28.1 4.5 %all-to-all-start = ((bf16[8,256,128]{2,1,0:T(8,128)(2,1)}), bf16[8,256,128]{2,1,0:T(8,128)(2,1)S(1)}, u32[]{:S(2)}, u32[]{:S(2)}) async-start(bf16[8,256,128]{2,1,0:T(8,128)(2,1)} %get-tuple-element.34), calls=%async_computation | async-start | bytes 1048576 | tf_op jit(solution)/shard_map/all_to_all | solution.py:289
  32.5 3.3 %stage.1 = bf16[6144,640]{1,0:T(8,128)(2,1)S(1)} custom-call(bf16[6144,640]{1,0:T(8,128)(2,1)} %in_ref.1), custom_call_target="tpu_custom_call" | custom-call | tf_op jit(solution)/shard_map/stage/pallas_call | solution.py:213
  35.9 3.1 %copy-done = bf16[6144,640]{1,0:T(8,128)(2,1)} copy-done((bf16[6144,640]{1,0:T(8,128)(2,1)}, bf16[6144,640]{1,0:T(8,128)(2,1)S(1)}, u32[]{:S(2)}) %copy-start) | copy-done | bytes 7864344
  38.9 1.5 %collective-permute-start.16 = (bf16[64,768]{1,0:T(8,128)(2,1)S(1)}, bf16[64,768]{1,0:T(8,128)(2,1)S(1)}, u32[]{:S(2)}, u32[]{:S(2)}) collective-permute-start(bf16[64,768]{1,0:T(8,128)(2,1)S(1)} %get-tuple-element.37), channel_id=1, source_target_pairs={{0,2},{1,3},{2,0},{3,1},{4,6},{5,7},{6,4},{7,5},{8,10},{9,11},{10,... | collective-permute-start | bytes 294920 | tf_op jit(solution)/shard_map/ppermute | solution.py:252
  40.5 2.0 %collective-permute-start.8 = (bf16[128,768]{1,0:T(8,128)(2,1)S(1)}, bf16[128,768]{1,0:T(8,128)(2,1)S(1)}, u32[]{:S(2)}, u32[]{:S(2)}) collective-permute-start(bf16[128,768]{1,0:T(8,128)(2,1)S(1)} %constant_dynamic-update-slice_fusion), channel_id=1, source_target_pairs={{0,4},{4,0},{8,12},{12,8},{16,20},{20,16},{24,28},{28,24},{1,5},{5... | collective-permute-start | bytes 589832 | tf_op jit(solution)/shard_map/ppermute | solution.py:260
  42.5 1.5 %collective-permute-start.11 = (bf16[128,768]{1,0:T(8,128)(2,1)S(1)}, bf16[128,768]{1,0:T(8,128)(2,1)S(1)}, u32[]{:S(2)}, u32[]{:S(2)}) collective-permute-start(bf16[128,768]{1,0:T(8,128)(2,1)S(1)} %collective-permute-done.9), channel_id=1, source_target_pairs={{0,8},{4,12},{8,16},{12,20},{16,24},{20,28},{24,0},{28,4},{1,9},{5... | collective-permute-start | bytes 589832 | tf_op jit(solution)/shard_map/ppermute | solution.py:255
  44.5 1.5 %fusion.34 = f32[128,640]{1,0:T(8,128)S(1)} fusion(bf16[128,768]{1,0:T(8,128)(2,1)S(1)} %collective-permute-done.9, bf16[6144,640]{1,0:T(8,128)(2,1)} %copy-done, s32[]{:T(128)S(6)} %select_n.182), kind=kOutput, calls=%fused_computation.46 | convolution fusion | flops 125829120 | bytes 1507332 | tf_op jit(solution)/shard_map/dot_general | solution.py:278
  46.0 2.9 %collective-permute-done.8 = bf16[128,768]{1,0:T(8,128)(2,1)S(1)} collective-permute-done((bf16[128,768]{1,0:T(8,128)(2,1)S(1)}, bf16[128,768]{1,0:T(8,128)(2,1)S(1)}, u32[]{:S(2)}, u32[]{:S(2)}) %collective-permute-start.8) | collective-permute-done | bytes 196640 | tf_op jit(solution)/shard_map/ppermute | solution.py:260
  48.9 1.5 %fusion.40 = f32[128,640]{1,0:T(8,128)S(1)} fusion(bf16[128,768]{1,0:T(8,128)(2,1)S(1)} %collective-permute-done.8, bf16[6144,640]{1,0:T(8,128)(2,1)} %copy-done, s32[]{:T(128)S(6)} %select_n.180), kind=kOutput, calls=%fused_computation.52 | convolution fusion | flops 125829120 | bytes 1507332 | tf_op jit(solution)/shard_map/dot_general | solution.py:278
  50.5 1.5 %fusion.8 = f32[128,640]{1,0:T(8,128)S(1)} fusion(f32[128,640]{1,0:T(8,128)S(1)} %fusion.34, f32[128,640]{1,0:T(8,128)S(1)} %fusion.40, bf16[128,768]{1,0:T(8,128)(2,1)S(1)} %constant_dynamic-update-slice_fusion, bf16[6144,640]{1,0:T(8,128)(2,1)} %copy-done, s32[]{:T(128)S(6)} %select_n.179), kind=kOutput, calls=%fused_computation.20 | convolution fusion | flops 125992960 | bytes 2162692 | tf_op jit(solution)/shard_map/dot_general | solution.py:278
  52.0 1.9 %collective-permute-start.13 = (bf16[128,768]{1,0:T(8,128)(2,1)S(1)}, bf16[128,768]{1,0:T(8,128)(2,1)S(1)}, u32[]{:S(2)}, u32[]{:S(2)}) collective-permute-start(bf16[128,768]{1,0:T(8,128)(2,1)S(1)} %collective-permute-done.11), channel_id=1, source_target_pairs={{0,8},{4,12},{8,16},{12,20},{16,24},{20,28},{24,0},{28,4},{1,9},{5... | collective-permute-start | bytes 589832 | tf_op jit(solution)/shard_map/ppermute | solution.py:255
  54.9 1.5 %fusion.25 = f32[128,640]{1,0:T(8,128)S(1)} fusion(bf16[128,768]{1,0:T(8,128)(2,1)S(1)} %collective-permute-done.11, bf16[6144,640]{1,0:T(8,128)(2,1)} %copy-done, s32[]{:T(128)S(6)} %select_n.185), kind=kOutput, calls=%fused_computation.37 | convolution fusion | flops 125829120 | bytes 1507332 | tf_op jit(solution)/shard_map/dot_general | solution.py:278
  56.4 1.5 %fusion.7 = f32[128,640]{1,0:T(8,128)S(1)} fusion(f32[128,640]{1,0:T(8,128)S(1)} %fusion.25, f32[128,640]{1,0:T(8,128)S(1)} %fusion.8, bf16[128,768]{1,0:T(8,128)(2,1)S(1)} %collective-permute-done.10, bf16[6144,640]{1,0:T(8,128)(2,1)} %copy-done, s32[]{:T(128)S(6)} %select_n.183), kind=kOutput, calls=%fused_computation.18 | convolution fusion | flops 125992960 | bytes 2162692 | tf_op jit(solution)/shard_map/dot_general | solution.py:278
  58.0 2.7 %collective-permute-done.13 = bf16[128,768]{1,0:T(8,128)(2,1)S(1)} collective-permute-done((bf16[128,768]{1,0:T(8,128)(2,1)S(1)}, bf16[128,768]{1,0:T(8,128)(2,1)S(1)}, u32[]{:S(2)}, u32[]{:S(2)}) %collective-permute-start.13) | collective-permute-done | bytes 196640 | tf_op jit(solution)/shard_map/ppermute | solution.py:255
  60.7 1.5 %collective-permute-start.14 = (bf16[128,768]{1,0:T(8,128)(2,1)S(1)}, bf16[128,768]{1,0:T(8,128)(2,1)S(1)}, u32[]{:S(2)}, u32[]{:S(2)}) collective-permute-start(bf16[128,768]{1,0:T(8,128)(2,1)S(1)} %collective-permute-done.13), channel_id=1, source_target_pairs={{0,4},{4,0},{8,12},{12,8},{16,20},{20,16},{24,28},{28,24},{1,5},{5... | collective-permute-start | bytes 589832 | tf_op jit(solution)/shard_map/ppermute | solution.py:260
  62.1 1.5 %fusion.16 = f32[128,640]{1,0:T(8,128)S(1)} fusion(bf16[128,768]{1,0:T(8,128)(2,1)S(1)} %collective-permute-done.13, bf16[6144,640]{1,0:T(8,128)(2,1)} %copy-done, s32[]{:T(128)S(6)} %select_n.188), kind=kOutput, calls=%fused_computation.28 | convolution fusion | flops 125829120 | bytes 1507332 | tf_op jit(solution)/shard_map/dot_general | solution.py:278
  63.7 1.5 %fusion.6 = f32[128,640]{1,0:T(8,128)S(1)} fusion(f32[128,640]{1,0:T(8,128)S(1)} %fusion.16, f32[128,640]{1,0:T(8,128)S(1)} %fusion.7, bf16[128,768]{1,0:T(8,128)(2,1)S(1)} %collective-permute-done.12, bf16[6144,640]{1,0:T(8,128)(2,1)} %copy-done, s32[]{:T(128)S(6)} %select_n.186), kind=kOutput, calls=%fused_computation.16 | convolution fusion | flops 125992960 | bytes 2162692 | tf_op jit(solution)/shard_map/dot_general | solution.py:278
  65.2 1.8 %half_transform.3 = (bf16[64,768]{1,0:T(8,128)(2,1)S(1)}, bf16[64,768]{1,0:T(8,128)(2,1)S(1)}, bf16[64,768]{1,0:T(8,128)(2,1)S(1)}, bf16[64,768]{1,0:T(8,128)(2,1)S(1)}) custom-call(s32[2]{0:T(128)S(1)} %pad_add_fusion.place_ref, s32[8,128]{1,0:T(8,128)S(1)} %get-tuple-element.33.refs_0_, bf16[48,128,128]{2,1,0:T(8,128)(2,1)S(1)} %bitcast.32, ...), custom_call_target="tpu_custom_call" | custom-call | flops 67108864 | bytes 2490368 | tf_op jit(solution)/shard_map/half_transform/pallas_call | solution.py:146
  67.0 1.4 %collective-permute-start.25 = (bf16[64,768]{1,0:T(8,128)(2,1)S(1)}, bf16[64,768]{1,0:T(8,128)(2,1)S(1)}, u32[]{:S(2)}, u32[]{:S(2)}) collective-permute-start(bf16[64,768]{1,0:T(8,128)(2,1)S(1)} %get-tuple-element.39), channel_id=1, source_target_pairs={{0,2},{1,3},{2,0},{3,1},{4,6},{5,7},{6,4},{7,5},{8,10},{9,11},{10,... | collective-permute-start | bytes 294920 | tf_op jit(solution)/shard_map/ppermute | solution.py:252
  69.3 1.5 %convolution_add_fusion.8.refs_0_ = f32[128,640]{1,0:T(8,128)S(1)} fusion(f32[128,640]{1,0:T(8,128)S(1)} %fusion.6, bf16[128,768]{1,0:T(8,128)(2,1)S(1)} %collective-permute-done.14, bf16[6144,640]{1,0:T(8,128)(2,1)} %copy-done, s32[]{:T(128)S(6)} %select_n.189), kind=kOutput, calls=%fused_computation.14 | convolution fusion | flops 125911040 | bytes 1835012 | tf_op jit(solution)/shard_map/dot_general | solution.py:278
  72.0 1.6 %collective-permute-done.26 = bf16[64,768]{1,0:T(8,128)(2,1)S(1)} collective-permute-done((bf16[64,768]{1,0:T(8,128)(2,1)S(1)}, bf16[64,768]{1,0:T(8,128)(2,1)S(1)}, u32[]{:S(2)}, u32[]{:S(2)}) %collective-permute-start.26) | collective-permute-done | bytes 98336 | tf_op jit(solution)/shard_map/ppermute | solution.py:252
  74.2 1.7 %collective-permute-start.18 = (bf16[256,768]{1,0:T(8,128)(2,1)S(1)}, bf16[256,768]{1,0:T(8,128)(2,1)S(1)}, u32[]{:S(2)}, u32[]{:S(2)}) collective-permute-start(bf16[256,768]{1,0:T(8,128)(2,1)S(1)} %constant_dynamic-update-slice_fusion.2), channel_id=1, source_target_pairs={{0,4},{4,0},{8,12},{12,8},{16,20},{20,16},{24,28},{28,24},{1,5},{5... | collective-permute-start | bytes 1179656 | tf_op jit(solution)/shard_map/ppermute | solution.py:260
  76.2 7.0 %collective-permute-done.28 = bf16[128,768]{1,0:T(8,128)(2,1)S(1)} collective-permute-done((bf16[128,768]{1,0:T(8,128)(2,1)S(1)}, bf16[128,768]{1,0:T(8,128)(2,1)S(1)}, u32[]{:S(2)}, u32[]{:S(2)}) %collective-permute-start.28) | collective-permute-done | bytes 196640 | tf_op jit(solution)/shard_map/ppermute | solution.py:255
  83.6 1.5 %fusion.30 = f32[128,640]{1,0:T(8,128)S(1)} fusion(bf16[128,768]{1,0:T(8,128)(2,1)S(1)} %collective-permute-done.28, bf16[6144,640]{1,0:T(8,128)(2,1)} %copy-done, s32[]{:T(128)S(6)} %select_n.182), kind=kOutput, calls=%fused_computation.42 | convolution fusion | flops 125829120 | bytes 1507332 | tf_op jit(solution)/shard_map/dot_general | solution.py:278
  85.2 1.5 %fusion.36 = f32[128,640]{1,0:T(8,128)S(1)} fusion(bf16[128,768]{1,0:T(8,128)(2,1)S(1)} %collective-permute-done.27, bf16[6144,640]{1,0:T(8,128)(2,1)} %copy-done, s32[]{:T(128)S(6)} %select_n.180), kind=kOutput, calls=%fused_computation.48 | convolution fusion | flops 125829120 | bytes 1507332 | tf_op jit(solution)/shard_map/dot_general | solution.py:278
  86.7 1.7 %fusion.5 = f32[128,640]{1,0:T(8,128)S(1)} fusion(f32[128,640]{1,0:T(8,128)S(1)} %fusion.30, f32[128,640]{1,0:T(8,128)S(1)} %fusion.36, bf16[128,768]{1,0:T(8,128)(2,1)S(1)} %constant_dynamic-update-slice_fusion.6, bf16[6144,640]{1,0:T(8,128)(2,1)} %copy-done, s32[]{:T(128)S(6)} %select_n.179), kind=kOutput, calls=%fused_computation.13 | convolution fusion | flops 125992960 | bytes 2162692 | tf_op jit(solution)/shard_map/dot_general | solution.py:278
  88.4 1.5 %collective-permute-done.18 = bf16[256,768]{1,0:T(8,128)(2,1)S(1)} collective-permute-done((bf16[256,768]{1,0:T(8,128)(2,1)S(1)}, bf16[256,768]{1,0:T(8,128)(2,1)S(1)}, u32[]{:S(2)}, u32[]{:S(2)}) %collective-permute-start.18) | collective-permute-done | bytes 393248 | tf_op jit(solution)/shard_map/ppermute | solution.py:260
  89.9 1.7 %fusion.38 = f32[256,640]{1,0:T(8,128)S(1)} fusion(bf16[256,768]{1,0:T(8,128)(2,1)S(1)} %collective-permute-done.18, bf16[6144,640]{1,0:T(8,128)(2,1)} %copy-done, s32[]{:T(128)S(6)} %select_n.180), kind=kOutput, calls=%fused_computation.50 | convolution fusion | flops 251658240 | bytes 2031620 | tf_op jit(solution)/shard_map/dot_general | solution.py:278
  91.6 1.7 %fusion.32 = f32[256,640]{1,0:T(8,128)S(1)} fusion(bf16[256,768]{1,0:T(8,128)(2,1)S(1)} %collective-permute-done.19, bf16[6144,640]{1,0:T(8,128)(2,1)} %copy-done, s32[]{:T(128)S(6)} %select_n.182), kind=kOutput, calls=%fused_computation.44 | convolution fusion | flops 251658240 | bytes 2031620 | tf_op jit(solution)/shard_map/dot_general | solution.py:278
  93.3 1.7 %fusion.2 = f32[256,640]{1,0:T(8,128)S(1)} fusion(f32[256,640]{1,0:T(8,128)S(1)} %fusion.32, f32[256,640]{1,0:T(8,128)S(1)} %fusion.38, bf16[256,768]{1,0:T(8,128)(2,1)S(1)} %constant_dynamic-update-slice_fusion.2, bf16[6144,640]{1,0:T(8,128)(2,1)} %copy-done, s32[]{:T(128)S(6)} %select_n.179), kind=kOutput, calls=%fused_computation.6 | convolution fusion | flops 251985920 | bytes 3342340 | tf_op jit(solution)/shard_map/dot_general | solution.py:278
  95.4 1.6 %collective-permute-start.31 = (bf16[128,768]{1,0:T(8,128)(2,1)S(1)}, bf16[128,768]{1,0:T(8,128)(2,1)S(1)}, u32[]{:S(2)}, u32[]{:S(2)}) collective-permute-start(bf16[128,768]{1,0:T(8,128)(2,1)S(1)} %collective-permute-done.30), channel_id=1, source_target_pairs={{0,4},{4,0},{8,12},{12,8},{16,20},{20,16},{24,28},{28,24},{1,5},{5... | collective-permute-start | bytes 589832 | tf_op jit(solution)/shard_map/ppermute | solution.py:260
  97.6 1.6 %collective-permute-start.20 = (bf16[256,768]{1,0:T(8,128)(2,1)S(1)}, bf16[256,768]{1,0:T(8,128)(2,1)S(1)}, u32[]{:S(2)}, u32[]{:S(2)}) collective-permute-start(bf16[256,768]{1,0:T(8,128)(2,1)S(1)} %collective-permute-done.19), channel_id=1, source_target_pairs={{0,4},{4,0},{8,12},{12,8},{16,20},{20,16},{24,28},{28,24},{1,5},{5... | collective-permute-start | bytes 1179656 | tf_op jit(solution)/shard_map/ppermute | solution.py:260
  99.9 4.8 %collective-permute-done.32 = bf16[128,768]{1,0:T(8,128)(2,1)S(1)} collective-permute-done((bf16[128,768]{1,0:T(8,128)(2,1)S(1)}, bf16[128,768]{1,0:T(8,128)(2,1)S(1)}, u32[]{:S(2)}, u32[]{:S(2)}) %collective-permute-start.32) | collective-permute-done | bytes 196640 | tf_op jit(solution)/shard_map/ppermute | solution.py:255
  105.8 5.5 %collective-permute-done.21 = bf16[256,768]{1,0:T(8,128)(2,1)S(1)} collective-permute-done((bf16[256,768]{1,0:T(8,128)(2,1)S(1)}, bf16[256,768]{1,0:T(8,128)(2,1)S(1)}, u32[]{:S(2)}, u32[]{:S(2)}) %collective-permute-start.21) | collective-permute-done | bytes 393248 | tf_op jit(solution)/shard_map/ppermute | solution.py:255
  112.4 2.8 %collective-permute-done.33 = bf16[128,768]{1,0:T(8,128)(2,1)S(1)} collective-permute-done((bf16[128,768]{1,0:T(8,128)(2,1)S(1)}, bf16[128,768]{1,0:T(8,128)(2,1)S(1)}, u32[]{:S(2)}, u32[]{:S(2)}) %collective-permute-start.33) | collective-permute-done | bytes 196640 | tf_op jit(solution)/shard_map/ppermute | solution.py:260
  116.0 6.1 %collective-permute-done.22 = bf16[256,768]{1,0:T(8,128)(2,1)S(1)} collective-permute-done((bf16[256,768]{1,0:T(8,128)(2,1)S(1)}, bf16[256,768]{1,0:T(8,128)(2,1)S(1)}, u32[]{:S(2)}, u32[]{:S(2)}) %collective-permute-start.22) | collective-permute-done | bytes 393248 | tf_op jit(solution)/shard_map/ppermute | solution.py:260
  124.4 9.2 %collective-permute-done.24 = bf16[256,768]{1,0:T(8,128)(2,1)S(1)} collective-permute-done((bf16[256,768]{1,0:T(8,128)(2,1)S(1)}, bf16[256,768]{1,0:T(8,128)(2,1)S(1)}, u32[]{:S(2)}, u32[]{:S(2)}) %collective-permute-start.24) | collective-permute-done | bytes 393248 | tf_op jit(solution)/shard_map/ppermute | solution.py:255
  134.0 1.6 %place.1 = bf16[32,16,640]{2,1,0:T(8,128)(2,1)} custom-call(s32[1]{0:T(128)} %bitcast.me_ref, f32[128,640]{1,0:T(8,128)S(1)} %convolution_add_fusion.8.refs_0_, f32[256,640]{1,0:T(8,128)S(1)} %convolution_add_fusion.refs_1_, f32[128,640]{1,0:T(8,128)S(1)} %convolution_add_fusion.4.refs_2_), custom_call_target="tpu_custom_call" | custom-call | tf_op jit(solution)/shard_map/place/pallas_call | solution.py:187
  (68 shorter events, 16.9 us)
Async XLA Ops:
  3.5 11.9 %collective-permute-start = (bf16[272,128]{1,0:T(8,128)(2,1)}, bf16[272,128]{1,0:T(8,128)(2,1)S(1)}, u32[]{:S(2)}, u32[]{:S(2)}) collective-permute-start(bf16[272,128]{1,0:T(8,128)(2,1)} %get-tuple-element.24), channel_id=1, source_target_pairs={{0,4},{4,0},{8,12},{12,8},{16,20},{20,16},{24,28},{28,24},{1,5},{5... | collective-permute-start | bytes 208904 | tf_op jit(solution)/shard_map/ppermute | solution.py:286
  6.6 11.2 %collective-permute-start.1 = (bf16[272,128]{1,0:T(8,128)(2,1)}, bf16[272,128]{1,0:T(8,128)(2,1)S(1)}, u32[]{:S(2)}, u32[]{:S(2)}) collective-permute-start(bf16[272,128]{1,0:T(8,128)(2,1)} %get-tuple-element.25), channel_id=1, source_target_pairs={{0,8},{4,12},{8,16},{12,20},{16,24},{20,28},{24,0},{28,4},{1,9},{5... | collective-permute-start | bytes 208904 | tf_op jit(solution)/shard_map/ppermute | solution.py:286
  8.2 10.0 %collective-permute-start.2 = (bf16[272,128]{1,0:T(8,128)(2,1)}, bf16[272,128]{1,0:T(8,128)(2,1)S(1)}, u32[]{:S(2)}, u32[]{:S(2)}) collective-permute-start(bf16[272,128]{1,0:T(8,128)(2,1)} %get-tuple-element.26), channel_id=1, source_target_pairs={{0,12},{4,8},{8,20},{12,16},{16,28},{20,24},{24,4},{28,0},{1,13},{... | collective-permute-start | bytes 208904 | tf_op jit(solution)/shard_map/ppermute | solution.py:286
  9.7 8.9 %collective-permute-start.3 = (bf16[272,128]{1,0:T(8,128)(2,1)}, bf16[272,128]{1,0:T(8,128)(2,1)S(1)}, u32[]{:S(2)}, u32[]{:S(2)}) collective-permute-start(bf16[272,128]{1,0:T(8,128)(2,1)} %get-tuple-element.27), channel_id=1, source_target_pairs={{0,16},{4,20},{8,24},{12,28},{16,0},{20,4},{24,8},{28,12},{1,17},{... | collective-permute-start | bytes 208904 | tf_op jit(solution)/shard_map/ppermute | solution.py:286
  10.8 10.3 %collective-permute-start.4 = (bf16[272,128]{1,0:T(8,128)(2,1)}, bf16[272,128]{1,0:T(8,128)(2,1)S(1)}, u32[]{:S(2)}, u32[]{:S(2)}) collective-permute-start(bf16[272,128]{1,0:T(8,128)(2,1)} %get-tuple-element.28), channel_id=1, source_target_pairs={{0,20},{4,16},{8,28},{12,24},{16,4},{20,0},{24,12},{28,8},{1,21},{... | collective-permute-start | bytes 208904 | tf_op jit(solution)/shard_map/ppermute | solution.py:286
  15.5 6.2 %collective-permute-start.5 = (bf16[272,128]{1,0:T(8,128)(2,1)}, bf16[272,128]{1,0:T(8,128)(2,1)S(1)}, u32[]{:S(2)}, u32[]{:S(2)}) collective-permute-start(bf16[272,128]{1,0:T(8,128)(2,1)} %get-tuple-element.29), channel_id=1, source_target_pairs={{0,24},{4,28},{8,0},{12,4},{16,8},{20,12},{24,16},{28,20},{1,25},{... | collective-permute-start | bytes 208904 | tf_op jit(solution)/shard_map/ppermute | solution.py:286
  17.8 5.4 %collective-permute-start.6 = (bf16[272,128]{1,0:T(8,128)(2,1)}, bf16[272,128]{1,0:T(8,128)(2,1)S(1)}, u32[]{:S(2)}, u32[]{:S(2)}) collective-permute-start(bf16[272,128]{1,0:T(8,128)(2,1)} %get-tuple-element.30), channel_id=1, source_target_pairs={{0,28},{4,24},{8,4},{12,0},{16,12},{20,8},{24,20},{28,16},{1,29},{... | collective-permute-start | bytes 208904 | tf_op jit(solution)/shard_map/ppermute | solution.py:286
  25.9 1.4 %collective-permute-start.7 = (bf16[64,768]{1,0:T(8,128)(2,1)S(1)}, bf16[64,768]{1,0:T(8,128)(2,1)S(1)}, u32[]{:S(2)}, u32[]{:S(2)}) collective-permute-start(bf16[64,768]{1,0:T(8,128)(2,1)S(1)} %get-tuple-element.32), channel_id=1, source_target_pairs={{0,1},{1,0},{2,3},{3,2},{4,5},{5,4},{6,7},{7,6},{8,9},{9,8},{10,11... | collective-permute-start | bytes 294920 | tf_op jit(solution)/shard_map/ppermute | solution.py:252
  27.3 15.2 %collective-permute-start.9 = (bf16[128,768]{1,0:T(8,128)(2,1)S(1)}, bf16[128,768]{1,0:T(8,128)(2,1)S(1)}, u32[]{:S(2)}, u32[]{:S(2)}) collective-permute-start(bf16[128,768]{1,0:T(8,128)(2,1)S(1)} %constant_dynamic-update-slice_fusion), channel_id=1, source_target_pairs={{0,8},{4,12},{8,16},{12,20},{16,24},{20,28},{24,0},{28,4},{1,9},{5... | collective-permute-start | bytes 589832 | tf_op jit(solution)/shard_map/ppermute | solution.py:255
  28.1 37.2 %all-to-all-start = ((bf16[8,256,128]{2,1,0:T(8,128)(2,1)}), bf16[8,256,128]{2,1,0:T(8,128)(2,1)S(1)}, u32[]{:S(2)}, u32[]{:S(2)}) async-start(bf16[8,256,128]{2,1,0:T(8,128)(2,1)} %get-tuple-element.34), calls=%async_computation | async-start | bytes 1048576 | tf_op jit(solution)/shard_map/all_to_all | solution.py:289
  35.9 3.1 %copy-start = (bf16[6144,640]{1,0:T(8,128)(2,1)}, bf16[6144,640]{1,0:T(8,128)(2,1)S(1)}, u32[]{:S(2)}) copy-start(bf16[6144,640]{1,0:T(8,128)(2,1)S(1)} %stage.1) | copy-start | bytes 23592964
  38.9 35.2 %collective-permute-start.16 = (bf16[64,768]{1,0:T(8,128)(2,1)S(1)}, bf16[64,768]{1,0:T(8,128)(2,1)S(1)}, u32[]{:S(2)}, u32[]{:S(2)}) collective-permute-start(bf16[64,768]{1,0:T(8,128)(2,1)S(1)} %get-tuple-element.37), channel_id=1, source_target_pairs={{0,2},{1,3},{2,0},{3,1},{4,6},{5,7},{6,4},{7,5},{8,10},{9,11},{10,... | collective-permute-start | bytes 294920 | tf_op jit(solution)/shard_map/ppermute | solution.py:252
  40.4 33.7 %collective-permute-start.17 = (bf16[64,768]{1,0:T(8,128)(2,1)S(1)}, bf16[64,768]{1,0:T(8,128)(2,1)S(1)}, u32[]{:S(2)}, u32[]{:S(2)}) collective-permute-start(bf16[64,768]{1,0:T(8,128)(2,1)S(1)} %get-tuple-element.38), channel_id=1, source_target_pairs={{0,3},{1,2},{2,1},{3,0},{4,7},{5,6},{6,5},{7,4},{8,11},{9,10},{10,... | collective-permute-start | bytes 294920 | tf_op jit(solution)/shard_map/ppermute | solution.py:252
  40.5 8.5 %collective-permute-start.8 = (bf16[128,768]{1,0:T(8,128)(2,1)S(1)}, bf16[128,768]{1,0:T(8,128)(2,1)S(1)}, u32[]{:S(2)}, u32[]{:S(2)}) collective-permute-start(bf16[128,768]{1,0:T(8,128)(2,1)S(1)} %constant_dynamic-update-slice_fusion), channel_id=1, source_target_pairs={{0,4},{4,0},{8,12},{12,8},{16,20},{20,16},{24,28},{28,24},{1,5},{5... | collective-permute-start | bytes 589832 | tf_op jit(solution)/shard_map/ppermute | solution.py:260
  42.5 9.6 %collective-permute-start.11 = (bf16[128,768]{1,0:T(8,128)(2,1)S(1)}, bf16[128,768]{1,0:T(8,128)(2,1)S(1)}, u32[]{:S(2)}, u32[]{:S(2)}) collective-permute-start(bf16[128,768]{1,0:T(8,128)(2,1)S(1)} %collective-permute-done.9), channel_id=1, source_target_pairs={{0,8},{4,12},{8,16},{12,20},{16,24},{20,28},{24,0},{28,4},{1,9},{5... | collective-permute-start | bytes 589832 | tf_op jit(solution)/shard_map/ppermute | solution.py:255
  43.9 12.5 %collective-permute-start.10 = (bf16[128,768]{1,0:T(8,128)(2,1)S(1)}, bf16[128,768]{1,0:T(8,128)(2,1)S(1)}, u32[]{:S(2)}, u32[]{:S(2)}) collective-permute-start(bf16[128,768]{1,0:T(8,128)(2,1)S(1)} %collective-permute-done.9), channel_id=1, source_target_pairs={{0,4},{4,0},{8,12},{12,8},{16,20},{20,16},{24,28},{28,24},{1,5},{5... | collective-permute-start | bytes 589832 | tf_op jit(solution)/shard_map/ppermute | solution.py:260
  52.0 8.6 %collective-permute-start.13 = (bf16[128,768]{1,0:T(8,128)(2,1)S(1)}, bf16[128,768]{1,0:T(8,128)(2,1)S(1)}, u32[]{:S(2)}, u32[]{:S(2)}) collective-permute-start(bf16[128,768]{1,0:T(8,128)(2,1)S(1)} %collective-permute-done.11), channel_id=1, source_target_pairs={{0,8},{4,12},{8,16},{12,20},{16,24},{20,28},{24,0},{28,4},{1,9},{5... | collective-permute-start | bytes 589832 | tf_op jit(solution)/shard_map/ppermute | solution.py:255
  53.9 9.8 %collective-permute-start.12 = (bf16[128,768]{1,0:T(8,128)(2,1)S(1)}, bf16[128,768]{1,0:T(8,128)(2,1)S(1)}, u32[]{:S(2)}, u32[]{:S(2)}) collective-permute-start(bf16[128,768]{1,0:T(8,128)(2,1)S(1)} %collective-permute-done.11), channel_id=1, source_target_pairs={{0,4},{4,0},{8,12},{12,8},{16,20},{20,16},{24,28},{28,24},{1,5},{5... | collective-permute-start | bytes 589832 | tf_op jit(solution)/shard_map/ppermute | solution.py:260
  60.7 7.8 %collective-permute-start.14 = (bf16[128,768]{1,0:T(8,128)(2,1)S(1)}, bf16[128,768]{1,0:T(8,128)(2,1)S(1)}, u32[]{:S(2)}, u32[]{:S(2)}) collective-permute-start(bf16[128,768]{1,0:T(8,128)(2,1)S(1)} %collective-permute-done.13), channel_id=1, source_target_pairs={{0,4},{4,0},{8,12},{12,8},{16,20},{20,16},{24,28},{28,24},{1,5},{5... | collective-permute-start | bytes 589832 | tf_op jit(solution)/shard_map/ppermute | solution.py:260
  67.0 32.2 %slice-start = ((s8[7864320]{0:T(1024)(128)(4,1)}), s8[4194304]{0:T(1024)(128)(4,1)S(1)}, s32[]{:S(2)}) async-start(s8[7864320]{0:T(1024)(128)(4,1)} %bitcast.29), calls=%async_computation.1 | async-start | bytes 8388608
  67.0 4.9 %collective-permute-start.25 = (bf16[64,768]{1,0:T(8,128)(2,1)S(1)}, bf16[64,768]{1,0:T(8,128)(2,1)S(1)}, u32[]{:S(2)}, u32[]{:S(2)}) collective-permute-start(bf16[64,768]{1,0:T(8,128)(2,1)S(1)} %get-tuple-element.39), channel_id=1, source_target_pairs={{0,2},{1,3},{2,0},{3,1},{4,6},{5,7},{6,4},{7,5},{8,10},{9,11},{10,... | collective-permute-start | bytes 294920 | tf_op jit(solution)/shard_map/ppermute | solution.py:252
  68.5 5.1 %collective-permute-start.26 = (bf16[64,768]{1,0:T(8,128)(2,1)S(1)}, bf16[64,768]{1,0:T(8,128)(2,1)S(1)}, u32[]{:S(2)}, u32[]{:S(2)}) collective-permute-start(bf16[64,768]{1,0:T(8,128)(2,1)S(1)} %get-tuple-element.40), channel_id=1, source_target_pairs={{0,3},{1,2},{2,1},{3,0},{4,7},{5,6},{6,5},{7,4},{8,11},{9,10},{10,... | collective-permute-start | bytes 294920 | tf_op jit(solution)/shard_map/ppermute | solution.py:252
  68.5 5.6 %collective-permute-start.15 = (bf16[64,768]{1,0:T(8,128)(2,1)S(1)}, bf16[64,768]{1,0:T(8,128)(2,1)S(1)}, u32[]{:S(2)}, u32[]{:S(2)}) collective-permute-start(bf16[64,768]{1,0:T(8,128)(2,1)S(1)} %get-tuple-element.36), channel_id=1, source_target_pairs={{0,1},{1,0},{2,3},{3,2},{4,5},{5,4},{6,7},{7,6},{8,9},{9,8},{10,11... | collective-permute-start | bytes 294920 | tf_op jit(solution)/shard_map/ppermute | solution.py:252
  73.6 9.6 %collective-permute-start.28 = (bf16[128,768]{1,0:T(8,128)(2,1)S(1)}, bf16[128,768]{1,0:T(8,128)(2,1)S(1)}, u32[]{:S(2)}, u32[]{:S(2)}) collective-permute-start(bf16[128,768]{1,0:T(8,128)(2,1)S(1)} %constant_dynamic-update-slice_fusion.6), channel_id=1, source_target_pairs={{0,8},{4,12},{8,16},{12,20},{16,24},{20,28},{24,0},{28,4},{1,9},{5... | collective-permute-start | bytes 589832 | tf_op jit(solution)/shard_map/ppermute | solution.py:255
  73.6 11.5 %collective-permute-start.27 = (bf16[128,768]{1,0:T(8,128)(2,1)S(1)}, bf16[128,768]{1,0:T(8,128)(2,1)S(1)}, u32[]{:S(2)}, u32[]{:S(2)}) collective-permute-start(bf16[128,768]{1,0:T(8,128)(2,1)S(1)} %constant_dynamic-update-slice_fusion.6), channel_id=1, source_target_pairs={{0,4},{4,0},{8,12},{12,8},{16,20},{20,16},{24,28},{28,24},{1,5},{5... | collective-permute-start | bytes 589832 | tf_op jit(solution)/shard_map/ppermute | solution.py:260
  74.2 15.7 %collective-permute-start.18 = (bf16[256,768]{1,0:T(8,128)(2,1)S(1)}, bf16[256,768]{1,0:T(8,128)(2,1)S(1)}, u32[]{:S(2)}, u32[]{:S(2)}) collective-permute-start(bf16[256,768]{1,0:T(8,128)(2,1)S(1)} %constant_dynamic-update-slice_fusion.2), channel_id=1, source_target_pairs={{0,4},{4,0},{8,12},{12,8},{16,20},{20,16},{24,28},{28,24},{1,5},{5... | collective-permute-start | bytes 1179656 | tf_op jit(solution)/shard_map/ppermute | solution.py:260
  75.8 15.8 %collective-permute-start.19 = (bf16[256,768]{1,0:T(8,128)(2,1)S(1)}, bf16[256,768]{1,0:T(8,128)(2,1)S(1)}, u32[]{:S(2)}, u32[]{:S(2)}) collective-permute-start(bf16[256,768]{1,0:T(8,128)(2,1)S(1)} %constant_dynamic-update-slice_fusion.2), channel_id=1, source_target_pairs={{0,8},{4,12},{8,16},{12,20},{16,24},{20,28},{24,0},{28,4},{1,9},{5... | collective-permute-start | bytes 1179656 | tf_op jit(solution)/shard_map/ppermute | solution.py:255
  83.2 11.8 %collective-permute-start.30 = (bf16[128,768]{1,0:T(8,128)(2,1)S(1)}, bf16[128,768]{1,0:T(8,128)(2,1)S(1)}, u32[]{:S(2)}, u32[]{:S(2)}) collective-permute-start(bf16[128,768]{1,0:T(8,128)(2,1)S(1)} %collective-permute-done.28), channel_id=1, source_target_pairs={{0,8},{4,12},{8,16},{12,20},{16,24},{20,28},{24,0},{28,4},{1,9},{5... | collective-permute-start | bytes 589832 | tf_op jit(solution)/shard_map/ppermute | solution.py:255
  83.2 16.4 %collective-permute-start.29 = (bf16[128,768]{1,0:T(8,128)(2,1)S(1)}, bf16[128,768]{1,0:T(8,128)(2,1)S(1)}, u32[]{:S(2)}, u32[]{:S(2)}) collective-permute-start(bf16[128,768]{1,0:T(8,128)(2,1)S(1)} %collective-permute-done.28), channel_id=1, source_target_pairs={{0,4},{4,0},{8,12},{12,8},{16,20},{20,16},{24,28},{28,24},{1,5},{5... | collective-permute-start | bytes 589832 | tf_op jit(solution)/shard_map/ppermute | solution.py:260
  86.7 12.5 %slice-start.1 = ((s8[7864320]{0:T(1024)(128)(4,1)}), s8[3670016]{0:T(1024)(128)(4,1)S(1)}, s32[]{:S(2)}) async-start(s8[7864320]{0:T(1024)(128)(4,1)} %bitcast.29), calls=%async_computation.2 | async-start | bytes 7340032
  95.0 9.6 %collective-permute-start.32 = (bf16[128,768]{1,0:T(8,128)(2,1)S(1)}, bf16[128,768]{1,0:T(8,128)(2,1)S(1)}, u32[]{:S(2)}, u32[]{:S(2)}) collective-permute-start(bf16[128,768]{1,0:T(8,128)(2,1)S(1)} %collective-permute-done.30), channel_id=1, source_target_pairs={{0,8},{4,12},{8,16},{12,20},{16,24},{20,28},{24,0},{28,4},{1,9},{5... | collective-permute-start | bytes 589832 | tf_op jit(solution)/shard_map/ppermute | solution.py:255
  95.4 10.0 %collective-permute-start.31 = (bf16[128,768]{1,0:T(8,128)(2,1)S(1)}, bf16[128,768]{1,0:T(8,128)(2,1)S(1)}, u32[]{:S(2)}, u32[]{:S(2)}) collective-permute-start(bf16[128,768]{1,0:T(8,128)(2,1)S(1)} %collective-permute-done.30), channel_id=1, source_target_pairs={{0,4},{4,0},{8,12},{12,8},{16,20},{20,16},{24,28},{28,24},{1,5},{5... | collective-permute-start | bytes 589832 | tf_op jit(solution)/shard_map/ppermute | solution.py:260
  97.0 14.2 %collective-permute-start.21 = (bf16[256,768]{1,0:T(8,128)(2,1)S(1)}, bf16[256,768]{1,0:T(8,128)(2,1)S(1)}, u32[]{:S(2)}, u32[]{:S(2)}) collective-permute-start(bf16[256,768]{1,0:T(8,128)(2,1)S(1)} %collective-permute-done.19), channel_id=1, source_target_pairs={{0,8},{4,12},{8,16},{12,20},{16,24},{20,28},{24,0},{28,4},{1,9},{5... | collective-permute-start | bytes 1179656 | tf_op jit(solution)/shard_map/ppermute | solution.py:255
  97.6 17.9 %collective-permute-start.20 = (bf16[256,768]{1,0:T(8,128)(2,1)S(1)}, bf16[256,768]{1,0:T(8,128)(2,1)S(1)}, u32[]{:S(2)}, u32[]{:S(2)}) collective-permute-start(bf16[256,768]{1,0:T(8,128)(2,1)S(1)} %collective-permute-done.19), channel_id=1, source_target_pairs={{0,4},{4,0},{8,12},{12,8},{16,20},{20,16},{24,28},{28,24},{1,5},{5... | collective-permute-start | bytes 1179656 | tf_op jit(solution)/shard_map/ppermute | solution.py:260
  104.6 10.6 %collective-permute-start.33 = (bf16[128,768]{1,0:T(8,128)(2,1)S(1)}, bf16[128,768]{1,0:T(8,128)(2,1)S(1)}, u32[]{:S(2)}, u32[]{:S(2)}) collective-permute-start(bf16[128,768]{1,0:T(8,128)(2,1)S(1)} %collective-permute-done.32), channel_id=1, source_target_pairs={{0,4},{4,0},{8,12},{12,8},{16,20},{20,16},{24,28},{28,24},{1,5},{5... | collective-permute-start | bytes 589832 | tf_op jit(solution)/shard_map/ppermute | solution.py:260
  111.3 12.1 %collective-permute-start.23 = (bf16[256,768]{1,0:T(8,128)(2,1)S(1)}, bf16[256,768]{1,0:T(8,128)(2,1)S(1)}, u32[]{:S(2)}, u32[]{:S(2)}) collective-permute-start(bf16[256,768]{1,0:T(8,128)(2,1)S(1)} %collective-permute-done.21), channel_id=1, source_target_pairs={{0,8},{4,12},{8,16},{12,20},{16,24},{20,28},{24,0},{28,4},{1,9},{5... | collective-permute-start | bytes 1179656 | tf_op jit(solution)/shard_map/ppermute | solution.py:255
  111.3 10.8 %collective-permute-start.22 = (bf16[256,768]{1,0:T(8,128)(2,1)S(1)}, bf16[256,768]{1,0:T(8,128)(2,1)S(1)}, u32[]{:S(2)}, u32[]{:S(2)}) collective-permute-start(bf16[256,768]{1,0:T(8,128)(2,1)S(1)} %collective-permute-done.21), channel_id=1, source_target_pairs={{0,4},{4,0},{8,12},{12,8},{16,20},{20,16},{24,28},{28,24},{1,5},{5... | collective-permute-start | bytes 1179656 | tf_op jit(solution)/shard_map/ppermute | solution.py:260
  122.1 11.4 %collective-permute-start.24 = (bf16[256,768]{1,0:T(8,128)(2,1)S(1)}, bf16[256,768]{1,0:T(8,128)(2,1)S(1)}, u32[]{:S(2)}, u32[]{:S(2)}) collective-permute-start(bf16[256,768]{1,0:T(8,128)(2,1)S(1)} %collective-permute-done.22), channel_id=1, source_target_pairs={{0,8},{4,12},{8,16},{12,20},{16,24},{20,28},{24,0},{28,4},{1,9},{5... | collective-permute-start | bytes 1179656 | tf_op jit(solution)/shard_map/ppermute | solution.py:255
